TPU v7x, 32 devices: a whole 2x2x4 slice. The times are simulated.
32 devices in a mesh: dp: 4 (over y, core), ctx: 8 (over z, x).
Axes of the slice: x: 2, y: 2, z: 4, core: 2. Of those that a mesh axis runs over, the one named last changes fastest.
Arguments:
- inputs: bfloat16 [8, 1024, 768], P('dp', 'ctx'), may hold values from -6 to 6
- out_grad: bfloat16 [8, 1024, 768], P('dp', 'ctx'), may hold values from -6 to 6
- lengths: int32 [8], P('dp'), may hold values from 256 to 1024, as said below
- token_types: int32 [8, 1024], P('dp', 'ctx'), may hold values from 0 to 1
- query_weight: bfloat16 [768, 768], P(('dp', 'ctx')), may hold values from -0.21875 to 0.21875
- key_weight: bfloat16 [768, 768], P(('dp', 'ctx')), may hold values from -0.21875 to 0.21875
- value_weight: bfloat16 [768, 768], P(('dp', 'ctx')), may hold values from -0.21875 to 0.21875
- value_bias: bfloat16 [768], P(('dp', 'ctx')), may hold values from -1.796875 to 1.796875
- position_weight: bfloat16 [768, 768], P(('dp', 'ctx')), may hold values from -0.21875 to 0.21875
- content_bias: bfloat16 [768], P(('dp', 'ctx')), may hold values from -0.8984375 to 0.8984375
- position_bias: bfloat16 [768], P(('dp', 'ctx')), may hold values from -0.8984375 to 0.8984375
- type_bias: bfloat16 [768], P(('dp', 'ctx')), may hold values from -0.8984375 to 0.8984375
- type_embed: bfloat16 [2, 768], P(None, ('dp', 'ctx')), may hold values from -3 to 3
- output_weight: bfloat16 [768, 768], P(('dp', 'ctx')), may hold values from -0.875 to 0.875
- output_bias: bfloat16 [768], P(('dp', 'ctx')), may hold values from -1.796875 to 1.796875
- first_gain: bfloat16 [768], P(('dp', 'ctx')), may hold values from 0.5 to 1.5
- first_shift: bfloat16 [768], P(('dp', 'ctx')), may hold values from -1.796875 to 1.796875
- inner_weight: bfloat16 [768, 3072], P(('dp', 'ctx')), may hold values from -0.21875 to 0.21875
- inner_bias: bfloat16 [3072], P(('dp', 'ctx')), may hold values from -1.796875 to 1.796875
- outer_weight: bfloat16 [3072, 768], P(('dp', 'ctx')), may hold values from -0.109375 to 0.109375
- outer_bias: bfloat16 [768], P(('dp', 'ctx')), may hold values from -1.796875 to 1.796875
- second_gain: bfloat16 [768], P(('dp', 'ctx')), may hold values from 0.5 to 1.5
- second_shift: bfloat16 [768], P(('dp', 'ctx')), may hold values from -1.796875 to 1.796875
Outputs:
- output: bfloat16 [8, 1024, 768], P('dp', 'ctx')
- input_grad: bfloat16 [8, 1024, 768], P('dp', 'ctx')
- query_weight_grad: float32 [768, 768], P(('dp', 'ctx'))
- key_weight_grad: float32 [768, 768], P(('dp', 'ctx'))
- value_weight_grad: float32 [768, 768], P(('dp', 'ctx'))
- value_bias_grad: float32 [768], P(('dp', 'ctx'))
- position_weight_grad: float32 [768, 768], P(('dp', 'ctx'))
- content_bias_grad: float32 [768], P(('dp', 'ctx'))
- position_bias_grad: float32 [768], P(('dp', 'ctx'))
- type_bias_grad: float32 [768], P(('dp', 'ctx'))
- type_embed_grad: float32 [2, 768], P(None, ('dp', 'ctx'))
- output_weight_grad: float32 [768, 768], P(('dp', 'ctx'))
- output_bias_grad: float32 [768], P(('dp', 'ctx'))
- first_gain_grad: float32 [768], P(('dp', 'ctx'))
- first_shift_grad: float32 [768], P(('dp', 'ctx'))
- inner_weight_grad: float32 [768, 3072], P(('dp', 'ctx'))
- inner_bias_grad: float32 [3072], P(('dp', 'ctx'))
- outer_weight_grad: float32 [3072, 768], P(('dp', 'ctx'))
- outer_bias_grad: float32 [768], P(('dp', 'ctx'))
- second_gain_grad: float32 [768], P(('dp', 'ctx'))
- second_shift_grad: float32 [768], P(('dp', 'ctx'))
- mean_squares: float32 [8, 3], P('dp')
Inputs may be any that keep to these rules, and one draw needn't show every extreme that they name: Sequence s holds lengths[s] valid tokens in its first slots; sequence 0 is full.
All inputs are finite; a program needn't handle non-finite values.
Results may differ from a plain program's by a relative error of at most 0.038.
Values may be sent and summed in bfloat16 or wider, within the bound.
No kernel may reach another device: no remote copies, remote signals or barrier semaphores. Data moves between devices by JAX's collectives and lax.ppermute only.
A program may use at most 320 MiB of HBM per device.

v0:
```python
import functools

import jax
import jax.numpy as jnp
from jax import lax
from jax.experimental import pallas as pl
from jax.experimental.pallas import tpu as pltpu
from jax.sharding import PartitionSpec as P

DP = "dp"
CTX = "ctx"
ALL = (DP, CTX)
H = 12
DH = 64
KEY_BLOCK = 512
MICRO = 2
SEQ_MB = 1


epsilon = 1e-06
masked_score = -1e30
maximal_precision = lax.Precision.HIGHEST


def layer_norm(hidden, gain_values, shift_values):
    center = hidden - jnp.mean(hidden, axis=-1, keepdims=True)
    variance = jnp.mean(center * center, axis=-1, keepdims=True)
    return center * lax.rsqrt(variance + epsilon) * gain_values + shift_values


def gelu_tanh(inner):
    return jax.nn.gelu(inner, approximate=True)


def position_table(anchor, number, columns):
    offsets = (anchor + jnp.arange(number, dtype=jnp.int32)).astype(jnp.float32)
    exponent = 2.0 * jnp.arange(columns // 2, dtype=jnp.float32) / columns
    angles = offsets[:, None] * (10000.0 ** (-exponent))[None, :]
    return jnp.concatenate([jnp.sin(angles), jnp.cos(angles)], axis=1)


def skew_rows(unscaled_scores, keys_count):
    leading = unscaled_scores.shape[:-2]
    rows_count = unscaled_scores.shape[-2]
    span_cols = unscaled_scores.shape[-1]
    flattened = unscaled_scores.reshape(leading + (rows_count * span_cols,))
    flattened = jnp.pad(flattened, [(0, 0)] * len(leading) + [(0, rows_count)])
    return flattened.reshape(leading + (rows_count, span_cols + 1))[..., :keys_count][..., ::-1]


def unskew_rows(grads_block, span_cols):
    leading = grads_block.shape[:-2]
    rows_count = grads_block.shape[-2]
    keys_count = grads_block.shape[-1]
    padded = jnp.pad(
        grads_block[..., ::-1], [(0, 0)] * (len(leading) + 1) + [(0, span_cols + 1 - keys_count)]
    )
    flattened = padded.reshape(leading + (rows_count * (span_cols + 1),))
    return flattened[..., : rows_count * span_cols].reshape(leading + (rows_count, span_cols))


def block_scores(
    query_content,
    query_relative_term,
    type_terms,
    query_kinds,
    key_rows,
    key_kinds,
    key_valid,
    relative_rows,
):
    content = jnp.einsum(
        "bqhd,bkhd->bhqk", query_content, key_rows, preferred_element_type=jnp.float32
    )
    unscaled_scores = jnp.einsum(
        "uply,xly->ulpx", query_relative_term, relative_rows, preferred_element_type=jnp.float32
    )
    same_kind = query_kinds[:, :, None] == key_kinds[:, None, :]
    type_same = jnp.transpose(type_terms[..., 1], (0, 2, 1))[..., None]
    type_other = jnp.transpose(type_terms[..., 0], (0, 2, 1))[..., None]
    summed = (
        content
        + skew_rows(unscaled_scores, key_rows.shape[1])
        + jnp.where(same_kind[:, None], type_same, type_other)
    )
    return (jnp.where(key_valid[:, None, None, :], summed, masked_score), same_kind)


def block_grads(
    query_content,
    query_relative_term,
    type_terms,
    query_kinds,
    log_total,
    row_delta,
    grad_rows,
    key_rows,
    value_rows,
    key_kinds,
    key_valid,
    relative_rows,
):
    scores, same_kind = block_scores(
        query_content,
        query_relative_term,
        type_terms,
        query_kinds,
        key_rows,
        key_kinds,
        key_valid,
        relative_rows,
    )
    probability = jnp.exp(scores - log_total[..., None])
    value_grad = jnp.einsum(
        "bhqk,bqhd->bkhd",
        probability.astype(jnp.bfloat16),
        grad_rows,
        preferred_element_type=jnp.float32,
    )
    prob_grad = jnp.einsum(
        "bqhd,bkhd->bhqk", grad_rows, value_rows, preferred_element_type=jnp.float32
    )
    score_grad = (probability * (prob_grad - row_delta[..., None])).astype(jnp.bfloat16)
    content_grad = jnp.einsum(
        "bhqk,bkhd->bqhd", score_grad, key_rows, preferred_element_type=jnp.float32
    )
    key_grad = jnp.einsum(
        "bhqk,bqhd->bkhd", score_grad, query_content, preferred_element_type=jnp.float32
    )
    unscaled_gradient = unskew_rows(score_grad, relative_rows.shape[0])
    position_grad = jnp.einsum(
        "aioy,yin->aoin", unscaled_gradient, relative_rows, preferred_element_type=jnp.float32
    )
    rel_grad = jnp.einsum(
        "gcrj,grcl->jcl", unscaled_gradient, query_relative_term, preferred_element_type=jnp.float32
    )
    wide_grad = score_grad.astype(jnp.float32)
    same_sum = jnp.sum(jnp.where(same_kind[:, None], wide_grad, 0.0), axis=-1)
    other_sum = jnp.sum(jnp.where(same_kind[:, None], 0.0, wide_grad), axis=-1)
    type_grad = jnp.transpose(jnp.stack([other_sum, same_sum], axis=-1), (0, 2, 1, 3))
    return (content_grad, position_grad, type_grad, key_grad, value_grad, rel_grad)


def per_device(
    inputs,
    out_grad,
    lengths,
    token_types,
    query_weight,
    key_weight,
    value_weight,
    value_bias,
    position_weight,
    content_bias,
    position_bias,
    type_bias,
    type_embed,
    output_weight,
    output_bias,
    first_gain,
    first_shift,
    inner_weight,
    inner_bias,
    outer_weight,
    outer_bias,
    second_gain,
    second_shift,
):
    stretch = inputs.shape[1]
    width = inputs.shape[2]
    seq_len = stretch * lax.axis_size(CTX)
    stretch_start = lax.axis_index(CTX) * stretch
    window = seq_len + stretch - 1
    scale_query = DH ** (-0.5)
    own_positions = stretch_start + jnp.arange(stretch, dtype=jnp.int32)
    table_forward = position_table(stretch_start - seq_len + 1, window, width).astype(jnp.bfloat16)
    outputs_list = []
    input_grads = []
    stat_rows = []
    grads_total = None
    rel_total = jnp.zeros((window, width), jnp.float32)
    for micro_index in range(MICRO):
        first_seq = micro_index * SEQ_MB
        sequence_input = inputs[first_seq : first_seq + SEQ_MB]
        seq_grad = out_grad[first_seq : first_seq + SEQ_MB]
        seq_kinds = token_types[first_seq : first_seq + SEQ_MB].astype(jnp.bfloat16)
        length_col = lengths[first_seq : first_seq + SEQ_MB][:, None]
        seq_count = sequence_input.shape[0]
        heads_shape = (seq_count, stretch, H, DH)
        full_shape = (seq_count, seq_len, H, DH)
        row_valid = (own_positions[None, :] < length_col).astype(jnp.float32)[..., None]
        gathered = (
            lax.all_gather(query_weight, ALL, axis=0, tiled=True),
            lax.all_gather(key_weight, ALL, axis=0, tiled=True),
            lax.all_gather(value_weight, ALL, axis=0, tiled=True),
            lax.all_gather(value_bias, ALL, axis=0, tiled=True),
            lax.all_gather(position_weight, ALL, axis=0, tiled=True),
            lax.all_gather(content_bias, ALL, axis=0, tiled=True),
            lax.all_gather(position_bias, ALL, axis=0, tiled=True),
            lax.all_gather(type_bias, ALL, axis=0, tiled=True),
            lax.all_gather(type_embed, ALL, axis=1, tiled=True),
            lax.all_gather(output_weight, ALL, axis=0, tiled=True),
            lax.all_gather(output_bias, ALL, axis=0, tiled=True),
            lax.all_gather(first_gain, ALL, axis=0, tiled=True),
            lax.all_gather(first_shift, ALL, axis=0, tiled=True),
            lax.all_gather(inner_weight, ALL, axis=0, tiled=True),
            lax.all_gather(inner_bias, ALL, axis=0, tiled=True),
            lax.all_gather(outer_weight, ALL, axis=0, tiled=True),
            lax.all_gather(outer_bias, ALL, axis=0, tiled=True),
            lax.all_gather(second_gain, ALL, axis=0, tiled=True),
            lax.all_gather(second_shift, ALL, axis=0, tiled=True),
        )
        (
            query_matrix,
            key_matrix,
            value_matrix,
            value_add,
            position_mat,
            content_add,
            position_add,
            type_add,
            type_table,
            output_matrix,
            output_add,
            gain_one,
            shift_one,
            inner_matrix,
            inner_add,
            outer_matrix,
            outer_add,
            gain_two,
            shift_two,
        ) = gathered
        scaled = (
            jnp.dot(sequence_input, query_matrix, preferred_element_type=jnp.float32) * scale_query
        )
        query_content = (
            (scaled + content_add.astype(jnp.float32)).astype(jnp.bfloat16).reshape(heads_shape)
        )
        query_relative_term = (
            (scaled + position_add.astype(jnp.float32)).astype(jnp.bfloat16).reshape(heads_shape)
        )
        with_type = (scaled + type_add.astype(jnp.float32)).reshape(heads_shape)
        type_heads = type_table.astype(jnp.float32).reshape(2, H, DH)
        type_terms = jnp.einsum(
            "bqhd,shd->bqhs", with_type, type_heads, precision=maximal_precision
        )
        key_rows = jnp.dot(sequence_input, key_matrix, preferred_element_type=jnp.float32).astype(
            jnp.bfloat16
        )
        value_rows = (
            jnp.dot(sequence_input, value_matrix, preferred_element_type=jnp.float32)
            + value_add.astype(jnp.float32)
        ).astype(jnp.bfloat16)
        rel_forward = (
            jnp.dot(table_forward, position_mat, preferred_element_type=jnp.float32)
            .astype(jnp.bfloat16)
            .reshape(window, H, DH)
        )
        start_state = (
            jnp.full((seq_count, H, stretch), masked_score, jnp.float32),
            jnp.zeros((seq_count, H, stretch), jnp.float32),
            jnp.zeros(heads_shape, jnp.float32),
        )
        piece_keys = lax.all_gather(key_rows, CTX, axis=1, tiled=True)
        piece_values = lax.all_gather(value_rows, CTX, axis=1, tiled=True)
        piece_kinds = lax.all_gather(seq_kinds, CTX, axis=1, tiled=True)
        number = piece_keys.shape[1]
        block_rows = KEY_BLOCK

        def one_block(running, offset):
            run_max, run_total, run_acc = running
            part_keys = lax.dynamic_slice_in_dim(piece_keys, offset, block_rows, 1).reshape(
                seq_count, block_rows, H, DH
            )
            part_values = lax.dynamic_slice_in_dim(piece_values, offset, block_rows, 1).reshape(
                seq_count, block_rows, H, DH
            )
            part_kinds = lax.dynamic_slice_in_dim(piece_kinds, offset, block_rows, 1)
            relative_rows = lax.dynamic_slice_in_dim(
                rel_forward, seq_len - offset - block_rows, stretch + block_rows - 1, 0
            )
            key_valid = (offset + jnp.arange(block_rows, dtype=jnp.int32))[None, :] < length_col
            scores, same_kind = block_scores(
                query_content,
                query_relative_term,
                type_terms,
                seq_kinds,
                part_keys,
                part_kinds,
                key_valid,
                relative_rows,
            )
            new_max = jnp.maximum(run_max, jnp.max(scores, axis=-1))
            factor = jnp.exp(run_max - new_max)
            weights_block = jnp.exp(scores - new_max[..., None])
            run_total = run_total * factor + jnp.sum(weights_block, axis=-1)
            mixed_rows = jnp.einsum(
                "bhqk,bkhd->bqhd",
                weights_block.astype(jnp.bfloat16),
                part_values,
                preferred_element_type=jnp.float32,
            )
            run_acc = run_acc * jnp.transpose(factor, (0, 2, 1))[..., None] + mixed_rows
            return ((new_max, run_total, run_acc), None)

        offsets = jnp.arange(number // block_rows, dtype=jnp.int32) * block_rows
        result_state, unused = lax.scan(one_block, start_state, offsets)
        run_max, run_total, run_acc = result_state
        log_total = run_max + jnp.log(run_total)
        attended = run_acc / jnp.transpose(run_total, (0, 2, 1))[..., None]
        attended_reduced = attended.astype(jnp.bfloat16).reshape(seq_count, stretch, width)
        attn_out = jnp.dot(
            attended_reduced, output_matrix, preferred_element_type=jnp.float32
        ) + output_add.astype(jnp.float32)
        first_sum = sequence_input.astype(jnp.float32) + attn_out
        normed = layer_norm(first_sum, gain_one.astype(jnp.float32), shift_one.astype(jnp.float32))
        normed_reduced = normed.astype(jnp.bfloat16)
        inner = jnp.dot(
            normed_reduced, inner_matrix, preferred_element_type=jnp.float32
        ) + inner_add.astype(jnp.float32)
        activated_reduced = gelu_tanh(inner).astype(jnp.bfloat16)
        outer = jnp.dot(
            activated_reduced, outer_matrix, preferred_element_type=jnp.float32
        ) + outer_add.astype(jnp.float32)
        second_sum = normed + outer
        result = layer_norm(second_sum, gain_two.astype(jnp.float32), shift_two.astype(jnp.float32))
        outputs_list.append(result.astype(jnp.bfloat16))
        stat_rows.append(
            jnp.stack(
                [
                    jnp.sum(first_sum * first_sum * row_valid, axis=(1, 2)),
                    jnp.sum(attn_out * attn_out * row_valid, axis=(1, 2)),
                    jnp.sum(outer * outer * row_valid, axis=(1, 2)),
                ],
                axis=1,
            )
        )
        back_set = (
            lax.all_gather(query_weight, ALL, axis=0, tiled=True),
            lax.all_gather(key_weight, ALL, axis=0, tiled=True),
            lax.all_gather(value_weight, ALL, axis=0, tiled=True),
            lax.all_gather(value_bias, ALL, axis=0, tiled=True),
            lax.all_gather(position_weight, ALL, axis=0, tiled=True),
            lax.all_gather(content_bias, ALL, axis=0, tiled=True),
            lax.all_gather(position_bias, ALL, axis=0, tiled=True),
            lax.all_gather(type_bias, ALL, axis=0, tiled=True),
            lax.all_gather(type_embed, ALL, axis=1, tiled=True),
            lax.all_gather(output_weight, ALL, axis=0, tiled=True),
            lax.all_gather(output_bias, ALL, axis=0, tiled=True),
            lax.all_gather(first_gain, ALL, axis=0, tiled=True),
            lax.all_gather(first_shift, ALL, axis=0, tiled=True),
            lax.all_gather(inner_weight, ALL, axis=0, tiled=True),
            lax.all_gather(inner_bias, ALL, axis=0, tiled=True),
            lax.all_gather(outer_weight, ALL, axis=0, tiled=True),
            lax.all_gather(outer_bias, ALL, axis=0, tiled=True),
            lax.all_gather(second_gain, ALL, axis=0, tiled=True),
            lax.all_gather(second_shift, ALL, axis=0, tiled=True),
        )
        (
            query_matrix,
            key_matrix,
            value_matrix,
            value_add,
            position_mat,
            content_add,
            position_add,
            type_add,
            type_table,
            output_matrix,
            output_add,
            gain_one,
            shift_one,
            inner_matrix,
            inner_add,
            outer_matrix,
            outer_add,
            gain_two,
            shift_two,
        ) = back_set
        type_heads = type_table.astype(jnp.float32).reshape(2, H, DH)
        cotangent = seq_grad.astype(jnp.float32) * row_valid
        unused_two, second_back = jax.vjp(
            layer_norm, second_sum, gain_two.astype(jnp.float32), shift_two.astype(jnp.float32)
        )
        second_grad, gain_two_grad, shift_two_grad = second_back(cotangent)
        outer_reduced = second_grad.astype(jnp.bfloat16)
        outer_add_grad = jnp.sum(outer_reduced.astype(jnp.float32), axis=(0, 1))
        outer_mat_grad = jnp.einsum(
            "hpi,hpt->it", activated_reduced, outer_reduced, preferred_element_type=jnp.float32
        )
        activated_grad = jnp.einsum(
            "unk,rk->unr", outer_reduced, outer_matrix, preferred_element_type=jnp.float32
        )
        unused_three, gelu_back = jax.vjp(gelu_tanh, inner)
        inner_reduced = gelu_back(activated_grad)[0].astype(jnp.bfloat16)
        inner_add_grad = jnp.sum(inner_reduced.astype(jnp.float32), axis=(0, 1))
        inner_mat_grad = jnp.einsum(
            "psu,psy->uy", normed_reduced, inner_reduced, preferred_element_type=jnp.float32
        )
        normed_grad = second_grad + jnp.einsum(
            "tma,ra->tmr", inner_reduced, inner_matrix, preferred_element_type=jnp.float32
        )
        unused_four, first_back = jax.vjp(
            layer_norm, first_sum, gain_one.astype(jnp.float32), shift_one.astype(jnp.float32)
        )
        first_grad, gain_one_grad, shift_one_grad = first_back(normed_grad)
        attention_reduced = first_grad.astype(jnp.bfloat16)
        output_add_grad = jnp.sum(attention_reduced.astype(jnp.float32), axis=(0, 1))
        output_mat_grad = jnp.einsum(
            "yim,yig->mg", attended_reduced, attention_reduced, preferred_element_type=jnp.float32
        )
        grad_rows = (
            jnp.einsum(
                "jcy,py->jcp", attention_reduced, output_matrix, preferred_element_type=jnp.float32
            )
            .astype(jnp.bfloat16)
            .reshape(heads_shape)
        )
        row_delta = jnp.einsum(
            "bqhd,bqhd->bhq", grad_rows.astype(jnp.float32), attended, precision=maximal_precision
        )
        all_keys, all_values, all_kinds = (
            lax.all_gather(key_rows, CTX, axis=1, tiled=True),
            lax.all_gather(value_rows, CTX, axis=1, tiled=True),
            lax.all_gather(seq_kinds, CTX, axis=1, tiled=True),
        )

        def key_step(running, key_start):
            content_acc, position_acc, type_acc, key_acc, value_acc, rel_acc = running
            part_keys = lax.dynamic_slice_in_dim(all_keys, key_start, KEY_BLOCK, 1).reshape(
                seq_count, KEY_BLOCK, H, DH
            )
            part_values = lax.dynamic_slice_in_dim(all_values, key_start, KEY_BLOCK, 1).reshape(
                seq_count, KEY_BLOCK, H, DH
            )
            part_kinds = lax.dynamic_slice_in_dim(all_kinds, key_start, KEY_BLOCK, 1)
            rel_start = seq_len - key_start - KEY_BLOCK
            relative_rows = lax.dynamic_slice_in_dim(
                rel_forward, rel_start, stretch + KEY_BLOCK - 1, 0
            )
            key_valid = (key_start + jnp.arange(KEY_BLOCK, dtype=jnp.int32))[None, :] < length_col
            pieces = block_grads(
                query_content,
                query_relative_term,
                type_terms,
                seq_kinds,
                log_total,
                row_delta,
                grad_rows,
                part_keys,
                part_values,
                part_kinds,
                key_valid,
                relative_rows,
            )
            content_part, position_part, type_part, key_part, value_part, rel_part = pieces
            key_acc = lax.dynamic_update_slice_in_dim(key_acc, key_part, key_start, 1)
            value_acc = lax.dynamic_update_slice_in_dim(value_acc, value_part, key_start, 1)
            rel_old = lax.dynamic_slice_in_dim(rel_acc, rel_start, stretch + KEY_BLOCK - 1, 0)
            rel_acc = lax.dynamic_update_slice_in_dim(rel_acc, rel_old + rel_part, rel_start, 0)
            return (
                (
                    content_acc + content_part,
                    position_acc + position_part,
                    type_acc + type_part,
                    key_acc,
                    value_acc,
                    rel_acc,
                ),
                None,
            )

        start_grads = (
            jnp.zeros(heads_shape, jnp.float32),
            jnp.zeros(heads_shape, jnp.float32),
            jnp.zeros((seq_count, stretch, H, 2), jnp.float32),
            jnp.zeros(full_shape, jnp.float32),
            jnp.zeros(full_shape, jnp.float32),
            jnp.zeros((window, H, DH), jnp.float32),
        )
        final_grads, unused_five = lax.scan(
            key_step, start_grads, jnp.arange(seq_len // KEY_BLOCK, dtype=jnp.int32) * KEY_BLOCK
        )
        content_grad, position_grad, type_grad, key_all, value_all, rel_grad = final_grads
        key_grad, value_grad = (
            lax.psum_scatter(
                key_all.astype(jnp.bfloat16), CTX, scatter_dimension=1, tiled=True
            ).astype(jnp.float32),
            lax.psum_scatter(
                value_all.astype(jnp.bfloat16), CTX, scatter_dimension=1, tiled=True
            ).astype(jnp.float32),
        )
        type_part_grad = jnp.einsum(
            "bqhs,shd->bqhd", type_grad, type_heads, precision=maximal_precision
        )
        query_grad = content_grad + position_grad + type_part_grad
        content_add_grad = jnp.sum(content_grad, axis=(0, 1)).reshape(width)
        position_add_grad = jnp.sum(position_grad, axis=(0, 1)).reshape(width)
        type_add_grad = jnp.sum(type_part_grad, axis=(0, 1)).reshape(width)
        rel_total = rel_total + rel_grad.reshape(window, width)
        query_reduced = query_grad.astype(jnp.bfloat16).reshape(seq_count, stretch, width)
        key_reduced = key_grad.astype(jnp.bfloat16).reshape(seq_count, stretch, width)
        value_reduced = value_grad.astype(jnp.bfloat16).reshape(seq_count, stretch, width)
        type_table_grad = jnp.einsum(
            "bqhs,bqhd->shd", type_grad, with_type, precision=maximal_precision
        ).reshape(2, width)
        query_mat_grad = (
            jnp.einsum(
                "orh,org->hg", sequence_input, query_reduced, preferred_element_type=jnp.float32
            )
            * scale_query
        )
        key_mat_grad = jnp.einsum(
            "orh,org->hg", sequence_input, key_reduced, preferred_element_type=jnp.float32
        )
        value_mat_grad = jnp.einsum(
            "orh,org->hg", sequence_input, value_reduced, preferred_element_type=jnp.float32
        )
        value_add_grad = jnp.sum(value_reduced.astype(jnp.float32), axis=(0, 1))
        input_grad = (
            first_grad
            + jnp.einsum(
                "sux,fx->suf", query_reduced, query_matrix, preferred_element_type=jnp.float32
            )
            * scale_query
            + jnp.einsum("sux,fx->suf", key_reduced, key_matrix, preferred_element_type=jnp.float32)
            + jnp.einsum(
                "sux,fx->suf", value_reduced, value_matrix, preferred_element_type=jnp.float32
            )
        )
        input_grads.append(input_grad.astype(jnp.bfloat16))
        micro_grads = (
            query_mat_grad,
            key_mat_grad,
            value_mat_grad,
            value_add_grad,
            content_add_grad,
            position_add_grad,
            type_add_grad,
            type_table_grad,
            output_mat_grad,
            output_add_grad,
            gain_one_grad,
            shift_one_grad,
            inner_mat_grad,
            inner_add_grad,
            outer_mat_grad,
            outer_add_grad,
            gain_two_grad,
            shift_two_grad,
        )
        if grads_total is None:
            grads_total = micro_grads
        else:
            grads_total = jax.tree.map(jnp.add, grads_total, micro_grads)
    rel_high = rel_total.astype(jnp.bfloat16)
    rel_rest = (rel_total - rel_high.astype(jnp.float32)).astype(jnp.bfloat16)
    contract_rows = (((0,), (0,)), ((), ()))
    position_mat_grad = lax.dot_general(
        table_forward, rel_high, contract_rows, preferred_element_type=jnp.float32
    ) + lax.dot_general(table_forward, rel_rest, contract_rows, preferred_element_type=jnp.float32)
    (
        query_total,
        key_total,
        value_total,
        value_add_total,
        content_total,
        position_total,
        type_total,
        table_total,
        output_total,
        output_add_total,
        gain_one_total,
        shift_one_total,
        inner_total,
        inner_add_total,
        outer_total,
        outer_add_total,
        gain_two_total,
        shift_two_total,
    ) = grads_total
    reduced = (
        lax.psum_scatter(query_total, ALL, scatter_dimension=0, tiled=True),
        lax.psum_scatter(key_total, ALL, scatter_dimension=0, tiled=True),
        lax.psum_scatter(value_total, ALL, scatter_dimension=0, tiled=True),
        lax.psum_scatter(value_add_total, ALL, scatter_dimension=0, tiled=True),
        lax.psum_scatter(position_mat_grad, ALL, scatter_dimension=0, tiled=True),
        lax.psum_scatter(content_total, ALL, scatter_dimension=0, tiled=True),
        lax.psum_scatter(position_total, ALL, scatter_dimension=0, tiled=True),
        lax.psum_scatter(type_total, ALL, scatter_dimension=0, tiled=True),
        lax.psum_scatter(table_total, ALL, scatter_dimension=1, tiled=True),
        lax.psum_scatter(output_total, ALL, scatter_dimension=0, tiled=True),
        lax.psum_scatter(output_add_total, ALL, scatter_dimension=0, tiled=True),
        lax.psum_scatter(gain_one_total, ALL, scatter_dimension=0, tiled=True),
        lax.psum_scatter(shift_one_total, ALL, scatter_dimension=0, tiled=True),
        lax.psum_scatter(inner_total, ALL, scatter_dimension=0, tiled=True),
        lax.psum_scatter(inner_add_total, ALL, scatter_dimension=0, tiled=True),
        lax.psum_scatter(outer_total, ALL, scatter_dimension=0, tiled=True),
        lax.psum_scatter(outer_add_total, ALL, scatter_dimension=0, tiled=True),
        lax.psum_scatter(gain_two_total, ALL, scatter_dimension=0, tiled=True),
        lax.psum_scatter(shift_two_total, ALL, scatter_dimension=0, tiled=True),
    )
    sums_all = lax.psum(jnp.concatenate(stat_rows, axis=0), CTX)
    mean_squares = sums_all / (lengths.astype(jnp.float32)[:, None] * width)
    return (
        (jnp.concatenate(outputs_list, axis=0), jnp.concatenate(input_grads, axis=0))
        + tuple(reduced)
        + (mean_squares,)
    )


LANES = 128
BF = jnp.bfloat16
F32 = jnp.float32
ROWS_CC = (((1,), (1,)), ((), ()))
COLS_CC = (((0,), (0,)), ((), ()))
ROWCOL = (((1,), (0,)), ((), ()))


def mm(a, b, dims):
    return lax.dot_general(a, b, dims, preferred_element_type=F32)


def split3(v):
    hi = v.astype(BF).astype(F32)
    mid = (v - hi).astype(BF).astype(F32)
    lo = (v - hi - mid).astype(BF).astype(F32)
    return hi, mid, lo


def attention_forward_kernel(tile, x_ref, w_ref, vec_ref, kext_ref, trig_ref,
                             att_ref, qt_ref, kb_ref, v1_ref, qp_ref, save_ref, scl_ref, wh_ref, kt_ref):
    step = pl.program_id(1)
    rows = x_ref.shape[0]
    width = x_ref.shape[1]
    half = width // 2
    lane = lax.broadcasted_iota(jnp.int32, (tile, LANES), 1)
    low = lane < DH

    @pl.when((pl.program_id(0) == 0) & (step == 0))
    def _():
        kt_ref[:, :width] = trig_ref[...].astype(BF)

    @pl.when(step == 0)
    def _():
        vec = vec_ref[0]
        w = w_ref[...].astype(F32).reshape(width, 2 * LANES).astype(BF)
        wh_ref[0] = w
        w_lane = lax.broadcasted_iota(jnp.int32, (width, LANES), 1)
        w_pos = jnp.where(w_lane < DH, pltpu.roll(w[:, LANES:].astype(F32), DH, 1), 0.0).astype(BF)

        def body(i, carry):
            at = pl.ds(pl.multiple_of(i * tile, tile), tile)
            proj = mm(x_ref[at, :], w, ROWCOL)
            kext = kext_ref[at, :].astype(F32)
            kind = kext[:, DH + 3:DH + 4]
            scaled = jnp.where(low, proj[:, :LANES] * DH ** -0.5, 0.0)
            scl_ref[0, at, :] = scaled
            kb = jnp.where(low, pltpu.roll(proj[:, :LANES], DH, 1), kext).astype(BF)
            kb_ref[0, at, :] = kb
            kt_ref[at, width:] = kb
            one_v = (lane >= DH) & (lane < DH + 3)
            v1_ref[0, at, :] = jnp.where(low, proj[:, LANES:] + vec[3:4, :], jnp.where(one_v, 1.0, 0.0)).astype(BF)
            with_type = scaled + vec[2:3, :]
            term0 = jnp.sum(with_type * vec[4:5, :], axis=1, keepdims=True)
            term1 = jnp.sum(with_type * vec[5:6, :], axis=1, keepdims=True)
            base = jnp.where(kind > 0.5, term0, term1)
            slope = jnp.where(kind > 0.5, term1 - term0, term0 - term1)
            b_hi, b_mid, b_lo = split3(base)
            s_hi, s_mid, s_lo = split3(slope)
            ext = jnp.where(lane == DH, b_hi, 0.0)
            ext = jnp.where(lane == DH + 1, b_mid, ext)
            ext = jnp.where(lane == DH + 2, b_lo, ext)
            ext = jnp.where(lane == DH + 3, s_hi, ext)
            ext = jnp.where(lane == DH + 4, s_mid, ext)
            ext = jnp.where(lane == DH + 5, 1.0, ext)
            qt_ref[0, at, width:] = jnp.where(low, scaled + vec[0:1, :], ext).astype(BF)
            qp = jnp.where(low, scaled + vec[1:2, :], 0.0).astype(BF)
            qp_ref[0, at, :] = qp
            grow = mm(qp, w_pos, ROWS_CC)
            q_sin = grow[:, :half]
            q_cos = grow[:, half:]
            c = trig_ref[at, :half]
            s = trig_ref[at, half:]
            qt_ref[0, at, :half] = (q_sin * s + q_cos * c).astype(BF)
            qt_ref[0, at, half:width] = (q_cos * s - q_sin * c).astype(BF)
            return carry

        lax.fori_loop(0, rows // tile, body, 0)

    at = pl.ds(pl.multiple_of(step * tile, tile), tile)
    scores = mm(qt_ref[0, at, :], kt_ref[...], ROWS_CC)
    top = jnp.max(scores, axis=1, keepdims=True)
    prob = jnp.exp(scores - top)
    mixed = mm(prob.astype(BF), v1_ref[0], ROWCOL)
    total = mixed[:, DH:DH + 1]
    att = mixed / total
    save_ref[0] = jnp.where(low, att, top + jnp.log(total))
    att_t = jnp.transpose(att)[:DH, :].astype(BF)
    for i in range(tile // LANES):
        att_ref[i] = att_t[:, i * LANES:(i + 1) * LANES]


def attention_backward_kernel(tile, do_ref, x_ref, w_ref, vec_ref, kext_ref, trig_ref,
                              qt_ref, kb_ref, v1_ref, qp_ref, save_ref, scl_ref,
                              dx_ref, dw_ref, small_ref,
                              kt_ref, q_ref, dk_acc, dv_acc, d_ref, dwp_ref, dx_acc):
    step = pl.program_id(1)
    width = trig_ref.shape[1]
    half = width // 2
    lane = lax.broadcasted_iota(jnp.int32, (tile, LANES), 1)
    low = lane < DH

    @pl.when((pl.program_id(0) == 0) & (step == 0))
    def _():
        kt_ref[:, :width] = trig_ref[...].astype(BF)

    @pl.when(step == 0)
    def _():
        kt_ref[:, width:] = kb_ref[0]
        dk_acc[...] = jnp.zeros_like(dk_acc)
        dv_acc[...] = jnp.zeros_like(dv_acc)
        dwp_ref[...] = jnp.zeros_like(dwp_ref)
        small_ref[...] = jnp.zeros_like(small_ref)

    at = pl.ds(pl.multiple_of(step * tile, tile), tile)
    w = w_ref[0]
    w_lane = lax.broadcasted_iota(jnp.int32, (width, LANES), 1)
    w_pos = jnp.where(w_lane < DH, pltpu.roll(w[:, LANES:].astype(F32), DH, 1), 0.0).astype(BF)
    save = save_ref[0]
    lse = save[:, DH:DH + 1]
    do_t = jnp.concatenate([do_ref[i] for i in range(tile // LANES)], axis=1).astype(F32)
    d_out = jnp.transpose(jnp.concatenate([do_t, jnp.zeros_like(do_t)], axis=0))
    delta = jnp.sum(d_out * save, axis=1, keepdims=True)
    l_hi, l_mid, l_lo = split3(-lse)
    d_hi, d_mid, d_lo = split3(-delta)
    q_block = qt_ref[0, :, width:].astype(F32)
    q_ref[:, :width] = qt_ref[0, :, :width]
    q_block = jnp.where(lane == DH + 6, l_hi, q_block)
    q_block = jnp.where(lane == DH + 7, l_mid, q_block)
    q_block = jnp.where(lane == DH + 8, l_lo, q_block)
    q_block = q_block.astype(BF)
    q_ref[:, width:] = q_block
    ext = jnp.where(lane == DH, d_hi, d_out)
    ext = jnp.where(lane == DH + 1, d_mid, ext)
    ext = jnp.where(lane == DH + 2, d_lo, ext)
    d_ext = ext.astype(BF)
    prob = jnp.exp(mm(q_ref[...], kt_ref[...], ROWS_CC))
    dv_acc[...] += mm(d_ext, prob.astype(BF), COLS_CC)
    d_score = (prob * mm(d_ext, v1_ref[0], ROWS_CC)).astype(BF)
    dk_acc[...] += mm(q_block, d_score, COLS_CC)
    dq = mm(d_score, kt_ref[...], ROWCOL)
    c = trig_ref[at, :half]
    s = trig_ref[at, half:]
    du_c = dq[:, :half]
    du_s = dq[:, half:width]
    back = jnp.concatenate([s * du_c - c * du_s, c * du_c + s * du_s], axis=1).astype(BF)
    d_block = dq[:, width:]
    d_pos = mm(back, w_pos, ROWCOL)
    dwp_ref[...] += mm(qp_ref[0], back, COLS_CC)[:DH, :]
    vec = vec_ref[0]
    kind = kext_ref[...][:, DH + 3:DH + 4].astype(F32)
    every = d_block[:, DH:DH + 1]
    ones = d_block[:, DH + 3:DH + 4]
    g_same = jnp.where(kind > 0.5, ones, every - ones)
    g_other = jnp.where(kind > 0.5, every - ones, ones)
    type_part = g_other * vec[4:5, :] + g_same * vec[5:6, :]
    d_content = jnp.where(low, d_block, 0.0)
    with_type = jnp.where(low, scl_ref[0] + vec[2:3, :], 0.0)
    d_scaled = d_content + d_pos + type_part
    d_ref[:DH, at] = (jnp.transpose(d_scaled)[:DH, :] * DH ** -0.5).astype(BF)
    sums = [jnp.sum(v, axis=0, keepdims=True) for v in
            (d_content, d_pos, type_part, g_other * with_type, g_same * with_type)]
    small_ref[0] += jnp.concatenate(sums + [jnp.zeros((3, LANES), F32)], axis=0)

    @pl.when(step == pl.num_programs(1) - 1)
    def _():
        d_ref[DH:2 * DH] = dk_acc[:DH, :].astype(BF)
        dv_low = dv_acc[:DH, :].astype(BF)
        d_ref[2 * DH:] = dv_low
        dv_sum = jnp.sum(dv_low.astype(F32), axis=1, keepdims=True)
        dv_sum = jnp.transpose(jnp.broadcast_to(jnp.concatenate([dv_sum, dv_sum], axis=0), (LANES, LANES)))
        small_ref[0, 5:6, :] = dv_sum[:1, :]
        d_wt = mm(d_ref[...], x_ref[...], ROWCOL)
        d_w = jnp.transpose(jnp.concatenate([d_wt, dwp_ref[...]], axis=0))
        shard = dw_ref.shape[1]
        for i in range(dw_ref.shape[0]):
            dw_ref[i] = d_w[i * shard:(i + 1) * shard, :].astype(BF)
        d_x = lax.dot_general(d_ref[...], w_ref[0][:, :3 * DH], (((0,), (1,)), ((), ())), preferred_element_type=F32)

        @pl.when(pl.program_id(0) == 0)
        def _():
            dx_acc[...] = d_x

        @pl.when(pl.program_id(0) > 0)
        def _():
            dx_acc[...] += d_x

        @pl.when(pl.program_id(0) == pl.num_programs(0) - 1)
        def _():
            dx_ref[...] = dx_acc[...].astype(BF)


def attention_forward(x, w_block, first, count, heads, vec, kext, trig, previous=(), tile=512):
    rows, width = x.shape
    owners = w_block.shape[0]
    shard = width // owners
    full = width + LANES
    per_head = lambda shape: pl.BlockSpec((1,) + shape, lambda h, t: (first + h, 0, 0))
    fixed = lambda shape: pl.BlockSpec(shape, lambda h, t: (0, 0))
    flops = count * rows * 2 * (width * 256 + rows * full + rows * LANES)
    S = jax.ShapeDtypeStruct
    kernel = functools.partial(attention_forward_kernel, tile)
    skip = len(previous)
    return pl.pallas_call(
        lambda *refs: kernel(*refs[:5], *refs[5 + skip:]),
        grid=(count, rows // tile),
        in_specs=[fixed((rows, width)), pl.BlockSpec((owners, shard, 2 * LANES), lambda h, t: (0, first + h, 0)),
                  per_head((8, LANES)), fixed((rows, LANES)), fixed((rows, width))]
        + [pl.BlockSpec(memory_space=pl.ANY)] * skip,
        out_specs=[pl.BlockSpec((tile // LANES, DH, LANES), lambda h, t: (t, first + h, 0)),
                   per_head((rows, full)), per_head((rows, LANES)), per_head((rows, LANES)),
                   per_head((rows, LANES)),
                   pl.BlockSpec((1, tile, LANES), lambda h, t: (first + h, t, 0)),
                   per_head((rows, LANES)), per_head((width, 2 * LANES))],
        out_shape=[S((rows // LANES, heads * DH, LANES), BF), S((heads, rows, full), BF),
                   S((heads, rows, LANES), BF), S((heads, rows, LANES), BF), S((heads, rows, LANES), BF),
                   S((heads, rows, LANES), F32), S((heads, rows, LANES), F32), S((heads, width, 2 * LANES), BF)],
        input_output_aliases={5 + i: i for i in range(skip)},
        scratch_shapes=[pltpu.VMEM((rows, full), BF)],
        compiler_params=pltpu.CompilerParams(dimension_semantics=("arbitrary", "arbitrary"),
                                             vmem_limit_bytes=56 * 2 ** 20),
        cost_estimate=pl.CostEstimate(flops=flops, bytes_accessed=rows * width * 16, transcendentals=count * rows * rows),
        name="attention_forward",
    )(x, w_block, vec, kext, trig, *previous)


def attention_backward(d_out, x, w, vec, kext, trig, qt, kb, v1, qp, save, scl, owners, block_rows, tile=512):
    heads, rows, full = qt.shape
    width = full - LANES
    shard = width // owners
    per_head = lambda shape: pl.BlockSpec((1,) + shape, lambda h, t: (h, 0, 0))
    per_tile = lambda cols: pl.BlockSpec((1, tile, cols), lambda h, t: (h, t, 0))
    fixed = lambda shape: pl.BlockSpec(shape, lambda h, t: (0, 0))
    flops = heads * rows * 2 * (2 * rows * full + 3 * rows * LANES)
    return pl.pallas_call(
        functools.partial(attention_backward_kernel, tile),
        grid=(heads, rows // tile),
        in_specs=[pl.BlockSpec((tile // LANES, DH, LANES), lambda h, t: (t, h, 0)), fixed((rows, width)),
                  per_head((width, 256)), per_head((8, LANES)),
                  pl.BlockSpec((tile, LANES), lambda h, t: (t, 0)), fixed((rows, width)),
                  per_tile(full), per_head((rows, LANES)), per_head((rows, LANES)), per_tile(LANES),
                  per_tile(LANES), per_tile(LANES)],
        out_specs=[fixed((rows, width)), pl.BlockSpec((owners, shard, 2 * LANES), lambda h, t: (0, h, 0)),
                   per_head((8, LANES))],
        out_shape=[jax.ShapeDtypeStruct((rows, width), BF),
                   jax.ShapeDtypeStruct((owners, block_rows, 2 * LANES), BF),
                   jax.ShapeDtypeStruct((heads, 8, LANES), F32)],
        scratch_shapes=[pltpu.VMEM((rows, full), BF), pltpu.VMEM((tile, full), BF),
                        pltpu.VMEM((LANES, rows), F32), pltpu.VMEM((LANES, rows), F32),
                        pltpu.VMEM((3 * DH, rows), BF), pltpu.VMEM((DH, width), F32),
                        pltpu.VMEM((rows, width), F32)],
        compiler_params=pltpu.CompilerParams(dimension_semantics=("arbitrary", "arbitrary"),
                                             vmem_limit_bytes=56 * 2 ** 20),
        cost_estimate=pl.CostEstimate(flops=flops, bytes_accessed=rows * width * 20, transcendentals=heads * rows * rows),
        name="attention_backward",
    )(d_out, x, w, vec, kext, trig, qt, kb, v1, qp, save, scl)


def key_extension(kinds, valid):
    rows = kinds.shape[0]
    lane = jnp.arange(LANES)[None, :]
    k = kinds[:, None]
    out = jnp.where((lane >= DH) & (lane < DH + 3) | (lane >= DH + 6) & (lane < DH + 9), 1.0, 0.0)
    out = jnp.where((lane == DH + 3) | (lane == DH + 4), k, out)
    out = jnp.where(lane == DH + 5, jnp.where(valid[:, None] > 0, 0.0, -1e30), out)
    return jnp.broadcast_to(out, (rows, LANES)).astype(BF)


def pack_kernel(heads, groups, *refs):
    mats, smalls, wide_ref, out_ref = refs[:4], refs[4:16], refs[16], refs[17]
    rows = mats[0].shape[0]
    for g in range(groups):
        for h in range(heads):
            at = pl.ds((g * heads + h) * DH, DH)
            out_ref[g, h * rows:(h + 1) * rows, :] = jnp.concatenate([m[:, at] for m in mats], axis=1)
    pad = jnp.zeros((1, LANES - rows), F32)
    lines = [jnp.concatenate([v[...].astype(F32), pad], axis=1) for v in smalls]
    none = jnp.zeros((1, LANES), F32)
    inner = jnp.concatenate([wide_ref[...].astype(F32), jnp.zeros((1, LANES - wide_ref.shape[1]), F32)], axis=1)
    left = jnp.concatenate(lines[:8], axis=0)
    right = jnp.concatenate(lines[8:] + [inner, none, none, none], axis=0)
    both = jnp.concatenate([left, right], axis=1).astype(BF)
    for g in range(groups):
        out_ref[g, heads * rows:, :] = both


def pack(mats, smalls, wide, heads, groups):
    rows = mats[0].shape[0]
    return pl.pallas_call(
        functools.partial(pack_kernel, heads, groups),
        out_shape=jax.ShapeDtypeStruct((groups, heads * rows + 8, 2 * LANES), BF),
        name="pack_columns",
    )(*mats, *smalls, wide)


def unpack_kernel(heads, groups, shard, g_ref, block_ref, vecs_ref, wide_ref, vec_ref):
    owners = block_ref.shape[0]
    wide = wide_ref.shape[1] // owners
    for o in range(owners):
        t = block_ref[o].astype(F32)
        vecs_ref[:8, o * shard:(o + 1) * shard] = t[:, :shard]
        vecs_ref[8:, o * shard:(o + 1) * shard] = t[:, LANES:LANES + shard]
        wide_ref[:, o * wide:(o + 1) * wide] = t[4:5, LANES:LANES + wide]
    zeros = jnp.zeros((8, LANES - DH), F32)
    for g in range(groups):
        @pl.when(g_ref[0] == g)
        def _():
            for h in range(heads):
                part = vecs_ref[:8, (g * heads + h) * DH:(g * heads + h + 1) * DH]
                vec_ref[h] = jnp.concatenate([part, zeros], axis=1)


def unpack(block, g, heads, groups, shard, wide):
    owners, rows, _ = block.shape
    return pl.pallas_call(
        functools.partial(unpack_kernel, heads, groups, shard),
        grid=(1,),
        in_specs=[pl.BlockSpec(memory_space=pltpu.SMEM),
                  pl.BlockSpec((owners, 8, 2 * LANES), lambda i: (0, rows // 8 - 1, 0))],
        out_specs=[pl.BlockSpec((16, owners * shard), lambda i: (0, 0)), pl.BlockSpec((1, owners * wide), lambda i: (0, 0)),
                   pl.BlockSpec((heads, 8, LANES), lambda i: (0, 0, 0))],
        out_shape=[jax.ShapeDtypeStruct((16, owners * shard), F32), jax.ShapeDtypeStruct((1, owners * wide), F32),
                   jax.ShapeDtypeStruct((heads, 8, LANES), F32)],
        name="unpack_small",
    )(g.reshape(1), block)


def small_kernel(heads, groups, shard, g_ref, heads_ref, rest_ref, wide_ref, unused_ref, out_ref, table_ref):
    owners = out_ref.shape[0]
    wide = wide_ref.shape[1] // owners
    table_ref[:6] = jnp.zeros((6, table_ref.shape[1]), F32)
    for g in range(groups):
        @pl.when(g_ref[0] == g)
        def _():
            for h in range(heads):
                table_ref[:6, (g * heads + h) * DH:(g * heads + h + 1) * DH] = heads_ref[h, :6, :DH]
    table_ref[6:12] = rest_ref[...]
    pad = jnp.zeros((8, LANES - shard), F32)
    for o in range(owners):
        left = table_ref[:8, o * shard:(o + 1) * shard]
        right = jnp.concatenate([table_ref[8:12, o * shard:(o + 1) * shard], jnp.zeros((4, LANES - shard), F32)], axis=1)
        inner = jnp.concatenate([wide_ref[:, o * wide:(o + 1) * wide], jnp.zeros((1, LANES - wide), F32)], axis=1)
        right = jnp.concatenate([right, inner, jnp.zeros((3, LANES), F32)], axis=0)
        out_ref[o] = jnp.concatenate([left, pad, right], axis=1).astype(BF)


def small_rows(block, g, head_sums, rest, wide_sums, groups, shard):
    owners, rows, _ = block.shape
    heads = head_sums.shape[0]
    whole = lambda a: pl.BlockSpec(a.shape, lambda i: (0,) * a.ndim)
    return pl.pallas_call(
        functools.partial(small_kernel, heads, groups, shard),
        grid=(1,),
        in_specs=[pl.BlockSpec(memory_space=pltpu.SMEM), whole(head_sums), whole(rest), whole(wide_sums),
                  pl.BlockSpec(memory_space=pl.ANY)],
        out_specs=pl.BlockSpec((owners, 8, 2 * LANES), lambda i: (0, rows // 8 - 1, 0)),
        out_shape=jax.ShapeDtypeStruct(block.shape, BF),
        input_output_aliases={4: 0},
        scratch_shapes=[pltpu.VMEM((16, owners * shard), F32)],
        name="small_gradients",
    )(g.reshape(1), head_sums, rest, wide_sums, block)


def finish_kernel(heads, block_ref, *refs):
    outs, small_ref = refs[:-1], refs[-1]
    groups = block_ref.shape[0]
    shard = outs[0].shape[0]
    small_ref[...] = sum(block_ref[g, heads * shard:, :].astype(F32) for g in range(groups))
    for g in range(groups):
        for h in range(heads):
            part = block_ref[g, h * shard:(h + 1) * shard, :].astype(F32)
            at = (g * heads + h) * DH
            for m in range(4):
                outs[m][:, at:at + DH] = part[:, m * DH:(m + 1) * DH]


def finish(block, heads, shard, width):
    return pl.pallas_call(
        functools.partial(finish_kernel, heads),
        out_shape=[jax.ShapeDtypeStruct((shard, width), F32)] * 4 + [jax.ShapeDtypeStruct((8, 2 * LANES), F32)],
        name="finish_columns",
    )(block)


def token_kernel(core_ref, valid_ref, mixed_ref, x_ref, og_ref, vec_ref, wide_ref,
                 inner_own, inner_other, outer_own, outer_other,
                 result_ref, first_ref, grad_ref, gi_keep, gi_send, go_keep, go_send, rest_ref, gw_ref,
                 wi, wo, act, slope, normed_t, acc, gi_ref, go_ref, sems):
    core = core_ref[0]
    seqs, width, stretch = mixed_ref.shape
    tokens = seqs * stretch
    count = wi.shape[1] // width
    members, rows = wo.shape[1], wo.shape[2]
    block = width // count
    shard = block // members
    wide = rows - shard
    copies = []
    for y in range(2):
        for i, (src_i, src_o, k) in enumerate(((inner_own, outer_own, core), (inner_other, outer_other, 1 - core))):
            at = 2 * y + k
            copies.append(pltpu.make_async_copy(
                src_o.at[y], wo.at[at], sems.at[2 * y + i]))
            copies.append(pltpu.make_async_copy(
                src_i.at[y], wi.at[pl.ds(pl.multiple_of(at * block, block), block), :], sems.at[4 + 2 * y + i]))
    for copy in copies:
        copy.start()
    for copy in copies[0::2]:
        copy.wait()
    w_out = wo[:, :, wide:, :].astype(F32).reshape(width, width).astype(BF)
    vec = vec_ref[...]
    line = lambda i: vec[i:i + 1, :]
    mean = lambda v: jnp.mean(v, axis=1, keepdims=True)
    attn = jnp.concatenate([mm(mixed_ref[b], w_out, COLS_CC) for b in range(seqs)], axis=0) + line(6)
    first = x_ref[...].astype(F32) + attn
    center = first - mean(first)
    r_one = lax.rsqrt(mean(center * center) + epsilon)
    hat_one = center * r_one
    normed = hat_one * line(7) + line(8)
    low = normed.astype(BF)
    normed_t[...] = jnp.transpose(normed).astype(BF)
    acc[...] = jnp.zeros_like(acc)
    for copy in copies[1::2]:
        copy.wait()

    def forward(j, carry):
        at = pl.ds(pl.multiple_of(j * width, width), width)
        u = mm(low, wi[:, at], ROWCOL) + wide_ref[:, at]
        c = 0.7978845608028654
        sq = u * u
        t = jnp.tanh(c * u * (1.0 + 0.044715 * sq))
        half = 0.5 * (1.0 + t)
        a = (u * half).astype(BF)
        act[:, at] = a
        slope[:, at] = half + 0.5 * u * (1.0 - t * t) * (c * (1.0 + 3 * 0.044715 * sq))
        acc[...] += mm(a, wo[j, :, :wide, :].reshape(width, width), ROWCOL)
        return carry

    lax.fori_loop(0, count, forward, 0)
    outer = acc[...] + line(9)
    second = normed + outer
    center = second - mean(second)
    r_two = lax.rsqrt(mean(center * center) + epsilon)
    hat_two = center * r_two
    result_ref[...] = (hat_two * line(10) + line(11)).astype(BF)
    valid = valid_ref[...]
    cot = og_ref[...].astype(F32) * valid
    d_hat = cot * line(10)
    d_second = r_two * (d_hat - mean(d_hat) - hat_two * mean(d_hat * hat_two))
    d_low = d_second.astype(BF)
    total = lambda v: jnp.sum(v, axis=0, keepdims=True)
    outer_sum = total(d_low.astype(F32))
    two = [total(cot * hat_two), total(cot)]
    acc[...] = d_second

    def backward(j, carry):
        at = pl.ds(pl.multiple_of(j * width, width), width)
        d_act = mm(d_low, wo[j, :, :wide, :].reshape(width, width), ROWS_CC)
        d_in = d_act * slope[:, at]
        d_in_low = d_in.astype(BF)
        gw_ref[:, at] = total(d_in_low.astype(F32))
        acc[...] += mm(d_in_low, wi[:, at], ROWS_CC)
        go = mm(act[:, at], d_low, COLS_CC)
        go_ref[(j % 2) ^ core, j // 2, :, :wide, :] = go.astype(BF).reshape(members, wide, width)
        for b in range(count):
            gi = mm(normed_t[b * block:(b + 1) * block, :], d_in_low, ROWCOL)
            gi_ref[(b % 2) ^ core, b // 2, :, at] = gi.astype(BF)
        return carry

    lax.fori_loop(0, count, backward, 0)
    backs = [pltpu.make_async_copy(gi_ref.at[0], gi_keep, sems.at[8]), pltpu.make_async_copy(gi_ref.at[1], gi_send, sems.at[9]),
             pltpu.make_async_copy(go_ref.at[0], go_keep, sems.at[10]), pltpu.make_async_copy(go_ref.at[1], go_send, sems.at[11])]
    backs[1].start()
    backs[0].start()
    d_normed = acc[...]
    one = [total(d_normed * hat_one), total(d_normed)]
    d_hat = d_normed * line(7)
    d_first = r_one * (d_hat - mean(d_hat) - hat_one * mean(d_hat * hat_one))
    first_ref[...] = d_first
    a_low = d_first.astype(BF)
    rest_ref[...] = jnp.concatenate([total(a_low.astype(F32))] + one + [outer_sum] + two, axis=0)
    grad = mm(w_out, a_low, ROWS_CC).astype(BF)
    span = grad_ref.shape[1] - 8
    groups = width // span
    lane = lax.broadcasted_iota(jnp.int32, (1, stretch), 1)
    sums = jnp.zeros((1, stretch), F32)
    everything = lambda v: jnp.sum(jnp.sum(v, axis=0, keepdims=True), axis=1, keepdims=True)
    for b in range(seqs):
        at = slice(b * stretch, (b + 1) * stretch)
        for i, v in enumerate((first, attn, outer)):
            sums = jnp.where(lane == 3 * b + i, everything(v[at] * v[at] * valid[at]), sums)
    high = sums.astype(BF).astype(F32)
    riders = jnp.concatenate([high, sums - high, jnp.zeros((6, stretch), F32)], axis=0).astype(BF)
    for b in range(seqs):
        for g in range(groups):
            grad_ref[b * groups + g, :span, :] = grad[g * span:(g + 1) * span, b * stretch:(b + 1) * stretch]
            grad_ref[b * groups + g, span:, :] = riders
    out = mm(mixed_ref[0], a_low[:stretch], ROWCOL)
    for b in range(1, seqs):
        out += mm(mixed_ref[b], a_low[b * stretch:(b + 1) * stretch], ROWCOL)
    for b in range(count):
        for i in range(members):
            at = b * block + i * shard
            go_ref[(b % 2) ^ core, b // 2, i, wide:, :] = out[at:at + shard, :].astype(BF)
    backs[3].start()
    backs[2].start()
    for back in backs:
        back.wait()


def token_block(core, valid, mixed, x, out_grad, vectors, inner_add, inner_own, inner_other, outer_own, outer_other, span):
    seqs, width, stretch = mixed.shape
    tokens = seqs * stretch
    ff = inner_add.shape[1]
    count = ff // width
    members, rows = outer_own.shape[1], outer_own.shape[2]
    groups = width // span
    vmem = pl.BlockSpec(memory_space=pltpu.VMEM)
    hbm = pl.BlockSpec(memory_space=pl.ANY)
    S = jax.ShapeDtypeStruct
    return pl.pallas_call(
        token_kernel,
        in_specs=[pl.BlockSpec(memory_space=pltpu.SMEM)] + [vmem] * 6 + [hbm] * 4,
        out_specs=[vmem] * 3 + [hbm] * 4 + [vmem] * 2,
        out_shape=[S((tokens, width), BF), S((tokens, width), F32), S((seqs * groups, span + 8, stretch), BF),
                   S((2, width // count, ff), BF), S((2, width // count, ff), BF),
                   S((2, members, rows, width), BF), S((2, members, rows, width), BF),
                   S((6, width), F32), S((1, ff), F32)],
        scratch_shapes=[pltpu.VMEM((width, ff), BF), pltpu.VMEM((count, members, rows, width), BF),
                        pltpu.VMEM((tokens, ff), BF), pltpu.VMEM((tokens, ff), F32),
                        pltpu.VMEM((width, tokens), BF), pltpu.VMEM((tokens, width), F32),
                        pltpu.VMEM((2, 2, width // count, ff), BF), pltpu.VMEM((2, 2, members, rows, width), BF),
                        pltpu.SemaphoreType.DMA((12,))],
        compiler_params=pltpu.CompilerParams(vmem_limit_bytes=60 * 2 ** 20),
        cost_estimate=pl.CostEstimate(flops=tokens * 2 * width * (6 * ff + 4 * width), bytes_accessed=30 * 2 ** 20, transcendentals=tokens * ff),
        name="token_block",
    )(core.reshape(1), valid, mixed, x, out_grad, vectors, inner_add, inner_own, inner_other, outer_own, outer_other)


def takes_head_layout(mesh):
    return dict(mesh.shape) == {DP: 4, CTX: 8}


def swap(x, axis, bit):
    count = lax.axis_size(axis)
    return lax.ppermute(x, axis, [(i, i ^ bit) for i in range(count)])


def in_order(bit, own, received, axis):
    first = jnp.where(bit == 0, own, received)
    second = jnp.where(bit == 0, received, own)
    return jnp.stack([first, second], axis=axis)


def flip_if(bit, x, axis):
    return jnp.where(bit == 0, x, jnp.flip(x, axis))


def pick(x, index, axis):
    return lax.dynamic_index_in_dim(x, index, axis, keepdims=False)


def after(x, *others):
    return lax.optimization_barrier((x,) + others)[0]


def add_low(a, b):
    return (a.astype(F32) + b.astype(F32)).astype(BF)


def in_z_order(pieces):
    z = lax.axis_index(CTX) // 2
    block = jnp.stack(pieces).reshape((2, 2) + pieces[0].shape)
    return flip_if(z // 2, flip_if(z % 2, block, 1), 0).reshape((4,) + pieces[0].shape)


def grow_y(block):
    return in_order(lax.axis_index(DP) // 2, block, swap(block, DP, 2), 0)


def grow_core(block):
    return in_order(lax.axis_index(DP) % 2, block, swap(block, DP, 1), 1)


def halve(block, axis, mesh_axis, step, bit):
    return add_low(pick(block, bit, axis), swap(pick(block, 1 - bit, axis), mesh_axis, step))


def end_scatter(block):
    z = lax.axis_index(CTX) // 2
    total = pick(block, z, 0).astype(F32)
    for m in (1, 2, 3):
        total = total + swap(pick(block, z ^ m, 0), CTX, 2 * m).astype(F32)
    return total


def head_layout(
    inputs,
    out_grad,
    lengths,
    token_types,
    query_weight,
    key_weight,
    value_weight,
    value_bias,
    position_weight,
    content_bias,
    position_bias,
    type_bias,
    type_embed,
    output_weight,
    output_bias,
    first_gain,
    first_shift,
    inner_weight,
    inner_bias,
    outer_weight,
    outer_bias,
    second_gain,
    second_shift,
):
    d, c = lax.axis_index(DP), lax.axis_index(CTX)
    members = lax.axis_size(CTX)
    devices = lax.axis_size(DP) * members
    seqs, stretch, width = inputs.shape
    seq_len = stretch * members
    groups = members // seqs
    heads = H // groups
    span = heads * DH
    half = width // 2
    shard = width // devices
    inner_shard = inner_bias.shape[0]
    s, g = c // groups, c % groups
    bit_b, bit_x = (c // 2) % 2, c % 2
    core, bit_y = d % 2, d // 2

    smalls = (
        content_bias,
        position_bias,
        type_bias,
        value_bias,
        type_embed[0],
        type_embed[1],
        output_bias,
        first_gain,
        first_shift,
        outer_bias,
        second_gain,
        second_shift,
    )
    stacked = pack(
        (query_weight, key_weight, value_weight, position_weight),
        tuple(v.reshape(1, shard) for v in smalls),
        inner_bias.reshape(1, inner_shard),
        heads,
        groups,
    )

    row = jnp.zeros((seqs, 8, half), BF).at[:, 0, :stretch].set(token_types.astype(BF))
    left = jnp.concatenate([inputs[:, :, :half], row], axis=1)
    right = inputs[:, :, half:]
    left = in_order(s, pick(left, s, 0), swap(pick(left, 1 - s, 0), CTX, 4), 0)
    right = in_order(s, pick(right, s, 0), swap(pick(right, 1 - s, 0), CTX, 4), 0)
    left = in_order(bit_x, left, swap(left, CTX, 1), 1)
    right = in_order(bit_b, right, swap(right, CTX, 2), 1)
    left = in_order(bit_b, left, swap(left, CTX, 2), 1)
    right = in_order(bit_x, right, swap(right, CTX, 1), 2)
    left = left.reshape(members, stretch + 8, half)
    right = right.reshape(members, stretch, half)
    x_seq = jnp.concatenate([left[:, :stretch], right], axis=2).reshape(seq_len, width)
    kind_seq = left[:, stretch, :stretch].reshape(seq_len).astype(F32)

    pieces = [pick(stacked, g, 0)]
    for r in range(1, groups):
        pieces.append(swap(pick(stacked, g ^ r, 0), CTX, r))
    block = jnp.stack(pieces).reshape((2, 2) + pieces[0].shape)
    block = flip_if(bit_b, flip_if(bit_x, block, 1), 0).reshape((groups,) + pieces[0].shape)
    block = in_order(s, block, swap(block, CTX, 4), 0)[None]
    block = grow_core(grow_y(block))
    block = block.reshape((devices,) + pieces[0].shape)
    exponent = 2.0 * jnp.arange(half, dtype=F32) / width
    rates = (10000.0 ** (-exponent))[None, :]
    starts = (jnp.arange(members, dtype=jnp.int32) * stretch).astype(F32)[:, None] * rates
    steps = jnp.arange(stretch, dtype=F32)[:, None] * rates
    starts, steps = lax.optimization_barrier((starts, steps))
    cos_a, sin_a = jnp.cos(starts)[:, None], jnp.sin(starts)[:, None]
    cos_b, sin_b = jnp.cos(steps)[None], jnp.sin(steps)[None]
    trig = jnp.concatenate(
        [cos_a * cos_b - sin_a * sin_b, sin_a * cos_b + cos_a * sin_b], axis=2
    ).reshape(seq_len, width)
    key_valid = (jnp.arange(seq_len, dtype=jnp.int32) < pick(lengths, s, 0)).astype(F32)
    kext = key_extension(kind_seq, key_valid)

    outer_shard = jnp.concatenate([outer_weight, output_weight], axis=0)
    inner_z = [swap(inner_weight, CTX, 2 * m) for m in (1, 2, 3)]
    outer_z = [swap(outer_shard, CTX, 2 * m) for m in (1, 2, 3)]
    x_seq, block, inner_z, outer_z = lax.optimization_barrier((x_seq, block, inner_z, outer_z))
    vectors, inner_add, vec = unpack(block, g, heads, groups, shard, inner_shard)
    inner_block = in_z_order([inner_weight] + inner_z)
    outer_block = in_z_order([outer_shard] + outer_z)
    inner_x = swap(inner_block, CTX, 1)
    outer_y = swap(outer_block, DP, 2)
    saved = attention_forward(
        x_seq, block, 0, 1, heads, after(vec, inner_block, outer_block), kext, trig
    )
    inner_x, outer_y, probe = lax.optimization_barrier((inner_x, outer_y, saved[0]))
    inner_block = in_order(bit_x, inner_block, inner_x, 1)
    outer_block = in_order(bit_y, outer_block, outer_y, 0)
    inner_y = swap(inner_block, DP, 2)
    outer_x = swap(outer_block, CTX, 1)
    saved = (probe,) + tuple(saved[1:])
    saved = attention_forward(
        x_seq, block, 1, heads - 1, heads, after(vec, inner_block, outer_block), kext, trig, saved
    )
    att, qt, kb, v1, qp, save, scl, w_heads = saved
    inner_y, outer_x, att = lax.optimization_barrier((inner_y, outer_x, att))
    mixed = lax.all_to_all(att, CTX, 0, 0, tiled=True).reshape(seqs, width, stretch)
    inner_own = in_order(bit_y, inner_block, inner_y, 0).reshape(2, -1, inner_weight.shape[1])
    outer_own = in_order(bit_x, outer_block, outer_x, 2)
    outer_own = outer_own.reshape(2, members, inner_shard + shard, width)
    inner_other = swap(inner_own, DP, 1)
    outer_other = swap(outer_own, DP, 1)

    own_slots = c * stretch + jnp.arange(stretch, dtype=jnp.int32)
    row_valid = (own_slots[None, :] < lengths[:, None]).astype(F32)
    result, first_grad, mixed_grad, inner_keep, inner_send, outer_keep, outer_send, rest, wide = (
        token_block(
            core,
            row_valid.reshape(-1, 1),
            mixed,
            inputs.reshape(-1, width),
            out_grad.reshape(-1, width),
            vectors,
            inner_add,
            inner_own,
            inner_other,
            outer_own,
            outer_other,
            span,
        )
    )
    result = result.reshape(inputs.shape)
    first_grad = first_grad.reshape(inputs.shape)

    d_out = lax.all_to_all(mixed_grad, CTX, 0, 0, tiled=True)
    sums_all = jnp.sum(d_out[:, span : span + 2].astype(F32), axis=(0, 1))
    sums_all = sums_all[: 3 * seqs].reshape(seqs, 3)
    mean_squares = sums_all / (lengths.astype(F32)[:, None] * width)
    inner_block = add_low(inner_keep, swap(inner_send, DP, 1)).reshape(2, 4, 2, shard, -1)
    outer_block = add_low(outer_keep, swap(outer_send, DP, 1))
    outer_block = outer_block.reshape(2, 4, 2, inner_shard + shard, width)
    inner_keep, inner_send = pick(inner_block, bit_y, 0), pick(inner_block, 1 - bit_y, 0)
    outer_keep, outer_send = pick(outer_block, bit_x, 2), pick(outer_block, 1 - bit_x, 2)
    inner_y = swap(inner_send, DP, 2)
    outer_x = swap(outer_send, CTX, 1)

    d_x, w_grad, head_sums = attention_backward(
        after(d_out, inner_send, outer_send),
        x_seq,
        w_heads,
        vec,
        kext,
        trig,
        qt,
        kb,
        v1,
        qp,
        save,
        scl,
        devices,
        heads * shard + 8,
    )
    d_x, inner_y, outer_x = lax.optimization_barrier((d_x, inner_y, outer_x))
    inner_block = halve(add_low(inner_keep, inner_y), 1, CTX, 1, bit_x)
    outer_block = halve(add_low(outer_keep, outer_x), 0, DP, 2, bit_y)

    block = small_rows(w_grad, g, head_sums, rest, wide, groups, shard)
    block = block.reshape((2, 2, 2, groups) + block.shape[1:])
    block = halve(block, 1, DP, 1, core)
    block = halve(block, 0, DP, 2, bit_y)
    block = halve(block, 0, CTX, 4, s)
    pieces = [pick(block, g, 0)]
    for r in range(1, groups):
        pieces.append(swap(pick(block, g ^ r, 0), CTX, r))
    block = jnp.stack(pieces).reshape((2, 2) + pieces[0].shape)
    block = flip_if(bit_b, flip_if(bit_x, block, 1), 0).reshape((groups,) + pieces[0].shape)
    query_own, key_own, value_own, position_own, small = finish(block, heads, shard, width)
    v = [small[i, :shard] for i in range(8)] + [small[i, LANES : LANES + shard] for i in range(4)]

    d_x = d_x.reshape(2, 2, 2, stretch, width)
    left, right = d_x[..., :half], d_x[..., half:]
    left = halve(left, 2, CTX, 1, bit_x)
    right = halve(right, 1, CTX, 2, bit_b)
    left = halve(left, 1, CTX, 2, bit_b)
    right = halve(right, 1, CTX, 1, bit_x)
    both = jnp.concatenate([left, right], axis=2)
    input_terms = in_order(s, pick(both, s, 0), swap(pick(both, 1 - s, 0), CTX, 4), 0)
    input_grad = (first_grad + input_terms.astype(F32)).astype(BF)

    inner_own = end_scatter(inner_block)
    outer_block = end_scatter(outer_block)
    outer_own, output_own = outer_block[:inner_shard], outer_block[inner_shard:]
    return (
        result,
        input_grad,
        query_own,
        key_own,
        value_own,
        v[5],
        position_own,
        v[0],
        v[1],
        v[2],
        jnp.stack([v[3], v[4]]),
        output_own,
        v[6],
        v[7],
        v[8],
        inner_own,
        small[4, LANES : LANES + inner_shard],
        outer_own,
        v[9],
        v[10],
        v[11],
        mean_squares,
    )


def solution(mesh):
    in_specs = (
        P(DP, CTX, None),
        P(DP, CTX, None),
        P(DP),
        P(DP, CTX),
        P(ALL, None),
        P(ALL, None),
        P(ALL, None),
        P(ALL),
        P(ALL, None),
        P(ALL),
        P(ALL),
        P(ALL),
        P(None, ALL),
        P(ALL, None),
        P(ALL),
        P(ALL),
        P(ALL),
        P(ALL, None),
        P(ALL),
        P(ALL, None),
        P(ALL),
        P(ALL),
        P(ALL),
    )
    out_specs = (
        P(DP, CTX, None),
        P(DP, CTX, None),
        P(ALL, None),
        P(ALL, None),
        P(ALL, None),
        P(ALL),
        P(ALL, None),
        P(ALL),
        P(ALL),
        P(ALL),
        P(None, ALL),
        P(ALL, None),
        P(ALL),
        P(ALL),
        P(ALL),
        P(ALL, None),
        P(ALL),
        P(ALL, None),
        P(ALL),
        P(ALL),
        P(ALL),
        P(DP, None),
    )
    body = head_layout if takes_head_layout(mesh) else per_device
    return jax.shard_map(
        body, mesh=mesh, in_specs=in_specs, out_specs=out_specs, check_vma=False
    )
```

profile of v0, /device:TPU:0, one launch (start us, length us, event | category | flops | bytes accessed | tf_op | source)
XLA Modules:
  0.0 353.1 jit_solution(10262583654470961022)
XLA Ops:
  2.4 3.0 collective-permute-start.15
  5.4 2.6 collective-permute-start.16
  9.2 1.7 pack_columns.1
  11.8 1.6 collective-permute-start.6
  13.8 1.5 collective-permute-start.8
  19.2 1.9 pad_maximum_fusion.refs_4_.trig_ref
  21.2 1.9 collective-permute-start
  24.3 14.4 %collective-permute-done.3 = bf16[128,384]{1,0:T(8,128)(2,1)S(1)} collective-permute-done((bf16[128,384]{1,0:T(8,128)(2,1)S(1)}, bf16[128,384]{1,0:T(8,128)(2,1)S(1)}, u32[]{:S(2)}, u32[]{:S(2)}) %collective-permute-start.3) | collective-permute-done | bytes 98336 | tf_op jit(solution)/shard_map/ppermute | solution.py:1157
  38.8 2.0 collective-permute-start.4
  40.8 6.3 %collective-permute-done.9 = bf16[4,80,256]{2,1,0:T(8,128)(2,1)S(1)} collective-permute-done((bf16[4,80,256]{2,1,0:T(8,128)(2,1)S(1)}, bf16[4,80,256]{2,1,0:T(8,128)(2,1)S(1)}, u32[]{:S(2)}, u32[]{:S(2)}) %collective-permute-start.9) | collective-permute-done | bytes 163872 | tf_op jit(solution)/shard_map/ppermute | solution.py:1157
  47.1 1.5 collective-permute-start.1
  48.7 1.6 collective-permute-start.10
  50.4 3.1 collective-permute-done.1
  53.5 1.5 collective-permute-start.5
  55.1 2.3 collective-permute-done.10
  57.6 5.4 %collective-permute-done.5 = bf16[2,2,128,384]{3,2,1,0:T(8,128)(2,1)S(1)} collective-permute-done((bf16[2,2,128,384]{3,2,1,0:T(8,128)(2,1)S(1)}, bf16[2,2,128,384]{3,2,1,0:T(8,128)(2,1)S(1)}, u32[]{:S(2)}, u32[]{:S(2)}) %collective-permute-start.5) | collective-permute-done | bytes 393248 | tf_op jit(solution)/shard_map/ppermute | solution.py:1157
  63.1 4.1 %collective-permute-done.2 = bf16[2,2,136,384]{3,2,1,0:T(8,128)(2,1)S(1)} collective-permute-done((bf16[2,2,136,384]{3,2,1,0:T(8,128)(2,1)S(1)}, bf16[2,2,136,384]{3,2,1,0:T(8,128)(2,1)S(1)}, u32[]{:S(2)}, u32[]{:S(2)}) %collective-permute-start.2) | collective-permute-done | bytes 417824 | tf_op jit(solution)/shard_map/ppermute | solution.py:1157
  67.8 1.3 pad_maximum_fusion.3.refs_0_.x_ref
  69.1 3.3 collective-permute-done.12
  72.4 3.7 %collective-permute-start.14 = (bf16[24,3072]{1,0:T(8,128)(2,1)S(1)}, bf16[24,3072]{1,0:T(8,128)(2,1)S(1)}, u32[]{:S(2)}, u32[]{:S(2)}) collective-permute-start(bf16[24,3072]{1,0:T(8,128)(2,1)S(1)} %copy-done.9), channel_id=1, source_target_pairs={{0,6},{1,7},{2,4},{3,5},{4,2},{5,3},{6,0},{7,1},{8,14},{9,15},{10,... | collective-permute-start | bytes 442376 | tf_op jit(solution)/shard_map/ppermute | solution.py:1157
  77.4 5.4 %collective-permute-done.13 = bf16[24,3072]{1,0:T(8,128)(2,1)S(1)} collective-permute-done((bf16[24,3072]{1,0:T(8,128)(2,1)S(1)}, bf16[24,3072]{1,0:T(8,128)(2,1)S(1)}, u32[]{:S(2)}, u32[]{:S(2)}) %collective-permute-start.13) | collective-permute-done | bytes 147488 | tf_op jit(solution)/shard_map/ppermute | solution.py:1157
  83.4 1.6 collective-permute-start.19
  86.7 1.8 unpack_small.1
  88.6 12.6 %attention_forward.2 = (bf16[8,192,128]{2,1,0:T(8,128)(2,1)}, bf16[3,1024,896]{2,1,0:T(8,128)(2,1)}, bf16[3,1024,128]{2,1,0:T(8,128)(2,1)}, bf16[3,1024,128]{2,1...) custom-call(bf16[1024,768]{1,0:T(8,128)(2,1)} %pad_maximum_fusion.3., ...), custom_call_target="tpu_custom_call" | custom-call | flops 2550136832 | bytes 12582912 | tf_op jit(solution)/shard_map/attention_forward/pallas_call | solution.py:816
  101.6 1.6 collective-permute-start.21
  103.9 20.6 %attention_forward.3 = (bf16[8,192,128]{2,1,0:T(8,128)(2,1)}, bf16[3,1024,896]{2,1,0:T(8,128)(2,1)}, bf16[3,1024,128]{2,1,0:T(8,128)(2,1)}, bf16[3,1024,128]{2,1...) custom-call(bf16[1024,768]{1,0:T(8,128)(2,1)} %pad_maximum_fusion.3., ...), custom_call_target="tpu_custom_call", output_to_operand_aliasing={{0}: (5, {}), {1}: (6, {}), {2}: (7, {}), {3}: (8, {}), {4}... | custom-call | flops 5100273664 | bytes 12582912 | tf_op jit(solution)/shard_map/attention_forward/pallas_call | solution.py:816
  124.5 4.9 %collective-permute-done.21 = bf16[2,4,120,768]{3,2,1,0:T(8,128)(2,1)S(1)} collective-permute-done((bf16[2,4,120,768]{3,2,1,0:T(8,128)(2,1)S(1)}, bf16[2,4,120,768]{3,2,1,0:T(8,128)(2,1)S(1)}, u32[]{:S(2)}, u32[]{:S(2)}) %collective-permute-start.21) | collective-permute-done | bytes 1474592 | tf_op jit(solution)/shard_map/ppermute | solution.py:1157
  131.5 1.6 pad_maximum_fusion.2.inner_own
  133.1 8.1 %all-to-all-start = ((bf16[8,192,128]{2,1,0:T(8,128)(2,1)}), bf16[8,192,128]{2,1,0:T(8,128)(2,1)S(1)}, u32[]{:S(2)}, u32[]{:S(2)}) async-start(bf16[8,192,128]{2,1,0:T(8,128)(2,1)} %get-tuple-element.117), calls=%async_computation | async-start | bytes 786432 | tf_op jit(solution)/shard_map/all_to_all | solution.py:1328
  142.2 11.5 %all-to-all-done = bf16[8,192,128]{2,1,0:T(8,128)(2,1)S(1)} async-done(((bf16[8,192,128]{2,1,0:T(8,128)(2,1)}), bf16[8,192,128]{2,1,0:T(8,128)(2,1)S(1)}, u32[]{:S(2)}, u32[]{:S(2)}) %all-to-all-start) | async-done | bytes 393248 | tf_op jit(solution)/shard_map/all_to_all | solution.py:1328
  154.4 23.6 %token_block.1 = (bf16[256,768]{1,0:T(8,128)(2,1)}, f32[256,768]{1,0:T(8,128)}, bf16[8,200,128]{2,1,0:T(8,128)(2,1)}, bf16[2,192,3072]{2,1,0:T(8,128)(2,1)}, bf1...) custom-call(s32[1]{0:T(128)} %bitcast.core_ref, ...), custom_call_target="tpu_custom_call" | custom-call | flops 8455716864 | bytes 31457280 | tf_op jit(solution)/shard_map/token_block/pallas_call | solution.py:1132
  178.5 3.7 %all-to-all-start.1 = ((bf16[8,200,128]{2,1,0:T(8,128)(2,1)}), bf16[8,200,128]{2,1,0:T(8,128)(2,1)S(1)}, u32[]{:S(2)}, u32[]{:S(2)}) async-start(bf16[8,200,128]{2,1,0:T(8,128)(2,1)} %get-tuple-element.124), calls=%async_computation.1 | async-start | bytes 819200 | tf_op jit(solution)/shard_map/all_to_all | solution.py:1356
  182.3 3.2 collective-permute-done.24
  185.5 3.3 add_convert_fusion.1
  191.1 1.6 copy-done.2
  192.7 2.6 add_convert_fusion
  195.3 1.3 dynamic-slice_bitcast_fusion
  197.4 31.0 %attention_backward.1 = (bf16[1024,768]{1,0:T(8,128)(2,1)}, bf16[32,80,256]{2,1,0:T(8,128)(2,1)}, f32[3,8,128]{2,1,0:T(8,128)}) custom-call(bf16[8,200,128]{2,1,0:T(8,128)(2,1)} %copy-done.7, bf16[1024,768]{1,0:T(8,128)(2,1)} %pad_maximum_fusion.3.refs_0_.x_ref, bf16[3,768,256]{2,1,0:T(8,128)(2,1)} %get-tuple-element.130.w_ref, ...), custom_call_target="tpu_custom_call" | custom-call | flops 13690208256 | bytes 15728640 | tf_op jit(solution)/shard_map/attention_backward/pallas_call | solution.py:847
  228.4 1.6 small_gradients.1
  230.0 2.0 dynamic-slice_bitcast_fusion.2
  232.1 2.3 collective-permute-done.33
  234.4 1.4 fusion.3
  236.5 9.3 %collective-permute-done.34 = bf16[2,4,80,256]{3,2,1,0:T(8,128)(2,1)S(1)} collective-permute-done((bf16[2,4,80,256]{3,2,1,0:T(8,128)(2,1)S(1)}, bf16[2,4,80,256]{3,2,1,0:T(8,128)(2,1)S(1)}, u32[]{:S(2)}, u32[]{:S(2)}) %collective-permute-start.34) | collective-permute-done | bytes 327712 | tf_op jit(solution)/shard_map/ppermute | solution.py:1157
  249.3 7.2 %collective-permute-done.35 = bf16[4,80,256]{2,1,0:T(8,128)(2,1)S(1)} collective-permute-done((bf16[4,80,256]{2,1,0:T(8,128)(2,1)}, bf16[4,80,256]{2,1,0:T(8,128)(2,1)S(1)}, u32[]{:S(2)}, u32[]{:S(2)}) %collective-permute-start.35) | collective-permute-done | bytes 163872 | tf_op jit(solution)/shard_map/ppermute | solution.py:1157
  257.0 3.2 collective-permute-start.38
  260.8 22.4 %collective-permute-done.36 = bf16[80,256]{1,0:T(8,128)(2,1)S(1)} collective-permute-done((bf16[80,256]{1,0:T(8,128)(2,1)S(1)}, bf16[80,256]{1,0:T(8,128)(2,1)S(1)}, u32[]{:S(2)}, u32[]{:S(2)}) %collective-permute-start.36) | collective-permute-done | bytes 40992 | tf_op jit(solution)/shard_map/ppermute | solution.py:1157
  284.0 1.7 finish_columns.1
  288.2 1.5 slice_bitcast_fusion
  289.7 2.1 fusion.1
  291.9 1.3 collective-permute-start.43
  293.4 1.8 collective-permute-start.30
  296.0 1.7 fusion
  297.7 1.6 collective-permute-start.39
  299.3 3.1 collective-permute-done.30
  303.1 12.5 %collective-permute-done.28 = bf16[2,2,128,384]{3,2,0,1:T(8,128)(2,1)S(1)} collective-permute-done((bf16[2,2,128,384]{3,2,0,1:T(8,128)(2,1)S(1)}, bf16[2,2,128,384]{3,2,0,1:T(8,128)(2,1)S(1)}, u32[]{:S(2)}, u32[]{:S(2)}) %collective-permute-start.28) | collective-permute-done | bytes 393248 | tf_op jit(solution)/shard_map/ppermute | solution.py:1157
  315.8 1.6 collective-permute-start.29
  318.1 2.4 collective-permute-start.45
  320.6 1.4 collective-permute-start.46
  322.1 2.5 collective-permute-done.29
  324.6 4.0 %collective-permute-start.32 = (bf16[128,768]{1,0:T(8,128)(2,1)S(1)}, bf16[128,768]{1,0:T(8,128)(2,1)S(1)}, u32[]{:S(2)}, u32[]{:S(2)}) collective-permute-start(bf16[128,768]{1,0:T(8,128)(2,1)S(1)} %fusion.18), channel_id=1, source_target_pairs={{0,4},{1,5},{2,6},{3,7},{4,0},{5,1},{6,2},{7,3},{8,12},{9,13},{10,... | collective-permute-start | bytes 589832 | tf_op jit(solution)/shard_map/ppermute | solution.py:1157
  328.9 2.8 collective-permute-start.40
  331.8 2.4 collective-permute-start.42
  336.0 12.6 %collective-permute-done.32 = bf16[128,768]{1,0:T(8,128)(2,1)S(1)} collective-permute-done((bf16[128,768]{1,0:T(8,128)(2,1)S(1)}, bf16[128,768]{1,0:T(8,128)(2,1)S(1)}, u32[]{:S(2)}, u32[]{:S(2)}) %collective-permute-start.32) | collective-permute-done | bytes 196640 | tf_op jit(solution)/shard_map/ppermute | solution.py:1157
  349.5 2.1 collective-permute-done.41
  (178 shorter events, 38.2 us)
Async XLA Ops:
  0.7 15.8 %copy-start.11 = (s32[2,128]{1,0:T(2,128)S(1)}, s32[2,128]{1,0:T(2,128)}, u32[]{:S(2)}) copy-start(s32[2,128]{1,0:T(2,128)} %param.28) | copy-start | bytes 3076
  0.7 16.0 %copy-start.10 = (s32[2]{0:T(128)S(1)}, s32[2]{0:T(128)}, u32[]{:S(2)}) copy-start(s32[2]{0:T(128)} %param.27) | copy-start | bytes 28
  2.4 80.5 %collective-permute-start.15 = (bf16[120,768]{1,0:T(8,128)(2,1)S(1)}, bf16[120,768]{1,0:T(8,128)(2,1)S(1)}, u32[]{:S(2)}, u32[]{:S(2)}) collective-permute-start(bf16[120,768]{1,0:T(8,128)(2,1)S(1)} %constant_dynamic-update-slice_fusion), channel_id=1, source_target_pairs={{0,2},{1,3},{2,0},{3,1},{4,6},{5,7},{6,4},{7,5},{8,10},{9,11},{10,... | collective-permute-start | bytes 552968 | tf_op jit(solution)/shard_map/ppermute | solution.py:1157
  5.4 77.4 %collective-permute-start.16 = (bf16[120,768]{1,0:T(8,128)(2,1)S(1)}, bf16[120,768]{1,0:T(8,128)(2,1)S(1)}, u32[]{:S(2)}, u32[]{:S(2)}) collective-permute-start(bf16[120,768]{1,0:T(8,128)(2,1)S(1)} %constant_dynamic-update-slice_fusion), channel_id=1, source_target_pairs={{0,4},{1,5},{2,6},{3,7},{4,0},{5,1},{6,2},{7,3},{8,12},{9,13},{10,... | collective-permute-start | bytes 552968 | tf_op jit(solution)/shard_map/ppermute | solution.py:1157
  11.8 9.3 %collective-permute-start.6 = (bf16[80,256]{1,0:T(8,128)(2,1)S(1)}, bf16[80,256]{1,0:T(8,128)(2,1)S(1)}, u32[]{:S(2)}, u32[]{:S(2)}) collective-permute-start(bf16[80,256]{1,0:T(8,128)(2,1)S(1)} %get-tuple-element.203), channel_id=1, source_target_pairs={{0,1},{1,0},{2,3},{3,2},{4,5},{5,4},{6,7},{7,6},{8,9},{9,8},{10,11... | collective-permute-start | bytes 122888 | tf_op jit(solution)/shard_map/ppermute | solution.py:1157
  13.4 7.8 %collective-permute-start.7 = (bf16[80,256]{1,0:T(8,128)(2,1)S(1)}, bf16[80,256]{1,0:T(8,128)(2,1)S(1)}, u32[]{:S(2)}, u32[]{:S(2)}) collective-permute-start(bf16[80,256]{1,0:T(8,128)(2,1)S(1)} %get-tuple-element.202), channel_id=1, source_target_pairs={{0,2},{1,3},{2,0},{3,1},{4,6},{5,7},{6,4},{7,5},{8,10},{9,11},{10,... | collective-permute-start | bytes 122888 | tf_op jit(solution)/shard_map/ppermute | solution.py:1157
  13.8 9.3 %collective-permute-start.8 = (bf16[80,256]{1,0:T(8,128)(2,1)S(1)}, bf16[80,256]{1,0:T(8,128)(2,1)S(1)}, u32[]{:S(2)}, u32[]{:S(2)}) collective-permute-start(bf16[80,256]{1,0:T(8,128)(2,1)S(1)} %get-tuple-element.201), channel_id=1, source_target_pairs={{0,3},{1,2},{2,1},{3,0},{4,7},{5,6},{6,5},{7,4},{8,11},{9,10},{10,... | collective-permute-start | bytes 122888 | tf_op jit(solution)/shard_map/ppermute | solution.py:1157
  21.1 61.7 %collective-permute-start.17 = (bf16[120,768]{1,0:T(8,128)(2,1)S(1)}, bf16[120,768]{1,0:T(8,128)(2,1)S(1)}, u32[]{:S(2)}, u32[]{:S(2)}) collective-permute-start(bf16[120,768]{1,0:T(8,128)(2,1)S(1)} %constant_dynamic-update-slice_fusion), channel_id=1, source_target_pairs={{0,6},{1,7},{2,4},{3,5},{4,2},{5,3},{6,0},{7,1},{8,14},{9,15},{10,... | collective-permute-start | bytes 552968 | tf_op jit(solution)/shard_map/ppermute | solution.py:1157
  21.2 17.5 %collective-permute-start = (bf16[136,384]{1,0:T(8,128)(2,1)S(1)}, bf16[136,384]{1,0:T(8,128)(2,1)S(1)}, u32[]{:S(2)}, u32[]{:S(2)}) collective-permute-start(bf16[136,384]{1,0:T(8,128)(2,1)S(1)} %dynamic-slice_bitcast_fusion.15), channel_id=1, source_target_pairs={{0,4},{1,5},{2,6},{3,7},{4,0},{5,1},{6,2},{7,3},{8,12},{9,13},{10,... | collective-permute-start | bytes 313352 | tf_op jit(solution)/shard_map/ppermute | solution.py:1157
  23.1 15.6 %collective-permute-start.3 = (bf16[128,384]{1,0:T(8,128)(2,1)S(1)}, bf16[128,384]{1,0:T(8,128)(2,1)S(1)}, u32[]{:S(2)}, u32[]{:S(2)}) collective-permute-start(bf16[128,384]{1,0:T(8,128)(2,1)S(1)} %dynamic-slice_bitcast_fusion.16), channel_id=1, source_target_pairs={{0,4},{1,5},{2,6},{3,7},{4,0},{5,1},{6,2},{7,3},{8,12},{9,13},{10,... | collective-permute-start | bytes 294920 | tf_op jit(solution)/shard_map/ppermute | solution.py:1157
  38.7 8.4 %collective-permute-start.9 = (bf16[4,80,256]{2,1,0:T(8,128)(2,1)S(1)}, bf16[4,80,256]{2,1,0:T(8,128)(2,1)S(1)}, u32[]{:S(2)}, u32[]{:S(2)}) collective-permute-start(bf16[4,80,256]{2,1,0:T(8,128)(2,1)S(1)} %bitcast.306), channel_id=1, source_target_pairs={{0,4},{1,5},{2,6},{3,7},{4,0},{5,1},{6,2},{7,3},{8,12},{9,13},{10,... | collective-permute-start | bytes 491528 | tf_op jit(solution)/shard_map/ppermute | solution.py:1157
  38.8 9.9 %collective-permute-start.4 = (bf16[2,128,384]{2,1,0:T(8,128)(2,1)S(1)}, bf16[2,128,384]{2,1,0:T(8,128)(2,1)S(1)}, u32[]{:S(2)}, u32[]{:S(2)}) collective-permute-start(bf16[2,128,384]{2,1,0:T(8,128)(2,1)S(1)} %pad_maximum_fusion.15), channel_id=1, source_target_pairs={{0,2},{1,3},{2,0},{3,1},{4,6},{5,7},{6,4},{7,5},{8,10},{9,11},{10,... | collective-permute-start | bytes 589832 | tf_op jit(solution)/shard_map/ppermute | solution.py:1157
  47.1 6.4 %collective-permute-start.1 = (bf16[2,136,384]{2,1,0:T(8,128)(2,1)S(1)}, bf16[2,136,384]{2,1,0:T(8,128)(2,1)S(1)}, u32[]{:S(2)}, u32[]{:S(2)}) collective-permute-start(bf16[2,136,384]{2,1,0:T(8,128)(2,1)S(1)} %pad_maximum_fusion.14), channel_id=1, source_target_pairs={{0,1},{1,0},{2,3},{3,2},{4,5},{5,4},{6,7},{7,6},{8,9},{9,8},{10,11... | collective-permute-start | bytes 626696 | tf_op jit(solution)/shard_map/ppermute | solution.py:1157
  48.7 8.7 %collective-permute-start.10 = (bf16[1,2,4,80,256]{4,3,2,1,0:T(8,128)(2,1)S(1)}, bf16[1,2,4,80,256]{4,3,2,1,0:T(8,128)(2,1)S(1)}, u32[]{:S(2)}, u32[]{:S(2)}) collective-permute-start(bf16[1,2,4,80,256]{4,3,2,1,0:T(8,128)(2,1)S(1)} %maximum_bitcast_fusion), channel_id=1, source_target_pairs={{0,16},{8,24},{16,0},{24,8},{1,17},{9,25},{17,1},{25,9},{2,18},{10... | collective-permute-start | bytes 983048 | tf_op jit(solution)/shard_map/ppermute | solution.py:1157
  53.5 9.4 %collective-permute-start.5 = (bf16[2,2,128,384]{3,2,1,0:T(8,128)(2,1)S(1)}, bf16[2,2,128,384]{3,2,1,0:T(8,128)(2,1)S(1)}, u32[]{:S(2)}, u32[]{:S(2)}) collective-permute-start(bf16[2,2,128,384]{3,2,1,0:T(8,128)(2,1)S(1)} %pad_maximum_fusion.13), channel_id=1, source_target_pairs={{0,1},{1,0},{2,3},{3,2},{4,5},{5,4},{6,7},{7,6},{8,9},{9,8},{10,11... | collective-permute-start | bytes 1179656 | tf_op jit(solution)/shard_map/ppermute | solution.py:1157
  57.4 9.8 %collective-permute-start.2 = (bf16[2,2,136,384]{3,2,1,0:T(8,128)(2,1)S(1)}, bf16[2,2,136,384]{3,2,1,0:T(8,128)(2,1)S(1)}, u32[]{:S(2)}, u32[]{:S(2)}) collective-permute-start(bf16[2,2,136,384]{3,2,1,0:T(8,128)(2,1)S(1)} %pad_maximum_fusion.12), channel_id=1, source_target_pairs={{0,2},{1,3},{2,0},{3,1},{4,6},{5,7},{6,4},{7,5},{8,10},{9,11},{10,... | collective-permute-start | bytes 1253384 | tf_op jit(solution)/shard_map/ppermute | solution.py:1157
  57.6 9.7 %copy-start.9 = (bf16[24,3072]{1,0:T(8,128)(2,1)S(1)}, bf16[24,3072]{1,0:T(8,128)(2,1)}, u32[]{:S(2)}) copy-start(bf16[24,3072]{1,0:T(8,128)(2,1)} %param.42) | copy-start | bytes 442372
  62.9 9.5 %collective-permute-start.11 = (bf16[2,1,2,4,80,256]{5,4,3,2,0,1:T(8,128)(2,1)S(1)}, bf16[2,1,2,4,80,256]{5,4,3,2,0,1:T(8,128)(2,1)S(1)}, u32[]{:S(2)}, u32[]{:S(2)}) collective-permute-start(bf16[2,1,2,4,80,256]{5,4,3,2,0,1:T(8,128)(2,1)S(1)} %pad_maximum_fusion.10), channel_id=1, source_target_pairs={{0,8},{8,0},{16,24},{24,16},{1,9},{9,1},{17,25},{25,17},{2,10},{10... | collective-permute-start | bytes 1966088 | tf_op jit(solution)/shard_map/ppermute | solution.py:1157
  67.2 5.2 %collective-permute-start.12 = (bf16[24,3072]{1,0:T(8,128)(2,1)S(1)}, bf16[24,3072]{1,0:T(8,128)(2,1)S(1)}, u32[]{:S(2)}, u32[]{:S(2)}) collective-permute-start(bf16[24,3072]{1,0:T(8,128)(2,1)S(1)} %copy-done.9), channel_id=1, source_target_pairs={{0,2},{1,3},{2,0},{3,1},{4,6},{5,7},{6,4},{7,5},{8,10},{9,11},{10,... | collective-permute-start | bytes 442376 | tf_op jit(solution)/shard_map/ppermute | solution.py:1157
  72.4 10.4 %collective-permute-start.13 = (bf16[24,3072]{1,0:T(8,128)(2,1)S(1)}, bf16[24,3072]{1,0:T(8,128)(2,1)S(1)}, u32[]{:S(2)}, u32[]{:S(2)}) collective-permute-start(bf16[24,3072]{1,0:T(8,128)(2,1)S(1)} %copy-done.9), channel_id=1, source_target_pairs={{0,4},{1,5},{2,6},{3,7},{4,0},{5,1},{6,2},{7,3},{8,12},{9,13},{10,... | collective-permute-start | bytes 442376 | tf_op jit(solution)/shard_map/ppermute | solution.py:1157
  72.4 10.4 %collective-permute-start.14 = (bf16[24,3072]{1,0:T(8,128)(2,1)S(1)}, bf16[24,3072]{1,0:T(8,128)(2,1)S(1)}, u32[]{:S(2)}, u32[]{:S(2)}) collective-permute-start(bf16[24,3072]{1,0:T(8,128)(2,1)S(1)} %copy-done.9), channel_id=1, source_target_pairs={{0,6},{1,7},{2,4},{3,5},{4,2},{5,3},{6,0},{7,1},{8,14},{9,15},{10,... | collective-permute-start | bytes 442376 | tf_op jit(solution)/shard_map/ppermute | solution.py:1157
  83.4 17.7 %collective-permute-start.19 = (bf16[4,120,768]{2,1,0:T(8,128)(2,1)S(1)}, bf16[4,120,768]{2,1,0:T(8,128)(2,1)S(1)}, u32[]{:S(2)}, u32[]{:S(2)}) collective-permute-start(bf16[4,120,768]{2,1,0:T(8,128)(2,1)S(1)} %bitcast.296), channel_id=1, source_target_pairs={{0,16},{8,24},{16,0},{24,8},{1,17},{9,25},{17,1},{25,9},{2,18},{10... | collective-permute-start | bytes 2211848 | tf_op jit(solution)/shard_map/ppermute | solution.py:1157
  85.1 16.0 %collective-permute-start.18 = (bf16[4,24,3072]{2,1,0:T(8,128)(2,1)S(1)}, bf16[4,24,3072]{2,1,0:T(8,128)(2,1)S(1)}, u32[]{:S(2)}, u32[]{:S(2)}) collective-permute-start(bf16[4,24,3072]{2,1,0:T(8,128)(2,1)S(1)} %bitcast.298), channel_id=1, source_target_pairs={{0,1},{1,0},{2,3},{3,2},{4,5},{5,4},{6,7},{7,6},{8,9},{9,8},{10,11... | collective-permute-start | bytes 1769480 | tf_op jit(solution)/shard_map/ppermute | solution.py:1157
  101.6 27.9 %collective-permute-start.21 = (bf16[2,4,120,768]{3,2,1,0:T(8,128)(2,1)S(1)}, bf16[2,4,120,768]{3,2,1,0:T(8,128)(2,1)S(1)}, u32[]{:S(2)}, u32[]{:S(2)}) collective-permute-start(bf16[2,4,120,768]{3,2,1,0:T(8,128)(2,1)S(1)} %pad_maximum_fusion.4), channel_id=1, source_target_pairs={{0,1},{1,0},{2,3},{3,2},{4,5},{5,4},{6,7},{7,6},{8,9},{9,8},{10,11... | collective-permute-start | bytes 4423688 | tf_op jit(solution)/shard_map/ppermute | solution.py:1157
  103.3 21.2 %collective-permute-start.20 = (bf16[4,2,24,3072]{3,2,1,0:T(8,128)(2,1)S(1)}, bf16[4,2,24,3072]{3,2,1,0:T(8,128)(2,1)S(1)}, u32[]{:S(2)}, u32[]{:S(2)}) collective-permute-start(bf16[4,2,24,3072]{3,2,1,0:T(8,128)(2,1)S(1)} %pad_maximum_fusion.6), channel_id=1, source_target_pairs={{0,16},{8,24},{16,0},{24,8},{1,17},{9,25},{17,1},{25,9},{2,18},{10... | collective-permute-start | bytes 3538952 | tf_op jit(solution)/shard_map/ppermute | solution.py:1157
  124.5 5.1 %copy-start.4 = (bf16[4,2,24,3072]{3,2,1,0:T(8,128)(2,1)}, bf16[4,2,24,3072]{3,2,1,0:T(8,128)(2,1)S(1)}, u32[]{:S(2)}) copy-start(bf16[4,2,24,3072]{3,2,1,0:T(8,128)(2,1)S(1)} %collective-permute-done.20) | copy-start | bytes 3538948
  129.7 1.4 copy-start.5
  129.9 1.6 copy-start.1
  130.0 23.7 %collective-permute-start.23 = (bf16[2,8,120,768]{3,2,1,0:T(8,128)(2,1)S(1)}, bf16[2,8,120,768]{3,2,1,0:T(8,128)(2,1)}, u32[]{:S(2)}, u32[]{:S(2)}) collective-permute-start(bf16[2,8,120,768]{3,2,1,0:T(8,128)(2,1)S(1)} %bitcast.294), channel_id=1, source_target_pairs={{0,8},{8,0},{16,24},{24,16},{1,9},{9,1},{17,25},{25,17},{2,10},{10... | collective-permute-start | bytes 8847368 | tf_op jit(solution)/shard_map/ppermute | solution.py:1157
  133.1 20.5 %collective-permute-start.22 = (bf16[2,192,3072]{2,1,0:T(8,128)(2,1)}, bf16[2,192,3072]{2,1,0:T(8,128)(2,1)}, u32[]{:S(2)}, u32[]{:S(2)}) collective-permute-start(bf16[2,192,3072]{2,1,0:T(8,128)(2,1)} %pad_maximum_fusion.2.inner_own), channel_id=1, source_target_pairs={{0,8},{8,0},{16,24},{24,16},{1,9},{9,1},{17,25},{25,17},{2,10},{10... | collective-permute-start | bytes 7077896 | tf_op jit(solution)/shard_map/ppermute | solution.py:1157
  133.1 20.5 %all-to-all-start = ((bf16[8,192,128]{2,1,0:T(8,128)(2,1)}), bf16[8,192,128]{2,1,0:T(8,128)(2,1)S(1)}, u32[]{:S(2)}, u32[]{:S(2)}) async-start(bf16[8,192,128]{2,1,0:T(8,128)(2,1)} %get-tuple-element.117), calls=%async_computation | async-start | bytes 786432 | tf_op jit(solution)/shard_map/all_to_all | solution.py:1328
  153.6 0.7 copy-start.8
  178.0 7.5 %collective-permute-start.24 = (bf16[2,192,3072]{2,1,0:T(8,128)(2,1)}, bf16[2,192,3072]{2,1,0:T(8,128)(2,1)}, u32[]{:S(2)}, u32[]{:S(2)}) collective-permute-start(bf16[2,192,3072]{2,1,0:T(8,128)(2,1)} %get-tuple-element.126), channel_id=1, source_target_pairs={{0,8},{8,0},{16,24},{24,16},{1,9},{9,1},{17,25},{25,17},{2,10},{10... | collective-permute-start | bytes 7077896 | tf_op jit(solution)/shard_map/ppermute | solution.py:1157
  178.1 13.1 %collective-permute-start.25 = (bf16[2,8,120,768]{3,2,1,0:T(8,128)(2,1)}, bf16[2,8,120,768]{3,2,1,0:T(8,128)(2,1)S(1)}, u32[]{:S(2)}, u32[]{:S(2)}) collective-permute-start(bf16[2,8,120,768]{3,2,1,0:T(8,128)(2,1)} %get-tuple-element.128), channel_id=1, source_target_pairs={{0,8},{8,0},{16,24},{24,16},{1,9},{9,1},{17,25},{25,17},{2,10},{10... | collective-permute-start | bytes 8847368 | tf_op jit(solution)/shard_map/ppermute | solution.py:1157
  178.5 18.1 %all-to-all-start.1 = ((bf16[8,200,128]{2,1,0:T(8,128)(2,1)}), bf16[8,200,128]{2,1,0:T(8,128)(2,1)S(1)}, u32[]{:S(2)}, u32[]{:S(2)}) async-start(bf16[8,200,128]{2,1,0:T(8,128)(2,1)} %get-tuple-element.124), calls=%async_computation.1 | async-start | bytes 819200 | tf_op jit(solution)/shard_map/all_to_all | solution.py:1356
  188.8 3.9 %copy-start = (bf16[2,8,120,768]{3,2,1,0:T(8,128)(2,1)S(1)}, bf16[2,8,120,768]{3,2,1,0:T(8,128)(2,1)}, u32[]{:S(2)}) copy-start(bf16[2,8,120,768]{3,2,1,0:T(8,128)(2,1)} %get-tuple-element.127) | copy-start | bytes 8847364
  191.1 1.6 copy-start.2
  196.6 0.8 copy-start.7
  232.0 2.4 collective-permute-start.33
  235.9 9.8 %collective-permute-start.34 = (bf16[2,4,80,256]{3,2,1,0:T(8,128)(2,1)S(1)}, bf16[2,4,80,256]{3,2,1,0:T(8,128)(2,1)S(1)}, u32[]{:S(2)}, u32[]{:S(2)}) collective-permute-start(bf16[2,4,80,256]{3,2,1,0:T(8,128)(2,1)S(1)} %dynamic-slice_bitcast_fusion.5), channel_id=1, source_target_pairs={{0,16},{8,24},{16,0},{24,8},{1,17},{9,25},{17,1},{25,9},{2,18},{10... | collective-permute-start | bytes 983048 | tf_op jit(solution)/shard_map/ppermute | solution.py:1157
  246.5 10.0 %collective-permute-start.35 = (bf16[4,80,256]{2,1,0:T(8,128)(2,1)}, bf16[4,80,256]{2,1,0:T(8,128)(2,1)S(1)}, u32[]{:S(2)}, u32[]{:S(2)}) collective-permute-start(bf16[4,80,256]{2,1,0:T(8,128)(2,1)} %dynamic-slice_bitcast_fusion.11), channel_id=1, source_target_pairs={{0,4},{1,5},{2,6},{3,7},{4,0},{5,1},{6,2},{7,3},{8,12},{9,13},{10,... | collective-permute-start | bytes 491528 | tf_op jit(solution)/shard_map/ppermute | solution.py:1157
  247.8 41.8 %collective-permute-start.26 = (bf16[4,2,24,3072]{3,2,0,1:T(8,128)(2,1)}, bf16[4,2,24,3072]{3,2,0,1:T(8,128)(2,1)}, u32[]{:S(2)}, u32[]{:S(2)}) collective-permute-start(bf16[4,2,24,3072]{3,2,0,1:T(8,128)(2,1)} %bitcast.301), channel_id=1, source_target_pairs={{0,16},{8,24},{16,0},{24,8},{1,17},{9,25},{17,1},{25,9},{2,18},{10... | collective-permute-start | bytes 3538952 | tf_op jit(solution)/shard_map/ppermute | solution.py:1157
  248.3 41.3 %collective-permute-start.27 = (bf16[2,4,120,768]{3,2,1,0:T(8,128)(2,1)}, bf16[2,4,120,768]{3,2,1,0:T(8,128)(2,1)}, u32[]{:S(2)}, u32[]{:S(2)}) collective-permute-start(bf16[2,4,120,768]{3,2,1,0:T(8,128)(2,1)} %dynamic-slice_bitcast_fusion), channel_id=1, source_target_pairs={{0,1},{1,0},{2,3},{3,2},{4,5},{5,4},{6,7},{7,6},{8,9},{9,8},{10,11... | collective-permute-start | bytes 4423688 | tf_op jit(solution)/shard_map/ppermute | solution.py:1157
  256.6 26.6 %collective-permute-start.36 = (bf16[80,256]{1,0:T(8,128)(2,1)S(1)}, bf16[80,256]{1,0:T(8,128)(2,1)S(1)}, u32[]{:S(2)}, u32[]{:S(2)}) collective-permute-start(bf16[80,256]{1,0:T(8,128)(2,1)S(1)} %get-tuple-element.199), channel_id=1, source_target_pairs={{0,1},{1,0},{2,3},{3,2},{4,5},{5,4},{6,7},{7,6},{8,9},{9,8},{10,11... | collective-permute-start | bytes 122888 | tf_op jit(solution)/shard_map/ppermute | solution.py:1157
  257.0 26.2 %collective-permute-start.37 = (bf16[80,256]{1,0:T(8,128)(2,1)S(1)}, bf16[80,256]{1,0:T(8,128)(2,1)S(1)}, u32[]{:S(2)}, u32[]{:S(2)}) collective-permute-start(bf16[80,256]{1,0:T(8,128)(2,1)S(1)} %get-tuple-element.198), channel_id=1, source_target_pairs={{0,2},{1,3},{2,0},{3,1},{4,6},{5,7},{6,4},{7,5},{8,10},{9,11},{10,... | collective-permute-start | bytes 122888 | tf_op jit(solution)/shard_map/ppermute | solution.py:1157
  257.0 26.2 %collective-permute-start.38 = (bf16[80,256]{1,0:T(8,128)(2,1)S(1)}, bf16[80,256]{1,0:T(8,128)(2,1)S(1)}, u32[]{:S(2)}, u32[]{:S(2)}) collective-permute-start(bf16[80,256]{1,0:T(8,128)(2,1)S(1)} %get-tuple-element.197), channel_id=1, source_target_pairs={{0,3},{1,2},{2,1},{3,0},{4,7},{5,6},{6,5},{7,4},{8,11},{9,10},{10,... | collective-permute-start | bytes 122888 | tf_op jit(solution)/shard_map/ppermute | solution.py:1157
  289.6 3.5 %copy-start.3 = (bf16[1024,768]{1,0:T(8,128)(2,1)S(1)}, bf16[1024,768]{1,0:T(8,128)(2,1)}, u32[]{:S(2)}) copy-start(bf16[1024,768]{1,0:T(8,128)(2,1)} %get-tuple-element.138) | copy-start | bytes 4718596
  291.9 25.5 %collective-permute-start.43 = (bf16[4,24,3072]{2,1,0:T(8,128)(2,1)S(1)}, bf16[4,24,3072]{2,1,0:T(8,128)(2,1)S(1)}, u32[]{:S(2)}, u32[]{:S(2)}) collective-permute-start(bf16[4,24,3072]{2,1,0:T(8,128)(2,1)S(1)} %dynamic-slice_bitcast_fusion.3), channel_id=1, source_target_pairs={{0,1},{1,0},{2,3},{3,2},{4,5},{5,4},{6,7},{7,6},{8,9},{9,8},{10,11... | collective-permute-start | bytes 1769480 | tf_op jit(solution)/shard_map/ppermute | solution.py:1157
  293.4 9.0 %collective-permute-start.30 = (bf16[2,2,128,384]{3,2,1,0:T(8,128)(2,1)S(1)}, bf16[2,2,128,384]{3,2,1,0:T(8,128)(2,1)S(1)}, u32[]{:S(2)}, u32[]{:S(2)}) collective-permute-start(bf16[2,2,128,384]{3,2,1,0:T(8,128)(2,1)S(1)} %dynamic-slice_bitcast_fusion.4), channel_id=1, source_target_pairs={{0,2},{1,3},{2,0},{3,1},{4,6},{5,7},{6,4},{7,5},{8,10},{9,11},{10,... | collective-permute-start | bytes 1179656 | tf_op jit(solution)/shard_map/ppermute | solution.py:1157
  295.4 20.3 %collective-permute-start.28 = (bf16[2,2,128,384]{3,2,0,1:T(8,128)(2,1)S(1)}, bf16[2,2,128,384]{3,2,0,1:T(8,128)(2,1)S(1)}, u32[]{:S(2)}, u32[]{:S(2)}) collective-permute-start(bf16[2,2,128,384]{3,2,0,1:T(8,128)(2,1)S(1)} %bitcast.310), channel_id=1, source_target_pairs={{0,1},{1,0},{2,3},{3,2},{4,5},{5,4},{6,7},{7,6},{8,9},{9,8},{10,11... | collective-permute-start | bytes 1179656 | tf_op jit(solution)/shard_map/ppermute | solution.py:1157
  297.7 30.9 %collective-permute-start.39 = (bf16[4,120,768]{2,1,0:T(8,128)(2,1)S(1)}, bf16[4,120,768]{2,1,0:T(8,128)(2,1)S(1)}, u32[]{:S(2)}, u32[]{:S(2)}) collective-permute-start(bf16[4,120,768]{2,1,0:T(8,128)(2,1)S(1)} %dynamic-slice_bitcast_fusion.1), channel_id=1, source_target_pairs={{0,16},{8,24},{16,0},{24,8},{1,17},{9,25},{17,1},{25,9},{2,18},{10... | collective-permute-start | bytes 2211848 | tf_op jit(solution)/shard_map/ppermute | solution.py:1157
  302.6 18.0 %collective-permute-start.31 = (bf16[2,128,384]{2,1,0:T(8,128)(2,1)S(1)}, bf16[2,128,384]{2,1,0:T(8,128)(2,1)S(1)}, u32[]{:S(2)}, u32[]{:S(2)}) collective-permute-start(bf16[2,128,384]{2,1,0:T(8,128)(2,1)S(1)} %dynamic-slice_bitcast_fusion.6), channel_id=1, source_target_pairs={{0,1},{1,0},{2,3},{3,2},{4,5},{5,4},{6,7},{7,6},{8,9},{9,8},{10,11... | collective-permute-start | bytes 589832 | tf_op jit(solution)/shard_map/ppermute | solution.py:1157
  315.8 8.8 %collective-permute-start.29 = (bf16[2,128,384]{2,1,0:T(8,128)(2,1)S(1)}, bf16[2,128,384]{2,1,0:T(8,128)(2,1)S(1)}, u32[]{:S(2)}, u32[]{:S(2)}) collective-permute-start(bf16[2,128,384]{2,1,0:T(8,128)(2,1)S(1)} %dynamic-slice_bitcast_fusion.7), channel_id=1, source_target_pairs={{0,2},{1,3},{2,0},{3,1},{4,6},{5,7},{6,4},{7,5},{8,10},{9,11},{10,... | collective-permute-start | bytes 589832 | tf_op jit(solution)/shard_map/ppermute | solution.py:1157
  317.5 14.2 %collective-permute-start.44 = (bf16[24,3072]{1,0:T(8,128)(2,1)S(1)}, bf16[24,3072]{1,0:T(8,128)(2,1)S(1)}, u32[]{:S(2)}, u32[]{:S(2)}) collective-permute-start(bf16[24,3072]{1,0:T(8,128)(2,1)S(1)} %get-tuple-element.175), channel_id=1, source_target_pairs={{0,2},{1,3},{2,0},{3,1},{4,6},{5,7},{6,4},{7,5},{8,10},{9,11},{10,... | collective-permute-start | bytes 442376 | tf_op jit(solution)/shard_map/ppermute | solution.py:1157
  318.1 13.7 %collective-permute-start.45 = (bf16[24,3072]{1,0:T(8,128)(2,1)S(1)}, bf16[24,3072]{1,0:T(8,128)(2,1)S(1)}, u32[]{:S(2)}, u32[]{:S(2)}) collective-permute-start(bf16[24,3072]{1,0:T(8,128)(2,1)S(1)} %get-tuple-element.177), channel_id=1, source_target_pairs={{0,4},{1,5},{2,6},{3,7},{4,0},{5,1},{6,2},{7,3},{8,12},{9,13},{10,... | collective-permute-start | bytes 442376 | tf_op jit(solution)/shard_map/ppermute | solution.py:1157
  320.6 14.7 %collective-permute-start.46 = (bf16[24,3072]{1,0:T(8,128)(2,1)S(1)}, bf16[24,3072]{1,0:T(8,128)(2,1)S(1)}, u32[]{:S(2)}, u32[]{:S(2)}) collective-permute-start(bf16[24,3072]{1,0:T(8,128)(2,1)S(1)} %get-tuple-element.176), channel_id=1, source_target_pairs={{0,6},{1,7},{2,4},{3,5},{4,2},{5,3},{6,0},{7,1},{8,14},{9,15},{10,... | collective-permute-start | bytes 442376 | tf_op jit(solution)/shard_map/ppermute | solution.py:1157
  324.6 24.0 %collective-permute-start.32 = (bf16[128,768]{1,0:T(8,128)(2,1)S(1)}, bf16[128,768]{1,0:T(8,128)(2,1)S(1)}, u32[]{:S(2)}, u32[]{:S(2)}) collective-permute-start(bf16[128,768]{1,0:T(8,128)(2,1)S(1)} %fusion.18), channel_id=1, source_target_pairs={{0,4},{1,5},{2,6},{3,7},{4,0},{5,1},{6,2},{7,3},{8,12},{9,13},{10,... | collective-permute-start | bytes 589832 | tf_op jit(solution)/shard_map/ppermute | solution.py:1157
  328.9 19.8 %copy-start.6 = (f32[256,768]{1,0:T(8,128)S(1)}, f32[256,768]{1,0:T(8,128)}, u32[]{:S(2)}) copy-start(f32[256,768]{1,0:T(8,128)} %get-tuple-element.123) | copy-start | bytes 2359300
  328.9 20.6 %collective-permute-start.40 = (bf16[120,768]{1,0:T(8,128)(2,1)S(1)}, bf16[120,768]{1,0:T(8,128)(2,1)S(1)}, u32[]{:S(2)}, u32[]{:S(2)}) collective-permute-start(bf16[120,768]{1,0:T(8,128)(2,1)S(1)} %get-tuple-element.170), channel_id=1, source_target_pairs={{0,2},{1,3},{2,0},{3,1},{4,6},{5,7},{6,4},{7,5},{8,10},{9,11},{10,... | collective-permute-start | bytes 552968 | tf_op jit(solution)/shard_map/ppermute | solution.py:1157
  331.8 19.8 %collective-permute-start.41 = (bf16[120,768]{1,0:T(8,128)(2,1)S(1)}, bf16[120,768]{1,0:T(8,128)(2,1)S(1)}, u32[]{:S(2)}, u32[]{:S(2)}) collective-permute-start(bf16[120,768]{1,0:T(8,128)(2,1)S(1)} %get-tuple-element.172), channel_id=1, source_target_pairs={{0,4},{1,5},{2,6},{3,7},{4,0},{5,1},{6,2},{7,3},{8,12},{9,13},{10,... | collective-permute-start | bytes 552968 | tf_op jit(solution)/shard_map/ppermute | solution.py:1157
  331.8 19.8 %collective-permute-start.42 = (bf16[120,768]{1,0:T(8,128)(2,1)S(1)}, bf16[120,768]{1,0:T(8,128)(2,1)S(1)}, u32[]{:S(2)}, u32[]{:S(2)}) collective-permute-start(bf16[120,768]{1,0:T(8,128)(2,1)S(1)} %get-tuple-element.171), channel_id=1, source_target_pairs={{0,6},{1,7},{2,4},{3,5},{4,2},{5,3},{6,0},{7,1},{8,14},{9,15},{10,... | collective-permute-start | bytes 552968 | tf_op jit(solution)/shard_map/ppermute | solution.py:1157
where the time goes:
time: 354 us; the launch traced here: 353 us
  waiting for transfers between devices  139 us (39%)
  Pallas kernels  94.7 us (27%)
  starting transfers between devices  66.9 us (19%)
  other arithmetic  27.1 us (8%)
  local copies, waits for them, and re-layouts  24 us (7%)
    ppermute x47, waiting for transfers between devices, swap(): return lax.ppermute(x, axis, [(i, i ^ bit) for i in range(count)])  127 us
    ppermute x47, starting transfers between devices, swap(): return lax.ppermute(x, axis, [(i, i ^ bit) for i in range(count)])  55 us
    pallas_call x2, Pallas kernels, attention_forward(): pl.pallas_call(lambda *refs: kernel(*refs[:5], *refs[5 + skip:]), grid=(c...  33.2 us
    pallas_call x1, Pallas kernels, attention_backward(): pl.pallas_call(functools.partial(attention_backward_kernel, tile), grid=(...  31 us
    pallas_call x1, Pallas kernels, token_block(): pl.pallas_call(token_kernel, in_specs=[pl.BlockSpec(memory_space=pltpu.SM...  23.6 us
    convert_element_type x13, other arithmetic, add_low(): return (a.astype(F32) + b.astype(F32)).astype(BF)  12 us
    all_to_all x1, waiting for transfers between devices, head_layout(): lax.all_to_all(att, CTX, 0, 0, tiled=True).reshape(seqs, width, stretch)  11.5 us
    all_to_all x1, starting transfers between devices, head_layout(): lax.all_to_all(att, CTX, 0, 0, tiled=True).reshape(seqs, width, stretch)  8.13 us
  transfers between devices with their start and end apart: 49, of which 21 were waited for; matrix products, arithmetic and copies ran while one was open for 10% of the time, Pallas kernels for 11%

commit v1 on v0

--- a/solution.py
+++ b/solution.py
@@ -630,7 +630,8 @@
 
 
 def attention_forward_kernel(tile, x_ref, w_ref, vec_ref, kext_ref, trig_ref,
-                             att_ref, qt_ref, kb_ref, v1_ref, qp_ref, save_ref, scl_ref, wh_ref, kt_ref):
+                             att_ref, qb_ref, kb_ref, v1_ref, qp_ref, save_ref, scl_ref, wh_ref, prob_ref,
+                             kt_ref, qt_ref):
     step = pl.program_id(1)
     rows = x_ref.shape[0]
     width = x_ref.shape[1]
@@ -640,7 +641,7 @@
 
     @pl.when((pl.program_id(0) == 0) & (step == 0))
     def _():
-        kt_ref[:, :width] = trig_ref[...].astype(BF)
+        kt_ref[:, :width] = trig_ref[...]
 
     @pl.when(step == 0)
     def _():
@@ -651,7 +652,9 @@
         w_pos = jnp.where(w_lane < DH, pltpu.roll(w[:, LANES:].astype(F32), DH, 1), 0.0).astype(BF)
 
         def body(i, carry):
-            at = pl.ds(pl.multiple_of(i * tile, tile), tile)
+            at = slice(i * 256, (i + 1) * 256)
+            lane = lax.broadcasted_iota(jnp.int32, (256, LANES), 1)
+            low = lane < DH
             proj = mm(x_ref[at, :], w, ROWCOL)
             kext = kext_ref[at, :].astype(F32)
             kind = kext[:, DH + 3:DH + 4]
@@ -675,37 +678,54 @@
             ext = jnp.where(lane == DH + 3, s_hi, ext)
             ext = jnp.where(lane == DH + 4, s_mid, ext)
             ext = jnp.where(lane == DH + 5, 1.0, ext)
-            qt_ref[0, at, width:] = jnp.where(low, scaled + vec[0:1, :], ext).astype(BF)
+            q_block = jnp.where(low, scaled + vec[0:1, :], ext).astype(BF)
+            qb_ref[0, at, :] = q_block
+            qt_ref[at, width:] = q_block
             qp = jnp.where(low, scaled + vec[1:2, :], 0.0).astype(BF)
             qp_ref[0, at, :] = qp
             grow = mm(qp, w_pos, ROWS_CC)
             q_sin = grow[:, :half]
             q_cos = grow[:, half:]
-            c = trig_ref[at, :half]
-            s = trig_ref[at, half:]
-            qt_ref[0, at, :half] = (q_sin * s + q_cos * c).astype(BF)
-            qt_ref[0, at, half:width] = (q_cos * s - q_sin * c).astype(BF)
+            c = trig_ref[at, :half].astype(F32)
+            s = trig_ref[at, half:].astype(F32)
+            qt_ref[at, :half] = (q_sin * s + q_cos * c).astype(BF)
+            qt_ref[at, half:width] = (q_cos * s - q_sin * c).astype(BF)
             return carry
 
-        lax.fori_loop(0, rows // tile, body, 0)
-
-    at = pl.ds(pl.multiple_of(step * tile, tile), tile)
-    scores = mm(qt_ref[0, at, :], kt_ref[...], ROWS_CC)
-    top = jnp.max(scores, axis=1, keepdims=True)
-    prob = jnp.exp(scores - top)
-    mixed = mm(prob.astype(BF), v1_ref[0], ROWCOL)
-    total = mixed[:, DH:DH + 1]
-    att = mixed / total
-    save_ref[0] = jnp.where(low, att, top + jnp.log(total))
-    att_t = jnp.transpose(att)[:DH, :].astype(BF)
-    for i in range(tile // LANES):
-        att_ref[i] = att_t[:, i * LANES:(i + 1) * LANES]
-
-
-def attention_backward_kernel(tile, do_ref, x_ref, w_ref, vec_ref, kext_ref, trig_ref,
-                              qt_ref, kb_ref, v1_ref, qp_ref, save_ref, scl_ref,
+        for i in range(rows // 256):
+            body(i, 0)
+
+    att_parts = att_ref.shape[0]
+    sub = 256
+    count = tile // sub
+    small_lane = lax.broadcasted_iota(jnp.int32, (sub, LANES), 1) < DH
+
+    def scores_of(i):
+        at = pl.ds(pl.multiple_of(step * tile + i * sub, sub), sub)
+        return mm(qt_ref[at, :], kt_ref[...], ROWS_CC)
+
+    later = scores_of(0)
+    for i in range(count):
+        scores = later
+        if i + 1 < count:
+            later = scores_of(i + 1)
+        top = jnp.max(scores, axis=1, keepdims=True)
+        prob = jnp.exp(scores - top).astype(BF)
+        prob_ref[0, i * sub:(i + 1) * sub, :] = prob
+        mixed = mm(prob, v1_ref[0], ROWCOL)
+        total = mixed[:, DH:DH + 1]
+        att = mixed / total
+        save_ref[0, i * sub:(i + 1) * sub, :] = jnp.where(small_lane, att, 1.0 / total)
+        att_t = jnp.transpose(att)[:DH, :].astype(BF)
+        for n in range(sub // LANES):
+            b = i * (sub // LANES) + n
+            att_ref[b % att_parts, b // att_parts] = att_t[:, n * LANES:(n + 1) * LANES]
+
+
+def attention_backward_kernel(tile, core_ref, do_ref, x_ref, w_ref, vec_ref, kext_ref, trig_ref,
+                              qb_ref, kb_ref, v1_ref, qp_ref, save_ref, scl_ref, prob_ref,
                               dx_ref, dw_ref, small_ref,
-                              kt_ref, q_ref, dk_acc, dv_acc, d_ref, dwp_ref, dx_acc):
+                              kt_ref, dk_acc, dv_acc, d_ref, dwp_ref, dx_acc):
     step = pl.program_id(1)
     width = trig_ref.shape[1]
     half = width // 2
@@ -714,7 +734,7 @@
 
     @pl.when((pl.program_id(0) == 0) & (step == 0))
     def _():
-        kt_ref[:, :width] = trig_ref[...].astype(BF)
+        kt_ref[:, :width] = trig_ref[...]
 
     @pl.when(step == 0)
     def _():
@@ -729,30 +749,25 @@
     w_lane = lax.broadcasted_iota(jnp.int32, (width, LANES), 1)
     w_pos = jnp.where(w_lane < DH, pltpu.roll(w[:, LANES:].astype(F32), DH, 1), 0.0).astype(BF)
     save = save_ref[0]
-    lse = save[:, DH:DH + 1]
-    do_t = jnp.concatenate([do_ref[i] for i in range(tile // LANES)], axis=1).astype(F32)
+    inverse = save[:, DH:DH + 1]
+    parts = do_ref.shape[0]
+    do_t = jnp.concatenate([do_ref[i % parts, i // parts] for i in range(tile // LANES)], axis=1).astype(F32)
     d_out = jnp.transpose(jnp.concatenate([do_t, jnp.zeros_like(do_t)], axis=0))
+    d_out = d_out * inverse
     delta = jnp.sum(d_out * save, axis=1, keepdims=True)
-    l_hi, l_mid, l_lo = split3(-lse)
     d_hi, d_mid, d_lo = split3(-delta)
-    q_block = qt_ref[0, :, width:].astype(F32)
-    q_ref[:, :width] = qt_ref[0, :, :width]
-    q_block = jnp.where(lane == DH + 6, l_hi, q_block)
-    q_block = jnp.where(lane == DH + 7, l_mid, q_block)
-    q_block = jnp.where(lane == DH + 8, l_lo, q_block)
-    q_block = q_block.astype(BF)
-    q_ref[:, width:] = q_block
+    q_block = qb_ref[0]
     ext = jnp.where(lane == DH, d_hi, d_out)
     ext = jnp.where(lane == DH + 1, d_mid, ext)
     ext = jnp.where(lane == DH + 2, d_lo, ext)
     d_ext = ext.astype(BF)
-    prob = jnp.exp(mm(q_ref[...], kt_ref[...], ROWS_CC))
-    dv_acc[...] += mm(d_ext, prob.astype(BF), COLS_CC)
-    d_score = (prob * mm(d_ext, v1_ref[0], ROWS_CC)).astype(BF)
+    prob = prob_ref[0]
+    dv_acc[...] += mm(d_ext, prob, COLS_CC)
+    d_score = (prob.astype(F32) * mm(d_ext, v1_ref[0], ROWS_CC)).astype(BF)
     dk_acc[...] += mm(q_block, d_score, COLS_CC)
     dq = mm(d_score, kt_ref[...], ROWCOL)
-    c = trig_ref[at, :half]
-    s = trig_ref[at, half:]
+    c = trig_ref[at, :half].astype(F32)
+    s = trig_ref[at, half:].astype(F32)
     du_c = dq[:, :half]
     du_s = dq[:, half:width]
     back = jnp.concatenate([s * du_c - c * du_s, c * du_c + s * du_s], axis=1).astype(BF)
@@ -784,9 +799,10 @@
         small_ref[0, 5:6, :] = dv_sum[:1, :]
         d_wt = mm(d_ref[...], x_ref[...], ROWCOL)
         d_w = jnp.transpose(jnp.concatenate([d_wt, dwp_ref[...]], axis=0))
-        shard = dw_ref.shape[1]
-        for i in range(dw_ref.shape[0]):
-            dw_ref[i] = d_w[i * shard:(i + 1) * shard, :].astype(BF)
+        shard = dw_ref.shape[3]
+        members = dw_ref.shape[2]
+        for i in range(4 * members):
+            dw_ref[(i // members % 2) ^ core_ref[0], i // (2 * members), i % members] = d_w[i * shard:(i + 1) * shard, :].astype(BF)
         d_x = lax.dot_general(d_ref[...], w_ref[0][:, :3 * DH], (((0,), (1,)), ((), ())), preferred_element_type=F32)
 
         @pl.when(pl.program_id(0) == 0)
@@ -802,7 +818,7 @@
             dx_ref[...] = dx_acc[...].astype(BF)
 
 
-def attention_forward(x, w_block, first, count, heads, vec, kext, trig, previous=(), tile=512):
+def attention_forward(x, w_block, first, count, heads, vec, kext, trig, previous=(), tile=1024):
     rows, width = x.shape
     owners = w_block.shape[0]
     shard = width // owners
@@ -819,16 +835,18 @@
         in_specs=[fixed((rows, width)), pl.BlockSpec((owners, shard, 2 * LANES), lambda h, t: (0, first + h, 0)),
                   per_head((8, LANES)), fixed((rows, LANES)), fixed((rows, width))]
         + [pl.BlockSpec(memory_space=pl.ANY)] * skip,
-        out_specs=[pl.BlockSpec((tile // LANES, DH, LANES), lambda h, t: (t, first + h, 0)),
-                   per_head((rows, full)), per_head((rows, LANES)), per_head((rows, LANES)),
+        out_specs=[pl.BlockSpec((2, tile // (2 * LANES), DH, LANES), lambda h, t: (0, t, first + h, 0)),
+                   per_head((rows, LANES)), per_head((rows, LANES)), per_head((rows, LANES)),
                    per_head((rows, LANES)),
                    pl.BlockSpec((1, tile, LANES), lambda h, t: (first + h, t, 0)),
-                   per_head((rows, LANES)), per_head((width, 2 * LANES))],
-        out_shape=[S((rows // LANES, heads * DH, LANES), BF), S((heads, rows, full), BF),
+                   per_head((rows, LANES)), per_head((width, 2 * LANES)),
+                   pl.BlockSpec((1, tile, rows), lambda h, t: (first + h, t, 0))],
+        out_shape=[S((2, rows // (2 * LANES), heads * DH, LANES), BF), S((heads, rows, LANES), BF),
                    S((heads, rows, LANES), BF), S((heads, rows, LANES), BF), S((heads, rows, LANES), BF),
-                   S((heads, rows, LANES), F32), S((heads, rows, LANES), F32), S((heads, width, 2 * LANES), BF)],
+                   S((heads, rows, LANES), F32), S((heads, rows, LANES), F32), S((heads, width, 2 * LANES), BF),
+                   S((heads, rows, rows), BF)],
         input_output_aliases={5 + i: i for i in range(skip)},
-        scratch_shapes=[pltpu.VMEM((rows, full), BF)],
+        scratch_shapes=[pltpu.VMEM((rows, full), BF), pltpu.VMEM((rows, full), BF)],
         compiler_params=pltpu.CompilerParams(dimension_semantics=("arbitrary", "arbitrary"),
                                              vmem_limit_bytes=56 * 2 ** 20),
         cost_estimate=pl.CostEstimate(flops=flops, bytes_accessed=rows * width * 16, transcendentals=count * rows * rows),
@@ -836,9 +854,10 @@
     )(x, w_block, vec, kext, trig, *previous)
 
 
-def attention_backward(d_out, x, w, vec, kext, trig, qt, kb, v1, qp, save, scl, owners, block_rows, tile=512):
-    heads, rows, full = qt.shape
-    width = full - LANES
+def attention_backward(core, d_out, x, w, vec, kext, trig, qb, kb, v1, qp, save, scl, prob, owners, block_rows, tile=1024):
+    heads, rows, _ = qb.shape
+    width = x.shape[1]
+    full = width + LANES
     shard = width // owners
     per_head = lambda shape: pl.BlockSpec((1,) + shape, lambda h, t: (h, 0, 0))
     per_tile = lambda cols: pl.BlockSpec((1, tile, cols), lambda h, t: (h, t, 0))
@@ -847,17 +866,17 @@
     return pl.pallas_call(
         functools.partial(attention_backward_kernel, tile),
         grid=(heads, rows // tile),
-        in_specs=[pl.BlockSpec((tile // LANES, DH, LANES), lambda h, t: (t, h, 0)), fixed((rows, width)),
+        in_specs=[pl.BlockSpec(memory_space=pltpu.SMEM), pl.BlockSpec((2, tile // (2 * LANES), DH, LANES), lambda h, t: (0, t, h, 0)), fixed((rows, width)),
                   per_head((width, 256)), per_head((8, LANES)),
                   pl.BlockSpec((tile, LANES), lambda h, t: (t, 0)), fixed((rows, width)),
-                  per_tile(full), per_head((rows, LANES)), per_head((rows, LANES)), per_tile(LANES),
-                  per_tile(LANES), per_tile(LANES)],
-        out_specs=[fixed((rows, width)), pl.BlockSpec((owners, shard, 2 * LANES), lambda h, t: (0, h, 0)),
+                  per_tile(LANES), per_head((rows, LANES)), per_head((rows, LANES)), per_tile(LANES),
+                  per_tile(LANES), per_tile(LANES), per_tile(rows)],
+        out_specs=[fixed((rows, width)), pl.BlockSpec((2, 2, owners // 4, shard, 2 * LANES), lambda h, t: (0, 0, 0, h, 0)),
                    per_head((8, LANES))],
         out_shape=[jax.ShapeDtypeStruct((rows, width), BF),
-                   jax.ShapeDtypeStruct((owners, block_rows, 2 * LANES), BF),
+                   jax.ShapeDtypeStruct((2, 2, owners // 4, block_rows, 2 * LANES), BF),
                    jax.ShapeDtypeStruct((heads, 8, LANES), F32)],
-        scratch_shapes=[pltpu.VMEM((rows, full), BF), pltpu.VMEM((tile, full), BF),
+        scratch_shapes=[pltpu.VMEM((rows, full), BF),
                         pltpu.VMEM((LANES, rows), F32), pltpu.VMEM((LANES, rows), F32),
                         pltpu.VMEM((3 * DH, rows), BF), pltpu.VMEM((DH, width), F32),
                         pltpu.VMEM((rows, width), F32)],
@@ -865,7 +884,7 @@
                                              vmem_limit_bytes=56 * 2 ** 20),
         cost_estimate=pl.CostEstimate(flops=flops, bytes_accessed=rows * width * 20, transcendentals=heads * rows * rows),
         name="attention_backward",
-    )(d_out, x, w, vec, kext, trig, qt, kb, v1, qp, save, scl)
+    )(core.reshape(1), d_out, x, w, vec, kext, trig, qb, kb, v1, qp, save, scl, prob)
 
 
 def key_extension(kinds, valid):
@@ -879,30 +898,43 @@
 
 
 def pack_kernel(heads, groups, *refs):
-    mats, smalls, wide_ref, out_ref = refs[:4], refs[4:16], refs[16], refs[17]
-    rows = mats[0].shape[0]
+    mats, smalls, (wide_ref, kinds_ref, inner_ref, outer_ref, output_ref, out_ref, packed_ref, third_ref) = refs[:4], refs[4:16], refs[16:]
+    rows, width = mats[0].shape
     for g in range(groups):
         for h in range(heads):
             at = pl.ds((g * heads + h) * DH, DH)
-            out_ref[g, h * rows:(h + 1) * rows, :] = jnp.concatenate([m[:, at] for m in mats], axis=1)
+            value = jnp.concatenate([m[:, at] for m in mats], axis=1)
+            for c in range(g, out_ref.shape[0], groups):
+                out_ref[c, h * rows:(h + 1) * rows, :] = value
     pad = jnp.zeros((1, LANES - rows), F32)
     lines = [jnp.concatenate([v[...].astype(F32), pad], axis=1) for v in smalls]
     none = jnp.zeros((1, LANES), F32)
     inner = jnp.concatenate([wide_ref[...].astype(F32), jnp.zeros((1, LANES - wide_ref.shape[1]), F32)], axis=1)
     left = jnp.concatenate(lines[:8], axis=0)
-    right = jnp.concatenate(lines[8:] + [inner, none, none, none], axis=0)
+    kinds = kinds_ref[...].astype(F32)
+    right = jnp.concatenate(lines[8:] + [inner, kinds, none], axis=0)
     both = jnp.concatenate([left, right], axis=1).astype(BF)
-    for g in range(groups):
-        out_ref[g, heads * rows:, :] = both
-
-
-def pack(mats, smalls, wide, heads, groups):
-    rows = mats[0].shape[0]
+    for c in range(out_ref.shape[0]):
+        out_ref[c, heads * rows:, :] = both
+    count = inner_ref.shape[1] // width
+    for i in range(count):
+        packed_ref[i * rows:(i + 1) * rows, :] = inner_ref[:, i * width:(i + 1) * width]
+    wide = outer_ref.shape[0] // 2
+    third_ref[...] = outer_ref[:wide, :]
+    packed_ref[count * rows:count * rows + wide, :] = outer_ref[wide:, :]
+    packed_ref[count * rows + wide:, :] = output_ref[...]
+
+
+def pack(mats, smalls, wide, kinds, inner, outer, output, heads, groups, members):
+    rows, width = mats[0].shape
+    third = outer.shape[0] // 2
+    total = inner.shape[1] // width * rows + third + output.shape[0]
     return pl.pallas_call(
         functools.partial(pack_kernel, heads, groups),
-        out_shape=jax.ShapeDtypeStruct((groups, heads * rows + 8, 2 * LANES), BF),
+        out_shape=[jax.ShapeDtypeStruct((members, heads * rows + 8, 2 * LANES), BF),
+                   jax.ShapeDtypeStruct((total, width), BF), jax.ShapeDtypeStruct((third, width), BF)],
         name="pack_columns",
-    )(*mats, *smalls, wide)
+    )(*mats, *smalls, wide, kinds, inner, outer, output)
 
 
 def unpack_kernel(heads, groups, shard, g_ref, block_ref, vecs_ref, wide_ref, vec_ref):
@@ -938,7 +970,8 @@
 
 
 def small_kernel(heads, groups, shard, g_ref, heads_ref, rest_ref, wide_ref, unused_ref, out_ref, table_ref):
-    owners = out_ref.shape[0]
+    members = out_ref.shape[2]
+    owners = 4 * members
     wide = wide_ref.shape[1] // owners
     table_ref[:6] = jnp.zeros((6, table_ref.shape[1]), F32)
     for g in range(groups):
@@ -953,11 +986,12 @@
         right = jnp.concatenate([table_ref[8:12, o * shard:(o + 1) * shard], jnp.zeros((4, LANES - shard), F32)], axis=1)
         inner = jnp.concatenate([wide_ref[:, o * wide:(o + 1) * wide], jnp.zeros((1, LANES - wide), F32)], axis=1)
         right = jnp.concatenate([right, inner, jnp.zeros((3, LANES), F32)], axis=0)
-        out_ref[o] = jnp.concatenate([left, pad, right], axis=1).astype(BF)
+        out_ref[(o // members % 2) ^ g_ref[1], o // (2 * members), o % members] = jnp.concatenate([left, pad, right], axis=1).astype(BF)
 
 
 def small_rows(block, g, head_sums, rest, wide_sums, groups, shard):
-    owners, rows, _ = block.shape
+    members, rows = block.shape[2:4]
+    owners = 4 * members
     heads = head_sums.shape[0]
     whole = lambda a: pl.BlockSpec(a.shape, lambda i: (0,) * a.ndim)
     return pl.pallas_call(
@@ -965,22 +999,23 @@
         grid=(1,),
         in_specs=[pl.BlockSpec(memory_space=pltpu.SMEM), whole(head_sums), whole(rest), whole(wide_sums),
                   pl.BlockSpec(memory_space=pl.ANY)],
-        out_specs=pl.BlockSpec((owners, 8, 2 * LANES), lambda i: (0, rows // 8 - 1, 0)),
+        out_specs=pl.BlockSpec((2, 2, members, 8, 2 * LANES), lambda i: (0, 0, 0, rows // 8 - 1, 0)),
         out_shape=jax.ShapeDtypeStruct(block.shape, BF),
         input_output_aliases={4: 0},
         scratch_shapes=[pltpu.VMEM((16, owners * shard), F32)],
         name="small_gradients",
-    )(g.reshape(1), head_sums, rest, wide_sums, block)
+    )(g, head_sums, rest, wide_sums, block)
 
 
 def finish_kernel(heads, block_ref, *refs):
     outs, small_ref = refs[:-1], refs[-1]
-    groups = block_ref.shape[0]
+    groups = block_ref.shape[0] // 2
     shard = outs[0].shape[0]
-    small_ref[...] = sum(block_ref[g, heads * shard:, :].astype(F32) for g in range(groups))
+    small_ref[...] = sum(block_ref[g, heads * shard:, :].astype(F32) for g in range(2 * groups))
     for g in range(groups):
         for h in range(heads):
             part = block_ref[g, h * shard:(h + 1) * shard, :].astype(F32)
+            part = part + block_ref[groups + g, h * shard:(h + 1) * shard, :].astype(F32)
             at = (g * heads + h) * DH
             for m in range(4):
                 outs[m][:, at:at + DH] = part[:, m * DH:(m + 1) * DH]
@@ -995,30 +1030,38 @@
 
 
 def token_kernel(core_ref, valid_ref, mixed_ref, x_ref, og_ref, vec_ref, wide_ref,
-                 inner_own, inner_other, outer_own, outer_other,
+                 inner_one, inner_two, inner_three, inner_four, outer_one, outer_two, outer_three, outer_four, third_one, third_two,
                  result_ref, first_ref, grad_ref, gi_keep, gi_send, go_keep, go_send, rest_ref, gw_ref,
-                 wi, wo, act, slope, normed_t, acc, gi_ref, go_ref, sems):
-    core = core_ref[0]
+                 packed, wi, act, slope, normed_t, acc, gi_ref, go_ref, sems):
+    core, bit_y, bit_x = core_ref[0], core_ref[1], core_ref[2]
     seqs, width, stretch = mixed_ref.shape
     tokens = seqs * stretch
     count = wi.shape[1] // width
-    members, rows = wo.shape[1], wo.shape[2]
+    members = 2 * packed.shape[1]
     block = width // count
     shard = block // members
-    wide = rows - shard
+    wide = packed.shape[3] - (count + 1) * shard
+    base = count * shard
     copies = []
-    for y in range(2):
-        for i, (src_i, src_o, k) in enumerate(((inner_own, outer_own, core), (inner_other, outer_other, 1 - core))):
-            at = 2 * y + k
-            copies.append(pltpu.make_async_copy(
-                src_o.at[y], wo.at[at], sems.at[2 * y + i]))
-            copies.append(pltpu.make_async_copy(
-                src_i.at[y], wi.at[pl.ds(pl.multiple_of(at * block, block), block), :], sems.at[4 + 2 * y + i]))
+    sources = ((outer_one, core, bit_x), (outer_two, 1 - core, bit_x), (outer_three, core, 1 - bit_x), (outer_four, 1 - core, 1 - bit_x))
+    for i, (src, k, x) in enumerate(sources):
+        for y in range(2):
+            copies.append(pltpu.make_async_copy(src.at[y], packed.at[2 * y + k, :, x, base + wide // 2:, :], sems.at[4 + 2 * i + y]))
+    for i, (src, k) in enumerate(((third_one, core), (third_two, 1 - core))):
+        for y in range(2):
+            copies.append(pltpu.make_async_copy(src.at[:, y], packed.at[2 * y + k, :, :, base:base + wide // 2, :], sems.at[26 + 2 * i + y]))
+    sources = ((inner_one, core, bit_y), (inner_two, 1 - core, bit_y), (inner_three, core, 1 - bit_y), (inner_four, 1 - core, 1 - bit_y))
+    for i, (src, k, y) in enumerate(sources):
+        for x in range(2):
+            copies.append(pltpu.make_async_copy(src.at[x], packed.at[2 * y + k, :, x, :base, :], sems.at[12 + 2 * i + x]))
     for copy in copies:
         copy.start()
-    for copy in copies[0::2]:
+    for copy in copies[:8]:
         copy.wait()
-    w_out = wo[:, :, wide:, :].astype(F32).reshape(width, width).astype(BF)
+    w_out = packed[:, :, :, base + wide:, :].astype(F32).reshape(width, width).astype(BF)
+    def w_outer(j):
+        return packed[j, :, :, base:base + wide, :].reshape(width, width)
+
     vec = vec_ref[...]
     line = lambda i: vec[i:i + 1, :]
     mean = lambda v: jnp.mean(v, axis=1, keepdims=True)
@@ -1031,8 +1074,11 @@
     low = normed.astype(BF)
     normed_t[...] = jnp.transpose(normed).astype(BF)
     acc[...] = jnp.zeros_like(acc)
-    for copy in copies[1::2]:
+
+    for copy in copies[8:]:
         copy.wait()
+    for i in range(count):
+        wi[:, i * width:(i + 1) * width] = packed[:, :, :, i * shard:(i + 1) * shard, :].astype(F32).reshape(width, width).astype(BF)
 
     def forward(j, carry):
         at = pl.ds(pl.multiple_of(j * width, width), width)
@@ -1044,7 +1090,7 @@
         a = (u * half).astype(BF)
         act[:, at] = a
         slope[:, at] = half + 0.5 * u * (1.0 - t * t) * (c * (1.0 + 3 * 0.044715 * sq))
-        acc[...] += mm(a, wo[j, :, :wide, :].reshape(width, width), ROWCOL)
+        acc[...] += mm(a, w_outer(j), ROWCOL)
         return carry
 
     lax.fori_loop(0, count, forward, 0)
@@ -1064,23 +1110,45 @@
     two = [total(cot * hat_two), total(cot)]
     acc[...] = d_second
 
+    def upper(which, y, j):
+        target = (go_keep, go_send)[which]
+        return pltpu.make_async_copy(go_ref.at[which, y, :, :wide, :], target.at[y, :, :wide, :], sems.at[20 + j])
+
+    def lower(which, y):
+        target = (go_keep, go_send)[which]
+        return pltpu.make_async_copy(go_ref.at[which, y, :, wide:, :], target.at[y, :, wide:, :], sems.at[2 * which + y])
+
     def backward(j, carry):
         at = pl.ds(pl.multiple_of(j * width, width), width)
-        d_act = mm(d_low, wo[j, :, :wide, :].reshape(width, width), ROWS_CC)
+        d_act = mm(d_low, w_outer(j), ROWS_CC)
         d_in = d_act * slope[:, at]
         d_in_low = d_in.astype(BF)
         gw_ref[:, at] = total(d_in_low.astype(F32))
         acc[...] += mm(d_in_low, wi[:, at], ROWS_CC)
         go = mm(act[:, at], d_low, COLS_CC)
-        go_ref[(j % 2) ^ core, j // 2, :, :wide, :] = go.astype(BF).reshape(members, wide, width)
+        which = (j % 2) ^ core
+        go_ref[which, j // 2, :, :wide, :] = go.astype(BF).reshape(members, wide, width)
+
+        @pl.when(which == 0)
+        def _():
+            upper(0, j // 2, j).start()
+
+        @pl.when(which == 1)
+        def _():
+            upper(1, j // 2, j).start()
+
         for b in range(count):
             gi = mm(normed_t[b * block:(b + 1) * block, :], d_in_low, ROWCOL)
-            gi_ref[(b % 2) ^ core, b // 2, :, at] = gi.astype(BF)
+            gi = gi.reshape(members, shard, width).astype(BF)
+            for n in range(count):
+                @pl.when(j == n)
+                def _():
+                    gi_ref[(b % 2) ^ core, b // 2, :, n * shard:(n + 1) * shard, :] = gi
         return carry
 
     lax.fori_loop(0, count, backward, 0)
-    backs = [pltpu.make_async_copy(gi_ref.at[0], gi_keep, sems.at[8]), pltpu.make_async_copy(gi_ref.at[1], gi_send, sems.at[9]),
-             pltpu.make_async_copy(go_ref.at[0], go_keep, sems.at[10]), pltpu.make_async_copy(go_ref.at[1], go_send, sems.at[11])]
+    backs = [pltpu.make_async_copy(gi_ref.at[0], gi_keep, sems.at[24]), pltpu.make_async_copy(gi_ref.at[1], gi_send, sems.at[25]),
+             ]
     backs[1].start()
     backs[0].start()
     d_normed = acc[...]
@@ -1113,39 +1181,45 @@
         for i in range(members):
             at = b * block + i * shard
             go_ref[(b % 2) ^ core, b // 2, i, wide:, :] = out[at:at + shard, :].astype(BF)
-    backs[3].start()
-    backs[2].start()
-    for back in backs:
+    lowers = [lower(which, y) for which in range(2) for y in range(2)]
+    for back in lowers:
+        back.start()
+    for j in range(count):
+        upper(0, 0, j).wait()
+    for back in backs + lowers:
         back.wait()
 
 
-def token_block(core, valid, mixed, x, out_grad, vectors, inner_add, inner_own, inner_other, outer_own, outer_other, span):
+def token_block(core, valid, mixed, x, out_grad, vectors, inner_add, inner_parts, outer_parts, third_parts, span):
     seqs, width, stretch = mixed.shape
     tokens = seqs * stretch
     ff = inner_add.shape[1]
     count = ff // width
-    members, rows = outer_own.shape[1], outer_own.shape[2]
+    members = inner_parts[0].shape[0] * inner_parts[0].shape[1]
+    owners = members * count
+    rows = ff // owners + width // owners
+    base = ff // width * (width // owners)
     groups = width // span
     vmem = pl.BlockSpec(memory_space=pltpu.VMEM)
     hbm = pl.BlockSpec(memory_space=pl.ANY)
     S = jax.ShapeDtypeStruct
     return pl.pallas_call(
         token_kernel,
-        in_specs=[pl.BlockSpec(memory_space=pltpu.SMEM)] + [vmem] * 6 + [hbm] * 4,
+        in_specs=[pl.BlockSpec(memory_space=pltpu.SMEM)] + [vmem] * 6 + [hbm] * 10,
         out_specs=[vmem] * 3 + [hbm] * 4 + [vmem] * 2,
         out_shape=[S((tokens, width), BF), S((tokens, width), F32), S((seqs * groups, span + 8, stretch), BF),
-                   S((2, width // count, ff), BF), S((2, width // count, ff), BF),
+                   S((2, members, base, width), BF), S((2, members, base, width), BF),
                    S((2, members, rows, width), BF), S((2, members, rows, width), BF),
                    S((6, width), F32), S((1, ff), F32)],
-        scratch_shapes=[pltpu.VMEM((width, ff), BF), pltpu.VMEM((count, members, rows, width), BF),
+        scratch_shapes=[pltpu.VMEM((count, members // 2, 2, (count + 1) * (width // owners) + ff // owners, width), BF), pltpu.VMEM((width, ff), BF),
                         pltpu.VMEM((tokens, ff), BF), pltpu.VMEM((tokens, ff), F32),
                         pltpu.VMEM((width, tokens), BF), pltpu.VMEM((tokens, width), F32),
-                        pltpu.VMEM((2, 2, width // count, ff), BF), pltpu.VMEM((2, 2, members, rows, width), BF),
-                        pltpu.SemaphoreType.DMA((12,))],
+                        pltpu.VMEM((2, 2, members, base, width), BF), pltpu.VMEM((2, 2, members, rows, width), BF),
+                        pltpu.SemaphoreType.DMA((30,))],
         compiler_params=pltpu.CompilerParams(vmem_limit_bytes=60 * 2 ** 20),
         cost_estimate=pl.CostEstimate(flops=tokens * 2 * width * (6 * ff + 4 * width), bytes_accessed=30 * 2 ** 20, transcendentals=tokens * ff),
         name="token_block",
-    )(core.reshape(1), valid, mixed, x, out_grad, vectors, inner_add, inner_own, inner_other, outer_own, outer_other)
+    )(core, valid, mixed, x, out_grad, vectors, inner_add, *inner_parts, *outer_parts, *third_parts)
 
 
 def takes_head_layout(mesh):
@@ -1163,10 +1237,6 @@
     return jnp.stack([first, second], axis=axis)
 
 
-def flip_if(bit, x, axis):
-    return jnp.where(bit == 0, x, jnp.flip(x, axis))
-
-
 def pick(x, index, axis):
     return lax.dynamic_index_in_dim(x, index, axis, keepdims=False)
 
@@ -1175,34 +1245,29 @@
     return lax.optimization_barrier((x,) + others)[0]
 
 
-def add_low(a, b):
-    return (a.astype(F32) + b.astype(F32)).astype(BF)
+def exchange(x, along_z):
+    count = lax.axis_size(CTX)
+    if along_z:
+        sets = [[m for m in range(count) if m % 2 == i] for i in range(2)]
+    else:
+        sets = [list(range(count // 2)), list(range(count // 2, count))]
+    return lax.all_to_all(x, CTX, 0, 0, axis_index_groups=sets, tiled=True)
 
 
 def in_z_order(pieces):
     z = lax.axis_index(CTX) // 2
     block = jnp.stack(pieces).reshape((2, 2) + pieces[0].shape)
-    return flip_if(z // 2, flip_if(z % 2, block, 1), 0).reshape((4,) + pieces[0].shape)
-
-
-def grow_y(block):
-    return in_order(lax.axis_index(DP) // 2, block, swap(block, DP, 2), 0)
-
-
-def grow_core(block):
-    return in_order(lax.axis_index(DP) % 2, block, swap(block, DP, 1), 1)
-
-
-def halve(block, axis, mesh_axis, step, bit):
-    return add_low(pick(block, bit, axis), swap(pick(block, 1 - bit, axis), mesh_axis, step))
-
-
-def end_scatter(block):
-    z = lax.axis_index(CTX) // 2
-    total = pick(block, z, 0).astype(F32)
-    for m in (1, 2, 3):
-        total = total + swap(pick(block, z ^ m, 0), CTX, 2 * m).astype(F32)
-    return total
+    for axis, bit in ((1, z % 2), (0, z // 2)):
+        block = jnp.where(bit == 0, block, jnp.flip(block, axis))
+    return block.reshape((4,) + pieces[0].shape)
+
+
+def total_low(terms):
+    return sum(t.astype(F32) for t in terms).astype(BF)
+
+
+def picks(terms, bit, axis):
+    return [pick(t, bit, axis) for t in terms]
 
 
 def head_layout(
@@ -1242,8 +1307,11 @@
     shard = width // devices
     inner_shard = inner_bias.shape[0]
     s, g = c // groups, c % groups
-    bit_b, bit_x = (c // 2) % 2, c % 2
+    bit_x = c % 2
     core, bit_y = d % 2, d // 2
+
+    x_send = pick(inputs, 1 - s, 0)
+    own = pick(inputs, s, 0)
 
     smalls = (
         content_bias,
@@ -1259,94 +1327,93 @@
         second_gain,
         second_shift,
     )
-    stacked = pack(
-        (query_weight, key_weight, value_weight, position_weight),
+    stacked, packed, third = pack(
+        (after(query_weight, x_send), key_weight, value_weight, position_weight),
         tuple(v.reshape(1, shard) for v in smalls),
         inner_bias.reshape(1, inner_shard),
+        token_types,
+        inner_weight,
+        outer_weight,
+        output_weight,
         heads,
         groups,
-    )
-
-    row = jnp.zeros((seqs, 8, half), BF).at[:, 0, :stretch].set(token_types.astype(BF))
-    left = jnp.concatenate([inputs[:, :, :half], row], axis=1)
-    right = inputs[:, :, half:]
-    left = in_order(s, pick(left, s, 0), swap(pick(left, 1 - s, 0), CTX, 4), 0)
-    right = in_order(s, pick(right, s, 0), swap(pick(right, 1 - s, 0), CTX, 4), 0)
-    left = in_order(bit_x, left, swap(left, CTX, 1), 1)
-    right = in_order(bit_b, right, swap(right, CTX, 2), 1)
-    left = in_order(bit_b, left, swap(left, CTX, 2), 1)
-    right = in_order(bit_x, right, swap(right, CTX, 1), 2)
-    left = left.reshape(members, stretch + 8, half)
-    right = right.reshape(members, stretch, half)
-    x_seq = jnp.concatenate([left[:, :stretch], right], axis=2).reshape(seq_len, width)
-    kind_seq = left[:, stretch, :stretch].reshape(seq_len).astype(F32)
-
-    pieces = [pick(stacked, g, 0)]
-    for r in range(1, groups):
-        pieces.append(swap(pick(stacked, g ^ r, 0), CTX, r))
-    block = jnp.stack(pieces).reshape((2, 2) + pieces[0].shape)
-    block = flip_if(bit_b, flip_if(bit_x, block, 1), 0).reshape((groups,) + pieces[0].shape)
-    block = in_order(s, block, swap(block, CTX, 4), 0)[None]
-    block = grow_core(grow_y(block))
-    block = block.reshape((devices,) + pieces[0].shape)
+        members,
+    )
+    cut = (inner_weight.shape[1] // width) * shard
+    block = lax.all_to_all(stacked, CTX, 0, 0, tiled=True)
+    x_pair = in_order(s, own, swap(x_send, CTX, 4), 0)
+    packed, third = after((packed, third), x_pair)
+    third_y = swap(third, DP, 2)
+    packed_z = [swap(packed, CTX, 2 * m) for m in (1, 2, 3)]
+    lines = block[:, heads * shard + 5 : heads * shard + 5 + seqs, LANES:]
+    kind_seq = pick(lines, s, 1).reshape(2, groups, stretch).transpose(1, 0, 2)
+    kind_seq = kind_seq.reshape(seq_len).astype(F32)
+    x_pair = jnp.broadcast_to(after(x_pair, block)[None], (groups, 2, stretch, width))
+    x_all = exchange(x_pair, False)
+    block = block[None]
+    block = in_order(bit_y, block, swap(block, DP, 2), 0)
+    third = in_order(bit_y, third, after(third_y, block), 0)
+    third_x = swap(third, CTX, 1)
+    packed_z = after(packed_z, x_pair, block, third)
+    packed_z = in_z_order([packed] + packed_z)
+    inner_block, outer_block = packed_z[:, :cut], packed_z[:, cut:]
+    inner_x, outer_y = swap(inner_block, CTX, 1), swap(outer_block, DP, 2)
+    block = in_order(core, block, after(swap(block, DP, 1), inner_block, outer_block), 1)
+    block = block.reshape((devices,) + stacked.shape[1:])
+    x_seq = after(x_all, block).reshape(seq_len, width)
+
     exponent = 2.0 * jnp.arange(half, dtype=F32) / width
     rates = (10000.0 ** (-exponent))[None, :]
-    starts = (jnp.arange(members, dtype=jnp.int32) * stretch).astype(F32)[:, None] * rates
+    owners = jnp.arange(members, dtype=jnp.int32).reshape(2, groups).T.reshape(-1)
+    starts = (owners * stretch).astype(F32)[:, None] * rates
     steps = jnp.arange(stretch, dtype=F32)[:, None] * rates
     starts, steps = lax.optimization_barrier((starts, steps))
     cos_a, sin_a = jnp.cos(starts)[:, None], jnp.sin(starts)[:, None]
     cos_b, sin_b = jnp.cos(steps)[None], jnp.sin(steps)[None]
     trig = jnp.concatenate(
         [cos_a * cos_b - sin_a * sin_b, sin_a * cos_b + cos_a * sin_b], axis=2
-    ).reshape(seq_len, width)
-    key_valid = (jnp.arange(seq_len, dtype=jnp.int32) < pick(lengths, s, 0)).astype(F32)
+    ).reshape(seq_len, width).astype(BF)
+    slots = owners[:, None] * stretch + jnp.arange(stretch, dtype=jnp.int32)[None, :]
+    key_valid = (slots.reshape(-1) < pick(lengths, s, 0)).astype(F32)
     kext = key_extension(kind_seq, key_valid)
 
-    outer_shard = jnp.concatenate([outer_weight, output_weight], axis=0)
-    inner_z = [swap(inner_weight, CTX, 2 * m) for m in (1, 2, 3)]
-    outer_z = [swap(outer_shard, CTX, 2 * m) for m in (1, 2, 3)]
-    x_seq, block, inner_z, outer_z = lax.optimization_barrier((x_seq, block, inner_z, outer_z))
     vectors, inner_add, vec = unpack(block, g, heads, groups, shard, inner_shard)
-    inner_block = in_z_order([inner_weight] + inner_z)
-    outer_block = in_z_order([outer_shard] + outer_z)
-    inner_x = swap(inner_block, CTX, 1)
-    outer_y = swap(outer_block, DP, 2)
+
+    inner_x, outer_y, third_x = after((inner_x, outer_y, third_x), x_seq)
+    third = in_order(bit_x, third, third_x, 1)
+    inner_block = in_order(bit_x, inner_block, inner_x, 0)
+    outer_block = in_order(bit_y, outer_block, outer_y, 0)
+    inner_y, outer_x = swap(inner_block, DP, 2), swap(outer_block, CTX, 1)
+    third_z = [swap(third, CTX, 2 * m) for m in (1, 2, 3)]
     saved = attention_forward(
-        x_seq, block, 0, 1, heads, after(vec, inner_block, outer_block), kext, trig
-    )
-    inner_x, outer_y, probe = lax.optimization_barrier((inner_x, outer_y, saved[0]))
-    inner_block = in_order(bit_x, inner_block, inner_x, 1)
-    outer_block = in_order(bit_y, outer_block, outer_y, 0)
-    inner_y = swap(inner_block, DP, 2)
-    outer_x = swap(outer_block, CTX, 1)
-    saved = (probe,) + tuple(saved[1:])
-    saved = attention_forward(
-        x_seq, block, 1, heads - 1, heads, after(vec, inner_block, outer_block), kext, trig, saved
-    )
-    att, qt, kb, v1, qp, save, scl, w_heads = saved
-    inner_y, outer_x, att = lax.optimization_barrier((inner_y, outer_x, att))
+        x_seq, block, 0, heads, heads, after(vec, inner_block, outer_block, third), kext, trig
+    )
+    att, q_block, kb, v1, qp, save, scl, w_heads, prob = saved
+    third_z = after(third_z, att)
+    att = after(att, third_z).reshape(members, span, stretch)
     mixed = lax.all_to_all(att, CTX, 0, 0, tiled=True).reshape(seqs, width, stretch)
-    inner_own = in_order(bit_y, inner_block, inner_y, 0).reshape(2, -1, inner_weight.shape[1])
-    outer_own = in_order(bit_x, outer_block, outer_x, 2)
-    outer_own = outer_own.reshape(2, members, inner_shard + shard, width)
-    inner_other = swap(inner_own, DP, 1)
-    outer_other = swap(outer_own, DP, 1)
+    inner_block, outer_block = after((inner_block, outer_block), att)
+    inner_far, outer_far = swap(inner_block, DP, 1), swap(outer_block, DP, 1)
+    third = in_z_order([third] + third_z)
+    inner_y, outer_x = after((inner_y, outer_x), mixed)
+    third_parts = (third, swap(third, DP, 1))
+    inner_parts = (inner_block, inner_far, inner_y, swap(inner_y, DP, 1))
+    outer_parts = (outer_block, outer_far, outer_x, swap(outer_x, DP, 1))
 
     own_slots = c * stretch + jnp.arange(stretch, dtype=jnp.int32)
     row_valid = (own_slots[None, :] < lengths[:, None]).astype(F32)
     result, first_grad, mixed_grad, inner_keep, inner_send, outer_keep, outer_send, rest, wide = (
         token_block(
-            core,
+            jnp.stack([core, bit_y, bit_x]),
             row_valid.reshape(-1, 1),
             mixed,
             inputs.reshape(-1, width),
             out_grad.reshape(-1, width),
             vectors,
             inner_add,
-            inner_own,
-            inner_other,
-            outer_own,
-            outer_other,
+            inner_parts,
+            outer_parts,
+            third_parts,
             span,
         )
     )
@@ -1354,63 +1421,93 @@
     first_grad = first_grad.reshape(inputs.shape)
 
     d_out = lax.all_to_all(mixed_grad, CTX, 0, 0, tiled=True)
-    sums_all = jnp.sum(d_out[:, span : span + 2].astype(F32), axis=(0, 1))
-    sums_all = sums_all[: 3 * seqs].reshape(seqs, 3)
-    mean_squares = sums_all / (lengths.astype(F32)[:, None] * width)
-    inner_block = add_low(inner_keep, swap(inner_send, DP, 1)).reshape(2, 4, 2, shard, -1)
-    outer_block = add_low(outer_keep, swap(outer_send, DP, 1))
-    outer_block = outer_block.reshape(2, 4, 2, inner_shard + shard, width)
-    inner_keep, inner_send = pick(inner_block, bit_y, 0), pick(inner_block, 1 - bit_y, 0)
-    outer_keep, outer_send = pick(outer_block, bit_x, 2), pick(outer_block, 1 - bit_x, 2)
+    z = c // 2
+    first_half = inner_shard // 2
+    inner_terms = [inner_keep, swap(inner_send, DP, 1)]
+    inner_terms = [t.reshape(2, 4, 2, cut, width) for t in inner_terms]
+    outer_terms = [outer_keep, swap(outer_send, DP, 1)]
+    outer_terms = [t.reshape(2, 4, 2, inner_shard + shard, width) for t in outer_terms]
+    inner_send = total_low(picks(inner_terms, 1 - bit_y, 0))
+    outer_terms[1] = after(outer_terms[1], inner_send)
+    third_terms = [t[..., :first_half, :] for t in outer_terms]
+    outer_terms = [t[..., first_half:, :] for t in outer_terms]
+    third_send = [total_low(picks(third_terms, z ^ m, 1)) for m in (1, 2, 3)]
+    outer_send = total_low(picks(outer_terms, 1 - bit_x, 2))
     inner_y = swap(inner_send, DP, 2)
     outer_x = swap(outer_send, CTX, 1)
+    third_z = [swap(third_send[m - 1], CTX, 2 * m) for m in (1, 2, 3)]
+    d_out = after(d_out, inner_send, outer_send, *third_send)
+    d_blocks = d_out.reshape(2, groups, span + 8, stretch)
 
     d_x, w_grad, head_sums = attention_backward(
-        after(d_out, inner_send, outer_send),
+        core,
+        d_blocks,
         x_seq,
         w_heads,
         vec,
         kext,
         trig,
-        qt,
+        q_block,
         kb,
         v1,
         qp,
         save,
         scl,
+        prob,
         devices,
         heads * shard + 8,
     )
-    d_x, inner_y, outer_x = lax.optimization_barrier((d_x, inner_y, outer_x))
-    inner_block = halve(add_low(inner_keep, inner_y), 1, CTX, 1, bit_x)
-    outer_block = halve(add_low(outer_keep, outer_x), 0, DP, 2, bit_y)
-
-    block = small_rows(w_grad, g, head_sums, rest, wide, groups, shard)
-    block = block.reshape((2, 2, 2, groups) + block.shape[1:])
-    block = halve(block, 1, DP, 1, core)
-    block = halve(block, 0, DP, 2, bit_y)
-    block = halve(block, 0, CTX, 4, s)
-    pieces = [pick(block, g, 0)]
-    for r in range(1, groups):
-        pieces.append(swap(pick(block, g ^ r, 0), CTX, r))
-    block = jnp.stack(pieces).reshape((2, 2) + pieces[0].shape)
-    block = flip_if(bit_b, flip_if(bit_x, block, 1), 0).reshape((groups,) + pieces[0].shape)
+    d_x, w_grad, head_sums, inner_y, outer_x, third_z = lax.optimization_barrier(
+        (d_x, w_grad, head_sums, inner_y, outer_x, third_z)
+    )
+    d_x = exchange(d_x.reshape(groups, 2, stretch, width), False)
+    outer_terms = picks(outer_terms, bit_x, 2) + [outer_x]
+    outer_send = [total_low(picks(outer_terms, z ^ m, 1)) for m in (1, 2, 3)]
+    outer_z = [swap(outer_send[m - 1], CTX, 2 * m) for m in (1, 2, 3)]
+    inner_terms = picks(inner_terms, bit_y, 0) + [inner_y]
+    inner_send = total_low(picks(inner_terms, 1 - bit_x, 1))
+    inner_x = swap(inner_send, CTX, 1)
+
+    w_grad = after(w_grad, inner_send, *outer_send)
+    block = small_rows(w_grad, jnp.stack([g, core]), head_sums, rest, wide, groups, shard)
+    block = [block[0], swap(block[1], DP, 1)]
+    third_terms = picks(third_terms, z, 1) + third_z
+    third_send = total_low(picks(third_terms, 1 - bit_y, 0))
+    block[1] = after(block[1], third_send)
+    third_y = swap(third_send, DP, 2)
+    block_send = total_low(picks(block, 1 - bit_y, 0))
+    block_y = swap(block_send, DP, 2)
+
+    d_x, outer_z, inner_x, third_y, block_y = lax.optimization_barrier(
+        (d_x, outer_z, inner_x, third_y, block_y)
+    )
+    d_x = jnp.sum(d_x.astype(F32), axis=0).astype(BF)
+    d_x_send = pick(d_x, 1 - s, 0)
+    d_x_z = swap(d_x_send, CTX, 4)
+    inner_sum = total_low(picks(inner_terms, bit_x, 1) + [after(inner_x, d_x_send)])
+    inner_z = [swap(pick(inner_sum, z ^ m, 0), CTX, 2 * m) for m in (1, 2, 3)]
+    block = total_low(picks(block, bit_y, 0) + [after(block_y, inner_sum)])
+    outer_z = after(outer_z, block)
+    block = lax.all_to_all(block, CTX, 0, 0, tiled=True)
+    outer_terms = picks(outer_terms, z, 1) + outer_z
+    outer_y = swap(total_low(picks(outer_terms, 1 - bit_y, 0)), DP, 2)
+    third_terms = picks(third_terms, bit_y, 0) + [third_y]
+    third_x = swap(total_low(picks(third_terms, 1 - bit_x, 0)), CTX, 1)
+    inner_own = sum(t.astype(F32) for t in [pick(inner_sum, z, 0)] + inner_z)
+    inner_own = jnp.concatenate(
+        [inner_own[i : i + shard] for i in range(0, cut, shard)], axis=1
+    )
+    third_own = sum(t.astype(F32) for t in picks(third_terms, bit_x, 0) + [third_x])
+    outer_sum = sum(t.astype(F32) for t in picks(outer_terms, bit_y, 0) + [outer_y])
+    outer_own = jnp.concatenate([third_own, outer_sum[:first_half]], axis=0)
+    output_own = outer_sum[first_half:]
     query_own, key_own, value_own, position_own, small = finish(block, heads, shard, width)
     v = [small[i, :shard] for i in range(8)] + [small[i, LANES : LANES + shard] for i in range(4)]
-
-    d_x = d_x.reshape(2, 2, 2, stretch, width)
-    left, right = d_x[..., :half], d_x[..., half:]
-    left = halve(left, 2, CTX, 1, bit_x)
-    right = halve(right, 1, CTX, 2, bit_b)
-    left = halve(left, 1, CTX, 2, bit_b)
-    right = halve(right, 1, CTX, 1, bit_x)
-    both = jnp.concatenate([left, right], axis=2)
-    input_terms = in_order(s, pick(both, s, 0), swap(pick(both, 1 - s, 0), CTX, 4), 0)
+    input_terms = in_order(s, pick(d_x, s, 0), d_x_z, 0)
     input_grad = (first_grad + input_terms.astype(F32)).astype(BF)
-
-    inner_own = end_scatter(inner_block)
-    outer_block = end_scatter(outer_block)
-    outer_own, output_own = outer_block[:inner_shard], outer_block[inner_shard:]
+    sums_all = jnp.sum(d_out[:, span : span + 2].astype(F32), axis=(0, 1))
+    sums_all = sums_all[: 3 * seqs].reshape(seqs, 3)
+    mean_squares = sums_all / (lengths.astype(F32)[:, None] * width)
     return (
         result,
         input_grad,

time: 354 us -> 284 us (0.80)
  waiting for transfers between devices: 139 us -> 57.8 us
  Pallas kernels: 94.7 us -> 75.4 us
  other arithmetic: 27.1 us -> 44 us
  starting transfers between devices: 66.9 us -> 78.6 us
    ppermute x47 -> x40, waiting for transfers between devices: 127 us -> 45.4 us  [swap(): return lax.ppermute(x, axis, [(i, i ^ bit) for i in range(count)])]
    all_to_all x0 -> x4, starting transfers between devices: none -> 16.1 us  [the longest x2 7.93 us: exchange(): return lax.all_to_all(x, CTX, 0, 0, axis_index_groups=sets, tiled=True)]
    pallas_call x2 -> x1, Pallas kernels: 33.2 us -> 18.5 us  [attention_forward(): pl.pallas_call(lambda *refs: kernel(*refs[:5], *refs[5 + skip:]), grid=(c...]
    slice x5 -> x11, local copies, waits for them, and re-layouts: 2.69 us -> 11.6 us  [the longest x2 4.08 us: head_layout(): outer_terms = [t[..., first_half:, :] for t in outer_terms]]
    convert_element_type x15 -> x13, other arithmetic: 12 us -> 20.8 us  [the longest x11 20.8 us: total_low(): return sum((t.astype(F32) for t in terms)).astype(BF)]
    pallas_call x1, Pallas kernels: 31 us -> 25 us  [attention_backward(): pl.pallas_call(functools.partial(attention_backward_kernel, tile), grid=(...]
    unnamed x27 -> x28, local copies, waits for them, and re-layouts: 5.43 us -> 0.15 us
    all_to_all x0 -> x4, waiting for transfers between devices: none -> 4.43 us  [the longest x2 4.15 us: exchange(): return lax.all_to_all(x, CTX, 0, 0, axis_index_groups=sets, tiled=True)]
  transfers between devices with their start and end apart: 49 -> 46, of which waited for: 21 -> 13; matrix products, arithmetic and copies ran while one was open for 10% -> 22% of each run, Pallas kernels for 11% -> 17%
where the time goes in v1:
time: 284 us; the launch traced here: 283 us
  starting transfers between devices  78.6 us (28%)
  Pallas kernels  75.4 us (27%)
  waiting for transfers between devices  57.8 us (20%)
  other arithmetic  44 us (15%)
  local copies, waits for them, and re-layouts  25.4 us (9%)
    ppermute x40, starting transfers between devices, swap(): return lax.ppermute(x, axis, [(i, i ^ bit) for i in range(count)])  52.5 us
    ppermute x40, waiting for transfers between devices, swap(): return lax.ppermute(x, axis, [(i, i ^ bit) for i in range(count)])  45.4 us
    pallas_call x1, Pallas kernels, attention_backward(): pl.pallas_call(functools.partial(attention_backward_kernel, tile), grid=(...  25 us
    pallas_call x1, Pallas kernels, token_block(): pl.pallas_call(token_kernel, in_specs=[pl.BlockSpec(memory_space=pltpu.SM...  24.6 us
    convert_element_type x11, other arithmetic, total_low(): return sum((t.astype(F32) for t in terms)).astype(BF)  20.8 us
    pallas_call x1, Pallas kernels, attention_forward(): pl.pallas_call(lambda *refs: kernel(*refs[:5], *refs[5 + skip:]), grid=(c...  18.5 us
    all_to_all x1, waiting for transfers between devices, head_layout(): lax.all_to_all(att, CTX, 0, 0, tiled=True).reshape(seqs, width, stretch)  7.97 us
    all_to_all x2, starting transfers between devices, exchange(): return lax.all_to_all(x, CTX, 0, 0, axis_index_groups=sets, tiled=True)  7.93 us
  transfers between devices with their start and end apart: 46, of which 13 were waited for; matrix products, arithmetic and copies ran while one was open for 22% of the time, Pallas kernels for 17%

profile of v1, /device:TPU:0, one launch (start us, length us, event | category | flops | bytes accessed | tf_op | source)
XLA Modules:
  0.0 282.6 jit_solution(17946891718498061547)
XLA Ops:
  1.6 4.1 %collective-permute-start = (bf16[128,768]{1,0:T(8,128)(2,1)S(1)}, bf16[128,768]{1,0:T(8,128)(2,1)S(1)}, u32[]{:S(2)}, u32[]{:S(2)}) collective-permute-start(bf16[128,768]{1,0:T(8,128)(2,1)S(1)} %dynamic-slice_bitcast_fusion.1), channel_id=1, source_target_pairs={{0,4},{1,5},{2,6},{3,7},{4,0},{5,1},{6,2},{7,3},{8,12},{9,13},{10,... | collective-permute-start | bytes 589832 | tf_op jit(solution)/shard_map/ppermute | solution.py:1231
  7.0 2.1 pack_columns.1
  9.1 3.8 %all-to-all-start = ((bf16[8,80,256]{2,1,0:T(8,128)(2,1)}), bf16[8,80,256]{2,1,0:T(8,128)(2,1)S(1)}, u32[]{:S(2)}, u32[]{:S(2)}) async-start(bf16[8,80,256]{2,1,0:T(8,128)(2,1)} %get-tuple-element.103), calls=%async_computation | async-start | bytes 655360 | tf_op jit(solution)/shard_map/all_to_all | solution.py:1343
  15.0 1.3 pad_maximum_fusion.refs_4_.trig_ref
  17.2 2.0 collective-permute-start.3
  19.2 2.6 collective-permute-start.4
  21.9 1.5 collective-permute-start.6
  23.7 1.5 collective-permute-start.1
  26.4 3.6 %all-to-all-start.1 = ((bf16[4,2,128,768]{3,2,1,0:T(8,128)(2,1)}), bf16[4,2,128,768]{3,2,1,0:T(8,128)(2,1)S(1)}, u32[]{:S(2)}, u32[]{:S(2)}) async-start(bf16[4,2,128,768]{3,2,1,0:T(8,128)(2,1)} %broadcast_in_dim.77), calls=%async_computation.1 | async-start | bytes 3145728 | tf_op jit(solution)/shard_map/all_to_all | solution.py:1254
  33.2 7.2 %collective-permute-done.4 = bf16[168,768]{1,0:T(8,128)(2,1)S(1)} collective-permute-done((bf16[168,768]{1,0:T(8,128)(2,1)S(1)}, bf16[168,768]{1,0:T(8,128)(2,1)S(1)}, u32[]{:S(2)}, u32[]{:S(2)}) %collective-permute-start.4) | collective-permute-done | bytes 258080 | tf_op jit(solution)/shard_map/ppermute | solution.py:1231
  43.5 1.4 collective-permute-start.9
  45.5 1.5 collective-permute-start.8
  47.4 1.3 copy.66
  48.6 1.7 unpack_small.1
  50.3 4.1 %all-to-all-done.1 = bf16[4,2,128,768]{3,2,1,0:T(8,128)(2,1)S(1)} async-done(((bf16[4,2,128,768]{3,2,1,0:T(8,128)(2,1)}), bf16[4,2,128,768]{3,2,1,0:T(8,128)(2,1)S(1)}, u32[]{:S(2)}, u32[]{:S(2)}) %all-to-all-start.1) | async-done | bytes 1572896 | tf_op jit(solution)/shard_map/all_to_all | solution.py:1254
  54.5 3.4 %collective-permute-done.8 = bf16[4,72,768]{2,1,0:T(8,128)(2,1)} collective-permute-done((bf16[4,72,768]{2,1,0:T(8,128)(2,1)}, bf16[4,72,768]{2,1,0:T(8,128)(2,1)}, u32[]{:S(2)}, u32[]{:S(2)}) %collective-permute-start.8) | collective-permute-done | bytes 442400 | tf_op jit(solution)/shard_map/ppermute | solution.py:1231
  57.9 5.6 %collective-permute-done.7 = bf16[4,96,768]{2,1,0:T(8,128)(2,1)S(1)} collective-permute-done((bf16[4,96,768]{2,1,0:T(8,128)(2,1)}, bf16[4,96,768]{2,1,0:T(8,128)(2,1)S(1)}, u32[]{:S(2)}, u32[]{:S(2)}) %collective-permute-start.7) | collective-permute-done | bytes 589856 | tf_op jit(solution)/shard_map/ppermute | solution.py:1231
  64.4 4.4 %collective-permute-start.10 = (bf16[2,2,48,768]{3,2,0,1:T(8,128)(2,1)S(1)}, bf16[2,2,48,768]{3,2,0,1:T(8,128)(2,1)}, u32[]{:S(2)}, u32[]{:S(2)}) collective-permute-start(bf16[2,2,48,768]{3,2,0,1:T(8,128)(2,1)S(1)} %get-tuple-element.212), channel_id=1, source_target_pairs={{0,2},{1,3},{2,0},{3,1},{4,6},{5,7},{6,4},{7,5},{8,10},{9,11},{10,... | collective-permute-start | bytes 884744 | tf_op jit(solution)/shard_map/ppermute | solution.py:1231
  70.0 1.4 collective-permute-start.12
  73.6 1.5 collective-permute-start.15
  75.2 1.6 collective-permute-start.14
  76.7 18.5 %attention_forward.1 = (bf16[2,4,192,128]{3,2,1,0:T(8,128)(2,1)}, bf16[3,1024,128]{2,1,0:T(8,128)(2,1)}, bf16[3,1024,128]{2,1,0:T(8,128)(2,1)}, bf16[3,1024,128]...) custom-call(bf16[1024,768]{1,0:T(8,128)(2,1)} %bitcast.285, ...), custom_call_target="tpu_custom_call" | custom-call | flops 7650410496 | bytes 12582912 | tf_op jit(solution)/shard_map/attention_forward/pallas_call | solution.py:832
  95.3 5.7 %all-to-all-start.2 = ((bf16[8,192,128]{2,1,0:T(8,128)(2,1)}), bf16[8,192,128]{2,1,0:T(8,128)(2,1)S(1)}, u32[]{:S(2)}, u32[]{:S(2)}) async-start(bf16[8,192,128]{2,1,0:T(8,128)(2,1)} %bitcast.293), calls=%async_computation.2 | async-start | bytes 786432 | tf_op jit(solution)/shard_map/all_to_all | solution.py:1394
  101.0 1.3 pad_maximum_fusion.3
  103.5 8.0 %all-to-all-done.2 = bf16[8,192,128]{2,1,0:T(8,128)(2,1)S(1)} async-done(((bf16[8,192,128]{2,1,0:T(8,128)(2,1)}), bf16[8,192,128]{2,1,0:T(8,128)(2,1)S(1)}, u32[]{:S(2)}, u32[]{:S(2)}) %all-to-all-start.2) | async-done | bytes 393248 | tf_op jit(solution)/shard_map/all_to_all | solution.py:1394
  113.5 2.4 collective-permute-done.17.outer_two
  117.2 24.6 %token_block.1 = (bf16[256,768]{1,0:T(8,128)(2,1)}, f32[256,768]{1,0:T(8,128)}, bf16[8,200,128]{2,1,0:T(8,128)(2,1)}, bf16[2,8,96,768]{3,2,1,0:T(8,128)(2,1)}, b...) custom-call(s32[3]{0:T(128)} %pad_add_fusion.core_ref, ...), custom_call_target="tpu_custom_call" | custom-call | flops 8455716864 | bytes 31457280 | tf_op jit(solution)/shard_map/token_block/pallas_call | solution.py:1206
  142.4 4.3 %all-to-all-start.3 = ((bf16[8,200,128]{2,1,0:T(8,128)(2,1)}), bf16[8,200,128]{2,1,0:T(8,128)(2,1)}, u32[]{:S(2)}, u32[]{:S(2)}) async-start(bf16[8,200,128]{2,1,0:T(8,128)(2,1)} %get-tuple-element.135), calls=%async_computation.3 | async-start | bytes 819200 | tf_op jit(solution)/shard_map/all_to_all | solution.py:1423
  146.8 1.4 slice.127
  148.1 2.1 slice.126
  151.0 2.6 fusion
  153.6 1.5 collective-permute-start.22
  155.1 1.3 slice.101
  156.5 2.0 slice.99
  159.6 1.4 collective-permute-start.24
  161.0 2.4 collective-permute-start.25
  165.1 1.5 collective-permute-start.23
  166.6 25.0 %attention_backward.1 = (bf16[1024,768]{1,0:T(8,128)(2,1)}, bf16[2,2,8,80,256]{4,3,2,1,0:T(8,128)(2,1)}, f32[3,8,128]{2,1,0:T(8,128)}) custom-call(s32[1]{0:T(128)} %bitcast.core_ref, bf16[2,4,200,128]{3,2,1,0:T(8,128)(2,1)} %bitcast.72.do_ref, bf16[1024,768]{1,0:T(8,128)(2,1)} %bitcast.286, bf16[3,768,256]{2,1,0:T(8,128)(2,1)} %get-tuple-element.142.w_ref, ...), custom_call_target="tpu_custom_call" | custom-call | flops 13690208256 | bytes 15728640 | tf_op jit(solution)/shard_map/attention_backward/pallas_call | solution.py:866
  191.6 4.4 %all-to-all-start.4 = ((bf16[4,2,128,768]{3,2,1,0:T(8,128)(2,1)}), bf16[4,2,128,768]{3,2,1,0:T(8,128)(2,1)}, u32[]{:S(2)}, u32[]{:S(2)}) async-start(bf16[4,2,128,768]{3,2,1,0:T(8,128)(2,1)} %bitcast.287), calls=%async_computation.4 | async-start | bytes 3145728 | tf_op jit(solution)/shard_map/all_to_all | solution.py:1254
  196.6 2.4 fusion.3
  199.1 2.1 fusion.9
  201.2 1.7 small_gradients.1
  202.9 2.5 fusion.29
  205.3 1.9 collective-permute-start.30
  207.3 2.0 fusion.17
  209.7 1.9 fusion.8
  211.6 1.5 collective-permute-start.33
  214.0 1.5 collective-permute-start.27
  215.4 1.4 collective-permute-start.28
  216.9 1.7 collective-permute-start.29
  219.2 5.4 %collective-permute-done.27 = bf16[2,72,768]{2,1,0:T(8,128)(2,1)} collective-permute-done((bf16[2,72,768]{2,1,0:T(8,128)(2,1)}, bf16[2,72,768]{2,1,0:T(8,128)(2,1)}, u32[]{:S(2)}, u32[]{:S(2)}) %collective-permute-start.27) | collective-permute-done | bytes 221216 | tf_op jit(solution)/shard_map/ppermute | solution.py:1231
  224.6 9.9 %collective-permute-done.28 = bf16[2,72,768]{2,1,0:T(8,128)(2,1)} collective-permute-done((bf16[2,72,768]{2,1,0:T(8,128)(2,1)}, bf16[2,72,768]{2,1,0:T(8,128)(2,1)}, u32[]{:S(2)}, u32[]{:S(2)}) %collective-permute-start.28) | collective-permute-done | bytes 221216 | tf_op jit(solution)/shard_map/ppermute | solution.py:1231
  234.5 1.8 fusion.24
  236.9 2.5 reduce_sum.21
  239.3 1.6 dynamic-slice_bitcast_fusion
  241.0 3.8 %collective-permute-start.34 = (bf16[128,768]{1,0:T(8,128)(2,1)}, bf16[128,768]{1,0:T(8,128)(2,1)}, u32[]{:S(2)}, u32[]{:S(2)}) collective-permute-start(bf16[128,768]{1,0:T(8,128)(2,1)} %dynamic-slice_bitcast_fusion), channel_id=1, source_target_pairs={{0,4},{1,5},{2,6},{3,7},{4,0},{5,1},{6,2},{7,3},{8,12},{9,13},{10,... | collective-permute-start | bytes 589832 | tf_op jit(solution)/shard_map/ppermute | solution.py:1231
  244.8 2.7 fusion.2
  247.5 1.9 fusion.7
  249.5 4.4 %all-to-all-start.5 = ((bf16[8,80,256]{2,1,0:T(8,128)(2,1)}), bf16[8,80,256]{2,1,0:T(8,128)(2,1)}, u32[]{:S(2)}, u32[]{:S(2)}) async-start(bf16[8,80,256]{2,1,0:T(8,128)(2,1)} %fusion.7), calls=%async_computation.5 | async-start | bytes 655360 | tf_op jit(solution)/shard_map/all_to_all | solution.py:1491
  256.7 2.1 collective-permute-start.36
  258.8 2.4 collective-permute-start.37
  265.0 8.4 %collective-permute-done.37 = bf16[96,768]{1,0:T(8,128)(2,1)S(1)} collective-permute-done((bf16[96,768]{1,0:T(8,128)(2,1)S(1)}, bf16[96,768]{1,0:T(8,128)(2,1)S(1)}, u32[]{:S(2)}, u32[]{:S(2)}) %collective-permute-start.37) | collective-permute-done | bytes 147488 | tf_op jit(solution)/shard_map/ppermute | solution.py:1231
  276.9 1.8 finish_columns.1
  278.8 1.5 slice_bitcast_fusion.1
  (150 shorter events, 42.6 us)
Async XLA Ops:
  0.7 13.3 %copy-start.13 = (s32[2]{0:T(128)S(1)}, s32[2]{0:T(128)}, u32[]{:S(2)}) copy-start(s32[2]{0:T(128)} %param.25) | copy-start | bytes 28
  1.6 15.4 %collective-permute-start = (bf16[128,768]{1,0:T(8,128)(2,1)S(1)}, bf16[128,768]{1,0:T(8,128)(2,1)S(1)}, u32[]{:S(2)}, u32[]{:S(2)}) collective-permute-start(bf16[128,768]{1,0:T(8,128)(2,1)S(1)} %dynamic-slice_bitcast_fusion.1), channel_id=1, source_target_pairs={{0,4},{1,5},{2,6},{3,7},{4,0},{5,1},{6,2},{7,3},{8,12},{9,13},{10,... | collective-permute-start | bytes 589832 | tf_op jit(solution)/shard_map/ppermute | solution.py:1231
  9.1 14.6 %all-to-all-start = ((bf16[8,80,256]{2,1,0:T(8,128)(2,1)}), bf16[8,80,256]{2,1,0:T(8,128)(2,1)S(1)}, u32[]{:S(2)}, u32[]{:S(2)}) async-start(bf16[8,80,256]{2,1,0:T(8,128)(2,1)} %get-tuple-element.103), calls=%async_computation | async-start | bytes 655360 | tf_op jit(solution)/shard_map/all_to_all | solution.py:1343
  15.0 2.1 copy-start.10
  16.3 1.0 copy-start.11
  16.3 5.6 %copy-start.12 = (bf16[48,768]{1,0:T(8,128)(2,1)S(1)}, bf16[48,768]{1,0:T(8,128)(2,1)}, u32[]{:S(2)}) copy-start(bf16[48,768]{1,0:T(8,128)(2,1)} %get-tuple-element.108) | copy-start | bytes 221188
  17.2 16.0 %collective-permute-start.3 = (bf16[168,768]{1,0:T(8,128)(2,1)S(1)}, bf16[168,768]{1,0:T(8,128)(2,1)S(1)}, u32[]{:S(2)}, u32[]{:S(2)}) collective-permute-start(bf16[168,768]{1,0:T(8,128)(2,1)S(1)} %copy-done.11), channel_id=1, source_target_pairs={{0,2},{1,3},{2,0},{3,1},{4,6},{5,7},{6,4},{7,5},{8,10},{9,11},{10,... | collective-permute-start | bytes 774152 | tf_op jit(solution)/shard_map/ppermute | solution.py:1231
  19.2 21.2 %collective-permute-start.4 = (bf16[168,768]{1,0:T(8,128)(2,1)S(1)}, bf16[168,768]{1,0:T(8,128)(2,1)S(1)}, u32[]{:S(2)}, u32[]{:S(2)}) collective-permute-start(bf16[168,768]{1,0:T(8,128)(2,1)S(1)} %copy-done.11), channel_id=1, source_target_pairs={{0,4},{1,5},{2,6},{3,7},{4,0},{5,1},{6,2},{7,3},{8,12},{9,13},{10,... | collective-permute-start | bytes 774152 | tf_op jit(solution)/shard_map/ppermute | solution.py:1231
  21.9 18.5 %collective-permute-start.5 = (bf16[168,768]{1,0:T(8,128)(2,1)S(1)}, bf16[168,768]{1,0:T(8,128)(2,1)}, u32[]{:S(2)}, u32[]{:S(2)}) collective-permute-start(bf16[168,768]{1,0:T(8,128)(2,1)S(1)} %copy-done.11), channel_id=1, source_target_pairs={{0,6},{1,7},{2,4},{3,5},{4,2},{5,3},{6,0},{7,1},{8,14},{9,15},{10,... | collective-permute-start | bytes 774152 | tf_op jit(solution)/shard_map/ppermute | solution.py:1231
  21.9 10.4 %collective-permute-start.6 = (bf16[48,768]{1,0:T(8,128)(2,1)S(1)}, bf16[48,768]{1,0:T(8,128)(2,1)}, u32[]{:S(2)}, u32[]{:S(2)}) collective-permute-start(bf16[48,768]{1,0:T(8,128)(2,1)S(1)} %copy-done.12), channel_id=1, source_target_pairs={{0,16},{8,24},{16,0},{24,8},{1,17},{9,25},{17,1},{25,9},{2,18},{10... | collective-permute-start | bytes 221192 | tf_op jit(solution)/shard_map/ppermute | solution.py:1231
  23.7 8.5 %collective-permute-start.1 = (bf16[1,8,80,256]{3,2,1,0:T(8,128)(2,1)S(1)}, bf16[1,8,80,256]{3,2,1,0:T(8,128)(2,1)S(1)}, u32[]{:S(2)}, u32[]{:S(2)}) collective-permute-start(bf16[1,8,80,256]{3,2,1,0:T(8,128)(2,1)S(1)} %bitcast.288), channel_id=1, source_target_pairs={{0,16},{8,24},{16,0},{24,8},{1,17},{9,25},{17,1},{25,9},{2,18},{10... | collective-permute-start | bytes 983048 | tf_op jit(solution)/shard_map/ppermute | solution.py:1231
  26.4 28.0 %all-to-all-start.1 = ((bf16[4,2,128,768]{3,2,1,0:T(8,128)(2,1)}), bf16[4,2,128,768]{3,2,1,0:T(8,128)(2,1)S(1)}, u32[]{:S(2)}, u32[]{:S(2)}) async-start(bf16[4,2,128,768]{3,2,1,0:T(8,128)(2,1)} %broadcast_in_dim.77), calls=%async_computation.1 | async-start | bytes 3145728 | tf_op jit(solution)/shard_map/all_to_all | solution.py:1254
  40.4 6.7 %collective-permute-start.2 = (bf16[2,1,8,80,256]{4,3,2,0,1:T(8,128)(2,1)S(1)}, bf16[2,1,8,80,256]{4,3,2,0,1:T(8,128)(2,1)S(1)}, u32[]{:S(2)}, u32[]{:S(2)}) collective-permute-start(bf16[2,1,8,80,256]{4,3,2,0,1:T(8,128)(2,1)S(1)} %pad_maximum_fusion.6), channel_id=1, source_target_pairs={{0,8},{8,0},{16,24},{24,16},{1,9},{9,1},{17,25},{25,17},{2,10},{10... | collective-permute-start | bytes 1966088 | tf_op jit(solution)/shard_map/ppermute | solution.py:1231
  43.5 11.0 %collective-permute-start.9 = (bf16[2,48,768]{2,1,0:T(8,128)(2,1)S(1)}, bf16[2,48,768]{2,1,0:T(8,128)(2,1)}, u32[]{:S(2)}, u32[]{:S(2)}) collective-permute-start(bf16[2,48,768]{2,1,0:T(8,128)(2,1)S(1)} %pad_maximum_fusion.11), channel_id=1, source_target_pairs={{0,1},{1,0},{2,3},{3,2},{4,5},{5,4},{6,7},{7,6},{8,9},{9,8},{10,11... | collective-permute-start | bytes 442376 | tf_op jit(solution)/shard_map/ppermute | solution.py:1231
  44.9 18.5 %collective-permute-start.7 = (bf16[4,96,768]{2,1,0:T(8,128)(2,1)}, bf16[4,96,768]{2,1,0:T(8,128)(2,1)S(1)}, u32[]{:S(2)}, u32[]{:S(2)}) collective-permute-start(bf16[4,96,768]{2,1,0:T(8,128)(2,1)} %slice.123), channel_id=1, source_target_pairs={{0,1},{1,0},{2,3},{3,2},{4,5},{5,4},{6,7},{7,6},{8,9},{9,8},{10,11... | collective-permute-start | bytes 1769480 | tf_op jit(solution)/shard_map/ppermute | solution.py:1231
  45.5 12.3 %collective-permute-start.8 = (bf16[4,72,768]{2,1,0:T(8,128)(2,1)}, bf16[4,72,768]{2,1,0:T(8,128)(2,1)}, u32[]{:S(2)}, u32[]{:S(2)}) collective-permute-start(bf16[4,72,768]{2,1,0:T(8,128)(2,1)} %slice.124), channel_id=1, source_target_pairs={{0,16},{8,24},{16,0},{24,8},{1,17},{9,25},{17,1},{25,9},{2,18},{10... | collective-permute-start | bytes 1327112 | tf_op jit(solution)/shard_map/ppermute | solution.py:1231
  54.5 18.0 %copy-start.4 = (bf16[4,2,128,768]{3,2,1,0:T(8,128)(2,1)}, bf16[4,2,128,768]{3,2,1,0:T(8,128)(2,1)S(1)}, u32[]{:S(2)}) copy-start(bf16[4,2,128,768]{3,2,1,0:T(8,128)(2,1)S(1)} %all-to-all-done.1) | copy-start | bytes 4718596
  64.4 30.9 %collective-permute-start.10 = (bf16[2,2,48,768]{3,2,0,1:T(8,128)(2,1)S(1)}, bf16[2,2,48,768]{3,2,0,1:T(8,128)(2,1)}, u32[]{:S(2)}, u32[]{:S(2)}) collective-permute-start(bf16[2,2,48,768]{3,2,0,1:T(8,128)(2,1)S(1)} %get-tuple-element.212), channel_id=1, source_target_pairs={{0,2},{1,3},{2,0},{3,1},{4,6},{5,7},{6,4},{7,5},{8,10},{9,11},{10,... | collective-permute-start | bytes 884744 | tf_op jit(solution)/shard_map/ppermute | solution.py:1231
  68.8 26.5 %collective-permute-start.11 = (bf16[2,2,48,768]{3,2,0,1:T(8,128)(2,1)S(1)}, bf16[2,2,48,768]{3,2,0,1:T(8,128)(2,1)}, u32[]{:S(2)}, u32[]{:S(2)}) collective-permute-start(bf16[2,2,48,768]{3,2,0,1:T(8,128)(2,1)S(1)} %get-tuple-element.212), channel_id=1, source_target_pairs={{0,4},{1,5},{2,6},{3,7},{4,0},{5,1},{6,2},{7,3},{8,12},{9,13},{10,... | collective-permute-start | bytes 884744 | tf_op jit(solution)/shard_map/ppermute | solution.py:1231
  70.0 25.3 %collective-permute-start.12 = (bf16[2,2,48,768]{3,2,0,1:T(8,128)(2,1)S(1)}, bf16[2,2,48,768]{3,2,0,1:T(8,128)(2,1)}, u32[]{:S(2)}, u32[]{:S(2)}) collective-permute-start(bf16[2,2,48,768]{3,2,0,1:T(8,128)(2,1)S(1)} %get-tuple-element.212), channel_id=1, source_target_pairs={{0,6},{1,7},{2,4},{3,5},{4,2},{5,3},{6,0},{7,1},{8,14},{9,15},{10,... | collective-permute-start | bytes 884744 | tf_op jit(solution)/shard_map/ppermute | solution.py:1231
  73.6 29.9 %collective-permute-start.15 = (bf16[2,4,72,768]{3,2,1,0:T(8,128)(2,1)}, bf16[2,4,72,768]{3,2,1,0:T(8,128)(2,1)}, u32[]{:S(2)}, u32[]{:S(2)}) collective-permute-start(bf16[2,4,72,768]{3,2,1,0:T(8,128)(2,1)} %pad_maximum_fusion.5.outer_one), channel_id=1, source_target_pairs={{0,1},{1,0},{2,3},{3,2},{4,5},{5,4},{6,7},{7,6},{8,9},{9,8},{10,11... | collective-permute-start | bytes 2654216 | tf_op jit(solution)/shard_map/ppermute | solution.py:1231
  75.2 27.8 %copy-start.7 = (bf16[2,4,96,768]{3,2,1,0:T(8,128)(2,1)}, bf16[2,4,96,768]{3,2,1,0:T(8,128)(2,1)S(1)}, u32[]{:S(2)}) copy-start(bf16[2,4,96,768]{3,2,1,0:T(8,128)(2,1)S(1)} %pad_maximum_fusion.2.inner_one) | copy-start | bytes 3538948
  75.2 36.3 %collective-permute-start.14 = (bf16[2,4,96,768]{3,2,1,0:T(8,128)(2,1)S(1)}, bf16[2,4,96,768]{3,2,1,0:T(8,128)(2,1)}, u32[]{:S(2)}, u32[]{:S(2)}) collective-permute-start(bf16[2,4,96,768]{3,2,1,0:T(8,128)(2,1)S(1)} %pad_maximum_fusion.2.inner_one), channel_id=1, source_target_pairs={{0,16},{8,24},{16,0},{24,8},{1,17},{9,25},{17,1},{25,9},{2,18},{10... | collective-permute-start | bytes 3538952 | tf_op jit(solution)/shard_map/ppermute | solution.py:1231
  95.3 16.1 %all-to-all-start.2 = ((bf16[8,192,128]{2,1,0:T(8,128)(2,1)}), bf16[8,192,128]{2,1,0:T(8,128)(2,1)S(1)}, u32[]{:S(2)}, u32[]{:S(2)}) async-start(bf16[8,192,128]{2,1,0:T(8,128)(2,1)} %bitcast.293), calls=%async_computation.2 | async-start | bytes 786432 | tf_op jit(solution)/shard_map/all_to_all | solution.py:1394
  102.9 14.3 %copy-start.6 = (bf16[2,2,2,2,48,768]{5,4,3,2,1,0:T(8,128)(2,1)}, bf16[2,2,2,2,48,768]{5,4,3,2,1,0:T(8,128)(2,1)S(1)}, u32[]{:S(2)}) copy-start(bf16[2,2,2,2,48,768]{5,4,3,2,1,0:T(8,128)(2,1)S(1)} %reverse_select_fusion) | copy-start | bytes 3538948
  102.9 13.0 %collective-permute-start.19 = (bf16[4,2,2,48,768]{4,3,2,1,0:T(8,128)(2,1)S(1)}, bf16[4,2,2,48,768]{4,3,2,1,0:T(8,128)(2,1)}, u32[]{:S(2)}, u32[]{:S(2)}) collective-permute-start(bf16[4,2,2,48,768]{4,3,2,1,0:T(8,128)(2,1)S(1)} %bitcast.289), channel_id=1, source_target_pairs={{0,8},{8,0},{16,24},{24,16},{1,9},{9,1},{17,25},{25,17},{2,10},{10... | collective-permute-start | bytes 3538952 | tf_op jit(solution)/shard_map/ppermute | solution.py:1231
  103.0 12.9 %collective-permute-start.13 = (bf16[2,4,96,768]{3,2,1,0:T(8,128)(2,1)S(1)}, bf16[2,4,96,768]{3,2,1,0:T(8,128)(2,1)}, u32[]{:S(2)}, u32[]{:S(2)}) collective-permute-start(bf16[2,4,96,768]{3,2,1,0:T(8,128)(2,1)S(1)} %pad_maximum_fusion.2.inner_one), channel_id=1, source_target_pairs={{0,8},{8,0},{16,24},{24,16},{1,9},{9,1},{17,25},{25,17},{2,10},{10... | collective-permute-start | bytes 3538952 | tf_op jit(solution)/shard_map/ppermute | solution.py:1231
  111.4 5.7 %copy-start.9 = (bf16[8,192,128]{2,1,0:T(8,128)(2,1)}, bf16[8,192,128]{2,1,0:T(8,128)(2,1)S(1)}, u32[]{:S(2)}) copy-start(bf16[8,192,128]{2,1,0:T(8,128)(2,1)S(1)} %all-to-all-done.2) | copy-start | bytes 1179652
  111.4 5.7 %collective-permute-start.16 = (bf16[2,4,96,768]{3,2,1,0:T(8,128)(2,1)}, bf16[2,4,96,768]{3,2,1,0:T(8,128)(2,1)}, u32[]{:S(2)}, u32[]{:S(2)}) collective-permute-start(bf16[2,4,96,768]{3,2,1,0:T(8,128)(2,1)} %collective-permute-done.14.inner_three), channel_id=1, source_target_pairs={{0,8},{8,0},{16,24},{24,16},{1,9},{9,1},{17,25},{25,17},{2,10},{10... | collective-permute-start | bytes 3538952 | tf_op jit(solution)/shard_map/ppermute | solution.py:1231
  111.4 4.5 %collective-permute-start.17 = (bf16[2,4,72,768]{3,2,1,0:T(8,128)(2,1)}, bf16[2,4,72,768]{3,2,1,0:T(8,128)(2,1)}, u32[]{:S(2)}, u32[]{:S(2)}) collective-permute-start(bf16[2,4,72,768]{3,2,1,0:T(8,128)(2,1)} %pad_maximum_fusion.5.outer_one), channel_id=1, source_target_pairs={{0,8},{8,0},{16,24},{24,16},{1,9},{9,1},{17,25},{25,17},{2,10},{10... | collective-permute-start | bytes 2654216 | tf_op jit(solution)/shard_map/ppermute | solution.py:1231
  111.9 5.2 %collective-permute-start.18 = (bf16[2,4,72,768]{3,2,1,0:T(8,128)(2,1)}, bf16[2,4,72,768]{3,2,1,0:T(8,128)(2,1)}, u32[]{:S(2)}, u32[]{:S(2)}) collective-permute-start(bf16[2,4,72,768]{3,2,1,0:T(8,128)(2,1)} %collective-permute-done.15.outer_three), channel_id=1, source_target_pairs={{0,8},{8,0},{16,24},{24,16},{1,9},{9,1},{17,25},{25,17},{2,10},{10... | collective-permute-start | bytes 2654216 | tf_op jit(solution)/shard_map/ppermute | solution.py:1231
  141.8 13.3 %collective-permute-start.21 = (bf16[2,8,120,768]{3,2,1,0:T(8,128)(2,1)}, bf16[2,8,120,768]{3,2,1,0:T(8,128)(2,1)}, u32[]{:S(2)}, u32[]{:S(2)}) collective-permute-start(bf16[2,8,120,768]{3,2,1,0:T(8,128)(2,1)} %get-tuple-element.139), channel_id=1, source_target_pairs={{0,8},{8,0},{16,24},{24,16},{1,9},{9,1},{17,25},{25,17},{2,10},{10... | collective-permute-start | bytes 8847368 | tf_op jit(solution)/shard_map/ppermute | solution.py:1231
  142.0 9.0 %collective-permute-start.20 = (bf16[2,8,96,768]{3,2,1,0:T(8,128)(2,1)}, bf16[2,8,96,768]{3,2,1,0:T(8,128)(2,1)}, u32[]{:S(2)}, u32[]{:S(2)}) collective-permute-start(bf16[2,8,96,768]{3,2,1,0:T(8,128)(2,1)} %get-tuple-element.137), channel_id=1, source_target_pairs={{0,8},{8,0},{16,24},{24,16},{1,9},{9,1},{17,25},{25,17},{2,10},{10... | collective-permute-start | bytes 7077896 | tf_op jit(solution)/shard_map/ppermute | solution.py:1231
  142.4 24.2 %all-to-all-start.3 = ((bf16[8,200,128]{2,1,0:T(8,128)(2,1)}), bf16[8,200,128]{2,1,0:T(8,128)(2,1)}, u32[]{:S(2)}, u32[]{:S(2)}) async-start(bf16[8,200,128]{2,1,0:T(8,128)(2,1)} %get-tuple-element.135), calls=%async_computation.3 | async-start | bytes 819200 | tf_op jit(solution)/shard_map/all_to_all | solution.py:1423
  148.1 10.4 %copy-start = (bf16[2,4,2,48,768]{4,3,2,1,0:T(8,128)(2,1)}, bf16[2,4,2,48,768]{4,3,2,1,0:T(8,128)(2,1)S(1)}, u32[]{:S(2)}) copy-start(bf16[2,4,2,48,768]{4,3,2,1,0:T(8,128)(2,1)S(1)} %slice.127) | copy-start | bytes 3538948
  148.1 2.9 %copy-start.3 = (bf16[2,8,96,768]{3,2,1,0:T(8,128)(2,1)S(1)}, bf16[2,8,96,768]{3,2,1,0:T(8,128)(2,1)}, u32[]{:S(2)}) copy-start(bf16[2,8,96,768]{3,2,1,0:T(8,128)(2,1)} %get-tuple-element.136) | copy-start | bytes 7077892
  153.6 37.9 %collective-permute-start.22 = (bf16[4,2,96,768]{3,2,0,1:T(8,128)(2,1)}, bf16[4,2,96,768]{3,2,0,1:T(8,128)(2,1)}, u32[]{:S(2)}, u32[]{:S(2)}) collective-permute-start(bf16[4,2,96,768]{3,2,0,1:T(8,128)(2,1)} %fusion), channel_id=1, source_target_pairs={{0,16},{8,24},{16,0},{24,8},{1,17},{9,25},{17,1},{25,9},{2,18},{10... | collective-permute-start | bytes 3538952 | tf_op jit(solution)/shard_map/ppermute | solution.py:1231
  156.5 2.0 copy-start.1
  159.6 32.0 %collective-permute-start.24 = (bf16[2,2,48,768]{3,2,1,0:T(8,128)(2,1)}, bf16[2,2,48,768]{3,2,1,0:T(8,128)(2,1)}, u32[]{:S(2)}, u32[]{:S(2)}) collective-permute-start(bf16[2,2,48,768]{3,2,1,0:T(8,128)(2,1)} %get-tuple-element.187), channel_id=1, source_target_pairs={{0,2},{1,3},{2,0},{3,1},{4,6},{5,7},{6,4},{7,5},{8,10},{9,11},{10,... | collective-permute-start | bytes 884744 | tf_op jit(solution)/shard_map/ppermute | solution.py:1231
  161.0 30.6 %collective-permute-start.25 = (bf16[2,2,48,768]{3,2,1,0:T(8,128)(2,1)}, bf16[2,2,48,768]{3,2,1,0:T(8,128)(2,1)}, u32[]{:S(2)}, u32[]{:S(2)}) collective-permute-start(bf16[2,2,48,768]{3,2,1,0:T(8,128)(2,1)} %get-tuple-element.186), channel_id=1, source_target_pairs={{0,4},{1,5},{2,6},{3,7},{4,0},{5,1},{6,2},{7,3},{8,12},{9,13},{10,... | collective-permute-start | bytes 884744 | tf_op jit(solution)/shard_map/ppermute | solution.py:1231
  163.4 28.2 %collective-permute-start.26 = (bf16[2,2,48,768]{3,2,1,0:T(8,128)(2,1)}, bf16[2,2,48,768]{3,2,1,0:T(8,128)(2,1)}, u32[]{:S(2)}, u32[]{:S(2)}) collective-permute-start(bf16[2,2,48,768]{3,2,1,0:T(8,128)(2,1)} %get-tuple-element.185), channel_id=1, source_target_pairs={{0,6},{1,7},{2,4},{3,5},{4,2},{5,3},{6,0},{7,1},{8,14},{9,15},{10,... | collective-permute-start | bytes 884744 | tf_op jit(solution)/shard_map/ppermute | solution.py:1231
  165.1 26.5 %collective-permute-start.23 = (bf16[2,4,72,768]{3,2,1,0:T(8,128)(2,1)}, bf16[2,4,72,768]{3,2,1,0:T(8,128)(2,1)}, u32[]{:S(2)}, u32[]{:S(2)}) collective-permute-start(bf16[2,4,72,768]{3,2,1,0:T(8,128)(2,1)} %fusion.4), channel_id=1, source_target_pairs={{0,1},{1,0},{2,3},{3,2},{4,5},{5,4},{6,7},{7,6},{8,9},{9,8},{10,11... | collective-permute-start | bytes 2654216 | tf_op jit(solution)/shard_map/ppermute | solution.py:1231
  191.6 42.9 %all-to-all-start.4 = ((bf16[4,2,128,768]{3,2,1,0:T(8,128)(2,1)}), bf16[4,2,128,768]{3,2,1,0:T(8,128)(2,1)}, u32[]{:S(2)}, u32[]{:S(2)}) async-start(bf16[4,2,128,768]{3,2,1,0:T(8,128)(2,1)} %bitcast.287), calls=%async_computation.4 | async-start | bytes 3145728 | tf_op jit(solution)/shard_map/all_to_all | solution.py:1254
  205.3 4.4 %collective-permute-start.32 = (bf16[2,8,80,256]{3,2,1,0:T(8,128)(2,1)}, bf16[2,8,80,256]{3,2,1,0:T(8,128)(2,1)}, u32[]{:S(2)}, u32[]{:S(2)}) collective-permute-start(bf16[2,8,80,256]{3,2,1,0:T(8,128)(2,1)} %get-tuple-element.193), channel_id=1, source_target_pairs={{0,8},{8,0},{16,24},{24,16},{1,9},{9,1},{17,25},{25,17},{2,10},{10... | collective-permute-start | bytes 1966088 | tf_op jit(solution)/shard_map/ppermute | solution.py:1231
  205.3 29.2 %collective-permute-start.30 = (bf16[4,96,768]{2,1,0:T(8,128)(2,1)}, bf16[4,96,768]{2,1,0:T(8,128)(2,1)}, u32[]{:S(2)}, u32[]{:S(2)}) collective-permute-start(bf16[4,96,768]{2,1,0:T(8,128)(2,1)} %fusion.3), channel_id=1, source_target_pairs={{0,1},{1,0},{2,3},{3,2},{4,5},{5,4},{6,7},{7,6},{8,9},{9,8},{10,11... | collective-permute-start | bytes 1769480 | tf_op jit(solution)/shard_map/ppermute | solution.py:1231
  209.2 7.6 %collective-permute-start.31 = (bf16[2,48,768]{2,1,0:T(8,128)(2,1)}, bf16[2,48,768]{2,1,0:T(8,128)(2,1)}, u32[]{:S(2)}, u32[]{:S(2)}) collective-permute-start(bf16[2,48,768]{2,1,0:T(8,128)(2,1)} %fusion.17), channel_id=1, source_target_pairs={{0,16},{8,24},{16,0},{24,8},{1,17},{9,25},{17,1},{25,9},{2,18},{10... | collective-permute-start | bytes 442376 | tf_op jit(solution)/shard_map/ppermute | solution.py:1231
  211.6 22.9 %collective-permute-start.33 = (bf16[8,80,256]{2,1,0:T(8,128)(2,1)}, bf16[8,80,256]{2,1,0:T(8,128)(2,1)}, u32[]{:S(2)}, u32[]{:S(2)}) collective-permute-start(bf16[8,80,256]{2,1,0:T(8,128)(2,1)} %fusion.8), channel_id=1, source_target_pairs={{0,16},{8,24},{16,0},{24,8},{1,17},{9,25},{17,1},{25,9},{2,18},{10... | collective-permute-start | bytes 983048 | tf_op jit(solution)/shard_map/ppermute | solution.py:1231
  214.0 10.7 %collective-permute-start.27 = (bf16[2,72,768]{2,1,0:T(8,128)(2,1)}, bf16[2,72,768]{2,1,0:T(8,128)(2,1)}, u32[]{:S(2)}, u32[]{:S(2)}) collective-permute-start(bf16[2,72,768]{2,1,0:T(8,128)(2,1)} %get-tuple-element.184), channel_id=1, source_target_pairs={{0,2},{1,3},{2,0},{3,1},{4,6},{5,7},{6,4},{7,5},{8,10},{9,11},{10,... | collective-permute-start | bytes 663560 | tf_op jit(solution)/shard_map/ppermute | solution.py:1231
  215.4 19.1 %collective-permute-start.28 = (bf16[2,72,768]{2,1,0:T(8,128)(2,1)}, bf16[2,72,768]{2,1,0:T(8,128)(2,1)}, u32[]{:S(2)}, u32[]{:S(2)}) collective-permute-start(bf16[2,72,768]{2,1,0:T(8,128)(2,1)} %get-tuple-element.183), channel_id=1, source_target_pairs={{0,4},{1,5},{2,6},{3,7},{4,0},{5,1},{6,2},{7,3},{8,12},{9,13},{10,... | collective-permute-start | bytes 663560 | tf_op jit(solution)/shard_map/ppermute | solution.py:1231
  216.9 17.6 %collective-permute-start.29 = (bf16[2,72,768]{2,1,0:T(8,128)(2,1)}, bf16[2,72,768]{2,1,0:T(8,128)(2,1)}, u32[]{:S(2)}, u32[]{:S(2)}) collective-permute-start(bf16[2,72,768]{2,1,0:T(8,128)(2,1)} %get-tuple-element.182), channel_id=1, source_target_pairs={{0,6},{1,7},{2,4},{3,5},{4,2},{5,3},{6,0},{7,1},{8,14},{9,15},{10,... | collective-permute-start | bytes 663560 | tf_op jit(solution)/shard_map/ppermute | solution.py:1231
  236.3 24.8 %collective-permute-start.39 = (bf16[48,768]{1,0:T(8,128)(2,1)}, bf16[48,768]{1,0:T(8,128)(2,1)}, u32[]{:S(2)}, u32[]{:S(2)}) collective-permute-start(bf16[48,768]{1,0:T(8,128)(2,1)} %fusion.24), channel_id=1, source_target_pairs={{0,1},{1,0},{2,3},{3,2},{4,5},{5,4},{6,7},{7,6},{8,9},{9,8},{10,11... | collective-permute-start | bytes 221192 | tf_op jit(solution)/shard_map/ppermute | solution.py:1231
  241.0 6.6 %copy-start.2 = (bf16[1,2,8,80,256]{4,3,2,1,0:T(8,128)(2,1)S(1)}, bf16[1,2,8,80,256]{4,3,2,1,0:T(8,128)(2,1)}, u32[]{:S(2)}) copy-start(bf16[1,2,8,80,256]{4,3,2,1,0:T(8,128)(2,1)} %get-tuple-element.192) | copy-start | bytes 1966084
  241.0 34.2 %collective-permute-start.34 = (bf16[128,768]{1,0:T(8,128)(2,1)}, bf16[128,768]{1,0:T(8,128)(2,1)}, u32[]{:S(2)}, u32[]{:S(2)}) collective-permute-start(bf16[128,768]{1,0:T(8,128)(2,1)} %dynamic-slice_bitcast_fusion), channel_id=1, source_target_pairs={{0,4},{1,5},{2,6},{3,7},{4,0},{5,1},{6,2},{7,3},{8,12},{9,13},{10,... | collective-permute-start | bytes 589832 | tf_op jit(solution)/shard_map/ppermute | solution.py:1231
  249.5 27.5 %all-to-all-start.5 = ((bf16[8,80,256]{2,1,0:T(8,128)(2,1)}), bf16[8,80,256]{2,1,0:T(8,128)(2,1)}, u32[]{:S(2)}, u32[]{:S(2)}) async-start(bf16[8,80,256]{2,1,0:T(8,128)(2,1)} %fusion.7), calls=%async_computation.5 | async-start | bytes 655360 | tf_op jit(solution)/shard_map/all_to_all | solution.py:1491
  255.0 7.4 %collective-permute-start.35 = (bf16[72,768]{1,0:T(8,128)(2,1)S(1)}, bf16[72,768]{1,0:T(8,128)(2,1)S(1)}, u32[]{:S(2)}, u32[]{:S(2)}) collective-permute-start(bf16[72,768]{1,0:T(8,128)(2,1)S(1)} %fusion.18), channel_id=1, source_target_pairs={{0,16},{8,24},{16,0},{24,8},{1,17},{9,25},{17,1},{25,9},{2,18},{10... | collective-permute-start | bytes 331784 | tf_op jit(solution)/shard_map/ppermute | solution.py:1231
  256.7 8.3 %collective-permute-start.36 = (bf16[96,768]{1,0:T(8,128)(2,1)S(1)}, bf16[96,768]{1,0:T(8,128)(2,1)S(1)}, u32[]{:S(2)}, u32[]{:S(2)}) collective-permute-start(bf16[96,768]{1,0:T(8,128)(2,1)S(1)} %get-tuple-element.198), channel_id=1, source_target_pairs={{0,2},{1,3},{2,0},{3,1},{4,6},{5,7},{6,4},{7,5},{8,10},{9,11},{10,... | collective-permute-start | bytes 442376 | tf_op jit(solution)/shard_map/ppermute | solution.py:1231
  258.8 14.6 %collective-permute-start.37 = (bf16[96,768]{1,0:T(8,128)(2,1)S(1)}, bf16[96,768]{1,0:T(8,128)(2,1)S(1)}, u32[]{:S(2)}, u32[]{:S(2)}) collective-permute-start(bf16[96,768]{1,0:T(8,128)(2,1)S(1)} %get-tuple-element.200), channel_id=1, source_target_pairs={{0,4},{1,5},{2,6},{3,7},{4,0},{5,1},{6,2},{7,3},{8,12},{9,13},{10,... | collective-permute-start | bytes 442376 | tf_op jit(solution)/shard_map/ppermute | solution.py:1231
  261.1 12.2 %collective-permute-start.38 = (bf16[96,768]{1,0:T(8,128)(2,1)S(1)}, bf16[96,768]{1,0:T(8,128)(2,1)S(1)}, u32[]{:S(2)}, u32[]{:S(2)}) collective-permute-start(bf16[96,768]{1,0:T(8,128)(2,1)S(1)} %get-tuple-element.199), channel_id=1, source_target_pairs={{0,6},{1,7},{2,4},{3,5},{4,2},{5,3},{6,0},{7,1},{8,14},{9,15},{10,... | collective-permute-start | bytes 442376 | tf_op jit(solution)/shard_map/ppermute | solution.py:1231
  264.2 10.9 %copy-start.5 = (bf16[2,128,768]{2,1,0:T(8,128)(2,1)S(1)}, bf16[2,128,768]{2,1,0:T(8,128)(2,1)}, u32[]{:S(2)}) copy-start(bf16[2,128,768]{2,1,0:T(8,128)(2,1)} %reduce_sum.21) | copy-start | bytes 1179652
  265.0 11.1 %copy-start.8 = (f32[256,768]{1,0:T(8,128)S(1)}, f32[256,768]{1,0:T(8,128)}, u32[]{:S(2)}) copy-start(f32[256,768]{1,0:T(8,128)} %get-tuple-element.134) | copy-start | bytes 2359300

commit v2 on v1

--- a/solution.py
+++ b/solution.py
@@ -848,7 +848,7 @@
         input_output_aliases={5 + i: i for i in range(skip)},
         scratch_shapes=[pltpu.VMEM((rows, full), BF), pltpu.VMEM((rows, full), BF)],
         compiler_params=pltpu.CompilerParams(dimension_semantics=("arbitrary", "arbitrary"),
-                                             vmem_limit_bytes=56 * 2 ** 20),
+                                             vmem_limit_bytes=63 * 2 ** 20),
         cost_estimate=pl.CostEstimate(flops=flops, bytes_accessed=rows * width * 16, transcendentals=count * rows * rows),
         name="attention_forward",
     )(x, w_block, vec, kext, trig, *previous)
@@ -881,7 +881,7 @@
                         pltpu.VMEM((3 * DH, rows), BF), pltpu.VMEM((DH, width), F32),
                         pltpu.VMEM((rows, width), F32)],
         compiler_params=pltpu.CompilerParams(dimension_semantics=("arbitrary", "arbitrary"),
-                                             vmem_limit_bytes=56 * 2 ** 20),
+                                             vmem_limit_bytes=63 * 2 ** 20),
         cost_estimate=pl.CostEstimate(flops=flops, bytes_accessed=rows * width * 20, transcendentals=heads * rows * rows),
         name="attention_backward",
     )(core.reshape(1), d_out, x, w, vec, kext, trig, qb, kb, v1, qp, save, scl, prob)
@@ -919,16 +919,14 @@
     count = inner_ref.shape[1] // width
     for i in range(count):
         packed_ref[i * rows:(i + 1) * rows, :] = inner_ref[:, i * width:(i + 1) * width]
-    wide = outer_ref.shape[0] // 2
-    third_ref[...] = outer_ref[:wide, :]
-    packed_ref[count * rows:count * rows + wide, :] = outer_ref[wide:, :]
-    packed_ref[count * rows + wide:, :] = output_ref[...]
+    packed_ref[count * rows:, :] = outer_ref[...]
+    third_ref[...] = output_ref[...]
 
 
 def pack(mats, smalls, wide, kinds, inner, outer, output, heads, groups, members):
     rows, width = mats[0].shape
-    third = outer.shape[0] // 2
-    total = inner.shape[1] // width * rows + third + output.shape[0]
+    third = output.shape[0]
+    total = inner.shape[1] // width * rows + outer.shape[0]
     return pl.pallas_call(
         functools.partial(pack_kernel, heads, groups),
         out_shape=[jax.ShapeDtypeStruct((members, heads * rows + 8, 2 * LANES), BF),
@@ -1003,15 +1001,22 @@
         out_shape=jax.ShapeDtypeStruct(block.shape, BF),
         input_output_aliases={4: 0},
         scratch_shapes=[pltpu.VMEM((16, owners * shard), F32)],
+        cost_estimate=pl.CostEstimate(flops=2 * 10 ** 10, bytes_accessed=2 ** 20, transcendentals=0),
         name="small_gradients",
     )(g, head_sums, rest, wide_sums, block)
 
 
 def finish_kernel(heads, block_ref, *refs):
-    outs, small_ref = refs[:-1], refs[-1]
+    outs, vectors, pair_ref, wide_ref = refs[:4], refs[4:14], refs[14], refs[15]
     groups = block_ref.shape[0] // 2
     shard = outs[0].shape[0]
-    small_ref[...] = sum(block_ref[g, heads * shard:, :].astype(F32) for g in range(2 * groups))
+    total = sum(block_ref[g, heads * shard:, :].astype(F32) for g in range(2 * groups))
+    for n, i in enumerate((0, 1, 2, 5, 6, 7)):
+        vectors[n][...] = total[i, :shard]
+    for i in range(4):
+        vectors[6 + i][...] = total[i, LANES:LANES + shard]
+    pair_ref[...] = total[3:5, :shard]
+    wide_ref[...] = total[4, LANES:LANES + wide_ref.shape[0]]
     for g in range(groups):
         for h in range(heads):
             part = block_ref[g, h * shard:(h + 1) * shard, :].astype(F32)
@@ -1021,18 +1026,39 @@
                 outs[m][:, at:at + DH] = part[:, m * DH:(m + 1) * DH]
 
 
-def finish(block, heads, shard, width):
+def finish(block, heads, shard, width, wide):
+    S = jax.ShapeDtypeStruct
     return pl.pallas_call(
         functools.partial(finish_kernel, heads),
-        out_shape=[jax.ShapeDtypeStruct((shard, width), F32)] * 4 + [jax.ShapeDtypeStruct((8, 2 * LANES), F32)],
+        out_shape=[S((shard, width), F32)] * 4 + [S((shard,), F32)] * 10 + [S((2, shard), F32), S((wide,), F32)],
         name="finish_columns",
     )(block)
 
 
+def row_sum_kernel(bit_ref, keep_ref, first_ref, *refs):
+    bit = bit_ref[0]
+    total = keep_ref[0, bit].astype(F32) + first_ref[bit].astype(F32)
+    for ref in refs[:-1]:
+        total = total + ref[...].astype(F32)
+    refs[-1][...] = total.astype(BF)
+
+
+def row_sum(bit, keep, first, *more):
+    vmem = pl.BlockSpec(memory_space=pltpu.VMEM)
+    return pl.pallas_call(
+        row_sum_kernel,
+        in_specs=[pl.BlockSpec(memory_space=pltpu.SMEM)] + [vmem] * (2 + len(more)),
+        out_specs=vmem,
+        out_shape=jax.ShapeDtypeStruct(first.shape[1:], BF),
+        cost_estimate=pl.CostEstimate(flops=2 * 10 ** 10, bytes_accessed=2 ** 20, transcendentals=0),
+        name="row_sum",
+    )(bit.reshape(1), keep, first, *more)
+
+
 def token_kernel(core_ref, valid_ref, mixed_ref, x_ref, og_ref, vec_ref, wide_ref,
                  inner_one, inner_two, inner_three, inner_four, outer_one, outer_two, outer_three, outer_four, third_one, third_two,
-                 result_ref, first_ref, grad_ref, gi_keep, gi_send, go_keep, go_send, rest_ref, gw_ref,
-                 packed, wi, act, slope, normed_t, acc, gi_ref, go_ref, sems):
+                 result_ref, first_ref, grad_ref, gi_keep, gi_send, go_keep, go_send, gt_keep, gt_send, rest_ref, gw_ref,
+                 packed, wi, act, slope, normed_t, acc, gi_ref, go_ref, sems, back_sems):
     core, bit_y, bit_x = core_ref[0], core_ref[1], core_ref[2]
     seqs, width, stretch = mixed_ref.shape
     tokens = seqs * stretch
@@ -1043,20 +1069,20 @@
     wide = packed.shape[3] - (count + 1) * shard
     base = count * shard
     copies = []
+    for i, (src, k) in enumerate(((third_one, core), (third_two, 1 - core))):
+        for y in range(2):
+            copies.append(pltpu.make_async_copy(src.at[:, y], packed.at[2 * y + k, :, :, base + wide:, :], sems.at[26 + 2 * i + y]))
     sources = ((outer_one, core, bit_x), (outer_two, 1 - core, bit_x), (outer_three, core, 1 - bit_x), (outer_four, 1 - core, 1 - bit_x))
     for i, (src, k, x) in enumerate(sources):
         for y in range(2):
-            copies.append(pltpu.make_async_copy(src.at[y], packed.at[2 * y + k, :, x, base + wide // 2:, :], sems.at[4 + 2 * i + y]))
-    for i, (src, k) in enumerate(((third_one, core), (third_two, 1 - core))):
-        for y in range(2):
-            copies.append(pltpu.make_async_copy(src.at[:, y], packed.at[2 * y + k, :, :, base:base + wide // 2, :], sems.at[26 + 2 * i + y]))
+            copies.append(pltpu.make_async_copy(src.at[y], packed.at[2 * y + k, :, x, base:base + wide, :], sems.at[4 + 2 * i + y]))
     sources = ((inner_one, core, bit_y), (inner_two, 1 - core, bit_y), (inner_three, core, 1 - bit_y), (inner_four, 1 - core, 1 - bit_y))
     for i, (src, k, y) in enumerate(sources):
         for x in range(2):
             copies.append(pltpu.make_async_copy(src.at[x], packed.at[2 * y + k, :, x, :base, :], sems.at[12 + 2 * i + x]))
     for copy in copies:
         copy.start()
-    for copy in copies[:8]:
+    for copy in copies[:4]:
         copy.wait()
     w_out = packed[:, :, :, base + wide:, :].astype(F32).reshape(width, width).astype(BF)
     def w_outer(j):
@@ -1075,7 +1101,7 @@
     normed_t[...] = jnp.transpose(normed).astype(BF)
     acc[...] = jnp.zeros_like(acc)
 
-    for copy in copies[8:]:
+    for copy in copies[4:]:
         copy.wait()
     for i in range(count):
         wi[:, i * width:(i + 1) * width] = packed[:, :, :, i * shard:(i + 1) * shard, :].astype(F32).reshape(width, width).astype(BF)
@@ -1110,13 +1136,22 @@
     two = [total(cot * hat_two), total(cot)]
     acc[...] = d_second
 
+    part = wide // 2
+
+    def inner_back(j):
+        return [
+            pltpu.make_async_copy(gi_ref.at[which, y, j], (gi_keep, gi_send)[which].at[y, j], back_sems.at[j, 2 * which + y])
+            for which in range(2) for y in range(2)]
+
     def upper(which, y, j):
-        target = (go_keep, go_send)[which]
-        return pltpu.make_async_copy(go_ref.at[which, y, :, :wide, :], target.at[y, :, :wide, :], sems.at[20 + j])
+        low_part = pltpu.make_async_copy(go_ref.at[which, y, :, :part, :], (gt_keep, gt_send)[which].at[y], sems.at[20 + j])
+        high_part = pltpu.make_async_copy(
+            go_ref.at[which, y, :, part:wide, :], (go_keep, go_send)[which].at[y, :, :part, :], sems.at[30 + j])
+        return low_part, high_part
 
     def lower(which, y):
         target = (go_keep, go_send)[which]
-        return pltpu.make_async_copy(go_ref.at[which, y, :, wide:, :], target.at[y, :, wide:, :], sems.at[2 * which + y])
+        return pltpu.make_async_copy(go_ref.at[which, y, :, wide:, :], target.at[y, :, part:, :], sems.at[2 * which + y])
 
     def backward(j, carry):
         at = pl.ds(pl.multiple_of(j * width, width), width)
@@ -1131,26 +1166,22 @@
 
         @pl.when(which == 0)
         def _():
-            upper(0, j // 2, j).start()
+            for copy in upper(0, j // 2, j):
+                copy.start()
 
         @pl.when(which == 1)
         def _():
-            upper(1, j // 2, j).start()
+            for copy in upper(1, j // 2, j):
+                copy.start()
 
         for b in range(count):
             gi = mm(normed_t[b * block:(b + 1) * block, :], d_in_low, ROWCOL)
-            gi = gi.reshape(members, shard, width).astype(BF)
-            for n in range(count):
-                @pl.when(j == n)
-                def _():
-                    gi_ref[(b % 2) ^ core, b // 2, :, n * shard:(n + 1) * shard, :] = gi
+            gi_ref[(b % 2) ^ core, b // 2, j] = gi.reshape(members, shard, width).astype(BF)
+        for copy in inner_back(j):
+            copy.start()
         return carry
 
     lax.fori_loop(0, count, backward, 0)
-    backs = [pltpu.make_async_copy(gi_ref.at[0], gi_keep, sems.at[24]), pltpu.make_async_copy(gi_ref.at[1], gi_send, sems.at[25]),
-             ]
-    backs[1].start()
-    backs[0].start()
     d_normed = acc[...]
     one = [total(d_normed * hat_one), total(d_normed)]
     d_hat = d_normed * line(7)
@@ -1185,8 +1216,12 @@
     for back in lowers:
         back.start()
     for j in range(count):
-        upper(0, 0, j).wait()
-    for back in backs + lowers:
+        for copy in upper(0, 0, j):
+            copy.wait()
+    for j in range(count):
+        for copy in inner_back(j):
+            copy.wait()
+    for back in lowers:
         back.wait()
 
 
@@ -1198,6 +1233,7 @@
     members = inner_parts[0].shape[0] * inner_parts[0].shape[1]
     owners = members * count
     rows = ff // owners + width // owners
+    half_rows = ff // owners // 2
     base = ff // width * (width // owners)
     groups = width // span
     vmem = pl.BlockSpec(memory_space=pltpu.VMEM)
@@ -1206,17 +1242,18 @@
     return pl.pallas_call(
         token_kernel,
         in_specs=[pl.BlockSpec(memory_space=pltpu.SMEM)] + [vmem] * 6 + [hbm] * 10,
-        out_specs=[vmem] * 3 + [hbm] * 4 + [vmem] * 2,
+        out_specs=[vmem] * 3 + [hbm] * 6 + [vmem] * 2,
         out_shape=[S((tokens, width), BF), S((tokens, width), F32), S((seqs * groups, span + 8, stretch), BF),
-                   S((2, members, base, width), BF), S((2, members, base, width), BF),
-                   S((2, members, rows, width), BF), S((2, members, rows, width), BF),
+                   S((2, count, members, width // owners, width), BF), S((2, count, members, width // owners, width), BF),
+                   S((2, members, rows - half_rows, width), BF), S((2, members, rows - half_rows, width), BF),
+                   S((2, members, half_rows, width), BF), S((2, members, half_rows, width), BF),
                    S((6, width), F32), S((1, ff), F32)],
         scratch_shapes=[pltpu.VMEM((count, members // 2, 2, (count + 1) * (width // owners) + ff // owners, width), BF), pltpu.VMEM((width, ff), BF),
                         pltpu.VMEM((tokens, ff), BF), pltpu.VMEM((tokens, ff), F32),
                         pltpu.VMEM((width, tokens), BF), pltpu.VMEM((tokens, width), F32),
-                        pltpu.VMEM((2, 2, members, base, width), BF), pltpu.VMEM((2, 2, members, rows, width), BF),
-                        pltpu.SemaphoreType.DMA((30,))],
-        compiler_params=pltpu.CompilerParams(vmem_limit_bytes=60 * 2 ** 20),
+                        pltpu.VMEM((2, 2, count, members, width // owners, width), BF), pltpu.VMEM((2, 2, members, rows, width), BF),
+                        pltpu.SemaphoreType.DMA((34,)), pltpu.SemaphoreType.DMA((count, 4))],
+        compiler_params=pltpu.CompilerParams(vmem_limit_bytes=63 * 2 ** 20),
         cost_estimate=pl.CostEstimate(flops=tokens * 2 * width * (6 * ff + 4 * width), bytes_accessed=30 * 2 ** 20, transcendentals=tokens * ff),
         name="token_block",
     )(core, valid, mixed, x, out_grad, vectors, inner_add, *inner_parts, *outer_parts, *third_parts)
@@ -1379,14 +1416,23 @@
 
     vectors, inner_add, vec = unpack(block, g, heads, groups, shard, inner_shard)
 
-    inner_x, outer_y, third_x = after((inner_x, outer_y, third_x), x_seq)
+    saved = attention_forward(x_seq, block, 0, 1, heads, vec, kext, trig)
+    inner_x, outer_y, third_x = after((inner_x, outer_y, third_x), saved[0])
     third = in_order(bit_x, third, third_x, 1)
     inner_block = in_order(bit_x, inner_block, inner_x, 0)
     outer_block = in_order(bit_y, outer_block, outer_y, 0)
     inner_y, outer_x = swap(inner_block, DP, 2), swap(outer_block, CTX, 1)
     third_z = [swap(third, CTX, 2 * m) for m in (1, 2, 3)]
     saved = attention_forward(
-        x_seq, block, 0, heads, heads, after(vec, inner_block, outer_block, third), kext, trig
+        x_seq,
+        block,
+        1,
+        heads - 1,
+        heads,
+        after(vec, inner_block, outer_block, third),
+        kext,
+        trig,
+        saved,
     )
     att, q_block, kb, v1, qp, save, scl, w_heads, prob = saved
     third_z = after(third_z, att)
@@ -1395,14 +1441,15 @@
     inner_block, outer_block = after((inner_block, outer_block), att)
     inner_far, outer_far = swap(inner_block, DP, 1), swap(outer_block, DP, 1)
     third = in_z_order([third] + third_z)
+    third_parts = (third, swap(third, DP, 1))
+    mixed = after(mixed, third_parts[1], inner_far, outer_far)
     inner_y, outer_x = after((inner_y, outer_x), mixed)
-    third_parts = (third, swap(third, DP, 1))
     inner_parts = (inner_block, inner_far, inner_y, swap(inner_y, DP, 1))
     outer_parts = (outer_block, outer_far, outer_x, swap(outer_x, DP, 1))
 
     own_slots = c * stretch + jnp.arange(stretch, dtype=jnp.int32)
     row_valid = (own_slots[None, :] < lengths[:, None]).astype(F32)
-    result, first_grad, mixed_grad, inner_keep, inner_send, outer_keep, outer_send, rest, wide = (
+    result, first_grad, mixed_grad, inner_keep, inner_send, outer_keep, outer_send, third_keep, third_send, rest, wide = (
         token_block(
             jnp.stack([core, bit_y, bit_x]),
             row_valid.reshape(-1, 1),
@@ -1423,19 +1470,21 @@
     d_out = lax.all_to_all(mixed_grad, CTX, 0, 0, tiled=True)
     z = c // 2
     first_half = inner_shard // 2
+    third_terms = [third_keep, swap(third_send, DP, 1)]
+    inner_send, outer_send = after((inner_send, outer_send), third_terms[1])
     inner_terms = [inner_keep, swap(inner_send, DP, 1)]
-    inner_terms = [t.reshape(2, 4, 2, cut, width) for t in inner_terms]
+    inner_terms = [t.reshape(2, -1, 4, 2, shard, width) for t in inner_terms]
+    third_terms = [t.reshape(2, 4, 2, first_half, width) for t in third_terms]
     outer_terms = [outer_keep, swap(outer_send, DP, 1)]
-    outer_terms = [t.reshape(2, 4, 2, inner_shard + shard, width) for t in outer_terms]
+    outer_terms = [t.reshape(2, 4, 2, first_half + shard, width) for t in outer_terms]
+    third_send = [total_low(picks(third_terms, z ^ m, 1)) for m in (1, 2, 3)]
+    third_z = [swap(third_send[m - 1], CTX, 2 * m) for m in (1, 2, 3)]
+    inner_terms[1] = after(inner_terms[1], *third_send)
     inner_send = total_low(picks(inner_terms, 1 - bit_y, 0))
+    inner_y = swap(inner_send, DP, 2)
     outer_terms[1] = after(outer_terms[1], inner_send)
-    third_terms = [t[..., :first_half, :] for t in outer_terms]
-    outer_terms = [t[..., first_half:, :] for t in outer_terms]
-    third_send = [total_low(picks(third_terms, z ^ m, 1)) for m in (1, 2, 3)]
     outer_send = total_low(picks(outer_terms, 1 - bit_x, 2))
-    inner_y = swap(inner_send, DP, 2)
     outer_x = swap(outer_send, CTX, 1)
-    third_z = [swap(third_send[m - 1], CTX, 2 * m) for m in (1, 2, 3)]
     d_out = after(d_out, inner_send, outer_send, *third_send)
     d_blocks = d_out.reshape(2, groups, span + 8, stretch)
 
@@ -1461,50 +1510,47 @@
         (d_x, w_grad, head_sums, inner_y, outer_x, third_z)
     )
     d_x = exchange(d_x.reshape(groups, 2, stretch, width), False)
+    w_both = small_rows(w_grad, jnp.stack([g, core]), head_sums, rest, wide, groups, shard)
+    w_far = swap(w_both[1], DP, 1)
+    outer_x, inner_y, third_z = after((outer_x, inner_y, third_z), w_both)
     outer_terms = picks(outer_terms, bit_x, 2) + [outer_x]
     outer_send = [total_low(picks(outer_terms, z ^ m, 1)) for m in (1, 2, 3)]
     outer_z = [swap(outer_send[m - 1], CTX, 2 * m) for m in (1, 2, 3)]
     inner_terms = picks(inner_terms, bit_y, 0) + [inner_y]
-    inner_send = total_low(picks(inner_terms, 1 - bit_x, 1))
+    inner_send = total_low(picks(inner_terms, 1 - bit_x, 2))
     inner_x = swap(inner_send, CTX, 1)
-
-    w_grad = after(w_grad, inner_send, *outer_send)
-    block = small_rows(w_grad, jnp.stack([g, core]), head_sums, rest, wide, groups, shard)
-    block = [block[0], swap(block[1], DP, 1)]
-    third_terms = picks(third_terms, z, 1) + third_z
+    w_far = after(w_far, inner_send, *outer_send)
+    block_send = row_sum(1 - bit_y, w_both, w_far)
+    block_y = swap(block_send, DP, 2)
+
+    d_x_send = jnp.sum(pick(d_x, 1 - s, 1).astype(F32), axis=0).astype(BF)
+    d_x_z = swap(d_x_send, CTX, 4)
+    block = row_sum(bit_y, w_both, w_far, after(block_y, d_x_send))
+    inner_sum = total_low(picks(inner_terms, bit_x, 2) + [after(inner_x, block)])
+    third_terms = picks(third_terms, z, 1) + after(third_z, block)
     third_send = total_low(picks(third_terms, 1 - bit_y, 0))
-    block[1] = after(block[1], third_send)
     third_y = swap(third_send, DP, 2)
-    block_send = total_low(picks(block, 1 - bit_y, 0))
-    block_y = swap(block_send, DP, 2)
-
-    d_x, outer_z, inner_x, third_y, block_y = lax.optimization_barrier(
-        (d_x, outer_z, inner_x, third_y, block_y)
-    )
-    d_x = jnp.sum(d_x.astype(F32), axis=0).astype(BF)
-    d_x_send = pick(d_x, 1 - s, 0)
-    d_x_z = swap(d_x_send, CTX, 4)
-    inner_sum = total_low(picks(inner_terms, bit_x, 1) + [after(inner_x, d_x_send)])
-    inner_z = [swap(pick(inner_sum, z ^ m, 0), CTX, 2 * m) for m in (1, 2, 3)]
-    block = total_low(picks(block, bit_y, 0) + [after(block_y, inner_sum)])
-    outer_z = after(outer_z, block)
     block = lax.all_to_all(block, CTX, 0, 0, tiled=True)
+    inner_send = [pick(inner_sum, z ^ m, 1) for m in (1, 2, 3)]
+    inner_z = [swap(inner_send[m - 1], CTX, 2 * m) for m in (1, 2, 3)]
+    outer_z = after(outer_z, *inner_send)
     outer_terms = picks(outer_terms, z, 1) + outer_z
     outer_y = swap(total_low(picks(outer_terms, 1 - bit_y, 0)), DP, 2)
-    third_terms = picks(third_terms, bit_y, 0) + [third_y]
+    third_terms = picks(third_terms, bit_y, 0) + [after(third_y, *inner_send)]
     third_x = swap(total_low(picks(third_terms, 1 - bit_x, 0)), CTX, 1)
-    inner_own = sum(t.astype(F32) for t in [pick(inner_sum, z, 0)] + inner_z)
-    inner_own = jnp.concatenate(
-        [inner_own[i : i + shard] for i in range(0, cut, shard)], axis=1
-    )
     third_own = sum(t.astype(F32) for t in picks(third_terms, bit_x, 0) + [third_x])
     outer_sum = sum(t.astype(F32) for t in picks(outer_terms, bit_y, 0) + [outer_y])
     outer_own = jnp.concatenate([third_own, outer_sum[:first_half]], axis=0)
     output_own = outer_sum[first_half:]
-    query_own, key_own, value_own, position_own, small = finish(block, heads, shard, width)
-    v = [small[i, :shard] for i in range(8)] + [small[i, LANES : LANES + shard] for i in range(4)]
-    input_terms = in_order(s, pick(d_x, s, 0), d_x_z, 0)
-    input_grad = (first_grad + input_terms.astype(F32)).astype(BF)
+    finished = finish(block, heads, shard, width, inner_shard)
+    query_own, key_own, value_own, position_own = finished[:4]
+    v = finished[4:14]
+    inner_z = after(inner_z, query_own)
+    inner_own = sum(t.astype(F32) for t in [pick(inner_sum, z, 1)] + inner_z)
+    inner_own = jnp.concatenate(list(inner_own), axis=1)
+    d_x_own = jnp.sum(pick(d_x, s, 1).astype(F32), axis=0)
+    input_terms = in_order(s, d_x_own, after(d_x_z, query_own).astype(F32), 0)
+    input_grad = (first_grad + input_terms).astype(BF)
     sums_all = jnp.sum(d_out[:, span : span + 2].astype(F32), axis=(0, 1))
     sums_all = sums_all[: 3 * seqs].reshape(seqs, 3)
     mean_squares = sums_all / (lengths.astype(F32)[:, None] * width)
@@ -1514,22 +1560,22 @@
         query_own,
         key_own,
         value_own,
-        v[5],
+        v[3],
         position_own,
         v[0],
         v[1],
         v[2],
-        jnp.stack([v[3], v[4]]),
+        finished[14],
         output_own,
+        v[4],
+        v[5],
         v[6],
+        inner_own,
+        finished[15],
+        outer_own,
         v[7],
         v[8],
-        inner_own,
-        small[4, LANES : LANES + inner_shard],
-        outer_own,
         v[9],
-        v[10],
-        v[11],
         mean_squares,
     )
 

time: 284 us -> 255 us (0.90)
  waiting for transfers between devices: 57.8 us -> 44.6 us
  local copies, waits for them, and re-layouts: 25.4 us -> 14.3 us
  other arithmetic: 44 us -> 35.4 us
  Pallas kernels: 75.4 us -> 82.1 us
  starting transfers between devices: 78.6 us -> 74.9 us
    ppermute x40 -> x41, waiting for transfers between devices: 45.4 us -> 21.5 us  [swap(): return lax.ppermute(x, axis, [(i, i ^ bit) for i in range(count)])]
    all_to_all x2, waiting for transfers between devices: 4.15 us -> 15.9 us  [exchange(): return lax.all_to_all(x, CTX, 0, 0, axis_index_groups=sets, tiled=True)]
    slice x6 -> x0, local copies, waits for them, and re-layouts: 9.27 us -> none  [the longest x2 4.08 us: head_layout(): outer_terms = [t[..., first_half:, :] for t in outer_terms]]
    convert_element_type x11 -> x9, other arithmetic: 20.8 us -> 14.5 us  [total_low(): return sum((t.astype(F32) for t in terms)).astype(BF)]
    pallas_call x1 -> x3, Pallas kernels: 1.81 us -> 6.51 us  [the longest x2 4.69 us: row_sum(): pl.pallas_call(row_sum_kernel, in_specs=[pl.BlockSpec(memory_space=pltpu....]
    pallas_call x1 -> x2, Pallas kernels: 18.5 us -> 22.9 us  [attention_forward(): pl.pallas_call(lambda *refs: kernel(*refs[:5], *refs[5 + skip:]), grid=(c...]
    all_to_all x1, waiting for transfers between devices: 7.97 us -> 4.38 us  [head_layout(): lax.all_to_all(att, CTX, 0, 0, tiled=True).reshape(seqs, width, stretch)]
    ppermute x40 -> x41, starting transfers between devices: 52.5 us -> 49.5 us  [swap(): return lax.ppermute(x, axis, [(i, i ^ bit) for i in range(count)])]
  transfers between devices with their start and end apart: 46 -> 47, of which waited for: 13 -> 13; matrix products, arithmetic and copies ran while one was open for 22% -> 16% of each run, Pallas kernels for 17% -> 23%
where the time goes in v2:
time: 255 us; the launch traced here: 253 us
  Pallas kernels  82.1 us (32%)
  starting transfers between devices  74.9 us (29%)
  waiting for transfers between devices  44.6 us (17%)
  other arithmetic  35.4 us (14%)
  local copies, waits for them, and re-layouts  14.3 us (6%)
    ppermute x41, starting transfers between devices, swap(): return lax.ppermute(x, axis, [(i, i ^ bit) for i in range(count)])  49.5 us
    pallas_call x1, Pallas kernels, attention_backward(): pl.pallas_call(functools.partial(attention_backward_kernel, tile), grid=(...  24.9 us
    pallas_call x2, Pallas kernels, attention_forward(): pl.pallas_call(lambda *refs: kernel(*refs[:5], *refs[5 + skip:]), grid=(c...  22.9 us
    pallas_call x1, Pallas kernels, token_block(): pl.pallas_call(token_kernel, in_specs=[pl.BlockSpec(memory_space=pltpu.SM...  22.1 us
    ppermute x41, waiting for transfers between devices, swap(): return lax.ppermute(x, axis, [(i, i ^ bit) for i in range(count)])  21.5 us
    all_to_all x2, waiting for transfers between devices, exchange(): return lax.all_to_all(x, CTX, 0, 0, axis_index_groups=sets, tiled=True)  15.9 us
    convert_element_type x9, other arithmetic, total_low(): return sum((t.astype(F32) for t in terms)).astype(BF)  14.5 us
    all_to_all x2, starting transfers between devices, exchange(): return lax.all_to_all(x, CTX, 0, 0, axis_index_groups=sets, tiled=True)  7.93 us
  transfers between devices with their start and end apart: 47, of which 13 were waited for; matrix products, arithmetic and copies ran while one was open for 16% of the time, Pallas kernels for 23%

profile of v2, /device:TPU:0, one launch (start us, length us, event | category | flops | bytes accessed | tf_op | source)
XLA Modules:
  0.0 252.7 jit_solution(16543527440659596060)
XLA Ops:
  1.6 4.1 %collective-permute-start = (bf16[128,768]{1,0:T(8,128)(2,1)S(1)}, bf16[128,768]{1,0:T(8,128)(2,1)S(1)}, u32[]{:S(2)}, u32[]{:S(2)}) collective-permute-start(bf16[128,768]{1,0:T(8,128)(2,1)S(1)} %dynamic-slice_bitcast_fusion), channel_id=1, source_target_pairs={{0,4},{1,5},{2,6},{3,7},{4,0},{5,1},{6,2},{7,3},{8,12},{9,13},{10,... | collective-permute-start | bytes 589832 | tf_op jit(solution)/shard_map/ppermute | solution.py:1268
  5.7 1.2 fusion.30
  7.0 2.1 pack_columns.1
  9.1 3.8 %all-to-all-start = ((bf16[8,80,256]{2,1,0:T(8,128)(2,1)}), bf16[8,80,256]{2,1,0:T(8,128)(2,1)S(1)}, u32[]{:S(2)}, u32[]{:S(2)}) async-start(bf16[8,80,256]{2,1,0:T(8,128)(2,1)} %get-tuple-element.134), calls=%async_computation | async-start | bytes 655360 | tf_op jit(solution)/shard_map/all_to_all | solution.py:1380
  15.0 1.3 pad_maximum_fusion.refs_4_.trig_ref
  17.3 2.0 collective-permute-start.3
  19.3 2.6 %collective-permute-start.4 = (bf16[192,768]{1,0:T(8,128)(2,1)S(1)}, bf16[192,768]{1,0:T(8,128)(2,1)S(1)}, u32[]{:S(2)}, u32[]{:S(2)}) collective-permute-start(bf16[192,768]{1,0:T(8,128)(2,1)S(1)} %copy-done.10), channel_id=1, source_target_pairs={{0,4},{1,5},{2,6},{3,7},{4,0},{5,1},{6,2},{7,3},{8,12},{9,13},{10,... | collective-permute-start | bytes 884744 | tf_op jit(solution)/shard_map/ppermute | solution.py:1268
  21.9 1.5 collective-permute-start.6
  23.7 1.5 collective-permute-start.1
  25.2 1.2 broadcast_in_dim.77
  26.4 4.4 %all-to-all-start.1 = ((bf16[4,2,128,768]{3,2,1,0:T(8,128)(2,1)}), bf16[4,2,128,768]{3,2,1,0:T(8,128)(2,1)}, u32[]{:S(2)}, u32[]{:S(2)}) async-start(bf16[4,2,128,768]{3,2,1,0:T(8,128)(2,1)} %broadcast_in_dim.77), calls=%async_computation.1 | async-start | bytes 3145728 | tf_op jit(solution)/shard_map/all_to_all | solution.py:1291
  32.1 2.1 collective-permute-start.9
  34.2 8.6 %collective-permute-done.4 = bf16[192,768]{1,0:T(8,128)(2,1)S(1)} collective-permute-done((bf16[192,768]{1,0:T(8,128)(2,1)S(1)}, bf16[192,768]{1,0:T(8,128)(2,1)S(1)}, u32[]{:S(2)}, u32[]{:S(2)}) %collective-permute-start.4) | collective-permute-done | bytes 294944 | tf_op jit(solution)/shard_map/ppermute | solution.py:1268
  43.4 1.2 fusion.27
  44.6 1.4 collective-permute-start.7
  46.1 1.5 collective-permute-start.8
  47.9 1.3 copy.75
  49.2 1.8 unpack_small.1
  51.0 5.9 %all-to-all-done.1 = bf16[4,2,128,768]{3,2,1,0:T(8,128)(2,1)} async-done(((bf16[4,2,128,768]{3,2,1,0:T(8,128)(2,1)}), bf16[4,2,128,768]{3,2,1,0:T(8,128)(2,1)}, u32[]{:S(2)}, u32[]{:S(2)}) %all-to-all-start.1) | async-done | bytes 1572896 | tf_op jit(solution)/shard_map/all_to_all | solution.py:1291
  56.9 9.0 %attention_forward.2 = (bf16[2,4,192,128]{3,2,1,0:T(8,128)(2,1)}, bf16[3,1024,128]{2,1,0:T(8,128)(2,1)}, bf16[3,1024,128]{2,1,0:T(8,128)(2,1)}, bf16[3,1024,128]...) custom-call(bf16[1024,768]{1,0:T(8,128)(2,1)} %bitcast.36.refs_0_.x_, ...), custom_call_target="tpu_custom_call" | custom-call | flops 2550136832 | bytes 12582912 | tf_op jit(solution)/shard_map/attention_forward/pallas_call | solution.py:832
  66.7 1.8 collective-permute-start.10
  68.6 2.6 %collective-permute-start.11 = (bf16[2,2,24,768]{3,2,0,1:T(8,128)(2,1)}, bf16[2,2,24,768]{3,2,0,1:T(8,128)(2,1)}, u32[]{:S(2)}, u32[]{:S(2)}) collective-permute-start(bf16[2,2,24,768]{3,2,0,1:T(8,128)(2,1)} %get-tuple-element.280), channel_id=1, source_target_pairs={{0,4},{1,5},{2,6},{3,7},{4,0},{5,1},{6,2},{7,3},{8,12},{9,13},{10,... | collective-permute-start | bytes 442376 | tf_op jit(solution)/shard_map/ppermute | solution.py:1268
  71.1 1.6 select_bitcast_fusion.2
  72.7 1.1 pad_maximum_fusion.4.outer_one
  73.9 1.5 collective-permute-start.17
  76.5 1.5 collective-permute-start.16
  78.0 13.8 %attention_forward.3 = (bf16[2,4,192,128]{3,2,1,0:T(8,128)(2,1)}, bf16[3,1024,128]{2,1,0:T(8,128)(2,1)}, bf16[3,1024,128]{2,1,0:T(8,128)(2,1)}, bf16[3,1024,128]...) custom-call(bf16[1024,768]{1,0:T(8,128)(2,1)} %bitcast.36.refs_0_.x_, ...), custom_call_target="tpu_custom_call", output_to_operand_aliasing={{0}: (5, {}), {1}: (6, {}), {2}: (7, {}), {3}: (8, {}), {4}... | custom-call | flops 5100273664 | bytes 12582912 | tf_op jit(solution)/shard_map/attention_forward/pallas_call | solution.py:832
  91.9 5.0 %all-to-all-start.2 = ((bf16[8,192,128]{2,1,0:T(8,128)(2,1)}), bf16[8,192,128]{2,1,0:T(8,128)(2,1)}, u32[]{:S(2)}, u32[]{:S(2)}) async-start(bf16[8,192,128]{2,1,0:T(8,128)(2,1)} %bitcast.249), calls=%async_computation.2 | async-start | bytes 786432 | tf_op jit(solution)/shard_map/all_to_all | solution.py:1440
  98.9 3.5 %collective-permute-done.13.third_two = bf16[4,2,2,24,768]{4,3,2,1,0:T(8,128)(2,1)} collective-permute-done((bf16[4,2,2,24,768]{4,3,2,1,0:T(8,128)(2,1)S(1)}, bf16[4,2,2,24,768]{4,3,2,1,0:T(8,128)(2,1)}, u32[]{:S(2)}, u32[]{:S(2)}) %collective-permute-start.13) | collective-permute-done | bytes 589856 | tf_op jit(solution)/shard_map/ppermute | solution.py:1268
  102.4 4.4 %all-to-all-done.2 = bf16[8,192,128]{2,1,0:T(8,128)(2,1)} async-done(((bf16[8,192,128]{2,1,0:T(8,128)(2,1)}), bf16[8,192,128]{2,1,0:T(8,128)(2,1)}, u32[]{:S(2)}, u32[]{:S(2)}) %all-to-all-start.2) | async-done | bytes 393248 | tf_op jit(solution)/shard_map/all_to_all | solution.py:1440
  110.1 1.7 collective-permute-done.19.outer_four
  111.7 22.1 %token_block.1 = (bf16[256,768]{1,0:T(8,128)(2,1)}, f32[256,768]{1,0:T(8,128)}, bf16[8,200,128]{2,1,0:T(8,128)(2,1)}, bf16[2,4,8,24,768]{4,3,2,1,0:T(8,128)(2,1)...) custom-call(s32[3]{0:T(128)} %pad_add_fusion.core_ref, ...), custom_call_target="tpu_custom_call" | custom-call | flops 8455716864 | bytes 31457280 | tf_op jit(solution)/shard_map/token_block/pallas_call | solution.py:1242
  134.1 2.9 %collective-permute-done.20 = bf16[2,8,48,768]{3,2,1,0:T(8,128)(2,1)S(1)} collective-permute-done((bf16[2,8,48,768]{3,2,1,0:T(8,128)(2,1)}, bf16[2,8,48,768]{3,2,1,0:T(8,128)(2,1)S(1)}, u32[]{:S(2)}, u32[]{:S(2)}) %collective-permute-start.20) | collective-permute-done | bytes 1179680 | tf_op jit(solution)/shard_map/ppermute | solution.py:1268
  137.5 4.4 %all-to-all-start.3 = ((bf16[8,200,128]{2,1,0:T(8,128)(2,1)}), bf16[8,200,128]{2,1,0:T(8,128)(2,1)}, u32[]{:S(2)}, u32[]{:S(2)}) async-start(bf16[8,200,128]{2,1,0:T(8,128)(2,1)} %get-tuple-element.176), calls=%async_computation.3 | async-start | bytes 819200 | tf_op jit(solution)/shard_map/all_to_all | solution.py:1470
  142.6 2.3 fusion.14
  144.9 1.6 collective-permute-start.25
  146.5 2.4 collective-permute-start.26
  149.3 1.4 fusion
  152.0 1.4 fusion.4
  153.4 2.0 collective-permute-start.24
  155.4 24.9 %attention_backward.1 = (bf16[1024,768]{1,0:T(8,128)(2,1)}, bf16[2,2,8,80,256]{4,3,2,1,0:T(8,128)(2,1)}, f32[3,8,128]{2,1,0:T(8,128)}) custom-call(s32[1]{0:T(128)} %bitcast.core_ref, bf16[2,4,200,128]{3,2,1,0:T(8,128)(2,1)} %bitcast.74.do_ref, bf16[1024,768]{1,0:T(8,128)(2,1)} %bitcast.36.refs_0_.x_ref, bf16[3,768,256]{2,1,0:T(8,128)(2,1)} %get-tuple-element.188.w_ref, ...), custom_call_target="tpu_custom_call" | custom-call | flops 13690208256 | bytes 15728640 | tf_op jit(solution)/shard_map/attention_backward/pallas_call | solution.py:866
  180.4 1.8 small_gradients.1.keep_ref
  182.1 2.0 slice_bitcast_fusion
  184.2 3.6 %all-to-all-start.4 = ((bf16[4,2,128,768]{3,2,1,0:T(8,128)(2,1)}), bf16[4,2,128,768]{3,2,1,0:T(8,128)(2,1)S(1)}, u32[]{:S(2)}, u32[]{:S(2)}) async-start(bf16[4,2,128,768]{3,2,1,0:T(8,128)(2,1)} %bitcast.248), calls=%async_computation.4 | async-start | bytes 3145728 | tf_op jit(solution)/shard_map/all_to_all | solution.py:1291
  187.8 1.5 fusion.3
  189.3 2.6 %fusion.7 = (bf16[2,72,768]{2,1,0:T(8,128)(2,1)S(1)}, bf16[2,72,768]{2,1,0:T(8,128)(2,1)}, bf16[2,72,768]{2,1,0:T(8,128)(2,1)}) fusion(s32[]{:T(128)S(6)} %select_n.356, bf16[2,4,2,72,768]{4,3,2,1,0:T(8,128)(2,1)} %bitcast.72, s32[]{:T(128)S(6)} %select_n.365, s32[]{:T(128)S(6)} %select_n.363, bf16[2,4,2,72,768]{4,3,2,1,0:T(8,128)(2,1)} %bitcast.244, ...), kind=kLoop, calls=%fused_computation.41 | loop fusion | flops 1990656 | bytes 2654236 | tf_op jit(solution)/shard_map/convert_element_type | solution.py:1303
  191.9 2.3 row_sum.2
  196.7 2.0 collective-permute-start.34
  198.7 1.5 collective-permute-start.31
  200.2 1.5 collective-permute-start.32
  201.7 1.4 collective-permute-start.33
  203.1 10.0 %all-to-all-done.4 = bf16[4,2,128,768]{3,2,1,0:T(8,128)(2,1)S(1)} async-done(((bf16[4,2,128,768]{3,2,1,0:T(8,128)(2,1)}), bf16[4,2,128,768]{3,2,1,0:T(8,128)(2,1)S(1)}, u32[]{:S(2)}, u32[]{:S(2)}) %all-to-all-start.4) | async-done | bytes 1572896 | tf_op jit(solution)/shard_map/all_to_all | solution.py:1291
  214.6 2.4 row_sum.3
  217.1 4.4 %all-to-all-start.5 = ((bf16[8,80,256]{2,1,0:T(8,128)(2,1)}), bf16[8,80,256]{2,1,0:T(8,128)(2,1)S(1)}, u32[]{:S(2)}, u32[]{:S(2)}) async-start(bf16[8,80,256]{2,1,0:T(8,128)(2,1)} %row_sum.3), calls=%async_computation.5 | async-start | bytes 655360 | tf_op jit(solution)/shard_map/all_to_all | solution.py:1533
  221.4 1.3 fusion.15
  223.8 1.7 fusion.2
  226.4 2.0 collective-permute-start.36
  228.4 2.4 collective-permute-start.37
  230.9 1.3 fusion.18
  234.4 2.7 %collective-permute-done.35 = bf16[72,768]{1,0:T(8,128)(2,1)S(1)} collective-permute-done((bf16[72,768]{1,0:T(8,128)(2,1)S(1)}, bf16[72,768]{1,0:T(8,128)(2,1)S(1)}, u32[]{:S(2)}, u32[]{:S(2)}) %collective-permute-start.35) | collective-permute-done | bytes 110624 | tf_op jit(solution)/shard_map/ppermute | solution.py:1268
  237.0 2.0 collective-permute-start.40
  239.0 1.3 fusion.19
  243.2 2.5 all-to-all-done.5.block_ref
  246.4 1.8 finish_columns.1
  (149 shorter events, 33.0 us)
Async XLA Ops:
  0.7 13.3 %copy-start.12 = (s32[2]{0:T(128)S(1)}, s32[2]{0:T(128)}, u32[]{:S(2)}) copy-start(s32[2]{0:T(128)} %param.25) | copy-start | bytes 28
  1.6 15.4 %collective-permute-start = (bf16[128,768]{1,0:T(8,128)(2,1)S(1)}, bf16[128,768]{1,0:T(8,128)(2,1)S(1)}, u32[]{:S(2)}, u32[]{:S(2)}) collective-permute-start(bf16[128,768]{1,0:T(8,128)(2,1)S(1)} %dynamic-slice_bitcast_fusion), channel_id=1, source_target_pairs={{0,4},{1,5},{2,6},{3,7},{4,0},{5,1},{6,2},{7,3},{8,12},{9,13},{10,... | collective-permute-start | bytes 589832 | tf_op jit(solution)/shard_map/ppermute | solution.py:1268
  9.1 14.6 %all-to-all-start = ((bf16[8,80,256]{2,1,0:T(8,128)(2,1)}), bf16[8,80,256]{2,1,0:T(8,128)(2,1)S(1)}, u32[]{:S(2)}, u32[]{:S(2)}) async-start(bf16[8,80,256]{2,1,0:T(8,128)(2,1)} %get-tuple-element.134), calls=%async_computation | async-start | bytes 655360 | tf_op jit(solution)/shard_map/all_to_all | solution.py:1380
  15.0 2.1 copy-start.9
  16.3 1.0 copy-start.10
  16.3 5.6 %copy-start.11 = (bf16[24,768]{1,0:T(8,128)(2,1)S(1)}, bf16[24,768]{1,0:T(8,128)(2,1)}, u32[]{:S(2)}) copy-start(bf16[24,768]{1,0:T(8,128)(2,1)} %get-tuple-element.139) | copy-start | bytes 110596
  17.3 17.0 %collective-permute-start.3 = (bf16[192,768]{1,0:T(8,128)(2,1)S(1)}, bf16[192,768]{1,0:T(8,128)(2,1)S(1)}, u32[]{:S(2)}, u32[]{:S(2)}) collective-permute-start(bf16[192,768]{1,0:T(8,128)(2,1)S(1)} %copy-done.10), channel_id=1, source_target_pairs={{0,2},{1,3},{2,0},{3,1},{4,6},{5,7},{6,4},{7,5},{8,10},{9,11},{10,... | collective-permute-start | bytes 884744 | tf_op jit(solution)/shard_map/ppermute | solution.py:1268
  19.3 23.5 %collective-permute-start.4 = (bf16[192,768]{1,0:T(8,128)(2,1)S(1)}, bf16[192,768]{1,0:T(8,128)(2,1)S(1)}, u32[]{:S(2)}, u32[]{:S(2)}) collective-permute-start(bf16[192,768]{1,0:T(8,128)(2,1)S(1)} %copy-done.10), channel_id=1, source_target_pairs={{0,4},{1,5},{2,6},{3,7},{4,0},{5,1},{6,2},{7,3},{8,12},{9,13},{10,... | collective-permute-start | bytes 884744 | tf_op jit(solution)/shard_map/ppermute | solution.py:1268
  21.9 20.9 %collective-permute-start.5 = (bf16[192,768]{1,0:T(8,128)(2,1)S(1)}, bf16[192,768]{1,0:T(8,128)(2,1)S(1)}, u32[]{:S(2)}, u32[]{:S(2)}) collective-permute-start(bf16[192,768]{1,0:T(8,128)(2,1)S(1)} %copy-done.10), channel_id=1, source_target_pairs={{0,6},{1,7},{2,4},{3,5},{4,2},{5,3},{6,0},{7,1},{8,14},{9,15},{10,... | collective-permute-start | bytes 884744 | tf_op jit(solution)/shard_map/ppermute | solution.py:1268
  21.9 10.2 %collective-permute-start.6 = (bf16[24,768]{1,0:T(8,128)(2,1)S(1)}, bf16[24,768]{1,0:T(8,128)(2,1)S(1)}, u32[]{:S(2)}, u32[]{:S(2)}) collective-permute-start(bf16[24,768]{1,0:T(8,128)(2,1)S(1)} %copy-done.11), channel_id=1, source_target_pairs={{0,16},{8,24},{16,0},{24,8},{1,17},{9,25},{17,1},{25,9},{2,18},{10... | collective-permute-start | bytes 110600 | tf_op jit(solution)/shard_map/ppermute | solution.py:1268
  23.7 8.2 %collective-permute-start.1 = (bf16[1,8,80,256]{3,2,1,0:T(8,128)(2,1)S(1)}, bf16[1,8,80,256]{3,2,1,0:T(8,128)(2,1)S(1)}, u32[]{:S(2)}, u32[]{:S(2)}) collective-permute-start(bf16[1,8,80,256]{3,2,1,0:T(8,128)(2,1)S(1)} %bitcast.250), channel_id=1, source_target_pairs={{0,16},{8,24},{16,0},{24,8},{1,17},{9,25},{17,1},{25,9},{2,18},{10... | collective-permute-start | bytes 983048 | tf_op jit(solution)/shard_map/ppermute | solution.py:1268
  26.4 30.5 %all-to-all-start.1 = ((bf16[4,2,128,768]{3,2,1,0:T(8,128)(2,1)}), bf16[4,2,128,768]{3,2,1,0:T(8,128)(2,1)}, u32[]{:S(2)}, u32[]{:S(2)}) async-start(bf16[4,2,128,768]{3,2,1,0:T(8,128)(2,1)} %broadcast_in_dim.77), calls=%async_computation.1 | async-start | bytes 3145728 | tf_op jit(solution)/shard_map/all_to_all | solution.py:1291
  32.1 33.9 %collective-permute-start.9 = (bf16[2,24,768]{2,1,0:T(8,128)(2,1)S(1)}, bf16[2,24,768]{2,1,0:T(8,128)(2,1)S(1)}, u32[]{:S(2)}, u32[]{:S(2)}) collective-permute-start(bf16[2,24,768]{2,1,0:T(8,128)(2,1)S(1)} %pad_maximum_fusion.11), channel_id=1, source_target_pairs={{0,1},{1,0},{2,3},{3,2},{4,5},{5,4},{6,7},{7,6},{8,9},{9,8},{10,11... | collective-permute-start | bytes 221192 | tf_op jit(solution)/shard_map/ppermute | solution.py:1268
  42.8 4.8 %collective-permute-start.2 = (bf16[2,1,8,80,256]{4,3,2,0,1:T(8,128)(2,1)S(1)}, bf16[2,1,8,80,256]{4,3,2,0,1:T(8,128)(2,1)S(1)}, u32[]{:S(2)}, u32[]{:S(2)}) collective-permute-start(bf16[2,1,8,80,256]{4,3,2,0,1:T(8,128)(2,1)S(1)} %pad_maximum_fusion.5), channel_id=1, source_target_pairs={{0,8},{8,0},{16,24},{24,16},{1,9},{9,1},{17,25},{25,17},{2,10},{10... | collective-permute-start | bytes 1966088 | tf_op jit(solution)/shard_map/ppermute | solution.py:1268
  43.4 4.3 %copy-start = (bf16[2,2,192,768]{3,2,1,0:T(8,128)(2,1)}, bf16[2,2,192,768]{3,2,1,0:T(8,128)(2,1)S(1)}, u32[]{:S(2)}) copy-start(bf16[2,2,192,768]{3,2,1,0:T(8,128)(2,1)S(1)} %reverse_select_fusion) | copy-start | bytes 3538948
  44.6 21.4 %collective-permute-start.7 = (bf16[4,96,768]{2,1,0:T(8,128)(2,1)}, bf16[4,96,768]{2,1,0:T(8,128)(2,1)S(1)}, u32[]{:S(2)}, u32[]{:S(2)}) collective-permute-start(bf16[4,96,768]{2,1,0:T(8,128)(2,1)} %get-tuple-element.259), channel_id=1, source_target_pairs={{0,1},{1,0},{2,3},{3,2},{4,5},{5,4},{6,7},{7,6},{8,9},{9,8},{10,11... | collective-permute-start | bytes 1769480 | tf_op jit(solution)/shard_map/ppermute | solution.py:1268
  46.1 19.9 %collective-permute-start.8 = (bf16[4,96,768]{2,1,0:T(8,128)(2,1)}, bf16[4,96,768]{2,1,0:T(8,128)(2,1)}, u32[]{:S(2)}, u32[]{:S(2)}) collective-permute-start(bf16[4,96,768]{2,1,0:T(8,128)(2,1)} %get-tuple-element.258), channel_id=1, source_target_pairs={{0,16},{8,24},{16,0},{24,8},{1,17},{9,25},{17,1},{25,9},{2,18},{10... | collective-permute-start | bytes 1769480 | tf_op jit(solution)/shard_map/ppermute | solution.py:1268
  66.7 25.1 %collective-permute-start.10 = (bf16[2,2,24,768]{3,2,0,1:T(8,128)(2,1)}, bf16[2,2,24,768]{3,2,0,1:T(8,128)(2,1)S(1)}, u32[]{:S(2)}, u32[]{:S(2)}) collective-permute-start(bf16[2,2,24,768]{3,2,0,1:T(8,128)(2,1)} %get-tuple-element.280), channel_id=1, source_target_pairs={{0,2},{1,3},{2,0},{3,1},{4,6},{5,7},{6,4},{7,5},{8,10},{9,11},{10,... | collective-permute-start | bytes 442376 | tf_op jit(solution)/shard_map/ppermute | solution.py:1268
  68.6 23.3 %collective-permute-start.11 = (bf16[2,2,24,768]{3,2,0,1:T(8,128)(2,1)}, bf16[2,2,24,768]{3,2,0,1:T(8,128)(2,1)}, u32[]{:S(2)}, u32[]{:S(2)}) collective-permute-start(bf16[2,2,24,768]{3,2,0,1:T(8,128)(2,1)} %get-tuple-element.280), channel_id=1, source_target_pairs={{0,4},{1,5},{2,6},{3,7},{4,0},{5,1},{6,2},{7,3},{8,12},{9,13},{10,... | collective-permute-start | bytes 442376 | tf_op jit(solution)/shard_map/ppermute | solution.py:1268
  71.1 20.7 %collective-permute-start.12 = (bf16[2,2,24,768]{3,2,0,1:T(8,128)(2,1)}, bf16[2,2,24,768]{3,2,0,1:T(8,128)(2,1)}, u32[]{:S(2)}, u32[]{:S(2)}) collective-permute-start(bf16[2,2,24,768]{3,2,0,1:T(8,128)(2,1)} %get-tuple-element.280), channel_id=1, source_target_pairs={{0,6},{1,7},{2,4},{3,5},{4,2},{5,3},{6,0},{7,1},{8,14},{9,15},{10,... | collective-permute-start | bytes 442376 | tf_op jit(solution)/shard_map/ppermute | solution.py:1268
  73.9 32.9 %collective-permute-start.17 = (bf16[2,4,96,768]{3,2,1,0:T(8,128)(2,1)}, bf16[2,4,96,768]{3,2,1,0:T(8,128)(2,1)}, u32[]{:S(2)}, u32[]{:S(2)}) collective-permute-start(bf16[2,4,96,768]{3,2,1,0:T(8,128)(2,1)} %pad_maximum_fusion.4.outer_one), channel_id=1, source_target_pairs={{0,1},{1,0},{2,3},{3,2},{4,5},{5,4},{6,7},{7,6},{8,9},{9,8},{10,11... | collective-permute-start | bytes 3538952 | tf_op jit(solution)/shard_map/ppermute | solution.py:1268
  76.5 30.3 %collective-permute-start.16 = (bf16[2,4,96,768]{3,2,1,0:T(8,128)(2,1)}, bf16[2,4,96,768]{3,2,1,0:T(8,128)(2,1)}, u32[]{:S(2)}, u32[]{:S(2)}) collective-permute-start(bf16[2,4,96,768]{3,2,1,0:T(8,128)(2,1)} %pad_maximum_fusion.3.inner_one), channel_id=1, source_target_pairs={{0,16},{8,24},{16,0},{24,8},{1,17},{9,25},{17,1},{25,9},{2,18},{10... | collective-permute-start | bytes 3538952 | tf_op jit(solution)/shard_map/ppermute | solution.py:1268
  91.9 14.9 %all-to-all-start.2 = ((bf16[8,192,128]{2,1,0:T(8,128)(2,1)}), bf16[8,192,128]{2,1,0:T(8,128)(2,1)}, u32[]{:S(2)}, u32[]{:S(2)}) async-start(bf16[8,192,128]{2,1,0:T(8,128)(2,1)} %bitcast.249), calls=%async_computation.2 | async-start | bytes 786432 | tf_op jit(solution)/shard_map/all_to_all | solution.py:1440
  96.9 9.9 %collective-permute-start.14 = (bf16[2,4,96,768]{3,2,1,0:T(8,128)(2,1)}, bf16[2,4,96,768]{3,2,1,0:T(8,128)(2,1)S(1)}, u32[]{:S(2)}, u32[]{:S(2)}) collective-permute-start(bf16[2,4,96,768]{3,2,1,0:T(8,128)(2,1)} %pad_maximum_fusion.3.inner_one), channel_id=1, source_target_pairs={{0,8},{8,0},{16,24},{24,16},{1,9},{9,1},{17,25},{25,17},{2,10},{10... | collective-permute-start | bytes 3538952 | tf_op jit(solution)/shard_map/ppermute | solution.py:1268
  96.9 9.9 %collective-permute-start.15 = (bf16[2,4,96,768]{3,2,1,0:T(8,128)(2,1)}, bf16[2,4,96,768]{3,2,1,0:T(8,128)(2,1)S(1)}, u32[]{:S(2)}, u32[]{:S(2)}) collective-permute-start(bf16[2,4,96,768]{3,2,1,0:T(8,128)(2,1)} %pad_maximum_fusion.4.outer_one), channel_id=1, source_target_pairs={{0,8},{8,0},{16,24},{24,16},{1,9},{9,1},{17,25},{25,17},{2,10},{10... | collective-permute-start | bytes 3538952 | tf_op jit(solution)/shard_map/ppermute | solution.py:1268
  98.7 13.0 %copy-start.8 = (bf16[2,2,2,2,24,768]{5,4,3,2,1,0:T(8,128)(2,1)}, bf16[2,2,2,2,24,768]{5,4,3,2,1,0:T(8,128)(2,1)S(1)}, u32[]{:S(2)}) copy-start(bf16[2,2,2,2,24,768]{5,4,3,2,1,0:T(8,128)(2,1)S(1)} %reverse_select_fusion.2) | copy-start | bytes 1769476
  98.7 3.7 %collective-permute-start.13 = (bf16[4,2,2,24,768]{4,3,2,1,0:T(8,128)(2,1)S(1)}, bf16[4,2,2,24,768]{4,3,2,1,0:T(8,128)(2,1)}, u32[]{:S(2)}, u32[]{:S(2)}) collective-permute-start(bf16[4,2,2,24,768]{4,3,2,1,0:T(8,128)(2,1)S(1)} %bitcast.260), channel_id=1, source_target_pairs={{0,8},{8,0},{16,24},{24,16},{1,9},{9,1},{17,25},{25,17},{2,10},{10... | collective-permute-start | bytes 1769480 | tf_op jit(solution)/shard_map/ppermute | solution.py:1268
  106.8 1.0 copy-start.13
  106.8 1.9 copy-start.14
  106.8 3.3 %collective-permute-start.18 = (bf16[2,4,96,768]{3,2,1,0:T(8,128)(2,1)}, bf16[2,4,96,768]{3,2,1,0:T(8,128)(2,1)}, u32[]{:S(2)}, u32[]{:S(2)}) collective-permute-start(bf16[2,4,96,768]{3,2,1,0:T(8,128)(2,1)} %collective-permute-done.16.inner_three), channel_id=1, source_target_pairs={{0,8},{8,0},{16,24},{24,16},{1,9},{9,1},{17,25},{25,17},{2,10},{10... | collective-permute-start | bytes 3538952 | tf_op jit(solution)/shard_map/ppermute | solution.py:1268
  106.9 4.9 %collective-permute-start.19 = (bf16[2,4,96,768]{3,2,1,0:T(8,128)(2,1)}, bf16[2,4,96,768]{3,2,1,0:T(8,128)(2,1)}, u32[]{:S(2)}, u32[]{:S(2)}) collective-permute-start(bf16[2,4,96,768]{3,2,1,0:T(8,128)(2,1)} %collective-permute-done.17.outer_three), channel_id=1, source_target_pairs={{0,8},{8,0},{16,24},{24,16},{1,9},{9,1},{17,25},{25,17},{2,10},{10... | collective-permute-start | bytes 3538952 | tf_op jit(solution)/shard_map/ppermute | solution.py:1268
  133.9 3.1 %collective-permute-start.20 = (bf16[2,8,48,768]{3,2,1,0:T(8,128)(2,1)}, bf16[2,8,48,768]{3,2,1,0:T(8,128)(2,1)S(1)}, u32[]{:S(2)}, u32[]{:S(2)}) collective-permute-start(bf16[2,8,48,768]{3,2,1,0:T(8,128)(2,1)} %get-tuple-element.180), channel_id=1, source_target_pairs={{0,8},{8,0},{16,24},{24,16},{1,9},{9,1},{17,25},{25,17},{2,10},{10... | collective-permute-start | bytes 3538952 | tf_op jit(solution)/shard_map/ppermute | solution.py:1268
  137.0 7.9 %copy-start.6 = (bf16[2,8,48,768]{3,2,1,0:T(8,128)(2,1)}, bf16[2,8,48,768]{3,2,1,0:T(8,128)(2,1)S(1)}, u32[]{:S(2)}) copy-start(bf16[2,8,48,768]{3,2,1,0:T(8,128)(2,1)S(1)} %collective-permute-done.20) | copy-start | bytes 3538948
  137.0 12.3 %collective-permute-start.21 = (bf16[2,4,8,24,768]{4,3,2,1,0:T(8,128)(2,1)}, bf16[2,4,8,24,768]{4,3,2,1,0:T(8,128)(2,1)S(1)}, u32[]{:S(2)}, u32[]{:S(2)}) collective-permute-start(bf16[2,4,8,24,768]{4,3,2,1,0:T(8,128)(2,1)} %get-tuple-element.181), channel_id=1, source_target_pairs={{0,8},{8,0},{16,24},{24,16},{1,9},{9,1},{17,25},{25,17},{2,10},{10... | collective-permute-start | bytes 7077896 | tf_op jit(solution)/shard_map/ppermute | solution.py:1268
  137.2 14.9 %collective-permute-start.22 = (bf16[2,8,72,768]{3,2,1,0:T(8,128)(2,1)}, bf16[2,8,72,768]{3,2,1,0:T(8,128)(2,1)}, u32[]{:S(2)}, u32[]{:S(2)}) collective-permute-start(bf16[2,8,72,768]{3,2,1,0:T(8,128)(2,1)} %get-tuple-element.185), channel_id=1, source_target_pairs={{0,8},{8,0},{16,24},{24,16},{1,9},{9,1},{17,25},{25,17},{2,10},{10... | collective-permute-start | bytes 5308424 | tf_op jit(solution)/shard_map/ppermute | solution.py:1268
  137.5 17.9 %all-to-all-start.3 = ((bf16[8,200,128]{2,1,0:T(8,128)(2,1)}), bf16[8,200,128]{2,1,0:T(8,128)(2,1)}, u32[]{:S(2)}, u32[]{:S(2)}) async-start(bf16[8,200,128]{2,1,0:T(8,128)(2,1)} %get-tuple-element.176), calls=%async_computation.3 | async-start | bytes 819200 | tf_op jit(solution)/shard_map/all_to_all | solution.py:1470
  142.6 6.7 %copy-start.1 = (bf16[2,4,8,24,768]{4,3,2,1,0:T(8,128)(2,1)S(1)}, bf16[2,4,8,24,768]{4,3,2,1,0:T(8,128)(2,1)}, u32[]{:S(2)}) copy-start(bf16[2,4,8,24,768]{4,3,2,1,0:T(8,128)(2,1)} %get-tuple-element.177) | copy-start | bytes 7077892
  144.9 35.4 %collective-permute-start.25 = (bf16[2,2,48,768]{3,2,1,0:T(8,128)(2,1)}, bf16[2,2,48,768]{3,2,1,0:T(8,128)(2,1)}, u32[]{:S(2)}, u32[]{:S(2)}) collective-permute-start(bf16[2,2,48,768]{3,2,1,0:T(8,128)(2,1)} %get-tuple-element.251), channel_id=1, source_target_pairs={{0,2},{1,3},{2,0},{3,1},{4,6},{5,7},{6,4},{7,5},{8,10},{9,11},{10,... | collective-permute-start | bytes 884744 | tf_op jit(solution)/shard_map/ppermute | solution.py:1268
  146.5 33.9 %collective-permute-start.26 = (bf16[2,2,48,768]{3,2,1,0:T(8,128)(2,1)}, bf16[2,2,48,768]{3,2,1,0:T(8,128)(2,1)}, u32[]{:S(2)}, u32[]{:S(2)}) collective-permute-start(bf16[2,2,48,768]{3,2,1,0:T(8,128)(2,1)} %get-tuple-element.250), channel_id=1, source_target_pairs={{0,4},{1,5},{2,6},{3,7},{4,0},{5,1},{6,2},{7,3},{8,12},{9,13},{10,... | collective-permute-start | bytes 884744 | tf_op jit(solution)/shard_map/ppermute | solution.py:1268
  148.8 31.5 %collective-permute-start.27 = (bf16[2,2,48,768]{3,2,1,0:T(8,128)(2,1)}, bf16[2,2,48,768]{3,2,1,0:T(8,128)(2,1)}, u32[]{:S(2)}, u32[]{:S(2)}) collective-permute-start(bf16[2,2,48,768]{3,2,1,0:T(8,128)(2,1)} %get-tuple-element.249), channel_id=1, source_target_pairs={{0,6},{1,7},{2,4},{3,5},{4,2},{5,3},{6,0},{7,1},{8,14},{9,15},{10,... | collective-permute-start | bytes 884744 | tf_op jit(solution)/shard_map/ppermute | solution.py:1268
  149.3 1.8 copy-start.3
  149.3 2.8 %copy-start.4 = (bf16[2,8,72,768]{3,2,1,0:T(8,128)(2,1)S(1)}, bf16[2,8,72,768]{3,2,1,0:T(8,128)(2,1)}, u32[]{:S(2)}) copy-start(bf16[2,8,72,768]{3,2,1,0:T(8,128)(2,1)} %get-tuple-element.184) | copy-start | bytes 5308420
  151.1 29.3 %collective-permute-start.23 = (bf16[4,4,2,24,768]{4,3,0,1,2:T(8,128)(2,1)}, bf16[4,4,2,24,768]{4,3,0,1,2:T(8,128)(2,1)}, u32[]{:S(2)}, u32[]{:S(2)}) collective-permute-start(bf16[4,4,2,24,768]{4,3,0,1,2:T(8,128)(2,1)} %fusion), channel_id=1, source_target_pairs={{0,16},{8,24},{16,0},{24,8},{1,17},{9,25},{17,1},{25,9},{2,18},{10... | collective-permute-start | bytes 3538952 | tf_op jit(solution)/shard_map/ppermute | solution.py:1268
  153.4 26.9 %collective-permute-start.24 = (bf16[2,4,72,768]{3,2,1,0:T(8,128)(2,1)S(1)}, bf16[2,4,72,768]{3,2,1,0:T(8,128)(2,1)}, u32[]{:S(2)}, u32[]{:S(2)}) collective-permute-start(bf16[2,4,72,768]{3,2,1,0:T(8,128)(2,1)S(1)} %fusion.4), channel_id=1, source_target_pairs={{0,1},{1,0},{2,3},{3,2},{4,5},{5,4},{6,7},{7,6},{8,9},{9,8},{10,11... | collective-permute-start | bytes 2654216 | tf_op jit(solution)/shard_map/ppermute | solution.py:1268
  180.4 3.8 %copy-start.2 = (bf16[2,4,8,24,768]{4,3,2,1,0:T(8,128)(2,1)S(1)}, bf16[2,4,8,24,768]{4,3,2,1,0:T(8,128)(2,1)}, u32[]{:S(2)}) copy-start(bf16[2,4,8,24,768]{4,3,2,1,0:T(8,128)(2,1)} %get-tuple-element.177) | copy-start | bytes 7077892
  184.2 7.8 %collective-permute-start.29 = (bf16[2,8,80,256]{3,2,1,0:T(8,128)(2,1)}, bf16[2,8,80,256]{3,2,1,0:T(8,128)(2,1)}, u32[]{:S(2)}, u32[]{:S(2)}) collective-permute-start(bf16[2,8,80,256]{3,2,1,0:T(8,128)(2,1)} %slice_bitcast_fusion), channel_id=1, source_target_pairs={{0,8},{8,0},{16,24},{24,16},{1,9},{9,1},{17,25},{25,17},{2,10},{10... | collective-permute-start | bytes 1966088 | tf_op jit(solution)/shard_map/ppermute | solution.py:1268
  184.2 28.9 %all-to-all-start.4 = ((bf16[4,2,128,768]{3,2,1,0:T(8,128)(2,1)}), bf16[4,2,128,768]{3,2,1,0:T(8,128)(2,1)S(1)}, u32[]{:S(2)}, u32[]{:S(2)}) async-start(bf16[4,2,128,768]{3,2,1,0:T(8,128)(2,1)} %bitcast.248), calls=%async_computation.4 | async-start | bytes 3145728 | tf_op jit(solution)/shard_map/all_to_all | solution.py:1291
  194.2 19.7 %collective-permute-start.30 = (bf16[8,80,256]{2,1,0:T(8,128)(2,1)}, bf16[8,80,256]{2,1,0:T(8,128)(2,1)S(1)}, u32[]{:S(2)}, u32[]{:S(2)}) collective-permute-start(bf16[8,80,256]{2,1,0:T(8,128)(2,1)} %row_sum.2), channel_id=1, source_target_pairs={{0,16},{8,24},{16,0},{24,8},{1,17},{9,25},{17,1},{25,9},{2,18},{10... | collective-permute-start | bytes 983048 | tf_op jit(solution)/shard_map/ppermute | solution.py:1268
  196.7 26.0 %collective-permute-start.34 = (bf16[4,4,24,768]{3,2,0,1:T(8,128)(2,1)S(1)}, bf16[4,4,24,768]{3,2,0,1:T(8,128)(2,1)}, u32[]{:S(2)}, u32[]{:S(2)}) collective-permute-start(bf16[4,4,24,768]{3,2,0,1:T(8,128)(2,1)S(1)} %fusion.3), channel_id=1, source_target_pairs={{0,1},{1,0},{2,3},{3,2},{4,5},{5,4},{6,7},{7,6},{8,9},{9,8},{10,11... | collective-permute-start | bytes 1769480 | tf_op jit(solution)/shard_map/ppermute | solution.py:1268
  198.7 27.7 %collective-permute-start.31 = (bf16[2,72,768]{2,1,0:T(8,128)(2,1)}, bf16[2,72,768]{2,1,0:T(8,128)(2,1)}, u32[]{:S(2)}, u32[]{:S(2)}) collective-permute-start(bf16[2,72,768]{2,1,0:T(8,128)(2,1)} %get-tuple-element.246), channel_id=1, source_target_pairs={{0,2},{1,3},{2,0},{3,1},{4,6},{5,7},{6,4},{7,5},{8,10},{9,11},{10,... | collective-permute-start | bytes 663560 | tf_op jit(solution)/shard_map/ppermute | solution.py:1268
  200.2 28.2 %collective-permute-start.32 = (bf16[2,72,768]{2,1,0:T(8,128)(2,1)}, bf16[2,72,768]{2,1,0:T(8,128)(2,1)}, u32[]{:S(2)}, u32[]{:S(2)}) collective-permute-start(bf16[2,72,768]{2,1,0:T(8,128)(2,1)} %get-tuple-element.245), channel_id=1, source_target_pairs={{0,4},{1,5},{2,6},{3,7},{4,0},{5,1},{6,2},{7,3},{8,12},{9,13},{10,... | collective-permute-start | bytes 663560 | tf_op jit(solution)/shard_map/ppermute | solution.py:1268
  201.7 29.1 %collective-permute-start.33 = (bf16[2,72,768]{2,1,0:T(8,128)(2,1)S(1)}, bf16[2,72,768]{2,1,0:T(8,128)(2,1)}, u32[]{:S(2)}, u32[]{:S(2)}) collective-permute-start(bf16[2,72,768]{2,1,0:T(8,128)(2,1)S(1)} %get-tuple-element.244), channel_id=1, source_target_pairs={{0,6},{1,7},{2,4},{3,5},{4,2},{5,3},{6,0},{7,1},{8,14},{9,15},{10,... | collective-permute-start | bytes 663560 | tf_op jit(solution)/shard_map/ppermute | solution.py:1268
  213.9 0.7 copy-start.15
  213.9 36.2 %collective-permute-start.28 = (bf16[128,768]{1,0:T(8,128)(2,1)}, bf16[128,768]{1,0:T(8,128)(2,1)}, u32[]{:S(2)}, u32[]{:S(2)}) collective-permute-start(bf16[128,768]{1,0:T(8,128)(2,1)} %dynamic-slice_reduce_fusion), channel_id=1, source_target_pairs={{0,4},{1,5},{2,6},{3,7},{4,0},{5,1},{6,2},{7,3},{8,12},{9,13},{10,... | collective-permute-start | bytes 589832 | tf_op jit(solution)/shard_map/ppermute | solution.py:1268
  217.1 28.7 %all-to-all-start.5 = ((bf16[8,80,256]{2,1,0:T(8,128)(2,1)}), bf16[8,80,256]{2,1,0:T(8,128)(2,1)S(1)}, u32[]{:S(2)}, u32[]{:S(2)}) async-start(bf16[8,80,256]{2,1,0:T(8,128)(2,1)} %row_sum.3), calls=%async_computation.5 | async-start | bytes 655360 | tf_op jit(solution)/shard_map/all_to_all | solution.py:1533
  222.7 9.5 %collective-permute-start.39 = (bf16[2,48,768]{2,1,0:T(8,128)(2,1)S(1)}, bf16[2,48,768]{2,1,0:T(8,128)(2,1)S(1)}, u32[]{:S(2)}, u32[]{:S(2)}) collective-permute-start(bf16[2,48,768]{2,1,0:T(8,128)(2,1)S(1)} %fusion.15), channel_id=1, source_target_pairs={{0,16},{8,24},{16,0},{24,8},{1,17},{9,25},{17,1},{25,9},{2,18},{10... | collective-permute-start | bytes 442376 | tf_op jit(solution)/shard_map/ppermute | solution.py:1268
  226.4 21.9 %collective-permute-start.36 = (bf16[4,24,768]{2,1,0:T(8,128)(2,1)}, bf16[4,24,768]{2,1,0:T(8,128)(2,1)}, u32[]{:S(2)}, u32[]{:S(2)}) collective-permute-start(bf16[4,24,768]{2,1,0:T(8,128)(2,1)} %get-tuple-element.266), channel_id=1, source_target_pairs={{0,2},{1,3},{2,0},{3,1},{4,6},{5,7},{6,4},{7,5},{8,10},{9,11},{10,... | collective-permute-start | bytes 442376 | tf_op jit(solution)/shard_map/ppermute | solution.py:1268
  228.4 20.6 %collective-permute-start.37 = (bf16[4,24,768]{2,1,0:T(8,128)(2,1)}, bf16[4,24,768]{2,1,0:T(8,128)(2,1)}, u32[]{:S(2)}, u32[]{:S(2)}) collective-permute-start(bf16[4,24,768]{2,1,0:T(8,128)(2,1)} %get-tuple-element.265), channel_id=1, source_target_pairs={{0,4},{1,5},{2,6},{3,7},{4,0},{5,1},{6,2},{7,3},{8,12},{9,13},{10,... | collective-permute-start | bytes 442376 | tf_op jit(solution)/shard_map/ppermute | solution.py:1268
  230.8 18.2 %collective-permute-start.38 = (bf16[4,24,768]{2,1,0:T(8,128)(2,1)}, bf16[4,24,768]{2,1,0:T(8,128)(2,1)S(1)}, u32[]{:S(2)}, u32[]{:S(2)}) collective-permute-start(bf16[4,24,768]{2,1,0:T(8,128)(2,1)} %get-tuple-element.264), channel_id=1, source_target_pairs={{0,6},{1,7},{2,4},{3,5},{4,2},{5,3},{6,0},{7,1},{8,14},{9,15},{10,... | collective-permute-start | bytes 442376 | tf_op jit(solution)/shard_map/ppermute | solution.py:1268
  232.2 4.8 %collective-permute-start.35 = (bf16[72,768]{1,0:T(8,128)(2,1)S(1)}, bf16[72,768]{1,0:T(8,128)(2,1)S(1)}, u32[]{:S(2)}, u32[]{:S(2)}) collective-permute-start(bf16[72,768]{1,0:T(8,128)(2,1)S(1)} %fusion.18), channel_id=1, source_target_pairs={{0,16},{8,24},{16,0},{24,8},{1,17},{9,25},{17,1},{25,9},{2,18},{10... | collective-permute-start | bytes 331784 | tf_op jit(solution)/shard_map/ppermute | solution.py:1268
  237.0 4.4 %collective-permute-start.40 = (bf16[48,768]{1,0:T(8,128)(2,1)S(1)}, bf16[48,768]{1,0:T(8,128)(2,1)S(1)}, u32[]{:S(2)}, u32[]{:S(2)}) collective-permute-start(bf16[48,768]{1,0:T(8,128)(2,1)S(1)} %fusion.22), channel_id=1, source_target_pairs={{0,1},{1,0},{2,3},{3,2},{4,5},{5,4},{6,7},{7,6},{8,9},{9,8},{10,11... | collective-permute-start | bytes 221192 | tf_op jit(solution)/shard_map/ppermute | solution.py:1268
  245.7 0.7 copy-start.5
  249.0 2.2 copy-start.7

commit v3 on v2

--- a/solution.py
+++ b/solution.py
@@ -1378,14 +1378,15 @@
     )
     cut = (inner_weight.shape[1] // width) * shard
     block = lax.all_to_all(stacked, CTX, 0, 0, tiled=True)
-    x_pair = in_order(s, own, swap(x_send, CTX, 4), 0)
-    packed, third = after((packed, third), x_pair)
+    x_other = swap(x_send, CTX, 4)
+    packed, third = after((packed, third), x_other)
     third_y = swap(third, DP, 2)
     packed_z = [swap(packed, CTX, 2 * m) for m in (1, 2, 3)]
     lines = block[:, heads * shard + 5 : heads * shard + 5 + seqs, LANES:]
     kind_seq = pick(lines, s, 1).reshape(2, groups, stretch).transpose(1, 0, 2)
     kind_seq = kind_seq.reshape(seq_len).astype(F32)
-    x_pair = jnp.broadcast_to(after(x_pair, block)[None], (groups, 2, stretch, width))
+    x_pair = in_order(s, own, after(x_other, block), 0)
+    x_pair = jnp.broadcast_to(x_pair[None], (groups, 2, stretch, width))
     x_all = exchange(x_pair, False)
     block = block[None]
     block = in_order(bit_y, block, swap(block, DP, 2), 0)

time: 255 us -> 255 us (level)
  no operation moved by 1% of the time
where the time goes in v3:
time: 255 us; the launch traced here: 252 us
  Pallas kernels  82.1 us (32%)
  starting transfers between devices  74.9 us (29%)
  waiting for transfers between devices  44.6 us (17%)
  other arithmetic  35.3 us (14%)
  local copies, waits for them, and re-layouts  14.2 us (6%)
    ppermute x41, starting transfers between devices, swap(): return lax.ppermute(x, axis, [(i, i ^ bit) for i in range(count)])  49.5 us
    pallas_call x1, Pallas kernels, attention_backward(): pl.pallas_call(functools.partial(attention_backward_kernel, tile), grid=(...  24.9 us
    pallas_call x2, Pallas kernels, attention_forward(): pl.pallas_call(lambda *refs: kernel(*refs[:5], *refs[5 + skip:]), grid=(c...  22.9 us
    pallas_call x1, Pallas kernels, token_block(): pl.pallas_call(token_kernel, in_specs=[pl.BlockSpec(memory_space=pltpu.SM...  22.1 us
    ppermute x41, waiting for transfers between devices, swap(): return lax.ppermute(x, axis, [(i, i ^ bit) for i in range(count)])  21.3 us
    all_to_all x2, waiting for transfers between devices, exchange(): return lax.all_to_all(x, CTX, 0, 0, axis_index_groups=sets, tiled=True)  16.1 us
    convert_element_type x9, other arithmetic, total_low(): return sum((t.astype(F32) for t in terms)).astype(BF)  14.5 us
    all_to_all x2, starting transfers between devices, exchange(): return lax.all_to_all(x, CTX, 0, 0, axis_index_groups=sets, tiled=True)  7.93 us
  transfers between devices with their start and end apart: 47, of which 13 were waited for; matrix products, arithmetic and copies ran while one was open for 16% of the time, Pallas kernels for 23%

profile of v3, /device:TPU:0, one launch (start us, length us, event | category | flops | bytes accessed | tf_op | source)
XLA Modules:
  0.0 252.5 jit_solution(14127839937350202533)
XLA Ops:
  1.6 4.1 %collective-permute-start = (bf16[128,768]{1,0:T(8,128)(2,1)S(1)}, bf16[128,768]{1,0:T(8,128)(2,1)S(1)}, u32[]{:S(2)}, u32[]{:S(2)}) collective-permute-start(bf16[128,768]{1,0:T(8,128)(2,1)S(1)} %dynamic-slice_bitcast_fusion), channel_id=1, source_target_pairs={{0,4},{1,5},{2,6},{3,7},{4,0},{5,1},{6,2},{7,3},{8,12},{9,13},{10,... | collective-permute-start | bytes 589832 | tf_op jit(solution)/shard_map/ppermute | solution.py:1268
  5.7 1.2 fusion.30
  7.0 2.1 pack_columns.1
  9.1 3.8 %all-to-all-start = ((bf16[8,80,256]{2,1,0:T(8,128)(2,1)}), bf16[8,80,256]{2,1,0:T(8,128)(2,1)S(1)}, u32[]{:S(2)}, u32[]{:S(2)}) async-start(bf16[8,80,256]{2,1,0:T(8,128)(2,1)} %get-tuple-element.134), calls=%async_computation | async-start | bytes 655360 | tf_op jit(solution)/shard_map/all_to_all | solution.py:1380
  15.0 1.3 pad_maximum_fusion.refs_4_.trig_ref
  17.0 2.1 collective-permute-start.3
  19.1 2.6 %collective-permute-start.4 = (bf16[192,768]{1,0:T(8,128)(2,1)S(1)}, bf16[192,768]{1,0:T(8,128)(2,1)S(1)}, u32[]{:S(2)}, u32[]{:S(2)}) collective-permute-start(bf16[192,768]{1,0:T(8,128)(2,1)S(1)} %copy-done.10), channel_id=1, source_target_pairs={{0,4},{1,5},{2,6},{3,7},{4,0},{5,1},{6,2},{7,3},{8,12},{9,13},{10,... | collective-permute-start | bytes 884744 | tf_op jit(solution)/shard_map/ppermute | solution.py:1268
  21.7 1.5 collective-permute-start.6
  23.7 1.5 collective-permute-start.1
  25.3 1.2 broadcast_in_dim.77
  26.5 4.4 %all-to-all-start.1 = ((bf16[4,2,128,768]{3,2,1,0:T(8,128)(2,1)}), bf16[4,2,128,768]{3,2,1,0:T(8,128)(2,1)}, u32[]{:S(2)}, u32[]{:S(2)}) async-start(bf16[4,2,128,768]{3,2,1,0:T(8,128)(2,1)} %broadcast_in_dim.77), calls=%async_computation.1 | async-start | bytes 3145728 | tf_op jit(solution)/shard_map/all_to_all | solution.py:1291
  32.2 2.0 collective-permute-start.9
  34.2 8.4 %collective-permute-done.4 = bf16[192,768]{1,0:T(8,128)(2,1)S(1)} collective-permute-done((bf16[192,768]{1,0:T(8,128)(2,1)S(1)}, bf16[192,768]{1,0:T(8,128)(2,1)S(1)}, u32[]{:S(2)}, u32[]{:S(2)}) %collective-permute-start.4) | collective-permute-done | bytes 294944 | tf_op jit(solution)/shard_map/ppermute | solution.py:1268
  43.3 1.2 fusion.27
  44.5 1.5 collective-permute-start.7
  45.9 1.5 collective-permute-start.8
  47.8 1.3 copy.75
  49.0 1.8 unpack_small.1
  50.9 6.1 %all-to-all-done.1 = bf16[4,2,128,768]{3,2,1,0:T(8,128)(2,1)} async-done(((bf16[4,2,128,768]{3,2,1,0:T(8,128)(2,1)}), bf16[4,2,128,768]{3,2,1,0:T(8,128)(2,1)}, u32[]{:S(2)}, u32[]{:S(2)}) %all-to-all-start.1) | async-done | bytes 1572896 | tf_op jit(solution)/shard_map/all_to_all | solution.py:1291
  56.9 9.0 %attention_forward.2 = (bf16[2,4,192,128]{3,2,1,0:T(8,128)(2,1)}, bf16[3,1024,128]{2,1,0:T(8,128)(2,1)}, bf16[3,1024,128]{2,1,0:T(8,128)(2,1)}, bf16[3,1024,128]...) custom-call(bf16[1024,768]{1,0:T(8,128)(2,1)} %bitcast.36.refs_0_.x_, ...), custom_call_target="tpu_custom_call" | custom-call | flops 2550136832 | bytes 12582912 | tf_op jit(solution)/shard_map/attention_forward/pallas_call | solution.py:832
  66.7 1.8 collective-permute-start.10
  68.6 2.4 collective-permute-start.11
  71.1 1.6 select_bitcast_fusion.2
  72.7 1.1 pad_maximum_fusion.4.outer_one
  73.9 1.4 collective-permute-start.17
  76.4 1.5 collective-permute-start.16
  77.9 13.8 %attention_forward.3 = (bf16[2,4,192,128]{3,2,1,0:T(8,128)(2,1)}, bf16[3,1024,128]{2,1,0:T(8,128)(2,1)}, bf16[3,1024,128]{2,1,0:T(8,128)(2,1)}, bf16[3,1024,128]...) custom-call(bf16[1024,768]{1,0:T(8,128)(2,1)} %bitcast.36.refs_0_.x_, ...), custom_call_target="tpu_custom_call", output_to_operand_aliasing={{0}: (5, {}), {1}: (6, {}), {2}: (7, {}), {3}: (8, {}), {4}... | custom-call | flops 5100273664 | bytes 12582912 | tf_op jit(solution)/shard_map/attention_forward/pallas_call | solution.py:832
  91.8 4.9 %all-to-all-start.2 = ((bf16[8,192,128]{2,1,0:T(8,128)(2,1)}), bf16[8,192,128]{2,1,0:T(8,128)(2,1)}, u32[]{:S(2)}, u32[]{:S(2)}) async-start(bf16[8,192,128]{2,1,0:T(8,128)(2,1)} %bitcast.249), calls=%async_computation.2 | async-start | bytes 786432 | tf_op jit(solution)/shard_map/all_to_all | solution.py:1441
  98.7 3.5 %collective-permute-done.13.third_two = bf16[4,2,2,24,768]{4,3,2,1,0:T(8,128)(2,1)} collective-permute-done((bf16[4,2,2,24,768]{4,3,2,1,0:T(8,128)(2,1)S(1)}, bf16[4,2,2,24,768]{4,3,2,1,0:T(8,128)(2,1)}, u32[]{:S(2)}, u32[]{:S(2)}) %collective-permute-start.13) | collective-permute-done | bytes 589856 | tf_op jit(solution)/shard_map/ppermute | solution.py:1268
  102.2 4.2 %all-to-all-done.2 = bf16[8,192,128]{2,1,0:T(8,128)(2,1)} async-done(((bf16[8,192,128]{2,1,0:T(8,128)(2,1)}), bf16[8,192,128]{2,1,0:T(8,128)(2,1)}, u32[]{:S(2)}, u32[]{:S(2)}) %all-to-all-start.2) | async-done | bytes 393248 | tf_op jit(solution)/shard_map/all_to_all | solution.py:1441
  109.7 1.7 collective-permute-done.19.outer_four
  111.4 22.1 %token_block.1 = (bf16[256,768]{1,0:T(8,128)(2,1)}, f32[256,768]{1,0:T(8,128)}, bf16[8,200,128]{2,1,0:T(8,128)(2,1)}, bf16[2,4,8,24,768]{4,3,2,1,0:T(8,128)(2,1)...) custom-call(s32[3]{0:T(128)} %pad_add_fusion.core_ref, ...), custom_call_target="tpu_custom_call" | custom-call | flops 8455716864 | bytes 31457280 | tf_op jit(solution)/shard_map/token_block/pallas_call | solution.py:1242
  133.8 2.9 %collective-permute-done.20 = bf16[2,8,48,768]{3,2,1,0:T(8,128)(2,1)S(1)} collective-permute-done((bf16[2,8,48,768]{3,2,1,0:T(8,128)(2,1)}, bf16[2,8,48,768]{3,2,1,0:T(8,128)(2,1)S(1)}, u32[]{:S(2)}, u32[]{:S(2)}) %collective-permute-start.20) | collective-permute-done | bytes 1179680 | tf_op jit(solution)/shard_map/ppermute | solution.py:1268
  137.2 4.4 %all-to-all-start.3 = ((bf16[8,200,128]{2,1,0:T(8,128)(2,1)}), bf16[8,200,128]{2,1,0:T(8,128)(2,1)}, u32[]{:S(2)}, u32[]{:S(2)}) async-start(bf16[8,200,128]{2,1,0:T(8,128)(2,1)} %get-tuple-element.176), calls=%async_computation.3 | async-start | bytes 819200 | tf_op jit(solution)/shard_map/all_to_all | solution.py:1471
  142.3 2.3 fusion.14
  144.6 1.9 collective-permute-start.25
  146.4 2.4 collective-permute-start.26
  149.0 1.4 fusion
  151.8 1.4 fusion.4
  153.1 2.0 collective-permute-start.24
  155.2 24.9 %attention_backward.1 = (bf16[1024,768]{1,0:T(8,128)(2,1)}, bf16[2,2,8,80,256]{4,3,2,1,0:T(8,128)(2,1)}, f32[3,8,128]{2,1,0:T(8,128)}) custom-call(s32[1]{0:T(128)} %bitcast.core_ref, bf16[2,4,200,128]{3,2,1,0:T(8,128)(2,1)} %bitcast.74.do_ref, bf16[1024,768]{1,0:T(8,128)(2,1)} %bitcast.36.refs_0_.x_ref, bf16[3,768,256]{2,1,0:T(8,128)(2,1)} %get-tuple-element.188.w_ref, ...), custom_call_target="tpu_custom_call" | custom-call | flops 13690208256 | bytes 15728640 | tf_op jit(solution)/shard_map/attention_backward/pallas_call | solution.py:866
  180.1 1.8 small_gradients.1.keep_ref
  181.9 2.0 slice_bitcast_fusion
  184.0 3.6 %all-to-all-start.4 = ((bf16[4,2,128,768]{3,2,1,0:T(8,128)(2,1)}), bf16[4,2,128,768]{3,2,1,0:T(8,128)(2,1)S(1)}, u32[]{:S(2)}, u32[]{:S(2)}) async-start(bf16[4,2,128,768]{3,2,1,0:T(8,128)(2,1)} %bitcast.248), calls=%async_computation.4 | async-start | bytes 3145728 | tf_op jit(solution)/shard_map/all_to_all | solution.py:1291
  187.6 1.5 fusion.3
  189.1 2.6 %fusion.7 = (bf16[2,72,768]{2,1,0:T(8,128)(2,1)S(1)}, bf16[2,72,768]{2,1,0:T(8,128)(2,1)}, bf16[2,72,768]{2,1,0:T(8,128)(2,1)}) fusion(s32[]{:T(128)S(6)} %select_n.356, bf16[2,4,2,72,768]{4,3,2,1,0:T(8,128)(2,1)} %bitcast.72, s32[]{:T(128)S(6)} %select_n.365, s32[]{:T(128)S(6)} %select_n.363, bf16[2,4,2,72,768]{4,3,2,1,0:T(8,128)(2,1)} %bitcast.244, ...), kind=kLoop, calls=%fused_computation.41 | loop fusion | flops 1990656 | bytes 2654236 | tf_op jit(solution)/shard_map/convert_element_type | solution.py:1303
  191.7 2.3 row_sum.2
  196.5 2.0 collective-permute-start.34
  198.4 1.5 collective-permute-start.31
  199.9 1.5 collective-permute-start.32
  201.4 1.4 collective-permute-start.33
  202.8 10.0 %all-to-all-done.4 = bf16[4,2,128,768]{3,2,1,0:T(8,128)(2,1)S(1)} async-done(((bf16[4,2,128,768]{3,2,1,0:T(8,128)(2,1)}), bf16[4,2,128,768]{3,2,1,0:T(8,128)(2,1)S(1)}, u32[]{:S(2)}, u32[]{:S(2)}) %all-to-all-start.4) | async-done | bytes 1572896 | tf_op jit(solution)/shard_map/all_to_all | solution.py:1291
  214.4 2.4 row_sum.3
  216.8 4.4 %all-to-all-start.5 = ((bf16[8,80,256]{2,1,0:T(8,128)(2,1)}), bf16[8,80,256]{2,1,0:T(8,128)(2,1)S(1)}, u32[]{:S(2)}, u32[]{:S(2)}) async-start(bf16[8,80,256]{2,1,0:T(8,128)(2,1)} %row_sum.3), calls=%async_computation.5 | async-start | bytes 655360 | tf_op jit(solution)/shard_map/all_to_all | solution.py:1534
  221.2 1.3 fusion.15
  223.6 1.7 fusion.2
  226.1 2.0 collective-permute-start.36
  228.1 2.4 collective-permute-start.37
  230.7 1.3 fusion.18
  234.1 2.7 %collective-permute-done.35 = bf16[72,768]{1,0:T(8,128)(2,1)S(1)} collective-permute-done((bf16[72,768]{1,0:T(8,128)(2,1)S(1)}, bf16[72,768]{1,0:T(8,128)(2,1)S(1)}, u32[]{:S(2)}, u32[]{:S(2)}) %collective-permute-start.35) | collective-permute-done | bytes 110624 | tf_op jit(solution)/shard_map/ppermute | solution.py:1268
  236.8 2.0 collective-permute-start.40
  238.7 1.3 fusion.19
  243.0 2.5 all-to-all-done.5.block_ref
  246.2 1.8 finish_columns.1
  (149 shorter events, 32.8 us)
Async XLA Ops:
  0.7 13.3 %copy-start.12 = (s32[2]{0:T(128)S(1)}, s32[2]{0:T(128)}, u32[]{:S(2)}) copy-start(s32[2]{0:T(128)} %param.25) | copy-start | bytes 28
  1.6 15.4 %collective-permute-start = (bf16[128,768]{1,0:T(8,128)(2,1)S(1)}, bf16[128,768]{1,0:T(8,128)(2,1)S(1)}, u32[]{:S(2)}, u32[]{:S(2)}) collective-permute-start(bf16[128,768]{1,0:T(8,128)(2,1)S(1)} %dynamic-slice_bitcast_fusion), channel_id=1, source_target_pairs={{0,4},{1,5},{2,6},{3,7},{4,0},{5,1},{6,2},{7,3},{8,12},{9,13},{10,... | collective-permute-start | bytes 589832 | tf_op jit(solution)/shard_map/ppermute | solution.py:1268
  9.1 14.6 %all-to-all-start = ((bf16[8,80,256]{2,1,0:T(8,128)(2,1)}), bf16[8,80,256]{2,1,0:T(8,128)(2,1)S(1)}, u32[]{:S(2)}, u32[]{:S(2)}) async-start(bf16[8,80,256]{2,1,0:T(8,128)(2,1)} %get-tuple-element.134), calls=%async_computation | async-start | bytes 655360 | tf_op jit(solution)/shard_map/all_to_all | solution.py:1380
  15.0 2.1 copy-start.10
  15.0 6.7 %copy-start.11 = (bf16[24,768]{1,0:T(8,128)(2,1)S(1)}, bf16[24,768]{1,0:T(8,128)(2,1)}, u32[]{:S(2)}) copy-start(bf16[24,768]{1,0:T(8,128)(2,1)} %get-tuple-element.139) | copy-start | bytes 110596
  15.0 10.2 %copy-start.9 = (bf16[2,128,768]{2,1,0:T(8,128)(2,1)S(1)}, bf16[2,128,768]{2,1,0:T(8,128)(2,1)}, u32[]{:S(2)}) copy-start(bf16[2,128,768]{2,1,0:T(8,128)(2,1)} %param.23) | copy-start | bytes 1179652
  17.0 17.2 %collective-permute-start.3 = (bf16[192,768]{1,0:T(8,128)(2,1)S(1)}, bf16[192,768]{1,0:T(8,128)(2,1)S(1)}, u32[]{:S(2)}, u32[]{:S(2)}) collective-permute-start(bf16[192,768]{1,0:T(8,128)(2,1)S(1)} %copy-done.10), channel_id=1, source_target_pairs={{0,2},{1,3},{2,0},{3,1},{4,6},{5,7},{6,4},{7,5},{8,10},{9,11},{10,... | collective-permute-start | bytes 884744 | tf_op jit(solution)/shard_map/ppermute | solution.py:1268
  19.1 23.5 %collective-permute-start.4 = (bf16[192,768]{1,0:T(8,128)(2,1)S(1)}, bf16[192,768]{1,0:T(8,128)(2,1)S(1)}, u32[]{:S(2)}, u32[]{:S(2)}) collective-permute-start(bf16[192,768]{1,0:T(8,128)(2,1)S(1)} %copy-done.10), channel_id=1, source_target_pairs={{0,4},{1,5},{2,6},{3,7},{4,0},{5,1},{6,2},{7,3},{8,12},{9,13},{10,... | collective-permute-start | bytes 884744 | tf_op jit(solution)/shard_map/ppermute | solution.py:1268
  21.7 20.9 %collective-permute-start.5 = (bf16[192,768]{1,0:T(8,128)(2,1)S(1)}, bf16[192,768]{1,0:T(8,128)(2,1)S(1)}, u32[]{:S(2)}, u32[]{:S(2)}) collective-permute-start(bf16[192,768]{1,0:T(8,128)(2,1)S(1)} %copy-done.10), channel_id=1, source_target_pairs={{0,6},{1,7},{2,4},{3,5},{4,2},{5,3},{6,0},{7,1},{8,14},{9,15},{10,... | collective-permute-start | bytes 884744 | tf_op jit(solution)/shard_map/ppermute | solution.py:1268
  21.7 10.4 %collective-permute-start.6 = (bf16[24,768]{1,0:T(8,128)(2,1)S(1)}, bf16[24,768]{1,0:T(8,128)(2,1)S(1)}, u32[]{:S(2)}, u32[]{:S(2)}) collective-permute-start(bf16[24,768]{1,0:T(8,128)(2,1)S(1)} %copy-done.11), channel_id=1, source_target_pairs={{0,16},{8,24},{16,0},{24,8},{1,17},{9,25},{17,1},{25,9},{2,18},{10... | collective-permute-start | bytes 110600 | tf_op jit(solution)/shard_map/ppermute | solution.py:1268
  23.7 8.3 %collective-permute-start.1 = (bf16[1,8,80,256]{3,2,1,0:T(8,128)(2,1)S(1)}, bf16[1,8,80,256]{3,2,1,0:T(8,128)(2,1)S(1)}, u32[]{:S(2)}, u32[]{:S(2)}) collective-permute-start(bf16[1,8,80,256]{3,2,1,0:T(8,128)(2,1)S(1)} %bitcast.250), channel_id=1, source_target_pairs={{0,16},{8,24},{16,0},{24,8},{1,17},{9,25},{17,1},{25,9},{2,18},{10... | collective-permute-start | bytes 983048 | tf_op jit(solution)/shard_map/ppermute | solution.py:1268
  26.5 30.4 %all-to-all-start.1 = ((bf16[4,2,128,768]{3,2,1,0:T(8,128)(2,1)}), bf16[4,2,128,768]{3,2,1,0:T(8,128)(2,1)}, u32[]{:S(2)}, u32[]{:S(2)}) async-start(bf16[4,2,128,768]{3,2,1,0:T(8,128)(2,1)} %broadcast_in_dim.77), calls=%async_computation.1 | async-start | bytes 3145728 | tf_op jit(solution)/shard_map/all_to_all | solution.py:1291
  32.2 33.8 %collective-permute-start.9 = (bf16[2,24,768]{2,1,0:T(8,128)(2,1)S(1)}, bf16[2,24,768]{2,1,0:T(8,128)(2,1)S(1)}, u32[]{:S(2)}, u32[]{:S(2)}) collective-permute-start(bf16[2,24,768]{2,1,0:T(8,128)(2,1)S(1)} %pad_maximum_fusion.11), channel_id=1, source_target_pairs={{0,1},{1,0},{2,3},{3,2},{4,5},{5,4},{6,7},{7,6},{8,9},{9,8},{10,11... | collective-permute-start | bytes 221192 | tf_op jit(solution)/shard_map/ppermute | solution.py:1268
  42.6 4.8 %collective-permute-start.2 = (bf16[2,1,8,80,256]{4,3,2,0,1:T(8,128)(2,1)S(1)}, bf16[2,1,8,80,256]{4,3,2,0,1:T(8,128)(2,1)S(1)}, u32[]{:S(2)}, u32[]{:S(2)}) collective-permute-start(bf16[2,1,8,80,256]{4,3,2,0,1:T(8,128)(2,1)S(1)} %pad_maximum_fusion.5), channel_id=1, source_target_pairs={{0,8},{8,0},{16,24},{24,16},{1,9},{9,1},{17,25},{25,17},{2,10},{10... | collective-permute-start | bytes 1966088 | tf_op jit(solution)/shard_map/ppermute | solution.py:1268
  43.3 4.3 %copy-start = (bf16[2,2,192,768]{3,2,1,0:T(8,128)(2,1)}, bf16[2,2,192,768]{3,2,1,0:T(8,128)(2,1)S(1)}, u32[]{:S(2)}) copy-start(bf16[2,2,192,768]{3,2,1,0:T(8,128)(2,1)S(1)} %reverse_select_fusion) | copy-start | bytes 3538948
  44.5 21.5 %collective-permute-start.7 = (bf16[4,96,768]{2,1,0:T(8,128)(2,1)}, bf16[4,96,768]{2,1,0:T(8,128)(2,1)S(1)}, u32[]{:S(2)}, u32[]{:S(2)}) collective-permute-start(bf16[4,96,768]{2,1,0:T(8,128)(2,1)} %get-tuple-element.259), channel_id=1, source_target_pairs={{0,1},{1,0},{2,3},{3,2},{4,5},{5,4},{6,7},{7,6},{8,9},{9,8},{10,11... | collective-permute-start | bytes 1769480 | tf_op jit(solution)/shard_map/ppermute | solution.py:1268
  45.9 20.1 %collective-permute-start.8 = (bf16[4,96,768]{2,1,0:T(8,128)(2,1)}, bf16[4,96,768]{2,1,0:T(8,128)(2,1)}, u32[]{:S(2)}, u32[]{:S(2)}) collective-permute-start(bf16[4,96,768]{2,1,0:T(8,128)(2,1)} %get-tuple-element.258), channel_id=1, source_target_pairs={{0,16},{8,24},{16,0},{24,8},{1,17},{9,25},{17,1},{25,9},{2,18},{10... | collective-permute-start | bytes 1769480 | tf_op jit(solution)/shard_map/ppermute | solution.py:1268
  66.7 25.0 %collective-permute-start.10 = (bf16[2,2,24,768]{3,2,0,1:T(8,128)(2,1)}, bf16[2,2,24,768]{3,2,0,1:T(8,128)(2,1)S(1)}, u32[]{:S(2)}, u32[]{:S(2)}) collective-permute-start(bf16[2,2,24,768]{3,2,0,1:T(8,128)(2,1)} %get-tuple-element.280), channel_id=1, source_target_pairs={{0,2},{1,3},{2,0},{3,1},{4,6},{5,7},{6,4},{7,5},{8,10},{9,11},{10,... | collective-permute-start | bytes 442376 | tf_op jit(solution)/shard_map/ppermute | solution.py:1268
  68.6 23.2 %collective-permute-start.11 = (bf16[2,2,24,768]{3,2,0,1:T(8,128)(2,1)}, bf16[2,2,24,768]{3,2,0,1:T(8,128)(2,1)}, u32[]{:S(2)}, u32[]{:S(2)}) collective-permute-start(bf16[2,2,24,768]{3,2,0,1:T(8,128)(2,1)} %get-tuple-element.280), channel_id=1, source_target_pairs={{0,4},{1,5},{2,6},{3,7},{4,0},{5,1},{6,2},{7,3},{8,12},{9,13},{10,... | collective-permute-start | bytes 442376 | tf_op jit(solution)/shard_map/ppermute | solution.py:1268
  71.0 20.8 %collective-permute-start.12 = (bf16[2,2,24,768]{3,2,0,1:T(8,128)(2,1)}, bf16[2,2,24,768]{3,2,0,1:T(8,128)(2,1)}, u32[]{:S(2)}, u32[]{:S(2)}) collective-permute-start(bf16[2,2,24,768]{3,2,0,1:T(8,128)(2,1)} %get-tuple-element.280), channel_id=1, source_target_pairs={{0,6},{1,7},{2,4},{3,5},{4,2},{5,3},{6,0},{7,1},{8,14},{9,15},{10,... | collective-permute-start | bytes 442376 | tf_op jit(solution)/shard_map/ppermute | solution.py:1268
  73.9 32.6 %collective-permute-start.17 = (bf16[2,4,96,768]{3,2,1,0:T(8,128)(2,1)}, bf16[2,4,96,768]{3,2,1,0:T(8,128)(2,1)}, u32[]{:S(2)}, u32[]{:S(2)}) collective-permute-start(bf16[2,4,96,768]{3,2,1,0:T(8,128)(2,1)} %pad_maximum_fusion.4.outer_one), channel_id=1, source_target_pairs={{0,1},{1,0},{2,3},{3,2},{4,5},{5,4},{6,7},{7,6},{8,9},{9,8},{10,11... | collective-permute-start | bytes 3538952 | tf_op jit(solution)/shard_map/ppermute | solution.py:1268
  76.4 30.1 %collective-permute-start.16 = (bf16[2,4,96,768]{3,2,1,0:T(8,128)(2,1)}, bf16[2,4,96,768]{3,2,1,0:T(8,128)(2,1)}, u32[]{:S(2)}, u32[]{:S(2)}) collective-permute-start(bf16[2,4,96,768]{3,2,1,0:T(8,128)(2,1)} %pad_maximum_fusion.3.inner_one), channel_id=1, source_target_pairs={{0,16},{8,24},{16,0},{24,8},{1,17},{9,25},{17,1},{25,9},{2,18},{10... | collective-permute-start | bytes 3538952 | tf_op jit(solution)/shard_map/ppermute | solution.py:1268
  91.8 14.7 %all-to-all-start.2 = ((bf16[8,192,128]{2,1,0:T(8,128)(2,1)}), bf16[8,192,128]{2,1,0:T(8,128)(2,1)}, u32[]{:S(2)}, u32[]{:S(2)}) async-start(bf16[8,192,128]{2,1,0:T(8,128)(2,1)} %bitcast.249), calls=%async_computation.2 | async-start | bytes 786432 | tf_op jit(solution)/shard_map/all_to_all | solution.py:1441
  96.7 9.7 %collective-permute-start.14 = (bf16[2,4,96,768]{3,2,1,0:T(8,128)(2,1)}, bf16[2,4,96,768]{3,2,1,0:T(8,128)(2,1)S(1)}, u32[]{:S(2)}, u32[]{:S(2)}) collective-permute-start(bf16[2,4,96,768]{3,2,1,0:T(8,128)(2,1)} %pad_maximum_fusion.3.inner_one), channel_id=1, source_target_pairs={{0,8},{8,0},{16,24},{24,16},{1,9},{9,1},{17,25},{25,17},{2,10},{10... | collective-permute-start | bytes 3538952 | tf_op jit(solution)/shard_map/ppermute | solution.py:1268
  96.7 9.7 %collective-permute-start.15 = (bf16[2,4,96,768]{3,2,1,0:T(8,128)(2,1)}, bf16[2,4,96,768]{3,2,1,0:T(8,128)(2,1)S(1)}, u32[]{:S(2)}, u32[]{:S(2)}) collective-permute-start(bf16[2,4,96,768]{3,2,1,0:T(8,128)(2,1)} %pad_maximum_fusion.4.outer_one), channel_id=1, source_target_pairs={{0,8},{8,0},{16,24},{24,16},{1,9},{9,1},{17,25},{25,17},{2,10},{10... | collective-permute-start | bytes 3538952 | tf_op jit(solution)/shard_map/ppermute | solution.py:1268
  98.5 12.9 %copy-start.8 = (bf16[2,2,2,2,24,768]{5,4,3,2,1,0:T(8,128)(2,1)}, bf16[2,2,2,2,24,768]{5,4,3,2,1,0:T(8,128)(2,1)S(1)}, u32[]{:S(2)}) copy-start(bf16[2,2,2,2,24,768]{5,4,3,2,1,0:T(8,128)(2,1)S(1)} %reverse_select_fusion.2) | copy-start | bytes 1769476
  98.6 3.7 %collective-permute-start.13 = (bf16[4,2,2,24,768]{4,3,2,1,0:T(8,128)(2,1)S(1)}, bf16[4,2,2,24,768]{4,3,2,1,0:T(8,128)(2,1)}, u32[]{:S(2)}, u32[]{:S(2)}) collective-permute-start(bf16[4,2,2,24,768]{4,3,2,1,0:T(8,128)(2,1)S(1)} %bitcast.260), channel_id=1, source_target_pairs={{0,8},{8,0},{16,24},{24,16},{1,9},{9,1},{17,25},{25,17},{2,10},{10... | collective-permute-start | bytes 1769480 | tf_op jit(solution)/shard_map/ppermute | solution.py:1268
  106.4 1.0 copy-start.13
  106.5 1.9 copy-start.14
  106.5 3.3 %collective-permute-start.18 = (bf16[2,4,96,768]{3,2,1,0:T(8,128)(2,1)}, bf16[2,4,96,768]{3,2,1,0:T(8,128)(2,1)}, u32[]{:S(2)}, u32[]{:S(2)}) collective-permute-start(bf16[2,4,96,768]{3,2,1,0:T(8,128)(2,1)} %collective-permute-done.16.inner_three), channel_id=1, source_target_pairs={{0,8},{8,0},{16,24},{24,16},{1,9},{9,1},{17,25},{25,17},{2,10},{10... | collective-permute-start | bytes 3538952 | tf_op jit(solution)/shard_map/ppermute | solution.py:1268
  106.6 4.9 %collective-permute-start.19 = (bf16[2,4,96,768]{3,2,1,0:T(8,128)(2,1)}, bf16[2,4,96,768]{3,2,1,0:T(8,128)(2,1)}, u32[]{:S(2)}, u32[]{:S(2)}) collective-permute-start(bf16[2,4,96,768]{3,2,1,0:T(8,128)(2,1)} %collective-permute-done.17.outer_three), channel_id=1, source_target_pairs={{0,8},{8,0},{16,24},{24,16},{1,9},{9,1},{17,25},{25,17},{2,10},{10... | collective-permute-start | bytes 3538952 | tf_op jit(solution)/shard_map/ppermute | solution.py:1268
  133.6 3.1 %collective-permute-start.20 = (bf16[2,8,48,768]{3,2,1,0:T(8,128)(2,1)}, bf16[2,8,48,768]{3,2,1,0:T(8,128)(2,1)S(1)}, u32[]{:S(2)}, u32[]{:S(2)}) collective-permute-start(bf16[2,8,48,768]{3,2,1,0:T(8,128)(2,1)} %get-tuple-element.180), channel_id=1, source_target_pairs={{0,8},{8,0},{16,24},{24,16},{1,9},{9,1},{17,25},{25,17},{2,10},{10... | collective-permute-start | bytes 3538952 | tf_op jit(solution)/shard_map/ppermute | solution.py:1268
  136.7 7.9 %copy-start.6 = (bf16[2,8,48,768]{3,2,1,0:T(8,128)(2,1)}, bf16[2,8,48,768]{3,2,1,0:T(8,128)(2,1)S(1)}, u32[]{:S(2)}) copy-start(bf16[2,8,48,768]{3,2,1,0:T(8,128)(2,1)S(1)} %collective-permute-done.20) | copy-start | bytes 3538948
  136.7 12.3 %collective-permute-start.21 = (bf16[2,4,8,24,768]{4,3,2,1,0:T(8,128)(2,1)}, bf16[2,4,8,24,768]{4,3,2,1,0:T(8,128)(2,1)S(1)}, u32[]{:S(2)}, u32[]{:S(2)}) collective-permute-start(bf16[2,4,8,24,768]{4,3,2,1,0:T(8,128)(2,1)} %get-tuple-element.181), channel_id=1, source_target_pairs={{0,8},{8,0},{16,24},{24,16},{1,9},{9,1},{17,25},{25,17},{2,10},{10... | collective-permute-start | bytes 7077896 | tf_op jit(solution)/shard_map/ppermute | solution.py:1268
  136.8 14.9 %collective-permute-start.22 = (bf16[2,8,72,768]{3,2,1,0:T(8,128)(2,1)}, bf16[2,8,72,768]{3,2,1,0:T(8,128)(2,1)}, u32[]{:S(2)}, u32[]{:S(2)}) collective-permute-start(bf16[2,8,72,768]{3,2,1,0:T(8,128)(2,1)} %get-tuple-element.185), channel_id=1, source_target_pairs={{0,8},{8,0},{16,24},{24,16},{1,9},{9,1},{17,25},{25,17},{2,10},{10... | collective-permute-start | bytes 5308424 | tf_op jit(solution)/shard_map/ppermute | solution.py:1268
  137.2 17.9 %all-to-all-start.3 = ((bf16[8,200,128]{2,1,0:T(8,128)(2,1)}), bf16[8,200,128]{2,1,0:T(8,128)(2,1)}, u32[]{:S(2)}, u32[]{:S(2)}) async-start(bf16[8,200,128]{2,1,0:T(8,128)(2,1)} %get-tuple-element.176), calls=%async_computation.3 | async-start | bytes 819200 | tf_op jit(solution)/shard_map/all_to_all | solution.py:1471
  142.3 6.7 %copy-start.1 = (bf16[2,4,8,24,768]{4,3,2,1,0:T(8,128)(2,1)S(1)}, bf16[2,4,8,24,768]{4,3,2,1,0:T(8,128)(2,1)}, u32[]{:S(2)}) copy-start(bf16[2,4,8,24,768]{4,3,2,1,0:T(8,128)(2,1)} %get-tuple-element.177) | copy-start | bytes 7077892
  144.6 35.5 %collective-permute-start.25 = (bf16[2,2,48,768]{3,2,1,0:T(8,128)(2,1)}, bf16[2,2,48,768]{3,2,1,0:T(8,128)(2,1)}, u32[]{:S(2)}, u32[]{:S(2)}) collective-permute-start(bf16[2,2,48,768]{3,2,1,0:T(8,128)(2,1)} %get-tuple-element.251), channel_id=1, source_target_pairs={{0,2},{1,3},{2,0},{3,1},{4,6},{5,7},{6,4},{7,5},{8,10},{9,11},{10,... | collective-permute-start | bytes 884744 | tf_op jit(solution)/shard_map/ppermute | solution.py:1268
  146.4 33.6 %collective-permute-start.26 = (bf16[2,2,48,768]{3,2,1,0:T(8,128)(2,1)}, bf16[2,2,48,768]{3,2,1,0:T(8,128)(2,1)}, u32[]{:S(2)}, u32[]{:S(2)}) collective-permute-start(bf16[2,2,48,768]{3,2,1,0:T(8,128)(2,1)} %get-tuple-element.250), channel_id=1, source_target_pairs={{0,4},{1,5},{2,6},{3,7},{4,0},{5,1},{6,2},{7,3},{8,12},{9,13},{10,... | collective-permute-start | bytes 884744 | tf_op jit(solution)/shard_map/ppermute | solution.py:1268
  148.8 31.3 %collective-permute-start.27 = (bf16[2,2,48,768]{3,2,1,0:T(8,128)(2,1)}, bf16[2,2,48,768]{3,2,1,0:T(8,128)(2,1)}, u32[]{:S(2)}, u32[]{:S(2)}) collective-permute-start(bf16[2,2,48,768]{3,2,1,0:T(8,128)(2,1)} %get-tuple-element.249), channel_id=1, source_target_pairs={{0,6},{1,7},{2,4},{3,5},{4,2},{5,3},{6,0},{7,1},{8,14},{9,15},{10,... | collective-permute-start | bytes 884744 | tf_op jit(solution)/shard_map/ppermute | solution.py:1268
  149.0 1.8 copy-start.3
  149.0 2.8 %copy-start.4 = (bf16[2,8,72,768]{3,2,1,0:T(8,128)(2,1)S(1)}, bf16[2,8,72,768]{3,2,1,0:T(8,128)(2,1)}, u32[]{:S(2)}) copy-start(bf16[2,8,72,768]{3,2,1,0:T(8,128)(2,1)} %get-tuple-element.184) | copy-start | bytes 5308420
  150.8 29.3 %collective-permute-start.23 = (bf16[4,4,2,24,768]{4,3,0,1,2:T(8,128)(2,1)}, bf16[4,4,2,24,768]{4,3,0,1,2:T(8,128)(2,1)}, u32[]{:S(2)}, u32[]{:S(2)}) collective-permute-start(bf16[4,4,2,24,768]{4,3,0,1,2:T(8,128)(2,1)} %fusion), channel_id=1, source_target_pairs={{0,16},{8,24},{16,0},{24,8},{1,17},{9,25},{17,1},{25,9},{2,18},{10... | collective-permute-start | bytes 3538952 | tf_op jit(solution)/shard_map/ppermute | solution.py:1268
  153.1 26.9 %collective-permute-start.24 = (bf16[2,4,72,768]{3,2,1,0:T(8,128)(2,1)S(1)}, bf16[2,4,72,768]{3,2,1,0:T(8,128)(2,1)}, u32[]{:S(2)}, u32[]{:S(2)}) collective-permute-start(bf16[2,4,72,768]{3,2,1,0:T(8,128)(2,1)S(1)} %fusion.4), channel_id=1, source_target_pairs={{0,1},{1,0},{2,3},{3,2},{4,5},{5,4},{6,7},{7,6},{8,9},{9,8},{10,11... | collective-permute-start | bytes 2654216 | tf_op jit(solution)/shard_map/ppermute | solution.py:1268
  180.1 3.8 %copy-start.2 = (bf16[2,4,8,24,768]{4,3,2,1,0:T(8,128)(2,1)S(1)}, bf16[2,4,8,24,768]{4,3,2,1,0:T(8,128)(2,1)}, u32[]{:S(2)}) copy-start(bf16[2,4,8,24,768]{4,3,2,1,0:T(8,128)(2,1)} %get-tuple-element.177) | copy-start | bytes 7077892
  183.9 7.8 %collective-permute-start.29 = (bf16[2,8,80,256]{3,2,1,0:T(8,128)(2,1)}, bf16[2,8,80,256]{3,2,1,0:T(8,128)(2,1)}, u32[]{:S(2)}, u32[]{:S(2)}) collective-permute-start(bf16[2,8,80,256]{3,2,1,0:T(8,128)(2,1)} %slice_bitcast_fusion), channel_id=1, source_target_pairs={{0,8},{8,0},{16,24},{24,16},{1,9},{9,1},{17,25},{25,17},{2,10},{10... | collective-permute-start | bytes 1966088 | tf_op jit(solution)/shard_map/ppermute | solution.py:1268
  184.0 28.9 %all-to-all-start.4 = ((bf16[4,2,128,768]{3,2,1,0:T(8,128)(2,1)}), bf16[4,2,128,768]{3,2,1,0:T(8,128)(2,1)S(1)}, u32[]{:S(2)}, u32[]{:S(2)}) async-start(bf16[4,2,128,768]{3,2,1,0:T(8,128)(2,1)} %bitcast.248), calls=%async_computation.4 | async-start | bytes 3145728 | tf_op jit(solution)/shard_map/all_to_all | solution.py:1291
  194.0 19.7 %collective-permute-start.30 = (bf16[8,80,256]{2,1,0:T(8,128)(2,1)}, bf16[8,80,256]{2,1,0:T(8,128)(2,1)S(1)}, u32[]{:S(2)}, u32[]{:S(2)}) collective-permute-start(bf16[8,80,256]{2,1,0:T(8,128)(2,1)} %row_sum.2), channel_id=1, source_target_pairs={{0,16},{8,24},{16,0},{24,8},{1,17},{9,25},{17,1},{25,9},{2,18},{10... | collective-permute-start | bytes 983048 | tf_op jit(solution)/shard_map/ppermute | solution.py:1268
  196.5 26.0 %collective-permute-start.34 = (bf16[4,4,24,768]{3,2,0,1:T(8,128)(2,1)S(1)}, bf16[4,4,24,768]{3,2,0,1:T(8,128)(2,1)}, u32[]{:S(2)}, u32[]{:S(2)}) collective-permute-start(bf16[4,4,24,768]{3,2,0,1:T(8,128)(2,1)S(1)} %fusion.3), channel_id=1, source_target_pairs={{0,1},{1,0},{2,3},{3,2},{4,5},{5,4},{6,7},{7,6},{8,9},{9,8},{10,11... | collective-permute-start | bytes 1769480 | tf_op jit(solution)/shard_map/ppermute | solution.py:1268
  198.4 27.7 %collective-permute-start.31 = (bf16[2,72,768]{2,1,0:T(8,128)(2,1)}, bf16[2,72,768]{2,1,0:T(8,128)(2,1)}, u32[]{:S(2)}, u32[]{:S(2)}) collective-permute-start(bf16[2,72,768]{2,1,0:T(8,128)(2,1)} %get-tuple-element.246), channel_id=1, source_target_pairs={{0,2},{1,3},{2,0},{3,1},{4,6},{5,7},{6,4},{7,5},{8,10},{9,11},{10,... | collective-permute-start | bytes 663560 | tf_op jit(solution)/shard_map/ppermute | solution.py:1268
  199.9 28.2 %collective-permute-start.32 = (bf16[2,72,768]{2,1,0:T(8,128)(2,1)}, bf16[2,72,768]{2,1,0:T(8,128)(2,1)}, u32[]{:S(2)}, u32[]{:S(2)}) collective-permute-start(bf16[2,72,768]{2,1,0:T(8,128)(2,1)} %get-tuple-element.245), channel_id=1, source_target_pairs={{0,4},{1,5},{2,6},{3,7},{4,0},{5,1},{6,2},{7,3},{8,12},{9,13},{10,... | collective-permute-start | bytes 663560 | tf_op jit(solution)/shard_map/ppermute | solution.py:1268
  201.4 29.1 %collective-permute-start.33 = (bf16[2,72,768]{2,1,0:T(8,128)(2,1)S(1)}, bf16[2,72,768]{2,1,0:T(8,128)(2,1)}, u32[]{:S(2)}, u32[]{:S(2)}) collective-permute-start(bf16[2,72,768]{2,1,0:T(8,128)(2,1)S(1)} %get-tuple-element.244), channel_id=1, source_target_pairs={{0,6},{1,7},{2,4},{3,5},{4,2},{5,3},{6,0},{7,1},{8,14},{9,15},{10,... | collective-permute-start | bytes 663560 | tf_op jit(solution)/shard_map/ppermute | solution.py:1268
  213.7 0.7 copy-start.15
  213.7 36.2 %collective-permute-start.28 = (bf16[128,768]{1,0:T(8,128)(2,1)}, bf16[128,768]{1,0:T(8,128)(2,1)}, u32[]{:S(2)}, u32[]{:S(2)}) collective-permute-start(bf16[128,768]{1,0:T(8,128)(2,1)} %dynamic-slice_reduce_fusion), channel_id=1, source_target_pairs={{0,4},{1,5},{2,6},{3,7},{4,0},{5,1},{6,2},{7,3},{8,12},{9,13},{10,... | collective-permute-start | bytes 589832 | tf_op jit(solution)/shard_map/ppermute | solution.py:1268
  216.8 28.7 %all-to-all-start.5 = ((bf16[8,80,256]{2,1,0:T(8,128)(2,1)}), bf16[8,80,256]{2,1,0:T(8,128)(2,1)S(1)}, u32[]{:S(2)}, u32[]{:S(2)}) async-start(bf16[8,80,256]{2,1,0:T(8,128)(2,1)} %row_sum.3), calls=%async_computation.5 | async-start | bytes 655360 | tf_op jit(solution)/shard_map/all_to_all | solution.py:1534
  222.5 9.5 %collective-permute-start.39 = (bf16[2,48,768]{2,1,0:T(8,128)(2,1)S(1)}, bf16[2,48,768]{2,1,0:T(8,128)(2,1)S(1)}, u32[]{:S(2)}, u32[]{:S(2)}) collective-permute-start(bf16[2,48,768]{2,1,0:T(8,128)(2,1)S(1)} %fusion.15), channel_id=1, source_target_pairs={{0,16},{8,24},{16,0},{24,8},{1,17},{9,25},{17,1},{25,9},{2,18},{10... | collective-permute-start | bytes 442376 | tf_op jit(solution)/shard_map/ppermute | solution.py:1268
  226.1 21.9 %collective-permute-start.36 = (bf16[4,24,768]{2,1,0:T(8,128)(2,1)}, bf16[4,24,768]{2,1,0:T(8,128)(2,1)}, u32[]{:S(2)}, u32[]{:S(2)}) collective-permute-start(bf16[4,24,768]{2,1,0:T(8,128)(2,1)} %get-tuple-element.266), channel_id=1, source_target_pairs={{0,2},{1,3},{2,0},{3,1},{4,6},{5,7},{6,4},{7,5},{8,10},{9,11},{10,... | collective-permute-start | bytes 442376 | tf_op jit(solution)/shard_map/ppermute | solution.py:1268
  228.1 20.6 %collective-permute-start.37 = (bf16[4,24,768]{2,1,0:T(8,128)(2,1)}, bf16[4,24,768]{2,1,0:T(8,128)(2,1)}, u32[]{:S(2)}, u32[]{:S(2)}) collective-permute-start(bf16[4,24,768]{2,1,0:T(8,128)(2,1)} %get-tuple-element.265), channel_id=1, source_target_pairs={{0,4},{1,5},{2,6},{3,7},{4,0},{5,1},{6,2},{7,3},{8,12},{9,13},{10,... | collective-permute-start | bytes 442376 | tf_op jit(solution)/shard_map/ppermute | solution.py:1268
  230.5 18.2 %collective-permute-start.38 = (bf16[4,24,768]{2,1,0:T(8,128)(2,1)}, bf16[4,24,768]{2,1,0:T(8,128)(2,1)S(1)}, u32[]{:S(2)}, u32[]{:S(2)}) collective-permute-start(bf16[4,24,768]{2,1,0:T(8,128)(2,1)} %get-tuple-element.264), channel_id=1, source_target_pairs={{0,6},{1,7},{2,4},{3,5},{4,2},{5,3},{6,0},{7,1},{8,14},{9,15},{10,... | collective-permute-start | bytes 442376 | tf_op jit(solution)/shard_map/ppermute | solution.py:1268
  232.0 4.8 %collective-permute-start.35 = (bf16[72,768]{1,0:T(8,128)(2,1)S(1)}, bf16[72,768]{1,0:T(8,128)(2,1)S(1)}, u32[]{:S(2)}, u32[]{:S(2)}) collective-permute-start(bf16[72,768]{1,0:T(8,128)(2,1)S(1)} %fusion.18), channel_id=1, source_target_pairs={{0,16},{8,24},{16,0},{24,8},{1,17},{9,25},{17,1},{25,9},{2,18},{10... | collective-permute-start | bytes 331784 | tf_op jit(solution)/shard_map/ppermute | solution.py:1268
  236.8 4.4 %collective-permute-start.40 = (bf16[48,768]{1,0:T(8,128)(2,1)S(1)}, bf16[48,768]{1,0:T(8,128)(2,1)S(1)}, u32[]{:S(2)}, u32[]{:S(2)}) collective-permute-start(bf16[48,768]{1,0:T(8,128)(2,1)S(1)} %fusion.22), channel_id=1, source_target_pairs={{0,1},{1,0},{2,3},{3,2},{4,5},{5,4},{6,7},{7,6},{8,9},{9,8},{10,11... | collective-permute-start | bytes 221192 | tf_op jit(solution)/shard_map/ppermute | solution.py:1268
  245.5 0.7 copy-start.5
  248.7 2.2 copy-start.7

commit v4 on v3

--- a/solution.py
+++ b/solution.py
@@ -854,7 +854,7 @@
     )(x, w_block, vec, kext, trig, *previous)
 
 
-def attention_backward(core, d_out, x, w, vec, kext, trig, qb, kb, v1, qp, save, scl, prob, owners, block_rows, tile=1024):
+def attention_backward(core, d_out, x, w, vec, kext, trig, qb, kb, v1, qp, save, scl, prob, owners, block_rows, tile=512):
     heads, rows, _ = qb.shape
     width = x.shape[1]
     full = width + LANES

time: 255 us -> 256 us (level)
  no operation moved by 1% of the time
where the time goes in v4:
time: 256 us; the launch traced here: 254 us
  Pallas kernels  83.4 us (33%)
  starting transfers between devices  74.9 us (29%)
  waiting for transfers between devices  44.6 us (17%)
  other arithmetic  35.3 us (14%)
  local copies, waits for them, and re-layouts  14.2 us (6%)
    ppermute x41, starting transfers between devices, swap(): return lax.ppermute(x, axis, [(i, i ^ bit) for i in range(count)])  49.5 us
    pallas_call x1, Pallas kernels, attention_backward(): pl.pallas_call(functools.partial(attention_backward_kernel, tile), grid=(...  26.1 us
    pallas_call x2, Pallas kernels, attention_forward(): pl.pallas_call(lambda *refs: kernel(*refs[:5], *refs[5 + skip:]), grid=(c...  22.9 us
    pallas_call x1, Pallas kernels, token_block(): pl.pallas_call(token_kernel, in_specs=[pl.BlockSpec(memory_space=pltpu.SM...  22.1 us
    ppermute x41, waiting for transfers between devices, swap(): return lax.ppermute(x, axis, [(i, i ^ bit) for i in range(count)])  21.3 us
    all_to_all x2, waiting for transfers between devices, exchange(): return lax.all_to_all(x, CTX, 0, 0, axis_index_groups=sets, tiled=True)  16.1 us
    convert_element_type x9, other arithmetic, total_low(): return sum((t.astype(F32) for t in terms)).astype(BF)  14.5 us
    all_to_all x2, starting transfers between devices, exchange(): return lax.all_to_all(x, CTX, 0, 0, axis_index_groups=sets, tiled=True)  7.93 us
  transfers between devices with their start and end apart: 47, of which 13 were waited for; matrix products, arithmetic and copies ran while one was open for 16% of the time, Pallas kernels for 23%

profile of v4, /device:TPU:0, one launch (start us, length us, event | category | flops | bytes accessed | tf_op | source)
XLA Modules:
  0.0 253.7 jit_solution(17628069070512301038)
XLA Ops:
  1.6 4.1 %collective-permute-start = (bf16[128,768]{1,0:T(8,128)(2,1)S(1)}, bf16[128,768]{1,0:T(8,128)(2,1)S(1)}, u32[]{:S(2)}, u32[]{:S(2)}) collective-permute-start(bf16[128,768]{1,0:T(8,128)(2,1)S(1)} %dynamic-slice_bitcast_fusion), channel_id=1, source_target_pairs={{0,4},{1,5},{2,6},{3,7},{4,0},{5,1},{6,2},{7,3},{8,12},{9,13},{10,... | collective-permute-start | bytes 589832 | tf_op jit(solution)/shard_map/ppermute | solution.py:1268
  5.7 1.2 fusion.30
  7.0 2.1 pack_columns.1
  9.1 3.8 %all-to-all-start = ((bf16[8,80,256]{2,1,0:T(8,128)(2,1)}), bf16[8,80,256]{2,1,0:T(8,128)(2,1)S(1)}, u32[]{:S(2)}, u32[]{:S(2)}) async-start(bf16[8,80,256]{2,1,0:T(8,128)(2,1)} %get-tuple-element.134), calls=%async_computation | async-start | bytes 655360 | tf_op jit(solution)/shard_map/all_to_all | solution.py:1380
  15.0 1.3 pad_maximum_fusion.refs_4_.trig_ref
  17.0 2.1 collective-permute-start.3
  19.1 2.6 %collective-permute-start.4 = (bf16[192,768]{1,0:T(8,128)(2,1)S(1)}, bf16[192,768]{1,0:T(8,128)(2,1)S(1)}, u32[]{:S(2)}, u32[]{:S(2)}) collective-permute-start(bf16[192,768]{1,0:T(8,128)(2,1)S(1)} %copy-done.10), channel_id=1, source_target_pairs={{0,4},{1,5},{2,6},{3,7},{4,0},{5,1},{6,2},{7,3},{8,12},{9,13},{10,... | collective-permute-start | bytes 884744 | tf_op jit(solution)/shard_map/ppermute | solution.py:1268
  21.7 1.5 collective-permute-start.6
  23.7 1.5 collective-permute-start.1
  25.3 1.2 broadcast_in_dim.77
  26.5 4.4 %all-to-all-start.1 = ((bf16[4,2,128,768]{3,2,1,0:T(8,128)(2,1)}), bf16[4,2,128,768]{3,2,1,0:T(8,128)(2,1)}, u32[]{:S(2)}, u32[]{:S(2)}) async-start(bf16[4,2,128,768]{3,2,1,0:T(8,128)(2,1)} %broadcast_in_dim.77), calls=%async_computation.1 | async-start | bytes 3145728 | tf_op jit(solution)/shard_map/all_to_all | solution.py:1291
  32.2 2.0 collective-permute-start.9
  34.2 8.4 %collective-permute-done.4 = bf16[192,768]{1,0:T(8,128)(2,1)S(1)} collective-permute-done((bf16[192,768]{1,0:T(8,128)(2,1)S(1)}, bf16[192,768]{1,0:T(8,128)(2,1)S(1)}, u32[]{:S(2)}, u32[]{:S(2)}) %collective-permute-start.4) | collective-permute-done | bytes 294944 | tf_op jit(solution)/shard_map/ppermute | solution.py:1268
  43.3 1.2 fusion.27
  44.5 1.5 collective-permute-start.7
  45.9 1.5 collective-permute-start.8
  47.8 1.3 copy.75
  49.0 1.8 unpack_small.1
  50.9 6.1 %all-to-all-done.1 = bf16[4,2,128,768]{3,2,1,0:T(8,128)(2,1)} async-done(((bf16[4,2,128,768]{3,2,1,0:T(8,128)(2,1)}), bf16[4,2,128,768]{3,2,1,0:T(8,128)(2,1)}, u32[]{:S(2)}, u32[]{:S(2)}) %all-to-all-start.1) | async-done | bytes 1572896 | tf_op jit(solution)/shard_map/all_to_all | solution.py:1291
  56.9 9.0 %attention_forward.2 = (bf16[2,4,192,128]{3,2,1,0:T(8,128)(2,1)}, bf16[3,1024,128]{2,1,0:T(8,128)(2,1)}, bf16[3,1024,128]{2,1,0:T(8,128)(2,1)}, bf16[3,1024,128]...) custom-call(bf16[1024,768]{1,0:T(8,128)(2,1)} %bitcast.36.refs_0_.x_, ...), custom_call_target="tpu_custom_call" | custom-call | flops 2550136832 | bytes 12582912 | tf_op jit(solution)/shard_map/attention_forward/pallas_call | solution.py:832
  66.7 1.8 collective-permute-start.10
  68.6 2.4 collective-permute-start.11
  71.1 1.6 select_bitcast_fusion.2
  72.7 1.1 pad_maximum_fusion.4.outer_one
  73.9 1.4 collective-permute-start.17
  76.4 1.5 collective-permute-start.16
  77.9 13.8 %attention_forward.3 = (bf16[2,4,192,128]{3,2,1,0:T(8,128)(2,1)}, bf16[3,1024,128]{2,1,0:T(8,128)(2,1)}, bf16[3,1024,128]{2,1,0:T(8,128)(2,1)}, bf16[3,1024,128]...) custom-call(bf16[1024,768]{1,0:T(8,128)(2,1)} %bitcast.36.refs_0_.x_, ...), custom_call_target="tpu_custom_call", output_to_operand_aliasing={{0}: (5, {}), {1}: (6, {}), {2}: (7, {}), {3}: (8, {}), {4}... | custom-call | flops 5100273664 | bytes 12582912 | tf_op jit(solution)/shard_map/attention_forward/pallas_call | solution.py:832
  91.8 4.9 %all-to-all-start.2 = ((bf16[8,192,128]{2,1,0:T(8,128)(2,1)}), bf16[8,192,128]{2,1,0:T(8,128)(2,1)}, u32[]{:S(2)}, u32[]{:S(2)}) async-start(bf16[8,192,128]{2,1,0:T(8,128)(2,1)} %bitcast.249), calls=%async_computation.2 | async-start | bytes 786432 | tf_op jit(solution)/shard_map/all_to_all | solution.py:1441
  98.7 3.5 %collective-permute-done.13.third_two = bf16[4,2,2,24,768]{4,3,2,1,0:T(8,128)(2,1)} collective-permute-done((bf16[4,2,2,24,768]{4,3,2,1,0:T(8,128)(2,1)S(1)}, bf16[4,2,2,24,768]{4,3,2,1,0:T(8,128)(2,1)}, u32[]{:S(2)}, u32[]{:S(2)}) %collective-permute-start.13) | collective-permute-done | bytes 589856 | tf_op jit(solution)/shard_map/ppermute | solution.py:1268
  102.2 4.2 %all-to-all-done.2 = bf16[8,192,128]{2,1,0:T(8,128)(2,1)} async-done(((bf16[8,192,128]{2,1,0:T(8,128)(2,1)}), bf16[8,192,128]{2,1,0:T(8,128)(2,1)}, u32[]{:S(2)}, u32[]{:S(2)}) %all-to-all-start.2) | async-done | bytes 393248 | tf_op jit(solution)/shard_map/all_to_all | solution.py:1441
  109.7 1.7 collective-permute-done.19.outer_four
  111.4 22.1 %token_block.1 = (bf16[256,768]{1,0:T(8,128)(2,1)}, f32[256,768]{1,0:T(8,128)}, bf16[8,200,128]{2,1,0:T(8,128)(2,1)}, bf16[2,4,8,24,768]{4,3,2,1,0:T(8,128)(2,1)...) custom-call(s32[3]{0:T(128)} %pad_add_fusion.core_ref, ...), custom_call_target="tpu_custom_call" | custom-call | flops 8455716864 | bytes 31457280 | tf_op jit(solution)/shard_map/token_block/pallas_call | solution.py:1242
  133.8 2.9 %collective-permute-done.20 = bf16[2,8,48,768]{3,2,1,0:T(8,128)(2,1)S(1)} collective-permute-done((bf16[2,8,48,768]{3,2,1,0:T(8,128)(2,1)}, bf16[2,8,48,768]{3,2,1,0:T(8,128)(2,1)S(1)}, u32[]{:S(2)}, u32[]{:S(2)}) %collective-permute-start.20) | collective-permute-done | bytes 1179680 | tf_op jit(solution)/shard_map/ppermute | solution.py:1268
  137.2 4.4 %all-to-all-start.3 = ((bf16[8,200,128]{2,1,0:T(8,128)(2,1)}), bf16[8,200,128]{2,1,0:T(8,128)(2,1)}, u32[]{:S(2)}, u32[]{:S(2)}) async-start(bf16[8,200,128]{2,1,0:T(8,128)(2,1)} %get-tuple-element.176), calls=%async_computation.3 | async-start | bytes 819200 | tf_op jit(solution)/shard_map/all_to_all | solution.py:1471
  142.3 2.3 fusion.14
  144.6 1.9 collective-permute-start.25
  146.4 2.4 collective-permute-start.26
  149.0 1.4 fusion
  151.8 1.4 fusion.4
  153.1 2.0 collective-permute-start.24
  155.2 26.1 %attention_backward.1 = (bf16[1024,768]{1,0:T(8,128)(2,1)}, bf16[2,2,8,80,256]{4,3,2,1,0:T(8,128)(2,1)}, f32[3,8,128]{2,1,0:T(8,128)}) custom-call(s32[1]{0:T(128)} %bitcast.core_ref, bf16[2,4,200,128]{3,2,1,0:T(8,128)(2,1)} %bitcast.74.do_ref, bf16[1024,768]{1,0:T(8,128)(2,1)} %bitcast.36.refs_0_.x_ref, bf16[3,768,256]{2,1,0:T(8,128)(2,1)} %get-tuple-element.188.w_ref, ...), custom_call_target="tpu_custom_call" | custom-call | flops 13690208256 | bytes 15728640 | tf_op jit(solution)/shard_map/attention_backward/pallas_call | solution.py:866
  181.3 1.8 small_gradients.1.keep_ref
  183.1 2.0 slice_bitcast_fusion
  185.2 3.6 %all-to-all-start.4 = ((bf16[4,2,128,768]{3,2,1,0:T(8,128)(2,1)}), bf16[4,2,128,768]{3,2,1,0:T(8,128)(2,1)S(1)}, u32[]{:S(2)}, u32[]{:S(2)}) async-start(bf16[4,2,128,768]{3,2,1,0:T(8,128)(2,1)} %bitcast.248), calls=%async_computation.4 | async-start | bytes 3145728 | tf_op jit(solution)/shard_map/all_to_all | solution.py:1291
  188.8 1.5 fusion.3
  190.3 2.6 %fusion.7 = (bf16[2,72,768]{2,1,0:T(8,128)(2,1)S(1)}, bf16[2,72,768]{2,1,0:T(8,128)(2,1)}, bf16[2,72,768]{2,1,0:T(8,128)(2,1)}) fusion(s32[]{:T(128)S(6)} %select_n.356, bf16[2,4,2,72,768]{4,3,2,1,0:T(8,128)(2,1)} %bitcast.72, s32[]{:T(128)S(6)} %select_n.365, s32[]{:T(128)S(6)} %select_n.363, bf16[2,4,2,72,768]{4,3,2,1,0:T(8,128)(2,1)} %bitcast.244, ...), kind=kLoop, calls=%fused_computation.41 | loop fusion | flops 1990656 | bytes 2654236 | tf_op jit(solution)/shard_map/convert_element_type | solution.py:1303
  192.9 2.3 row_sum.2
  197.7 2.0 collective-permute-start.34
  199.7 1.5 collective-permute-start.31
  201.1 1.5 collective-permute-start.32
  202.7 1.4 collective-permute-start.33
  204.1 10.1 %all-to-all-done.4 = bf16[4,2,128,768]{3,2,1,0:T(8,128)(2,1)S(1)} async-done(((bf16[4,2,128,768]{3,2,1,0:T(8,128)(2,1)}), bf16[4,2,128,768]{3,2,1,0:T(8,128)(2,1)S(1)}, u32[]{:S(2)}, u32[]{:S(2)}) %all-to-all-start.4) | async-done | bytes 1572896 | tf_op jit(solution)/shard_map/all_to_all | solution.py:1291
  215.6 2.4 row_sum.3
  218.0 4.4 %all-to-all-start.5 = ((bf16[8,80,256]{2,1,0:T(8,128)(2,1)}), bf16[8,80,256]{2,1,0:T(8,128)(2,1)S(1)}, u32[]{:S(2)}, u32[]{:S(2)}) async-start(bf16[8,80,256]{2,1,0:T(8,128)(2,1)} %row_sum.3), calls=%async_computation.5 | async-start | bytes 655360 | tf_op jit(solution)/shard_map/all_to_all | solution.py:1534
  222.4 1.3 fusion.15
  224.8 1.7 fusion.2
  227.3 2.0 collective-permute-start.36
  229.4 2.4 collective-permute-start.37
  231.9 1.3 fusion.18
  235.3 2.7 %collective-permute-done.35 = bf16[72,768]{1,0:T(8,128)(2,1)S(1)} collective-permute-done((bf16[72,768]{1,0:T(8,128)(2,1)S(1)}, bf16[72,768]{1,0:T(8,128)(2,1)S(1)}, u32[]{:S(2)}, u32[]{:S(2)}) %collective-permute-start.35) | collective-permute-done | bytes 110624 | tf_op jit(solution)/shard_map/ppermute | solution.py:1268
  238.0 2.0 collective-permute-start.40
  240.0 1.3 fusion.19
  244.2 2.5 all-to-all-done.5.block_ref
  247.4 1.8 finish_columns.1
  (149 shorter events, 32.8 us)
Async XLA Ops:
  0.7 13.3 %copy-start.12 = (s32[2]{0:T(128)S(1)}, s32[2]{0:T(128)}, u32[]{:S(2)}) copy-start(s32[2]{0:T(128)} %param.25) | copy-start | bytes 28
  1.6 15.4 %collective-permute-start = (bf16[128,768]{1,0:T(8,128)(2,1)S(1)}, bf16[128,768]{1,0:T(8,128)(2,1)S(1)}, u32[]{:S(2)}, u32[]{:S(2)}) collective-permute-start(bf16[128,768]{1,0:T(8,128)(2,1)S(1)} %dynamic-slice_bitcast_fusion), channel_id=1, source_target_pairs={{0,4},{1,5},{2,6},{3,7},{4,0},{5,1},{6,2},{7,3},{8,12},{9,13},{10,... | collective-permute-start | bytes 589832 | tf_op jit(solution)/shard_map/ppermute | solution.py:1268
  9.1 14.6 %all-to-all-start = ((bf16[8,80,256]{2,1,0:T(8,128)(2,1)}), bf16[8,80,256]{2,1,0:T(8,128)(2,1)S(1)}, u32[]{:S(2)}, u32[]{:S(2)}) async-start(bf16[8,80,256]{2,1,0:T(8,128)(2,1)} %get-tuple-element.134), calls=%async_computation | async-start | bytes 655360 | tf_op jit(solution)/shard_map/all_to_all | solution.py:1380
  15.0 2.1 copy-start.10
  15.0 6.7 %copy-start.11 = (bf16[24,768]{1,0:T(8,128)(2,1)S(1)}, bf16[24,768]{1,0:T(8,128)(2,1)}, u32[]{:S(2)}) copy-start(bf16[24,768]{1,0:T(8,128)(2,1)} %get-tuple-element.139) | copy-start | bytes 110596
  15.0 10.2 %copy-start.9 = (bf16[2,128,768]{2,1,0:T(8,128)(2,1)S(1)}, bf16[2,128,768]{2,1,0:T(8,128)(2,1)}, u32[]{:S(2)}) copy-start(bf16[2,128,768]{2,1,0:T(8,128)(2,1)} %param.23) | copy-start | bytes 1179652
  17.0 17.2 %collective-permute-start.3 = (bf16[192,768]{1,0:T(8,128)(2,1)S(1)}, bf16[192,768]{1,0:T(8,128)(2,1)S(1)}, u32[]{:S(2)}, u32[]{:S(2)}) collective-permute-start(bf16[192,768]{1,0:T(8,128)(2,1)S(1)} %copy-done.10), channel_id=1, source_target_pairs={{0,2},{1,3},{2,0},{3,1},{4,6},{5,7},{6,4},{7,5},{8,10},{9,11},{10,... | collective-permute-start | bytes 884744 | tf_op jit(solution)/shard_map/ppermute | solution.py:1268
  19.1 23.5 %collective-permute-start.4 = (bf16[192,768]{1,0:T(8,128)(2,1)S(1)}, bf16[192,768]{1,0:T(8,128)(2,1)S(1)}, u32[]{:S(2)}, u32[]{:S(2)}) collective-permute-start(bf16[192,768]{1,0:T(8,128)(2,1)S(1)} %copy-done.10), channel_id=1, source_target_pairs={{0,4},{1,5},{2,6},{3,7},{4,0},{5,1},{6,2},{7,3},{8,12},{9,13},{10,... | collective-permute-start | bytes 884744 | tf_op jit(solution)/shard_map/ppermute | solution.py:1268
  21.7 20.9 %collective-permute-start.5 = (bf16[192,768]{1,0:T(8,128)(2,1)S(1)}, bf16[192,768]{1,0:T(8,128)(2,1)S(1)}, u32[]{:S(2)}, u32[]{:S(2)}) collective-permute-start(bf16[192,768]{1,0:T(8,128)(2,1)S(1)} %copy-done.10), channel_id=1, source_target_pairs={{0,6},{1,7},{2,4},{3,5},{4,2},{5,3},{6,0},{7,1},{8,14},{9,15},{10,... | collective-permute-start | bytes 884744 | tf_op jit(solution)/shard_map/ppermute | solution.py:1268
  21.7 10.4 %collective-permute-start.6 = (bf16[24,768]{1,0:T(8,128)(2,1)S(1)}, bf16[24,768]{1,0:T(8,128)(2,1)S(1)}, u32[]{:S(2)}, u32[]{:S(2)}) collective-permute-start(bf16[24,768]{1,0:T(8,128)(2,1)S(1)} %copy-done.11), channel_id=1, source_target_pairs={{0,16},{8,24},{16,0},{24,8},{1,17},{9,25},{17,1},{25,9},{2,18},{10... | collective-permute-start | bytes 110600 | tf_op jit(solution)/shard_map/ppermute | solution.py:1268
  23.7 8.3 %collective-permute-start.1 = (bf16[1,8,80,256]{3,2,1,0:T(8,128)(2,1)S(1)}, bf16[1,8,80,256]{3,2,1,0:T(8,128)(2,1)S(1)}, u32[]{:S(2)}, u32[]{:S(2)}) collective-permute-start(bf16[1,8,80,256]{3,2,1,0:T(8,128)(2,1)S(1)} %bitcast.250), channel_id=1, source_target_pairs={{0,16},{8,24},{16,0},{24,8},{1,17},{9,25},{17,1},{25,9},{2,18},{10... | collective-permute-start | bytes 983048 | tf_op jit(solution)/shard_map/ppermute | solution.py:1268
  26.5 30.4 %all-to-all-start.1 = ((bf16[4,2,128,768]{3,2,1,0:T(8,128)(2,1)}), bf16[4,2,128,768]{3,2,1,0:T(8,128)(2,1)}, u32[]{:S(2)}, u32[]{:S(2)}) async-start(bf16[4,2,128,768]{3,2,1,0:T(8,128)(2,1)} %broadcast_in_dim.77), calls=%async_computation.1 | async-start | bytes 3145728 | tf_op jit(solution)/shard_map/all_to_all | solution.py:1291
  32.2 33.8 %collective-permute-start.9 = (bf16[2,24,768]{2,1,0:T(8,128)(2,1)S(1)}, bf16[2,24,768]{2,1,0:T(8,128)(2,1)S(1)}, u32[]{:S(2)}, u32[]{:S(2)}) collective-permute-start(bf16[2,24,768]{2,1,0:T(8,128)(2,1)S(1)} %pad_maximum_fusion.11), channel_id=1, source_target_pairs={{0,1},{1,0},{2,3},{3,2},{4,5},{5,4},{6,7},{7,6},{8,9},{9,8},{10,11... | collective-permute-start | bytes 221192 | tf_op jit(solution)/shard_map/ppermute | solution.py:1268
  42.6 4.8 %collective-permute-start.2 = (bf16[2,1,8,80,256]{4,3,2,0,1:T(8,128)(2,1)S(1)}, bf16[2,1,8,80,256]{4,3,2,0,1:T(8,128)(2,1)S(1)}, u32[]{:S(2)}, u32[]{:S(2)}) collective-permute-start(bf16[2,1,8,80,256]{4,3,2,0,1:T(8,128)(2,1)S(1)} %pad_maximum_fusion.5), channel_id=1, source_target_pairs={{0,8},{8,0},{16,24},{24,16},{1,9},{9,1},{17,25},{25,17},{2,10},{10... | collective-permute-start | bytes 1966088 | tf_op jit(solution)/shard_map/ppermute | solution.py:1268
  43.3 4.3 %copy-start = (bf16[2,2,192,768]{3,2,1,0:T(8,128)(2,1)}, bf16[2,2,192,768]{3,2,1,0:T(8,128)(2,1)S(1)}, u32[]{:S(2)}) copy-start(bf16[2,2,192,768]{3,2,1,0:T(8,128)(2,1)S(1)} %reverse_select_fusion) | copy-start | bytes 3538948
  44.5 21.5 %collective-permute-start.7 = (bf16[4,96,768]{2,1,0:T(8,128)(2,1)}, bf16[4,96,768]{2,1,0:T(8,128)(2,1)S(1)}, u32[]{:S(2)}, u32[]{:S(2)}) collective-permute-start(bf16[4,96,768]{2,1,0:T(8,128)(2,1)} %get-tuple-element.259), channel_id=1, source_target_pairs={{0,1},{1,0},{2,3},{3,2},{4,5},{5,4},{6,7},{7,6},{8,9},{9,8},{10,11... | collective-permute-start | bytes 1769480 | tf_op jit(solution)/shard_map/ppermute | solution.py:1268
  45.9 20.1 %collective-permute-start.8 = (bf16[4,96,768]{2,1,0:T(8,128)(2,1)}, bf16[4,96,768]{2,1,0:T(8,128)(2,1)}, u32[]{:S(2)}, u32[]{:S(2)}) collective-permute-start(bf16[4,96,768]{2,1,0:T(8,128)(2,1)} %get-tuple-element.258), channel_id=1, source_target_pairs={{0,16},{8,24},{16,0},{24,8},{1,17},{9,25},{17,1},{25,9},{2,18},{10... | collective-permute-start | bytes 1769480 | tf_op jit(solution)/shard_map/ppermute | solution.py:1268
  66.7 25.0 %collective-permute-start.10 = (bf16[2,2,24,768]{3,2,0,1:T(8,128)(2,1)}, bf16[2,2,24,768]{3,2,0,1:T(8,128)(2,1)S(1)}, u32[]{:S(2)}, u32[]{:S(2)}) collective-permute-start(bf16[2,2,24,768]{3,2,0,1:T(8,128)(2,1)} %get-tuple-element.280), channel_id=1, source_target_pairs={{0,2},{1,3},{2,0},{3,1},{4,6},{5,7},{6,4},{7,5},{8,10},{9,11},{10,... | collective-permute-start | bytes 442376 | tf_op jit(solution)/shard_map/ppermute | solution.py:1268
  68.6 23.2 %collective-permute-start.11 = (bf16[2,2,24,768]{3,2,0,1:T(8,128)(2,1)}, bf16[2,2,24,768]{3,2,0,1:T(8,128)(2,1)}, u32[]{:S(2)}, u32[]{:S(2)}) collective-permute-start(bf16[2,2,24,768]{3,2,0,1:T(8,128)(2,1)} %get-tuple-element.280), channel_id=1, source_target_pairs={{0,4},{1,5},{2,6},{3,7},{4,0},{5,1},{6,2},{7,3},{8,12},{9,13},{10,... | collective-permute-start | bytes 442376 | tf_op jit(solution)/shard_map/ppermute | solution.py:1268
  71.0 20.8 %collective-permute-start.12 = (bf16[2,2,24,768]{3,2,0,1:T(8,128)(2,1)}, bf16[2,2,24,768]{3,2,0,1:T(8,128)(2,1)}, u32[]{:S(2)}, u32[]{:S(2)}) collective-permute-start(bf16[2,2,24,768]{3,2,0,1:T(8,128)(2,1)} %get-tuple-element.280), channel_id=1, source_target_pairs={{0,6},{1,7},{2,4},{3,5},{4,2},{5,3},{6,0},{7,1},{8,14},{9,15},{10,... | collective-permute-start | bytes 442376 | tf_op jit(solution)/shard_map/ppermute | solution.py:1268
  73.9 32.6 %collective-permute-start.17 = (bf16[2,4,96,768]{3,2,1,0:T(8,128)(2,1)}, bf16[2,4,96,768]{3,2,1,0:T(8,128)(2,1)}, u32[]{:S(2)}, u32[]{:S(2)}) collective-permute-start(bf16[2,4,96,768]{3,2,1,0:T(8,128)(2,1)} %pad_maximum_fusion.4.outer_one), channel_id=1, source_target_pairs={{0,1},{1,0},{2,3},{3,2},{4,5},{5,4},{6,7},{7,6},{8,9},{9,8},{10,11... | collective-permute-start | bytes 3538952 | tf_op jit(solution)/shard_map/ppermute | solution.py:1268
  76.4 30.1 %collective-permute-start.16 = (bf16[2,4,96,768]{3,2,1,0:T(8,128)(2,1)}, bf16[2,4,96,768]{3,2,1,0:T(8,128)(2,1)}, u32[]{:S(2)}, u32[]{:S(2)}) collective-permute-start(bf16[2,4,96,768]{3,2,1,0:T(8,128)(2,1)} %pad_maximum_fusion.3.inner_one), channel_id=1, source_target_pairs={{0,16},{8,24},{16,0},{24,8},{1,17},{9,25},{17,1},{25,9},{2,18},{10... | collective-permute-start | bytes 3538952 | tf_op jit(solution)/shard_map/ppermute | solution.py:1268
  91.8 14.7 %all-to-all-start.2 = ((bf16[8,192,128]{2,1,0:T(8,128)(2,1)}), bf16[8,192,128]{2,1,0:T(8,128)(2,1)}, u32[]{:S(2)}, u32[]{:S(2)}) async-start(bf16[8,192,128]{2,1,0:T(8,128)(2,1)} %bitcast.249), calls=%async_computation.2 | async-start | bytes 786432 | tf_op jit(solution)/shard_map/all_to_all | solution.py:1441
  96.7 9.7 %collective-permute-start.14 = (bf16[2,4,96,768]{3,2,1,0:T(8,128)(2,1)}, bf16[2,4,96,768]{3,2,1,0:T(8,128)(2,1)S(1)}, u32[]{:S(2)}, u32[]{:S(2)}) collective-permute-start(bf16[2,4,96,768]{3,2,1,0:T(8,128)(2,1)} %pad_maximum_fusion.3.inner_one), channel_id=1, source_target_pairs={{0,8},{8,0},{16,24},{24,16},{1,9},{9,1},{17,25},{25,17},{2,10},{10... | collective-permute-start | bytes 3538952 | tf_op jit(solution)/shard_map/ppermute | solution.py:1268
  96.7 9.7 %collective-permute-start.15 = (bf16[2,4,96,768]{3,2,1,0:T(8,128)(2,1)}, bf16[2,4,96,768]{3,2,1,0:T(8,128)(2,1)S(1)}, u32[]{:S(2)}, u32[]{:S(2)}) collective-permute-start(bf16[2,4,96,768]{3,2,1,0:T(8,128)(2,1)} %pad_maximum_fusion.4.outer_one), channel_id=1, source_target_pairs={{0,8},{8,0},{16,24},{24,16},{1,9},{9,1},{17,25},{25,17},{2,10},{10... | collective-permute-start | bytes 3538952 | tf_op jit(solution)/shard_map/ppermute | solution.py:1268
  98.5 12.9 %copy-start.8 = (bf16[2,2,2,2,24,768]{5,4,3,2,1,0:T(8,128)(2,1)}, bf16[2,2,2,2,24,768]{5,4,3,2,1,0:T(8,128)(2,1)S(1)}, u32[]{:S(2)}) copy-start(bf16[2,2,2,2,24,768]{5,4,3,2,1,0:T(8,128)(2,1)S(1)} %reverse_select_fusion.2) | copy-start | bytes 1769476
  98.6 3.7 %collective-permute-start.13 = (bf16[4,2,2,24,768]{4,3,2,1,0:T(8,128)(2,1)S(1)}, bf16[4,2,2,24,768]{4,3,2,1,0:T(8,128)(2,1)}, u32[]{:S(2)}, u32[]{:S(2)}) collective-permute-start(bf16[4,2,2,24,768]{4,3,2,1,0:T(8,128)(2,1)S(1)} %bitcast.260), channel_id=1, source_target_pairs={{0,8},{8,0},{16,24},{24,16},{1,9},{9,1},{17,25},{25,17},{2,10},{10... | collective-permute-start | bytes 1769480 | tf_op jit(solution)/shard_map/ppermute | solution.py:1268
  106.4 1.0 copy-start.13
  106.5 1.9 copy-start.14
  106.5 3.3 %collective-permute-start.18 = (bf16[2,4,96,768]{3,2,1,0:T(8,128)(2,1)}, bf16[2,4,96,768]{3,2,1,0:T(8,128)(2,1)}, u32[]{:S(2)}, u32[]{:S(2)}) collective-permute-start(bf16[2,4,96,768]{3,2,1,0:T(8,128)(2,1)} %collective-permute-done.16.inner_three), channel_id=1, source_target_pairs={{0,8},{8,0},{16,24},{24,16},{1,9},{9,1},{17,25},{25,17},{2,10},{10... | collective-permute-start | bytes 3538952 | tf_op jit(solution)/shard_map/ppermute | solution.py:1268
  106.6 4.9 %collective-permute-start.19 = (bf16[2,4,96,768]{3,2,1,0:T(8,128)(2,1)}, bf16[2,4,96,768]{3,2,1,0:T(8,128)(2,1)}, u32[]{:S(2)}, u32[]{:S(2)}) collective-permute-start(bf16[2,4,96,768]{3,2,1,0:T(8,128)(2,1)} %collective-permute-done.17.outer_three), channel_id=1, source_target_pairs={{0,8},{8,0},{16,24},{24,16},{1,9},{9,1},{17,25},{25,17},{2,10},{10... | collective-permute-start | bytes 3538952 | tf_op jit(solution)/shard_map/ppermute | solution.py:1268
  133.6 3.1 %collective-permute-start.20 = (bf16[2,8,48,768]{3,2,1,0:T(8,128)(2,1)}, bf16[2,8,48,768]{3,2,1,0:T(8,128)(2,1)S(1)}, u32[]{:S(2)}, u32[]{:S(2)}) collective-permute-start(bf16[2,8,48,768]{3,2,1,0:T(8,128)(2,1)} %get-tuple-element.180), channel_id=1, source_target_pairs={{0,8},{8,0},{16,24},{24,16},{1,9},{9,1},{17,25},{25,17},{2,10},{10... | collective-permute-start | bytes 3538952 | tf_op jit(solution)/shard_map/ppermute | solution.py:1268
  136.7 7.9 %copy-start.6 = (bf16[2,8,48,768]{3,2,1,0:T(8,128)(2,1)}, bf16[2,8,48,768]{3,2,1,0:T(8,128)(2,1)S(1)}, u32[]{:S(2)}) copy-start(bf16[2,8,48,768]{3,2,1,0:T(8,128)(2,1)S(1)} %collective-permute-done.20) | copy-start | bytes 3538948
  136.7 12.3 %collective-permute-start.21 = (bf16[2,4,8,24,768]{4,3,2,1,0:T(8,128)(2,1)}, bf16[2,4,8,24,768]{4,3,2,1,0:T(8,128)(2,1)S(1)}, u32[]{:S(2)}, u32[]{:S(2)}) collective-permute-start(bf16[2,4,8,24,768]{4,3,2,1,0:T(8,128)(2,1)} %get-tuple-element.181), channel_id=1, source_target_pairs={{0,8},{8,0},{16,24},{24,16},{1,9},{9,1},{17,25},{25,17},{2,10},{10... | collective-permute-start | bytes 7077896 | tf_op jit(solution)/shard_map/ppermute | solution.py:1268
  136.8 14.9 %collective-permute-start.22 = (bf16[2,8,72,768]{3,2,1,0:T(8,128)(2,1)}, bf16[2,8,72,768]{3,2,1,0:T(8,128)(2,1)}, u32[]{:S(2)}, u32[]{:S(2)}) collective-permute-start(bf16[2,8,72,768]{3,2,1,0:T(8,128)(2,1)} %get-tuple-element.185), channel_id=1, source_target_pairs={{0,8},{8,0},{16,24},{24,16},{1,9},{9,1},{17,25},{25,17},{2,10},{10... | collective-permute-start | bytes 5308424 | tf_op jit(solution)/shard_map/ppermute | solution.py:1268
  137.2 17.9 %all-to-all-start.3 = ((bf16[8,200,128]{2,1,0:T(8,128)(2,1)}), bf16[8,200,128]{2,1,0:T(8,128)(2,1)}, u32[]{:S(2)}, u32[]{:S(2)}) async-start(bf16[8,200,128]{2,1,0:T(8,128)(2,1)} %get-tuple-element.176), calls=%async_computation.3 | async-start | bytes 819200 | tf_op jit(solution)/shard_map/all_to_all | solution.py:1471
  142.3 6.7 %copy-start.1 = (bf16[2,4,8,24,768]{4,3,2,1,0:T(8,128)(2,1)S(1)}, bf16[2,4,8,24,768]{4,3,2,1,0:T(8,128)(2,1)}, u32[]{:S(2)}) copy-start(bf16[2,4,8,24,768]{4,3,2,1,0:T(8,128)(2,1)} %get-tuple-element.177) | copy-start | bytes 7077892
  144.6 36.7 %collective-permute-start.25 = (bf16[2,2,48,768]{3,2,1,0:T(8,128)(2,1)}, bf16[2,2,48,768]{3,2,1,0:T(8,128)(2,1)}, u32[]{:S(2)}, u32[]{:S(2)}) collective-permute-start(bf16[2,2,48,768]{3,2,1,0:T(8,128)(2,1)} %get-tuple-element.251), channel_id=1, source_target_pairs={{0,2},{1,3},{2,0},{3,1},{4,6},{5,7},{6,4},{7,5},{8,10},{9,11},{10,... | collective-permute-start | bytes 884744 | tf_op jit(solution)/shard_map/ppermute | solution.py:1268
  146.4 34.9 %collective-permute-start.26 = (bf16[2,2,48,768]{3,2,1,0:T(8,128)(2,1)}, bf16[2,2,48,768]{3,2,1,0:T(8,128)(2,1)}, u32[]{:S(2)}, u32[]{:S(2)}) collective-permute-start(bf16[2,2,48,768]{3,2,1,0:T(8,128)(2,1)} %get-tuple-element.250), channel_id=1, source_target_pairs={{0,4},{1,5},{2,6},{3,7},{4,0},{5,1},{6,2},{7,3},{8,12},{9,13},{10,... | collective-permute-start | bytes 884744 | tf_op jit(solution)/shard_map/ppermute | solution.py:1268
  148.8 32.5 %collective-permute-start.27 = (bf16[2,2,48,768]{3,2,1,0:T(8,128)(2,1)}, bf16[2,2,48,768]{3,2,1,0:T(8,128)(2,1)}, u32[]{:S(2)}, u32[]{:S(2)}) collective-permute-start(bf16[2,2,48,768]{3,2,1,0:T(8,128)(2,1)} %get-tuple-element.249), channel_id=1, source_target_pairs={{0,6},{1,7},{2,4},{3,5},{4,2},{5,3},{6,0},{7,1},{8,14},{9,15},{10,... | collective-permute-start | bytes 884744 | tf_op jit(solution)/shard_map/ppermute | solution.py:1268
  149.0 1.8 copy-start.3
  149.0 2.8 %copy-start.4 = (bf16[2,8,72,768]{3,2,1,0:T(8,128)(2,1)S(1)}, bf16[2,8,72,768]{3,2,1,0:T(8,128)(2,1)}, u32[]{:S(2)}) copy-start(bf16[2,8,72,768]{3,2,1,0:T(8,128)(2,1)} %get-tuple-element.184) | copy-start | bytes 5308420
  150.8 30.6 %collective-permute-start.23 = (bf16[4,4,2,24,768]{4,3,0,1,2:T(8,128)(2,1)}, bf16[4,4,2,24,768]{4,3,0,1,2:T(8,128)(2,1)}, u32[]{:S(2)}, u32[]{:S(2)}) collective-permute-start(bf16[4,4,2,24,768]{4,3,0,1,2:T(8,128)(2,1)} %fusion), channel_id=1, source_target_pairs={{0,16},{8,24},{16,0},{24,8},{1,17},{9,25},{17,1},{25,9},{2,18},{10... | collective-permute-start | bytes 3538952 | tf_op jit(solution)/shard_map/ppermute | solution.py:1268
  153.1 28.2 %collective-permute-start.24 = (bf16[2,4,72,768]{3,2,1,0:T(8,128)(2,1)S(1)}, bf16[2,4,72,768]{3,2,1,0:T(8,128)(2,1)}, u32[]{:S(2)}, u32[]{:S(2)}) collective-permute-start(bf16[2,4,72,768]{3,2,1,0:T(8,128)(2,1)S(1)} %fusion.4), channel_id=1, source_target_pairs={{0,1},{1,0},{2,3},{3,2},{4,5},{5,4},{6,7},{7,6},{8,9},{9,8},{10,11... | collective-permute-start | bytes 2654216 | tf_op jit(solution)/shard_map/ppermute | solution.py:1268
  181.3 3.8 %copy-start.2 = (bf16[2,4,8,24,768]{4,3,2,1,0:T(8,128)(2,1)S(1)}, bf16[2,4,8,24,768]{4,3,2,1,0:T(8,128)(2,1)}, u32[]{:S(2)}) copy-start(bf16[2,4,8,24,768]{4,3,2,1,0:T(8,128)(2,1)} %get-tuple-element.177) | copy-start | bytes 7077892
  185.1 7.8 %collective-permute-start.29 = (bf16[2,8,80,256]{3,2,1,0:T(8,128)(2,1)}, bf16[2,8,80,256]{3,2,1,0:T(8,128)(2,1)}, u32[]{:S(2)}, u32[]{:S(2)}) collective-permute-start(bf16[2,8,80,256]{3,2,1,0:T(8,128)(2,1)} %slice_bitcast_fusion), channel_id=1, source_target_pairs={{0,8},{8,0},{16,24},{24,16},{1,9},{9,1},{17,25},{25,17},{2,10},{10... | collective-permute-start | bytes 1966088 | tf_op jit(solution)/shard_map/ppermute | solution.py:1268
  185.2 28.9 %all-to-all-start.4 = ((bf16[4,2,128,768]{3,2,1,0:T(8,128)(2,1)}), bf16[4,2,128,768]{3,2,1,0:T(8,128)(2,1)S(1)}, u32[]{:S(2)}, u32[]{:S(2)}) async-start(bf16[4,2,128,768]{3,2,1,0:T(8,128)(2,1)} %bitcast.248), calls=%async_computation.4 | async-start | bytes 3145728 | tf_op jit(solution)/shard_map/all_to_all | solution.py:1291
  195.2 19.7 %collective-permute-start.30 = (bf16[8,80,256]{2,1,0:T(8,128)(2,1)}, bf16[8,80,256]{2,1,0:T(8,128)(2,1)S(1)}, u32[]{:S(2)}, u32[]{:S(2)}) collective-permute-start(bf16[8,80,256]{2,1,0:T(8,128)(2,1)} %row_sum.2), channel_id=1, source_target_pairs={{0,16},{8,24},{16,0},{24,8},{1,17},{9,25},{17,1},{25,9},{2,18},{10... | collective-permute-start | bytes 983048 | tf_op jit(solution)/shard_map/ppermute | solution.py:1268
  197.7 26.0 %collective-permute-start.34 = (bf16[4,4,24,768]{3,2,0,1:T(8,128)(2,1)S(1)}, bf16[4,4,24,768]{3,2,0,1:T(8,128)(2,1)}, u32[]{:S(2)}, u32[]{:S(2)}) collective-permute-start(bf16[4,4,24,768]{3,2,0,1:T(8,128)(2,1)S(1)} %fusion.3), channel_id=1, source_target_pairs={{0,1},{1,0},{2,3},{3,2},{4,5},{5,4},{6,7},{7,6},{8,9},{9,8},{10,11... | collective-permute-start | bytes 1769480 | tf_op jit(solution)/shard_map/ppermute | solution.py:1268
  199.7 27.7 %collective-permute-start.31 = (bf16[2,72,768]{2,1,0:T(8,128)(2,1)}, bf16[2,72,768]{2,1,0:T(8,128)(2,1)}, u32[]{:S(2)}, u32[]{:S(2)}) collective-permute-start(bf16[2,72,768]{2,1,0:T(8,128)(2,1)} %get-tuple-element.246), channel_id=1, source_target_pairs={{0,2},{1,3},{2,0},{3,1},{4,6},{5,7},{6,4},{7,5},{8,10},{9,11},{10,... | collective-permute-start | bytes 663560 | tf_op jit(solution)/shard_map/ppermute | solution.py:1268
  201.1 28.2 %collective-permute-start.32 = (bf16[2,72,768]{2,1,0:T(8,128)(2,1)}, bf16[2,72,768]{2,1,0:T(8,128)(2,1)}, u32[]{:S(2)}, u32[]{:S(2)}) collective-permute-start(bf16[2,72,768]{2,1,0:T(8,128)(2,1)} %get-tuple-element.245), channel_id=1, source_target_pairs={{0,4},{1,5},{2,6},{3,7},{4,0},{5,1},{6,2},{7,3},{8,12},{9,13},{10,... | collective-permute-start | bytes 663560 | tf_op jit(solution)/shard_map/ppermute | solution.py:1268
  202.7 29.1 %collective-permute-start.33 = (bf16[2,72,768]{2,1,0:T(8,128)(2,1)S(1)}, bf16[2,72,768]{2,1,0:T(8,128)(2,1)}, u32[]{:S(2)}, u32[]{:S(2)}) collective-permute-start(bf16[2,72,768]{2,1,0:T(8,128)(2,1)S(1)} %get-tuple-element.244), channel_id=1, source_target_pairs={{0,6},{1,7},{2,4},{3,5},{4,2},{5,3},{6,0},{7,1},{8,14},{9,15},{10,... | collective-permute-start | bytes 663560 | tf_op jit(solution)/shard_map/ppermute | solution.py:1268
  214.9 0.7 copy-start.15
  214.9 36.2 %collective-permute-start.28 = (bf16[128,768]{1,0:T(8,128)(2,1)}, bf16[128,768]{1,0:T(8,128)(2,1)}, u32[]{:S(2)}, u32[]{:S(2)}) collective-permute-start(bf16[128,768]{1,0:T(8,128)(2,1)} %dynamic-slice_reduce_fusion), channel_id=1, source_target_pairs={{0,4},{1,5},{2,6},{3,7},{4,0},{5,1},{6,2},{7,3},{8,12},{9,13},{10,... | collective-permute-start | bytes 589832 | tf_op jit(solution)/shard_map/ppermute | solution.py:1268
  218.0 28.7 %all-to-all-start.5 = ((bf16[8,80,256]{2,1,0:T(8,128)(2,1)}), bf16[8,80,256]{2,1,0:T(8,128)(2,1)S(1)}, u32[]{:S(2)}, u32[]{:S(2)}) async-start(bf16[8,80,256]{2,1,0:T(8,128)(2,1)} %row_sum.3), calls=%async_computation.5 | async-start | bytes 655360 | tf_op jit(solution)/shard_map/all_to_all | solution.py:1534
  223.7 9.5 %collective-permute-start.39 = (bf16[2,48,768]{2,1,0:T(8,128)(2,1)S(1)}, bf16[2,48,768]{2,1,0:T(8,128)(2,1)S(1)}, u32[]{:S(2)}, u32[]{:S(2)}) collective-permute-start(bf16[2,48,768]{2,1,0:T(8,128)(2,1)S(1)} %fusion.15), channel_id=1, source_target_pairs={{0,16},{8,24},{16,0},{24,8},{1,17},{9,25},{17,1},{25,9},{2,18},{10... | collective-permute-start | bytes 442376 | tf_op jit(solution)/shard_map/ppermute | solution.py:1268
  227.3 21.9 %collective-permute-start.36 = (bf16[4,24,768]{2,1,0:T(8,128)(2,1)}, bf16[4,24,768]{2,1,0:T(8,128)(2,1)}, u32[]{:S(2)}, u32[]{:S(2)}) collective-permute-start(bf16[4,24,768]{2,1,0:T(8,128)(2,1)} %get-tuple-element.266), channel_id=1, source_target_pairs={{0,2},{1,3},{2,0},{3,1},{4,6},{5,7},{6,4},{7,5},{8,10},{9,11},{10,... | collective-permute-start | bytes 442376 | tf_op jit(solution)/shard_map/ppermute | solution.py:1268
  229.4 20.6 %collective-permute-start.37 = (bf16[4,24,768]{2,1,0:T(8,128)(2,1)}, bf16[4,24,768]{2,1,0:T(8,128)(2,1)}, u32[]{:S(2)}, u32[]{:S(2)}) collective-permute-start(bf16[4,24,768]{2,1,0:T(8,128)(2,1)} %get-tuple-element.265), channel_id=1, source_target_pairs={{0,4},{1,5},{2,6},{3,7},{4,0},{5,1},{6,2},{7,3},{8,12},{9,13},{10,... | collective-permute-start | bytes 442376 | tf_op jit(solution)/shard_map/ppermute | solution.py:1268
  231.7 18.2 %collective-permute-start.38 = (bf16[4,24,768]{2,1,0:T(8,128)(2,1)}, bf16[4,24,768]{2,1,0:T(8,128)(2,1)S(1)}, u32[]{:S(2)}, u32[]{:S(2)}) collective-permute-start(bf16[4,24,768]{2,1,0:T(8,128)(2,1)} %get-tuple-element.264), channel_id=1, source_target_pairs={{0,6},{1,7},{2,4},{3,5},{4,2},{5,3},{6,0},{7,1},{8,14},{9,15},{10,... | collective-permute-start | bytes 442376 | tf_op jit(solution)/shard_map/ppermute | solution.py:1268
  233.2 4.8 %collective-permute-start.35 = (bf16[72,768]{1,0:T(8,128)(2,1)S(1)}, bf16[72,768]{1,0:T(8,128)(2,1)S(1)}, u32[]{:S(2)}, u32[]{:S(2)}) collective-permute-start(bf16[72,768]{1,0:T(8,128)(2,1)S(1)} %fusion.18), channel_id=1, source_target_pairs={{0,16},{8,24},{16,0},{24,8},{1,17},{9,25},{17,1},{25,9},{2,18},{10... | collective-permute-start | bytes 331784 | tf_op jit(solution)/shard_map/ppermute | solution.py:1268
  238.0 4.4 %collective-permute-start.40 = (bf16[48,768]{1,0:T(8,128)(2,1)S(1)}, bf16[48,768]{1,0:T(8,128)(2,1)S(1)}, u32[]{:S(2)}, u32[]{:S(2)}) collective-permute-start(bf16[48,768]{1,0:T(8,128)(2,1)S(1)} %fusion.22), channel_id=1, source_target_pairs={{0,1},{1,0},{2,3},{3,2},{4,5},{5,4},{6,7},{7,6},{8,9},{9,8},{10,11... | collective-permute-start | bytes 221192 | tf_op jit(solution)/shard_map/ppermute | solution.py:1268
  246.7 0.7 copy-start.5
  250.0 2.2 copy-start.7
